TPU v7x, 32 devices: a whole 2x2x4 slice. The times are simulated.
32 devices in a mesh: section: 4 (over z), dp: 4 (over y, core), mp: 2 (over x).
Axes of the slice: x: 2, y: 2, z: 4, core: 2. Of those that a mesh axis runs over, the one named last changes fastest.
Arguments:
- enc_rows: bfloat16 [4096, 4096], P(('section', 'dp'), 'mp'), may hold values from -6 to 6
- enc_len: int32 [64], P(('section', 'dp')), may hold values from 16 to 64
- dest_dp: int32 [64], P(('section', 'dp')), may hold values from 0 to 3, as said below
- peer_counts: int32 [16, 4], P(('section', 'dp')), may hold values from 0 to 2, as said below
- queries: bfloat16 [4096, 4096], P(('section', 'dp'), 'mp'), may hold values from -50 to 50
- ctx_grad: bfloat16 [4096, 4096], P(('section', 'dp'), 'mp'), may hold values from -6 to 6
- w_key: bfloat16 [4096, 4096], P(('section', 'dp'), 'mp'), may hold values from -0.09375 to 0.09375
- w_value: bfloat16 [4096, 4096], P(('section', 'dp'), 'mp'), may hold values from -0.09375 to 0.09375
Outputs:
- context: bfloat16 [4096, 4096], P(('section', 'dp'), 'mp')
- enc_grad: bfloat16 [4096, 4096], P(('section', 'dp'), 'mp')
Inputs may be any that keep to these rules, and one draw needn't show every extreme that they name: `dest_dp`: each device places at most 2 of its blocks on one decoder device of its section, some device exactly 2, and every device takes exactly 4 blocks. peer_counts agrees with dest_dp; each row sums to 4.
All inputs are finite; a program needn't handle non-finite values.
Results may differ from a plain program's by a relative error of at most 0.014.
Values may be sent and summed in bfloat16 or wider, within the bound.
No kernel may reach another device: no remote copies, remote signals or barrier semaphores. Data moves between devices by JAX's collectives and lax.ppermute only.
A program may use at most 128 MiB of HBM per device.

v0:
```python
import jax
import jax.numpy as jnp
from jax import lax
from jax.sharding import PartitionSpec as P

DH = 64
BLOCK = 64


def attend(query_rows, key_rows, value_rows, grad_rows, key_lengths):
    block_count = key_lengths.shape[0]
    head_count = query_rows.shape[1] // DH
    shape_four = (block_count, BLOCK, head_count, DH)
    query_heads = query_rows.reshape(shape_four)
    key_heads = key_rows.reshape(shape_four)
    value_heads = value_rows.reshape(shape_four)
    grad_heads = grad_rows.reshape(shape_four)
    score_scale = DH ** (-0.5)
    scores = (
        jnp.einsum("bihd,bjhd->bhij", query_heads, key_heads, preferred_element_type=jnp.float32)
        * score_scale
    )
    visible = (
        jnp.arange(BLOCK, dtype=jnp.float32)[None, None, None, :] < key_lengths[:, None, None, None]
    )
    scores = jnp.where(visible, scores, -1e30)
    row_max = jnp.max(scores, axis=-1, keepdims=True)
    weights_exp = jnp.exp(scores - row_max)
    probabilities = weights_exp / jnp.sum(weights_exp, axis=-1, keepdims=True)
    prob_bf = probabilities.astype(jnp.bfloat16)
    context = jnp.einsum(
        "bhij,bjhd->bihd", prob_bf, value_heads, preferred_element_type=jnp.float32
    ).astype(jnp.bfloat16)
    prob_grad = jnp.einsum(
        "bihd,bjhd->bhij", grad_heads, value_heads, preferred_element_type=jnp.float32
    )
    row_dot = jnp.sum(probabilities * prob_grad, axis=-1, keepdims=True)
    score_grad = (probabilities * (prob_grad - row_dot) * score_scale).astype(jnp.bfloat16)
    key_grad = jnp.einsum(
        "bhij,bihd->bjhd", score_grad, query_heads, preferred_element_type=jnp.float32
    ).astype(jnp.bfloat16)
    value_grad = jnp.einsum(
        "bhij,bihd->bjhd", prob_bf, grad_heads, preferred_element_type=jnp.float32
    ).astype(jnp.bfloat16)
    flat_shape = (block_count * BLOCK, head_count * DH)
    return (
        context.reshape(flat_shape),
        key_grad.reshape(flat_shape),
        value_grad.reshape(flat_shape),
    )


def through(table, data, lead_shape):
    moved = jnp.dot(table, data, preferred_element_type=jnp.float32).astype(jnp.bfloat16)
    return moved.reshape(lead_shape + data.shape[1:])


def shards(enc_rows, enc_len, dest_dp, peer_counts, queries, ctx_grad, w_key, w_value):
    peer_count = lax.axis_size("dp")
    model_groups = lax.axis_size("mp")
    block_count = dest_dp.shape[0]
    slot_count = max(2, -(-block_count // peer_count))
    row_count, feature_width = enc_rows.shape
    key_full, value_full = (
        lax.all_gather(w_key, ("section", "dp"), axis=0, tiled=True),
        lax.all_gather(w_value, ("section", "dp"), axis=0, tiled=True),
    )
    positions = jnp.arange(block_count, dtype=jnp.int32)
    same_dest = dest_dp[:, None] == dest_dp[None, :]
    slot_rank = jnp.sum(
        (same_dest & (positions[None, :] < positions[:, None])).astype(jnp.int32), axis=1
    )
    target_slot = dest_dp * slot_count + slot_rank
    slot_ids = jnp.arange(peer_count * slot_count, dtype=jnp.int32)
    send_map = (slot_ids[:, None] == target_slot[None, :]).astype(jnp.bfloat16)
    arrivals = peer_counts[0]
    arrival_ends = jnp.cumsum(arrivals)
    sender = jnp.sum((arrival_ends[None, :] <= positions[:, None]).astype(jnp.int32), axis=1)
    first_pos = jnp.take(arrival_ends, sender) - jnp.take(arrivals, sender)
    slot_pick = sender * slot_count + positions - first_pos
    recv_map = (slot_pick[:, None] == slot_ids[None, :]).astype(jnp.bfloat16)
    lengths_own = enc_len.astype(jnp.float32).astype(jnp.bfloat16).reshape(block_count, 1)
    all_slots = peer_count * slot_count
    outgoing = through(send_map, enc_rows.reshape(block_count, -1), (peer_count, slot_count))
    outgoing_len = through(send_map, lengths_own, (peer_count, slot_count))
    incoming, incoming_len = (
        lax.all_to_all(outgoing, "dp", split_axis=0, concat_axis=0, tiled=True),
        lax.all_to_all(outgoing_len, "dp", split_axis=0, concat_axis=0, tiled=True),
    )
    rows_here = through(recv_map, incoming.reshape(all_slots, -1), (block_count,)).reshape(
        row_count, feature_width
    )
    lengths_here = through(recv_map, incoming_len.reshape(all_slots, 1), (block_count,))[
        :, 0
    ].astype(jnp.float32)
    shard_cols = lax.all_gather(rows_here, "mp", axis=1, tiled=True)
    key_part = key_full
    value_part = value_full
    key_acc = jnp.dot(shard_cols, key_part, preferred_element_type=jnp.float32)
    value_acc = jnp.dot(shard_cols, value_part, preferred_element_type=jnp.float32)
    context, key_grad, value_grad = attend(
        queries,
        key_acc.astype(jnp.bfloat16),
        value_acc.astype(jnp.bfloat16),
        ctx_grad,
        lengths_here,
    )
    col_span = key_full.shape[0] // model_groups
    pieces_out = []
    for group_idx in range(model_groups):
        key_part = key_full[group_idx * col_span : (group_idx + 1) * col_span]
        value_part = value_full[group_idx * col_span : (group_idx + 1) * col_span]
        partial_value = lax.dot_general(
            key_grad, key_part, (((1,), (1,)), ((), ())), preferred_element_type=jnp.float32
        )
        partial_value = partial_value + lax.dot_general(
            value_grad, value_part, (((1,), (1,)), ((), ())), preferred_element_type=jnp.float32
        )
        pieces_out.append(partial_value.astype(jnp.bfloat16))
    summed = lax.psum_scatter(
        jnp.concatenate(pieces_out, axis=1), "mp", scatter_dimension=1, tiled=True
    )
    outgoing_grad = through(recv_map.T, summed.reshape(block_count, -1), (peer_count, slot_count))
    returned = lax.all_to_all(outgoing_grad, "dp", split_axis=0, concat_axis=0, tiled=True)
    enc_grad = through(send_map.T, returned.reshape(all_slots, -1), (block_count,)).reshape(
        row_count, feature_width
    )
    return (context, enc_grad)


def solution(mesh):
    placed = (
        P(("section", "dp"), "mp"),
        P(("section", "dp")),
        P(("section", "dp")),
        P(("section", "dp"), None),
        P(("section", "dp"), "mp"),
        P(("section", "dp"), "mp"),
        P(("section", "dp"), "mp"),
        P(("section", "dp"), "mp"),
    )
    return jax.shard_map(
        shards,
        mesh=mesh,
        in_specs=placed,
        out_specs=(P(("section", "dp"), "mp"), P(("section", "dp"), "mp")),
        check_vma=False,
    )
```

profile of v0, /device:TPU:0, one launch (start us, length us, event | category | flops | bytes accessed | tf_op | source)
XLA Modules:
  0.0 483.3 jit_solution(16782184727400103692)
XLA Ops:
  7.2 0.9 convert_reduce_fusion
  8.7 2.0 reshape.130
  10.7 0.7 convolution_convert_fusion.1
  11.4 2.6 reshape.131
  14.1 4.4 all-to-all-start
  20.0 24.1 %all-to-all-done = bf16[4,2,131072]{2,1,0:T(2,128)(2,1)S(1)} async-done(((bf16[4,2,131072]{2,1,0:T(2,128)(2,1)}), bf16[4,2,131072]{2,1,0:T(2,128)(2,1)S(1)}, u32[]{:S(2)}, u32[]{:S(2)}) %all-to-all-start) | async-done | bytes 2097184 | tf_op jit(solution)/shard_map/all_to_all | solution.py:87
  44.1 2.1 reshape.132
  46.3 2.3 convolution_convert_fusion.3
  48.6 1.9 reshape.133
  50.6 0.7 all-gather.6.cloned.1.call-update
  51.3 0.7 all-gather.8.cloned.1.call-update
  52.8 3.2 all-to-all-start.1
  56.3 2.2 reshape.138
  58.5 4.7 reshape.140
  63.6 21.3 %all-gather.4.cloned.1.call-done = bf16[256,4096]{1,0:T(8,128)(2,1)} async-done(((bf16[256,2048]{1,0:T(8,128)(2,1)}), bf16[256,4096]{1,0:T(8,128)(2,1)}) %all-gather.4.cloned.1.call-update) | async-done | bytes 2097168 | tf_op jit(solution)/shard_map/all_gather | solution.py:96
  84.9 129.1 %all-gather.6.cloned.1.call-done = bf16[4096,2048]{1,0:T(8,128)(2,1)} async-done(((bf16[256,2048]{1,0:T(8,128)(2,1)}), bf16[4096,2048]{1,0:T(8,128)(2,1)}) %all-gather.6.cloned.1.call-update) | async-done | bytes 16777232 | tf_op jit(solution)/shard_map/all_gather | solution.py:66
  214.0 10.9 %convolution_convert_fusion.5 = bf16[256,2048]{1,0:T(8,128)(2,1)S(1)} fusion(bf16[256,4096]{1,0:T(8,128)(2,1)} %all-gather.4.cloned.1.call-done, bf16[4096,2048]{1,0:T(8,128)(2,1)} %all-gather.6.cloned.1.call-done), kind=kOutput, calls=%fused_computation.31 | convolution fusion | flops 4295491584 | bytes 19922944 | tf_op jit(solution)/shard_map/dot_general | solution.py:100
  224.9 3.2 reshape.134
  228.1 113.1 %all-gather.8.cloned.1.call-done = bf16[4096,2048]{1,0:T(8,128)(2,1)} async-done(((bf16[256,2048]{1,0:T(8,128)(2,1)}), bf16[4096,2048]{1,0:T(8,128)(2,1)}) %all-gather.8.cloned.1.call-update) | async-done | bytes 16777232 | tf_op jit(solution)/shard_map/all_gather | solution.py:65
  341.2 10.9 %convolution_convert_fusion.4 = bf16[256,2048]{1,0:T(8,128)(2,1)S(1)} fusion(bf16[256,4096]{1,0:T(8,128)(2,1)} %all-gather.4.cloned.1.call-done, bf16[4096,2048]{1,0:T(8,128)(2,1)} %all-gather.8.cloned.1.call-done), kind=kOutput, calls=%fused_computation.30 | convolution fusion | flops 4295491584 | bytes 19922944 | tf_op jit(solution)/shard_map/dot_general | solution.py:99
  352.1 3.4 reshape.137
  355.5 2.9 fusion.31
  358.5 1.9 fusion.62
  360.4 1.1 convert_bitcast_fusion
  361.5 1.0 copy-done.7
  362.4 1.4 copy.56
  363.8 1.6 reshape.142
  365.5 5.7 %fusion.38 = f32[4,32,64,64]{3,2,1,0:T(8,128)} fusion(bf16[4,64,32,64]{3,2,1,0:T(8,128)(2,1)} %reshape.140, bf16[4,64,32,64]{3,2,1,0:T(8,128)(2,1)} %reshape.134), kind=kOutput, calls=%fused_computation.46 | convolution fusion | flops 67108864 | bytes 4194304 | tf_op jit(solution)/shard_map/bihd,bjhd->bhij/dot_general | solution.py:34
  371.1 9.8 %convert_bitcast_fusion.1 = bf16[4,64,32,64]{3,1,2,0:T(8,128)(2,1)} fusion(f32[4,32,64,64]{3,2,1,0:T(8,128)} %fusion.38, bf16[4,64,32,64]{3,2,1,0:T(8,128)(2,1)S(1)} %copy-done.2, f32[4,32,64,64]{2,3,1,0:T(8,128)} %copy-done.7, f32[4,32,64]{2,1,0:T(8,128)S(1)} %get-tuple-element.3), kind=kOutput, calls=%fused_computation.38 | convolution fusion | flops 71311424 | bytes 6324224 | tf_op jit(solution)/shard_map/bhij,bihd->bjhd/dot_general | solution.py:39
  380.9 2.9 copy.54
  383.8 2.8 reshape.141
  386.7 5.9 %fusion.2 = f32[256,2048]{1,0:T(8,128)S(1)} fusion(bf16[256,2048]{1,0:T(8,128)(2,1)S(1)} %reshape.142, bf16[4096,2048]{1,0:T(8,128)(2,1)} %all-gather.6.cloned.1.call-done), kind=kOutput, calls=%fused_computation.8 | convolution fusion | flops 2147483648 | bytes 11534336 | tf_op jit(solution)/shard_map/dot_general | solution.py:116
  392.6 5.9 %fusion.6 = f32[256,2048]{1,0:T(8,128)S(1)} fusion(bf16[256,2048]{1,0:T(8,128)(2,1)S(1)} %reshape.142, bf16[4096,2048]{1,0:T(8,128)(2,1)} %all-gather.6.cloned.1.call-done), kind=kOutput, calls=%fused_computation.12 | convolution fusion | flops 2147483648 | bytes 11534336 | tf_op jit(solution)/shard_map/dot_general | solution.py:116
  398.6 2.4 fusion.23
  400.9 2.4 fusion.26
  403.3 1.4 pad_maximum_fusion
  404.8 30.2 %reduce-scatter.2.cloned.1.call-done = bf16[256,2048]{1,0:T(8,128)(2,1)} async-done(((bf16[256,4096]{1,0:T(8,128)(2,1)}), bf16[256,2048]{1,0:T(8,128)(2,1)}) %reduce-scatter.2.cloned.1.call-update) | async-done | bytes 1048592 | tf_op jit(solution)/shard_map/reduce_scatter | solution.py:120
  434.9 2.0 reshape.143
  436.9 1.2 convolution_convert_fusion
  438.1 2.6 reshape.144
  440.7 3.8 all-to-all-start.2
  444.5 5.3 %convert_bitcast_fusion.2 = bf16[4,64,32,64]{1,3,2,0:T(8,128)(2,1)} fusion(bf16[4,64,32,64]{3,2,1,0:T(8,128)(2,1)} %reshape.134, f32[4,32,64,64]{2,3,1,0:T(8,128)} %copy-done.7, f32[4,32,64]{2,1,0:T(8,128)S(1)} %get-tuple-element.3), kind=kOutput, calls=%fused_computation.39 | convolution fusion | flops 68681728 | bytes 4227072 | tf_op jit(solution)/shard_map/bhij,bjhd->bihd/dot_general | solution.py:31
  449.8 5.2 %copy.50 = bf16[4,64,32,64]{3,2,1,0:T(8,128)(2,1)} copy(bf16[4,64,32,64]{1,3,2,0:T(8,128)(2,1)} %convert_bitcast_fusion.2) | data formatting | bytes 2097152 | tf_op jit(solution)/shard_map/convert_element_type | solution.py:33
  455.0 4.2 reshape.139
  459.3 10.9 %all-to-all-done.2 = bf16[4,2,131072]{2,1,0:T(2,128)(2,1)S(1)} async-done(((bf16[4,2,131072]{2,1,0:T(2,128)(2,1)}), bf16[4,2,131072]{2,1,0:T(2,128)(2,1)S(1)}, u32[]{:S(2)}, u32[]{:S(2)}) %all-to-all-start.2) | async-done | bytes 2097184 | tf_op jit(solution)/shard_map/all_to_all | solution.py:124
  470.2 2.1 reshape.145
  472.3 2.3 convolution_convert_fusion.2
  474.6 1.9 reshape.146
  (45 shorter events, 3.8 us)
Async XLA Ops:
  14.1 4.4 copy-start
  14.1 30.1 %all-to-all-start = ((bf16[4,2,131072]{2,1,0:T(2,128)(2,1)}), bf16[4,2,131072]{2,1,0:T(2,128)(2,1)S(1)}, u32[]{:S(2)}, u32[]{:S(2)}) async-start(bf16[4,2,131072]{2,1,0:T(2,128)(2,1)} %reshape.131), calls=%async_computation | async-start | bytes 4194304 | tf_op jit(solution)/shard_map/all_to_all | solution.py:87
  18.4 66.5 %all-gather.4.cloned.1.call-start = ((), (), s32[]{:S(2)}) async-start(), calls=%async_computation.4 | async-start | bytes 3145728 | tf_op jit(solution)/shard_map/all_gather | solution.py:96
  50.5 1.5 copy-start.6
  50.5 5.8 %copy-start.4 = (bf16[256,2048]{1,0:T(8,128)(2,1)S(1)}, bf16[256,2048]{1,0:T(8,128)(2,1)}, u32[]{:S(2)}) copy-start(bf16[256,2048]{1,0:T(8,128)(2,1)} %param.14) | copy-start | bytes 3145732
  50.5 163.4 %all-gather.6.cloned.1.call-start = ((), (), s32[]{:S(2)}) async-start(), calls=%async_computation.5 | async-start | bytes 17825792 | tf_op jit(solution)/shard_map/all_gather | solution.py:66
  51.3 290.0 %all-gather.8.cloned.1.call-start = ((), (), s32[]{:S(2)}) async-start(), calls=%async_computation.6 | async-start | bytes 17825792 | tf_op jit(solution)/shard_map/all_gather | solution.py:65
  52.8 10.4 %all-to-all-start.1 = ((bf16[4,2,1]{1,2,0:T(2,128)(2,1)}), bf16[4,2,1]{1,2,0:T(2,128)(2,1)S(1)}, u32[]{:S(2)}, u32[]{:S(2)}) async-start(bf16[4,2,1]{1,2,0:T(2,128)(2,1)} %reshape.173), calls=%async_computation.1 | async-start | bytes 4096 | tf_op jit(solution)/shard_map/all_to_all | solution.py:88
  56.0 378.9 %reduce-scatter.2.cloned.1.call-start = ((), (), s32[]{:S(2)}) async-start(), calls=%async_computation.7 | async-start | bytes 3145728 | tf_op jit(solution)/shard_map/reduce_scatter | solution.py:120
  58.5 297.1 %copy-start.1 = (bf16[4,64,32,64]{3,2,1,0:T(8,128)(2,1)}, bf16[4,64,32,64]{3,2,1,0:T(8,128)(2,1)S(1)}, u32[]{:S(2)}) copy-start(bf16[4,64,32,64]{3,2,1,0:T(8,128)(2,1)S(1)} %reshape.138) | copy-start | bytes 3145732
  358.5 1.9 copy-start.3
  360.4 2.1 copy-start.7
  365.4 5.7 %copy-start.2 = (bf16[4,64,32,64]{3,2,1,0:T(8,128)(2,1)S(1)}, bf16[4,64,32,64]{3,2,1,0:T(8,128)(2,1)}, u32[]{:S(2)}) copy-start(bf16[4,64,32,64]{3,2,1,0:T(8,128)(2,1)} %copy-done.1) | copy-start | bytes 3145732
  386.7 11.9 %slice-start = ((s8[16777216]{0:T(1024)(128)(4,1)}), s8[4194304]{0:T(1024)(128)(4,1)S(1)}, s32[]{:S(2)}) async-start(s8[16777216]{0:T(1024)(128)(4,1)} %bitcast.73), calls=%async_computation.8 | async-start | bytes 8388608
  386.7 11.9 %slice-start.1 = ((s8[16777216]{0:T(1024)(128)(4,1)}), s8[4194304]{0:T(1024)(128)(4,1)S(1)}, s32[]{:S(2)}) async-start(s8[16777216]{0:T(1024)(128)(4,1)} %bitcast.73), calls=%async_computation.9 | async-start | bytes 8388608
  386.7 11.9 %slice-start.2 = ((s8[16777216]{0:T(1024)(128)(4,1)}), s8[4194304]{0:T(1024)(128)(4,1)S(1)}, s32[]{:S(2)}) async-start(s8[16777216]{0:T(1024)(128)(4,1)} %bitcast.73), calls=%async_computation.10 | async-start | bytes 8388608
  392.6 6.0 %copy-start.5 = (bf16[256,2048]{1,0:T(8,128)(2,1)S(1)}, bf16[256,2048]{1,0:T(8,128)(2,1)}, u32[]{:S(2)}) copy-start(bf16[256,2048]{1,0:T(8,128)(2,1)} %reshape.141) | copy-start | bytes 3145732
  392.6 6.0 %slice-start.3 = ((s8[16777216]{0:T(1024)(128)(4,1)}), s8[4194304]{0:T(1024)(128)(4,1)S(1)}, s32[]{:S(2)}) async-start(s8[16777216]{0:T(1024)(128)(4,1)} %bitcast.73), calls=%async_computation.11 | async-start | bytes 8388608
  440.7 29.4 %all-to-all-start.2 = ((bf16[4,2,131072]{2,1,0:T(2,128)(2,1)}), bf16[4,2,131072]{2,1,0:T(2,128)(2,1)S(1)}, u32[]{:S(2)}, u32[]{:S(2)}) async-start(bf16[4,2,131072]{2,1,0:T(2,128)(2,1)} %reshape.144), calls=%async_computation.3 | async-start | bytes 4194304 | tf_op jit(solution)/shard_map/all_to_all | solution.py:124
Sparse Core Ops, SparseCore 0:
  50.6 34.1 all-gather.3
  87.0 126.8 all-gather.5
  216.1 125.0 all-gather.7
  404.9 29.9 reduce-scatter.1
where the time goes:
time: 489 us; the launch traced here: 483 us
  waiting for transfers between devices  330 us (67%)
  matrix products  69.9 us (14%)
  local copies, waits for them, and re-layouts  52 us (11%)
  between operations  14.3 us (3%)
  starting transfers between devices  11.7 us (2%)
  other arithmetic  5.3 us (1%)
    all_gather x1, waiting for transfers between devices, shards(): lax.all_gather(w_value, ('section', 'dp'), axis=0, tiled=True)  129 us
    all_gather x1, waiting for transfers between devices, shards(): lax.all_gather(w_key, ('section', 'dp'), axis=0, tiled=True)  113 us
    reduce_scatter x1, waiting for transfers between devices, shards(): lax.psum_scatter(jnp.concatenate(pieces_out, axis=1), 'mp', scatter_dimen...  30.2 us
    all_to_all x1, waiting for transfers between devices, shards(): lax.all_to_all(outgoing, 'dp', split_axis=0, concat_axis=0, tiled=True)  24.1 us
    all_gather x1, waiting for transfers between devices, shards(): shard_cols = lax.all_gather(rows_here, 'mp', axis=1, tiled=True)  21.3 us
    dot_general x2, matrix products, shards(): lax.dot_general(value_grad, value_part, (((1,), (1,)), ((), ())), preferr...  11.8 us
    all_to_all x1, waiting for transfers between devices, shards(): lax.all_to_all(outgoing_grad, 'dp', split_axis=0, concat_axis=0, tiled=True)  10.9 us
    dot_general x1, matrix products, shards(): jnp.dot(shard_cols, value_part, preferred_element_type=jnp.float32)  10.9 us
  transfers between devices with their start and end apart: 7, of which 6 were waited for; matrix products, arithmetic and copies ran while one was open for 8% of the time, Pallas kernels for 0%

commit v1 on v0

--- a/solution.py
+++ b/solution.py
@@ -1,10 +1,16 @@
+import functools
+
 import jax
 import jax.numpy as jnp
 from jax import lax
+from jax.experimental import pallas as pl
+from jax.experimental.pallas import tpu as pltpu
 from jax.sharding import PartitionSpec as P
 
 DH = 64
 BLOCK = 64
+F32 = jnp.float32
+BF16 = jnp.bfloat16
 
 
 def attend(query_rows, key_rows, value_rows, grad_rows, key_lengths):
@@ -55,7 +61,7 @@
     return moved.reshape(lead_shape + data.shape[1:])
 
 
-def shards(enc_rows, enc_len, dest_dp, peer_counts, queries, ctx_grad, w_key, w_value):
+def shards_general(enc_rows, enc_len, dest_dp, peer_counts, queries, ctx_grad, w_key, w_value):
     peer_count = lax.axis_size("dp")
     model_groups = lax.axis_size("mp")
     block_count = dest_dp.shape[0]
@@ -94,10 +100,8 @@
         :, 0
     ].astype(jnp.float32)
     shard_cols = lax.all_gather(rows_here, "mp", axis=1, tiled=True)
-    key_part = key_full
-    value_part = value_full
-    key_acc = jnp.dot(shard_cols, key_part, preferred_element_type=jnp.float32)
-    value_acc = jnp.dot(shard_cols, value_part, preferred_element_type=jnp.float32)
+    key_acc = jnp.dot(shard_cols, key_full, preferred_element_type=jnp.float32)
+    value_acc = jnp.dot(shard_cols, value_full, preferred_element_type=jnp.float32)
     context, key_grad, value_grad = attend(
         queries,
         key_acc.astype(jnp.bfloat16),
@@ -128,6 +132,284 @@
     return (context, enc_grad)
 
 
+PAIR = 2 * DH
+
+
+def nt(a, b):
+    return lax.dot_general(a, b, (((1,), (1,)), ((), ())), preferred_element_type=F32)
+
+
+def tn(a, b):
+    return lax.dot_general(a, b, (((0,), (0,)), ((), ())), preferred_element_type=F32)
+
+
+def forward_kernel(blocks, tab, x_ref, w_ref, q_ref, g_ref, ctx_ref, dkv_ref, acc, kv):
+    step = pl.program_id(0)
+    last = pl.num_programs(0) - 1
+    part = jnp.dot(x_ref[...], w_ref[...], preferred_element_type=F32)
+
+    @pl.when(step == 0)
+    def _():
+        acc[...] = part
+
+    @pl.when((step > 0) & (step < last))
+    def _():
+        acc[...] += part
+
+    @pl.when(step == last)
+    def _():
+        kv[...] = (acc[...] + part).astype(BF16)
+        lane = lax.broadcasted_iota(jnp.int32, (BLOCK, PAIR), 1) < DH
+        key_pos = lax.broadcasted_iota(jnp.int32, (BLOCK, PAIR), 0)
+        scale = DH ** (-0.5)
+        zero = jnp.zeros((BLOCK, PAIR), BF16)
+
+        def one(b):
+            src = tab[b]
+            rows = pl.ds(pl.multiple_of(src * BLOCK, BLOCK), BLOCK)
+            here = pl.ds(b * BLOCK, BLOCK)
+            key = kv[rows, 0:PAIR]
+            value = kv[rows, PAIR : 2 * PAIR]
+            query = q_ref[here, :]
+            grad = g_ref[here, :]
+            query2 = jnp.concatenate(
+                [jnp.where(lane, query, zero), jnp.where(lane, zero, query)], axis=0
+            )
+            grad2 = jnp.concatenate(
+                [jnp.where(lane, grad, zero), jnp.where(lane, zero, grad)], axis=0
+            )
+            scores = jnp.where(key_pos < tab[blocks + b], nt(key, query2) * scale, -1e30)
+            weights = jnp.exp(scores - jnp.max(scores, axis=0, keepdims=True))
+            probs = weights / jnp.sum(weights, axis=0, keepdims=True)
+            prob_bf = probs.astype(BF16)
+            ctx2 = tn(prob_bf, value)
+            ctx_ref[here, :] = jnp.where(lane, ctx2[:BLOCK], ctx2[BLOCK:]).astype(BF16)
+            prob_grad = nt(value, grad2)
+            row_dot = jnp.sum(probs * prob_grad, axis=0, keepdims=True)
+            score_grad = (probs * (prob_grad - row_dot) * scale).astype(BF16)
+            dkv_ref[rows, 0:PAIR] = jnp.dot(
+                score_grad, query2, preferred_element_type=F32
+            ).astype(BF16)
+            dkv_ref[rows, PAIR : 2 * PAIR] = jnp.dot(
+                prob_bf, grad2, preferred_element_type=F32
+            ).astype(BF16)
+
+        for b in range(blocks):
+            one(b)
+
+
+def forward_chunk(table, x, w, queries, grads, chunk, blocks, parts):
+    rows, width = x.shape
+    cols = w.shape[1]
+    span = width // parts
+    return pl.pallas_call(
+        functools.partial(forward_kernel, blocks),
+        grid_spec=pltpu.PrefetchScalarGridSpec(
+            num_scalar_prefetch=1,
+            grid=(parts,),
+            in_specs=[
+                pl.BlockSpec((rows, span), lambda a, t: (0, t[2 * blocks + a])),
+                pl.BlockSpec((span, cols), lambda a, t: (a, 0)),
+                pl.BlockSpec((rows, PAIR), lambda a, t: (0, chunk)),
+                pl.BlockSpec((rows, PAIR), lambda a, t: (0, chunk)),
+            ],
+            out_specs=[
+                pl.BlockSpec((rows, PAIR), lambda a, t: (0, 0)),
+                pl.BlockSpec((rows, 2 * PAIR), lambda a, t: (0, 0)),
+            ],
+            scratch_shapes=[
+                pltpu.VMEM((rows, cols), F32),
+                pltpu.VMEM((rows, cols), BF16),
+            ],
+        ),
+        out_shape=[
+            jax.ShapeDtypeStruct((rows, PAIR), BF16),
+            jax.ShapeDtypeStruct((rows, 2 * PAIR), BF16),
+        ],
+        compiler_params=pltpu.CompilerParams(vmem_limit_bytes=32 << 20),
+        cost_estimate=pl.CostEstimate(
+            flops=2 * rows * width * cols + 10 * rows * BLOCK * 2 * PAIR,
+            bytes_accessed=2 * rows * width + 2 * width * cols + 6 * rows * PAIR * 2,
+            transcendentals=rows * BLOCK * 2,
+        ),
+        name="fwd",
+    )(table, x, w, queries, grads)
+
+
+def backward_kernel(has_acc, tab, dkv_ref, w_ref, *refs):
+    out_ref = refs[-1]
+    part = nt(dkv_ref[...], w_ref[...])
+    if has_acc:
+        part = part + refs[0][...]
+    out_ref[...] = part.astype(out_ref.dtype)
+
+
+def backward_chunk(table, dkv, w, acc, blocks, parts, row_at, row_n, out_dtype, alias):
+    rows, cols = dkv.shape
+    width = w.shape[0]
+    span = width // parts
+    tile = min(row_n, 512)
+    first = row_at // tile
+    in_specs = [
+        pl.BlockSpec((tile, cols), lambda r, a, t: (first + r, 0)),
+        pl.BlockSpec((span, cols), lambda r, a, t: (a, 0)),
+    ]
+    operands = [table, dkv, w]
+    if acc is not None:
+        in_specs.append(
+            pl.BlockSpec((tile, span), lambda r, a, t: (first + r, t[2 * blocks + a]))
+        )
+        operands.append(acc)
+    return pl.pallas_call(
+        functools.partial(backward_kernel, acc is not None),
+        grid_spec=pltpu.PrefetchScalarGridSpec(
+            num_scalar_prefetch=1,
+            grid=(row_n // tile, parts),
+            in_specs=in_specs,
+            out_specs=pl.BlockSpec((tile, span), lambda r, a, t: (r, t[2 * blocks + a])),
+        ),
+        out_shape=jax.ShapeDtypeStruct((row_n, width), out_dtype),
+        input_output_aliases={3: 0} if alias else {},
+        compiler_params=pltpu.CompilerParams(vmem_limit_bytes=32 << 20),
+        cost_estimate=pl.CostEstimate(
+            flops=2 * row_n * width * cols,
+            bytes_accessed=2 * row_n * cols + 2 * width * cols + 8 * row_n * width,
+            transcendentals=0,
+        ),
+        name="bwd",
+    )(*operands)
+
+
+def shards_section(enc_rows, enc_len, dest_dp, peer_counts, queries, ctx_grad, w_key, w_value):
+    n_sec, n_dp, n_mp = (lax.axis_size(a) for a in ("section", "dp", "mp"))
+    z, d, m = (lax.axis_index(a) for a in ("section", "dp", "mp"))
+    own_blocks = dest_dp.shape[0]
+    blocks = own_blocks * n_dp
+    own_rows, half = enc_rows.shape
+    head_cols = w_key.shape[1] // n_dp
+    chunks = head_cols // PAIR
+
+    core = [(i, i ^ 1) for i in range(n_dp)]
+    ypairs = [(i, i ^ 2) for i in range(n_dp)]
+    xpairs = [(0, 1), (1, 0)]
+    up = [(i, i + 1) for i in range(n_sec - 1)]
+    down = [(i + 1, i) for i in range(n_sec - 1)]
+    over_two = [(i, i ^ 2) for i in range(n_sec)]
+    ends = [(1, 0), (2, 3)]
+
+    packed = jnp.concatenate([enc_len, dest_dp, peer_counts[0]])
+    packed = lax.all_gather(packed, "dp", axis=0, tiled=False)
+    lens = packed[:, :own_blocks].reshape(-1)
+    dest = packed[:, own_blocks : 2 * own_blocks]
+    counts = packed[:, 2 * own_blocks :]
+    pos = jnp.arange(own_blocks, dtype=jnp.int32)
+    peer = jnp.arange(n_dp, dtype=jnp.int32)
+    counts_before = jnp.sum(
+        jnp.where(peer[None, None, :] < peer[None, :, None], counts[:, None, :], 0), axis=2
+    )
+    ends_at = counts_before + counts
+    sender = jnp.sum((ends_at[:, None, :] <= pos[None, :, None]).astype(jnp.int32), axis=2)
+    is_sender = sender[:, :, None] == peer[None, None, :]
+    rank = pos[None, :] - jnp.sum(jnp.where(is_sender, counts_before[:, None, :], 0), axis=2)
+    same = dest[:, :, None] == dest[:, None, :]
+    slot_rank = jnp.sum((same & (pos[None, None, :] < pos[None, :, None])).astype(jnp.int32), axis=2)
+    hit = (
+        is_sender[:, :, :, None]
+        & (dest[None, None] == peer[:, None, None, None])
+        & (slot_rank[None, None] == rank[:, :, None, None])
+    ).reshape(blocks, blocks)
+    near = peer ^ d
+    slot = jnp.where(near == 1, 2, jnp.where(near == 2, 1, near))
+    place = (slot[:, None] * own_blocks + pos[None, :]).reshape(-1)
+    src = jnp.sum(jnp.where(hit, place[None, :], 0), axis=1)
+    src_len = jnp.sum(jnp.where(hit, lens[None, :], 0), axis=1)
+    sec_at = (z + jnp.arange(n_sec, dtype=jnp.int32)) % n_sec
+    sec_half = n_sec // n_mp
+    col_at = ((sec_at // sec_half) ^ m) * sec_half + sec_at % sec_half
+    table = jnp.concatenate([src, src_len, col_at]).astype(jnp.int32)
+
+    def weight_chunk(c):
+        def cut(w):
+            return w.reshape(own_rows, n_dp, head_cols)[:, :, c * PAIR : (c + 1) * PAIR]
+
+        both = jnp.concatenate([cut(w_key), cut(w_value)], axis=2).transpose(1, 0, 2)
+        got = lax.all_to_all(both, "dp", split_axis=0, concat_axis=0, tiled=True)
+        return got.reshape(n_dp * own_rows, 2 * PAIR)
+
+    own = [weight_chunk(c) for c in range(chunks)]
+
+    e_y = lax.ppermute(enc_rows, "dp", ypairs)
+    e_x = lax.ppermute(enc_rows, "mp", xpairs)
+    e_yx = lax.ppermute(e_y, "mp", xpairs)
+    top = jnp.concatenate(
+        [jnp.concatenate([enc_rows, e_x], axis=1), jnp.concatenate([e_y, e_yx], axis=1)], axis=0
+    )
+    x = jnp.concatenate([top, lax.ppermute(top, "dp", core)], axis=0)
+
+    def to_heads(rows):
+        parts = rows.reshape(own_rows, n_dp, head_cols).transpose(1, 0, 2)
+        got = lax.all_to_all(parts, "dp", split_axis=0, concat_axis=0, tiled=True)
+        return got.reshape(n_dp * own_rows, head_cols)
+
+    q_all = to_heads(queries)
+    g_all = to_heads(ctx_grad)
+
+    acc = None
+    contexts = []
+    gate = None
+    for c in range(chunks):
+        piece = own[c]
+        if gate is not None:
+            piece, _ = lax.optimization_barrier((piece, gate))
+        below = lax.ppermute(piece, "section", up)
+        above = lax.ppermute(piece, "section", down)
+        far = lax.ppermute(piece, "section", over_two)
+        end = lax.ppermute(far, "section", ends)
+        gate = far
+        w = jnp.concatenate(
+            [
+                own[c],
+                jnp.where(z == n_sec - 1, end, above),
+                far,
+                jnp.where(z == 0, end, below),
+            ],
+            axis=0,
+        )
+        ctx, dkv = forward_chunk(table, x, w, q_all, g_all, c, blocks, n_sec)
+        ctx4 = ctx.reshape(n_dp, own_rows, PAIR)
+        contexts.append(lax.all_to_all(ctx4, "dp", split_axis=0, concat_axis=0, tiled=True))
+        back = functools.partial(backward_chunk, table, dkv, w, acc, blocks, n_sec)
+        rows = x.shape[0]
+        if c < chunks - 1:
+            acc = back(0, rows, F32, acc is not None)
+        else:
+            give = back(rows // 2, rows // 2, BF16, False)
+            keep = back(0, rows // 2, F32, False)
+
+    context = jnp.stack(contexts, axis=2)
+    context = context.transpose(1, 0, 2, 3).reshape(own_rows, n_dp * head_cols)
+
+    keep = keep + lax.ppermute(give, "dp", core).astype(F32)
+    q4 = half // 2
+
+    def cols(a, lo):
+        return a[:, lo : lo + q4]
+
+    p_y = jnp.concatenate([cols(keep[own_rows:], 0), cols(keep[own_rows:], half)], axis=1)
+    q_x = cols(keep, half + q4)
+    got_y = lax.ppermute(p_y.astype(BF16), "dp", ypairs).astype(F32)
+    got_x = lax.ppermute(q_x.astype(BF16), "mp", xpairs).astype(F32)
+    p_own = cols(keep[:own_rows], 0) + got_y[:, :q4]
+    p_x = cols(keep[:own_rows], half) + got_y[:, q4:]
+    q_own = cols(keep, q4) + got_x
+    p_own = p_own + lax.ppermute(p_x.astype(BF16), "mp", xpairs).astype(F32)
+    q_fin = q_own[:own_rows] + lax.ppermute(
+        q_own[own_rows:].astype(BF16), "dp", ypairs
+    ).astype(F32)
+    enc_grad = jnp.concatenate([p_own.astype(BF16), q_fin.astype(BF16)], axis=1)
+    return (context, enc_grad)
+
+
 def solution(mesh):
     placed = (
         P(("section", "dp"), "mp"),
@@ -139,8 +421,10 @@
         P(("section", "dp"), "mp"),
         P(("section", "dp"), "mp"),
     )
+    sizes = tuple(mesh.shape[a] for a in ("section", "dp", "mp"))
+    body = shards_section if sizes == (4, 4, 2) else shards_general
     return jax.shard_map(
-        shards,
+        body,
         mesh=mesh,
         in_specs=placed,
         out_specs=(P(("section", "dp"), "mp"), P(("section", "dp"), "mp")),

time: 489 us -> 399 us (0.82)
  waiting for transfers between devices: 330 us -> 107 us
  starting transfers between devices: 11.7 us -> 85.6 us
  Pallas kernels: 0 us -> 73.3 us
  matrix products: 69.9 us -> 0 us
  other arithmetic: 5.3 us -> 50.1 us
  blocking collectives: 0 us -> 43.7 us
  local copies, waits for them, and re-layouts: 52 us -> 34.8 us
  between operations: 14.3 us -> 1.9 us
    all_gather x3 -> x0, waiting for transfers between devices: 264 us -> none  [the longest x1 129 us: shards(): lax.all_gather(w_value, ('section', 'dp'), axis=0, tiled=True)]
    ppermute x0 -> x25, waiting for transfers between devices: none -> 94.9 us  [the longest x4 56.9 us: shards_section(): far = lax.ppermute(piece, 'section', over_two)]
    pallas_call x0 -> x9, Pallas kernels: none -> 73.3 us  [the longest x4 43 us: forward_chunk(): pl.pallas_call(functools.partial(forward_kernel, blocks), grid_spec=pltpu...]
    dot_general x17 -> x0, matrix products: 69.9 us -> none  [the longest x2 11.8 us: shards(): lax.dot_general(value_grad, value_part, (((1,), (1,)), ((), ())), preferr...]
    ppermute x0 -> x25, starting transfers between devices: none -> 51.6 us  [the longest x4 19.2 us: shards_section(): below = lax.ppermute(piece, 'section', up)]
    reshape x16 -> x5, local copies, waits for them, and re-layouts: 40.1 us -> 8.83 us  [the longest x2 4.58 us: to_heads(): parts = rows.reshape(own_rows, n_dp, head_cols).transpose(1, 0, 2)]
    reduce_scatter x1 -> x0, waiting for transfers between devices: 30.2 us -> none  [shards(): lax.psum_scatter(jnp.concatenate(pieces_out, axis=1), 'mp', scatter_dimen...]
    all_to_all x0 -> x1, blocking collectives: none -> 25.3 us  [shards_section(): lax.all_to_all(ctx4, 'dp', split_axis=0, concat_axis=0, tiled=True)]
  transfers between devices with their start and end apart: 7 -> 34, of which waited for: 6 -> 11; matrix products, arithmetic and copies ran while one was open for 8% -> 14% of each run, Pallas kernels for 0% -> 1%
where the time goes in v1:
time: 399 us; the launch traced here: 397 us
  waiting for transfers between devices  107 us (27%)
  starting transfers between devices  85.6 us (21%)
  Pallas kernels  73.3 us (18%)
  other arithmetic  50.1 us (13%)
  blocking collectives  43.7 us (11%)
  local copies, waits for them, and re-layouts  34.8 us (9%)
    ppermute x4, waiting for transfers between devices, shards_section(): far = lax.ppermute(piece, 'section', over_two)  56.9 us
    pallas_call x4, Pallas kernels, forward_chunk(): pl.pallas_call(functools.partial(forward_kernel, blocks), grid_spec=pltpu...  43 us
    pallas_call x5, Pallas kernels, backward_chunk(): pl.pallas_call(functools.partial(backward_kernel, acc is not None), grid_...  30.3 us
    all_to_all x1, blocking collectives, shards_section(): lax.all_to_all(ctx4, 'dp', split_axis=0, concat_axis=0, tiled=True)  25.3 us
    ppermute x4, starting transfers between devices, shards_section(): below = lax.ppermute(piece, 'section', up)  19.2 us
    unnamed x1, blocking collectives  18.4 us
    unnamed x50, local copies, waits for them, and re-layouts  18.1 us
    all_to_all x4, starting transfers between devices, weight_chunk(): got = lax.all_to_all(both, 'dp', split_axis=0, concat_axis=0, tiled=True)  13.9 us
  transfers between devices with their start and end apart: 34, of which 11 were waited for; matrix products, arithmetic and copies ran while one was open for 14% of the time, Pallas kernels for 1%

profile of v1, /device:TPU:0, one launch (start us, length us, event | category | flops | bytes accessed | tf_op | source)
XLA Modules:
  0.0 396.7 jit_solution(2253032895155843913)
XLA Ops:
  0.6 3.0 collective-permute-start
  10.9 3.5 all-to-all-start
  15.8 18.4 %all-reduce = s32[48]{0:T(128)S(1)} all-reduce(s32[48]{0:T(128)S(1)} %add_dynamic-update-slice_fusion), channel_id=2, replica_groups=mesh['section'=4,'dp'=4,'mp'=2] {'dp'}, use_global_device_ids=true, to_apply=%add | all-reduce | flops 48 | bytes 384
  38.7 3.5 all-to-all-start.4
  42.2 2.8 collective-permute-start.4
  47.6 11.8 %collective-permute-done.2 = bf16[256,2048]{1,0:T(8,128)(2,1)} collective-permute-done((bf16[256,2048]{1,0:T(8,128)(2,1)}, bf16[256,2048]{1,0:T(8,128)(2,1)}, u32[]{:S(2)}, u32[]{:S(2)}) %collective-permute-start.2) | collective-permute-done | bytes 1048608 | tf_op jit(solution)/shard_map/ppermute | solution.py:343
  60.8 2.6 pad_maximum_fusion.1
  63.5 3.5 collective-permute-start.7
  68.3 3.5 all-to-all-start.6
  71.8 3.7 collective-permute-start.8
  77.7 2.3 copy.47
  80.0 2.3 copy.46
  83.4 3.5 all-to-all-start.8
  86.9 19.6 %collective-permute-done.8 = bf16[1024,256]{1,0:T(8,128)(2,1)} collective-permute-done((bf16[1024,256]{1,0:T(8,128)(2,1)S(1)}, bf16[1024,256]{1,0:T(8,128)(2,1)}, u32[]{:S(2)}, u32[]{:S(2)}) %collective-permute-start.8) | collective-permute-done | bytes 524320 | tf_op jit(solution)/shard_map/ppermute | solution.py:366
  114.5 2.5 pad_maximum_fusion.2.w_ref
  117.8 3.5 all-to-all-start.1
  121.4 24.0 %collective-permute-done.12 = bf16[1024,256]{1,0:T(8,128)(2,1)} collective-permute-done((bf16[1024,256]{1,0:T(8,128)(2,1)S(1)}, bf16[1024,256]{1,0:T(8,128)(2,1)}, u32[]{:S(2)}, u32[]{:S(2)}) %collective-permute-start.12) | collective-permute-done | bytes 524320 | tf_op jit(solution)/shard_map/ppermute | solution.py:366
  148.0 2.7 collective-permute-start.16
  153.3 2.5 pad_maximum_fusion.3.w_ref
  155.8 3.2 collective-permute-done.15
  159.0 12.3 %collective-permute-start.19 = (bf16[1024,256]{1,0:T(8,128)(2,1)S(1)}, bf16[1024,256]{1,0:T(8,128)(2,1)S(1)}, u32[]{:S(2)}, u32[]{:S(2)}) collective-permute-start(bf16[1024,256]{1,0:T(8,128)(2,1)S(1)} %bitcast.59), channel_id=1, source_target_pairs={{0,8},{8,16},{16,24},{1,9},{9,17},{17,25},{2,10},{10,18},{18,26},{... | collective-permute-start | bytes 1572872 | tf_op jit(solution)/shard_map/ppermute | solution.py:364
  172.6 13.3 %collective-permute-done.16 = bf16[1024,256]{1,0:T(8,128)(2,1)S(1)} collective-permute-done((bf16[1024,256]{1,0:T(8,128)(2,1)}, bf16[1024,256]{1,0:T(8,128)(2,1)S(1)}, u32[]{:S(2)}, u32[]{:S(2)}) %collective-permute-start.16) | collective-permute-done | bytes 524320 | tf_op jit(solution)/shard_map/ppermute | solution.py:366
  187.3 2.5 pad_maximum_fusion.4.w_ref
  189.8 7.3 %collective-permute-done.18 = bf16[1024,256]{1,0:T(8,128)(2,1)S(1)} collective-permute-done((bf16[1024,256]{1,0:T(8,128)(2,1)S(1)}, bf16[1024,256]{1,0:T(8,128)(2,1)S(1)}, u32[]{:S(2)}, u32[]{:S(2)}) %collective-permute-start.18) | collective-permute-done | bytes 524320 | tf_op jit(solution)/shard_map/ppermute | solution.py:365
  197.1 8.3 %collective-permute-done.17 = bf16[1024,256]{1,0:T(8,128)(2,1)S(1)} collective-permute-done((bf16[1024,256]{1,0:T(8,128)(2,1)S(1)}, bf16[1024,256]{1,0:T(8,128)(2,1)S(1)}, u32[]{:S(2)}, u32[]{:S(2)}) %collective-permute-start.17) | collective-permute-done | bytes 524320 | tf_op jit(solution)/shard_map/ppermute | solution.py:367
  206.6 4.4 %all-to-all-start.2 = ((bf16[4,256,512]{2,1,0:T(8,128)(2,1)}), bf16[4,256,512]{2,1,0:T(8,128)(2,1)}, u32[]{:S(2)}, u32[]{:S(2)}) async-start(bf16[4,256,512]{2,1,0:T(8,128)(2,1)} %bitcast.37), calls=%async_computation.2 | async-start | bytes 2097152 | tf_op jit(solution)/shard_map/all_to_all | solution.py:351
  212.7 7.1 %pad_maximum_fusion.x_ref = bf16[1024,4096]{1,0:T(8,128)(2,1)} fusion(bf16[512,4096]{1,0:T(8,128)(2,1)} %collective-permute-done.3, bf16[256,4096]{1,0:T(8,128)(2,1)} %copy-done.7, bf16[256,4096]{1,0:T(8,128)(2,1)} %copy-done.6), kind=kLoop, calls=%fused_computation | loop fusion | flops 25165824 | bytes 16777216 | tf_op jit(solution)/shard_map/concatenate | solution.py:347
  219.8 5.6 %all-to-all-done.2 = bf16[4,256,512]{2,1,0:T(8,128)(2,1)} async-done(((bf16[4,256,512]{2,1,0:T(8,128)(2,1)}), bf16[4,256,512]{2,1,0:T(8,128)(2,1)}, u32[]{:S(2)}, u32[]{:S(2)}) %all-to-all-start.2) | async-done | bytes 1048608 | tf_op jit(solution)/shard_map/all_to_all | solution.py:351
  225.4 3.4 copy-done.1
  228.7 10.2 %fwd.7 = (bf16[1024,128]{1,0:T(8,128)(2,1)S(1)}, bf16[1024,256]{1,0:T(8,128)(2,1)S(1)}) custom-call(s32[36]{0:T(128)S(1)} %pad_add_fusion.tab, bf16[1024,4096]{1,0:T(8,128)(2,1)S(1)} %copy-done.1, bf16[4096,256]{1,0:T(8,128)(2,1)S(1)} %pad_maximum_fusion.5.w_ref, bf16[1024,512]{1,0:T(8,128)(2,1)S(1)} %bitcast.40, bf16[1024,512]{1,0:T(8,128)(2,1)} %bitcast.7.g_ref), custom_call_target="tpu_custom_call" | custom-call | flops 2315255808 | bytes 12058624 | tf_op jit(solution)/shard_map/fwd/pallas_call | solution.py:205
  238.9 10.9 %fwd.6 = (bf16[1024,128]{1,0:T(8,128)(2,1)}, bf16[1024,256]{1,0:T(8,128)(2,1)S(1)}) custom-call(s32[36]{0:T(128)S(1)} %pad_add_fusion.tab, bf16[1024,4096]{1,0:T(8,128)(2,1)S(1)} %copy-done.1, bf16[4096,256]{1,0:T(8,128)(2,1)S(1)} %copy-done.4, bf16[1024,512]{1,0:T(8,128)(2,1)S(1)} %bitcast.41, bf16[1024,512]{1,0:T(8,128)(2,1)} %bitcast.7.g_ref), custom_call_target="tpu_custom_call" | custom-call | flops 2315255808 | bytes 12058624 | tf_op jit(solution)/shard_map/fwd/pallas_call | solution.py:205
  249.8 10.9 %fwd.5 = (bf16[1024,128]{1,0:T(8,128)(2,1)}, bf16[1024,256]{1,0:T(8,128)(2,1)S(1)}) custom-call(s32[36]{0:T(128)S(1)} %pad_add_fusion.tab, bf16[1024,4096]{1,0:T(8,128)(2,1)S(1)} %copy-done.1, bf16[4096,256]{1,0:T(8,128)(2,1)S(1)} %copy-done.3, bf16[1024,512]{1,0:T(8,128)(2,1)S(1)} %bitcast.42, bf16[1024,512]{1,0:T(8,128)(2,1)} %bitcast.7.g_ref), custom_call_target="tpu_custom_call" | custom-call | flops 2315255808 | bytes 12058624 | tf_op jit(solution)/shard_map/fwd/pallas_call | solution.py:205
  260.7 11.1 %fwd.4 = (bf16[1024,128]{1,0:T(8,128)(2,1)}, bf16[1024,256]{1,0:T(8,128)(2,1)S(1)}) custom-call(s32[36]{0:T(128)S(1)} %pad_add_fusion.tab, bf16[1024,4096]{1,0:T(8,128)(2,1)S(1)} %copy-done.1, bf16[4096,256]{1,0:T(8,128)(2,1)S(1)} %copy-done.5, bf16[1024,512]{1,0:T(8,128)(2,1)S(1)} %bitcast.43, bf16[1024,512]{1,0:T(8,128)(2,1)} %bitcast.7.g_ref), custom_call_target="tpu_custom_call" | custom-call | flops 2315255808 | bytes 12058624 | tf_op jit(solution)/shard_map/fwd/pallas_call | solution.py:205
  271.8 5.4 %bwd.5.refs_0_ = f32[1024,4096]{1,0:T(8,128)S(1)} custom-call(s32[36]{0:T(128)S(1)} %pad_add_fusion.tab, bf16[1024,256]{1,0:T(8,128)(2,1)S(1)} %get-tuple-element.23.dkv_ref, bf16[4096,256]{1,0:T(8,128)(2,1)S(1)} %copy-done.5), custom_call_target="tpu_custom_call" | custom-call | flops 2147483648 | bytes 36175872 | tf_op jit(solution)/shard_map/bwd/pallas_call | solution.py:263
  277.2 6.7 %bwd.6.refs_0_ = f32[1024,4096]{1,0:T(8,128)S(1)} custom-call(s32[36]{0:T(128)S(1)} %pad_add_fusion.tab, bf16[1024,256]{1,0:T(8,128)(2,1)S(1)} %get-tuple-element.22.dkv_ref, bf16[4096,256]{1,0:T(8,128)(2,1)S(1)} %copy-done.3, f32[1024,4096]{1,0:T(8,128)S(1)} %bwd.5.refs_0_), custom_call_target="tpu_custom_call", output_to_operand_aliasing={{}: (3, {})} | custom-call | flops 2147483648 | bytes 36175872 | tf_op jit(solution)/shard_map/bwd/pallas_call | solution.py:263
  283.9 6.7 %bwd.7.refs_0_ = f32[1024,4096]{1,0:T(8,128)S(1)} custom-call(s32[36]{0:T(128)S(1)} %pad_add_fusion.tab, bf16[1024,256]{1,0:T(8,128)(2,1)S(1)} %get-tuple-element.21.dkv_ref, bf16[4096,256]{1,0:T(8,128)(2,1)S(1)} %copy-done.4, f32[1024,4096]{1,0:T(8,128)S(1)} %bwd.6.refs_0_), custom_call_target="tpu_custom_call", output_to_operand_aliasing={{}: (3, {})} | custom-call | flops 2147483648 | bytes 36175872 | tf_op jit(solution)/shard_map/bwd/pallas_call | solution.py:263
  290.6 5.8 %copy-done = f32[1024,4096]{1,0:T(8,128)} copy-done((f32[1024,4096]{1,0:T(8,128)}, f32[1024,4096]{1,0:T(8,128)S(1)}, u32[]{:S(2)}) %copy-start) | copy-done | bytes 16777240
  296.4 5.7 %bwd.9 = bf16[512,4096]{1,0:T(8,128)(2,1)S(1)} custom-call(s32[36]{0:T(128)S(1)} %pad_add_fusion.tab, bf16[1024,256]{1,0:T(8,128)(2,1)S(1)} %get-tuple-element.20.dkv_ref, bf16[4096,256]{1,0:T(8,128)(2,1)S(1)} %pad_maximum_fusion.5.w_ref, f32[1024,4096]{1,0:T(8,128)} %copy-done), custom_call_target="tpu_custom_call" | custom-call | flops 1073741824 | bytes 19136512 | tf_op jit(solution)/shard_map/bwd/pallas_call | solution.py:263
  302.1 5.9 %bwd.8 = f32[512,4096]{1,0:T(8,128)S(1)} custom-call(s32[36]{0:T(128)S(1)} %pad_add_fusion.tab, bf16[1024,256]{1,0:T(8,128)(2,1)S(1)} %get-tuple-element.20.dkv_ref, bf16[4096,256]{1,0:T(8,128)(2,1)S(1)} %pad_maximum_fusion.5.w_ref, f32[1024,4096]{1,0:T(8,128)} %copy-done), custom_call_target="tpu_custom_call" | custom-call | flops 1073741824 | bytes 19136512 | tf_op jit(solution)/shard_map/bwd/pallas_call | solution.py:263
  308.0 3.3 copy-done.2
  311.3 10.0 %fusion.7 = (bf16[512,4096]{1,0:T(8,128)(2,1)S(1)}, f32[512,4096]{1,0:T(8,128)}) fusion(f32[512,4096]{1,0:T(8,128)} %copy-done.2, bf16[512,4096]{1,0:T(8,128)(2,1)} %collective-permute-done.20), kind=kLoop, calls=%fused_computation.66 | loop fusion | flops 6291456 | bytes 25165824 | tf_op jit(solution)/shard_map/convert.5
  325.7 25.3 %all_to_all.50 = bf16[4,256,128]{2,1,0:T(8,128)(2,1)S(1)} all-to-all(bf16[4,256,128]{2,1,0:T(8,128)(2,1)S(1)} %bitcast.44), channel_id=1, replica_groups=mesh['section'=4,'dp'=4,'mp'=2] {'dp'}, dimensions={0} | all-to-all | bytes 524288 | tf_op jit(solution)/shard_map/all_to_all | solution.py:380
  351.1 4.0 %all-to-all-start.7 = ((bf16[4,256,128]{2,1,0:T(8,128)(2,1)}), bf16[4,256,128]{2,1,0:T(8,128)(2,1)}, u32[]{:S(2)}, u32[]{:S(2)}) async-start(bf16[4,256,128]{2,1,0:T(8,128)(2,1)} %bitcast.16), calls=%async_computation.7 | async-start | bytes 524288 | tf_op jit(solution)/shard_map/all_to_all | solution.py:380
  356.6 4.6 %all-to-all-done.7 = bf16[4,256,128]{2,1,0:T(8,128)(2,1)} async-done(((bf16[4,256,128]{2,1,0:T(8,128)(2,1)}), bf16[4,256,128]{2,1,0:T(8,128)(2,1)}, u32[]{:S(2)}, u32[]{:S(2)}) %all-to-all-start.7) | async-done | bytes 262176 | tf_op jit(solution)/shard_map/all_to_all | solution.py:380
  361.2 4.0 %all-to-all-start.5 = ((bf16[4,256,128]{2,1,0:T(8,128)(2,1)}), bf16[4,256,128]{2,1,0:T(8,128)(2,1)}, u32[]{:S(2)}, u32[]{:S(2)}) async-start(bf16[4,256,128]{2,1,0:T(8,128)(2,1)} %bitcast.12), calls=%async_computation.5 | async-start | bytes 524288 | tf_op jit(solution)/shard_map/all_to_all | solution.py:380
  365.2 2.1 fusion.1
  371.3 4.1 %all-to-all-start.3 = ((bf16[4,256,128]{2,1,0:T(8,128)(2,1)}), bf16[4,256,128]{2,1,0:T(8,128)(2,1)}, u32[]{:S(2)}, u32[]{:S(2)}) async-start(bf16[4,256,128]{2,1,0:T(8,128)(2,1)} %bitcast.8), calls=%async_computation.3 | async-start | bytes 524288 | tf_op jit(solution)/shard_map/all_to_all | solution.py:380
  386.8 7.3 %collective-permute-done.24 = bf16[256,1024]{1,0:T(8,128)(2,1)} collective-permute-done((bf16[256,1024]{1,0:T(8,128)(2,1)}, bf16[256,1024]{1,0:T(8,128)(2,1)}, u32[]{:S(2)}, u32[]{:S(2)}) %collective-permute-start.24) | collective-permute-done | bytes 524320 | tf_op jit(solution)/shard_map/ppermute | solution.py:406
  (133 shorter events, 64.3 us)
Async XLA Ops:
  0.6 7.5 %copy-start.11 = (bf16[256,2048]{1,0:T(8,128)(2,1)S(1)}, bf16[256,2048]{1,0:T(8,128)(2,1)}, u32[]{:S(2)}) copy-start(bf16[256,2048]{1,0:T(8,128)(2,1)} %param.15) | copy-start | bytes 3145732
  0.6 45.7 %collective-permute-start = (bf16[256,2048]{1,0:T(8,128)(2,1)}, bf16[256,2048]{1,0:T(8,128)(2,1)}, u32[]{:S(2)}, u32[]{:S(2)}) collective-permute-start(bf16[256,2048]{1,0:T(8,128)(2,1)} %param.8), channel_id=1, source_target_pairs={{0,1},{1,0},{2,3},{3,2},{4,5},{5,4},{6,7},{7,6},{8,9},{9,8},{10,11... | collective-permute-start | bytes 3145736 | tf_op jit(solution)/shard_map/ppermute | solution.py:342
  3.6 32.0 %collective-permute-start.1 = (bf16[256,2048]{1,0:T(8,128)(2,1)}, bf16[256,2048]{1,0:T(8,128)(2,1)}, u32[]{:S(2)}, u32[]{:S(2)}) collective-permute-start(bf16[256,2048]{1,0:T(8,128)(2,1)} %param.8), channel_id=1, source_target_pairs={{0,4},{2,6},{4,0},{6,2},{1,5},{3,7},{5,1},{7,3},{8,12},{10,14},{12... | collective-permute-start | bytes 3145736 | tf_op jit(solution)/shard_map/ppermute | solution.py:341
  8.1 6.4 %copy-start.18 = (u32[32]{0:T(128)S(1)}, u32[32]{0:T(128)}, u32[]{:S(2)}) copy-start(u32[32]{0:T(128)} %constant.59) | copy-start | bytes 388
  8.1 7.5 %copy-start.15 = (s32[1,4]{1,0:T(1,128)S(1)}, s32[1,4]{1,0:T(1,128)}, u32[]{:S(2)}) copy-start(s32[1,4]{1,0:T(1,128)} %param.11) | copy-start | bytes 52
  8.1 7.6 %copy-start.16 = (s32[4]{0:T(128)S(1)}, s32[4]{0:T(128)}, u32[]{:S(2)}) copy-start(s32[4]{0:T(128)} %param.10) | copy-start | bytes 52
  8.1 7.6 %copy-start.17 = (s32[4]{0:T(128)S(1)}, s32[4]{0:T(128)}, u32[]{:S(2)}) copy-start(s32[4]{0:T(128)} %param.9) | copy-start | bytes 52
  8.9 25.4 %copy-start.13 = (bf16[256,4,128]{2,1,0:T(4,128)(2,1)S(1)}, bf16[256,4,128]{2,1,0:T(4,128)(2,1)}, u32[]{:S(2)}) copy-start(bf16[256,4,128]{2,1,0:T(4,128)(2,1)} %get-tuple-element.33) | copy-start | bytes 786436
  10.9 27.7 %all-to-all-start = ((bf16[4,256,256]{2,1,0:T(8,128)(2,1)}), bf16[4,256,256]{2,1,0:T(8,128)(2,1)S(1)}, u32[]{:S(2)}, u32[]{:S(2)}) async-start(bf16[4,256,256]{2,1,0:T(8,128)(2,1)} %maximum_bitcast_fusion.1), calls=%async_computation | async-start | bytes 1048576 | tf_op jit(solution)/shard_map/all_to_all | solution.py:336
  35.7 23.7 %collective-permute-start.2 = (bf16[256,2048]{1,0:T(8,128)(2,1)}, bf16[256,2048]{1,0:T(8,128)(2,1)}, u32[]{:S(2)}, u32[]{:S(2)}) collective-permute-start(bf16[256,2048]{1,0:T(8,128)(2,1)} %collective-permute-done.1), channel_id=1, source_target_pairs={{0,1},{1,0},{2,3},{3,2},{4,5},{5,4},{6,7},{7,6},{8,9},{9,8},{10,11... | collective-permute-start | bytes 3145736 | tf_op jit(solution)/shard_map/ppermute | solution.py:343
  38.7 29.6 %all-to-all-start.4 = ((bf16[4,256,256]{2,1,0:T(8,128)(2,1)}), bf16[4,256,256]{2,1,0:T(8,128)(2,1)S(1)}, u32[]{:S(2)}, u32[]{:S(2)}) async-start(bf16[4,256,256]{2,1,0:T(8,128)(2,1)} %maximum_bitcast_fusion.2), calls=%async_computation.4 | async-start | bytes 1048576 | tf_op jit(solution)/shard_map/all_to_all | solution.py:336
  42.2 29.6 %collective-permute-start.4 = (bf16[1024,256]{1,0:T(8,128)(2,1)S(1)}, bf16[1024,256]{1,0:T(8,128)(2,1)}, u32[]{:S(2)}, u32[]{:S(2)}) collective-permute-start(bf16[1024,256]{1,0:T(8,128)(2,1)S(1)} %bitcast.45), channel_id=1, source_target_pairs={{0,16},{8,24},{16,0},{24,8},{1,17},{9,25},{17,1},{25,9},{2,18},{10... | collective-permute-start | bytes 1572872 | tf_op jit(solution)/shard_map/ppermute | solution.py:366
  47.6 15.7 %copy-start.6 = (bf16[256,4096]{1,0:T(8,128)(2,1)}, bf16[256,4096]{1,0:T(8,128)(2,1)S(1)}, u32[]{:S(2)}) copy-start(bf16[256,4096]{1,0:T(8,128)(2,1)S(1)} %constant_dynamic-update-slice_fusion) | copy-start | bytes 6291460
  63.4 149.3 %collective-permute-start.3 = (bf16[512,4096]{1,0:T(8,128)(2,1)}, bf16[512,4096]{1,0:T(8,128)(2,1)}, u32[]{:S(2)}, u32[]{:S(2)}) collective-permute-start(bf16[512,4096]{1,0:T(8,128)(2,1)} %pad_maximum_fusion.1), channel_id=1, source_target_pairs={{0,2},{2,0},{4,6},{6,4},{1,3},{3,1},{5,7},{7,5},{8,10},{10,8},{12,... | collective-permute-start | bytes 12582920 | tf_op jit(solution)/shard_map/ppermute | solution.py:347
  63.4 19.0 %copy-start.12 = (bf16[256,4,128]{2,1,0:T(4,128)(2,1)S(1)}, bf16[256,4,128]{2,1,0:T(4,128)(2,1)}, u32[]{:S(2)}) copy-start(bf16[256,4,128]{2,1,0:T(4,128)(2,1)} %get-tuple-element.39) | copy-start | bytes 786436
  63.5 45.1 %collective-permute-start.7 = (bf16[1024,256]{1,0:T(8,128)(2,1)S(1)}, bf16[1024,256]{1,0:T(8,128)(2,1)S(1)}, u32[]{:S(2)}, u32[]{:S(2)}) collective-permute-start(bf16[1024,256]{1,0:T(8,128)(2,1)S(1)} %bitcast.46), channel_id=1, source_target_pairs={{0,8},{8,16},{16,24},{1,9},{9,17},{17,25},{2,10},{10,18},{18,26},{... | collective-permute-start | bytes 1572872 | tf_op jit(solution)/shard_map/ppermute | solution.py:364
  67.0 42.9 %collective-permute-start.6 = (bf16[1024,256]{1,0:T(8,128)(2,1)S(1)}, bf16[1024,256]{1,0:T(8,128)(2,1)}, u32[]{:S(2)}, u32[]{:S(2)}) collective-permute-start(bf16[1024,256]{1,0:T(8,128)(2,1)S(1)} %bitcast.47), channel_id=1, source_target_pairs={{8,0},{16,8},{24,16},{9,1},{17,9},{25,17},{10,2},{18,10},{26,18},{... | collective-permute-start | bytes 1572872 | tf_op jit(solution)/shard_map/ppermute | solution.py:365
  68.3 15.1 %all-to-all-start.6 = ((bf16[4,256,256]{2,1,0:T(8,128)(2,1)}), bf16[4,256,256]{2,1,0:T(8,128)(2,1)S(1)}, u32[]{:S(2)}, u32[]{:S(2)}) async-start(bf16[4,256,256]{2,1,0:T(8,128)(2,1)} %maximum_bitcast_fusion.3), calls=%async_computation.6 | async-start | bytes 1048576 | tf_op jit(solution)/shard_map/all_to_all | solution.py:336
  71.8 34.7 %collective-permute-start.8 = (bf16[1024,256]{1,0:T(8,128)(2,1)S(1)}, bf16[1024,256]{1,0:T(8,128)(2,1)}, u32[]{:S(2)}, u32[]{:S(2)}) collective-permute-start(bf16[1024,256]{1,0:T(8,128)(2,1)S(1)} %bitcast.49), channel_id=1, source_target_pairs={{0,16},{8,24},{16,0},{24,8},{1,17},{9,25},{17,1},{25,9},{2,18},{10... | collective-permute-start | bytes 1572872 | tf_op jit(solution)/shard_map/ppermute | solution.py:366
  75.5 36.4 %collective-permute-start.5 = (bf16[1024,256]{1,0:T(8,128)(2,1)}, bf16[1024,256]{1,0:T(8,128)(2,1)}, u32[]{:S(2)}, u32[]{:S(2)}) collective-permute-start(bf16[1024,256]{1,0:T(8,128)(2,1)} %collective-permute-done.4), channel_id=1, source_target_pairs={{8,0},{16,24},{9,1},{17,25},{10,2},{18,26},{11,3},{19,27},{12,4},{... | collective-permute-start | bytes 1572872 | tf_op jit(solution)/shard_map/ppermute | solution.py:367
  83.4 33.6 %all-to-all-start.8 = ((bf16[4,256,256]{2,1,0:T(8,128)(2,1)}), bf16[4,256,256]{2,1,0:T(8,128)(2,1)S(1)}, u32[]{:S(2)}, u32[]{:S(2)}) async-start(bf16[4,256,256]{2,1,0:T(8,128)(2,1)} %maximum_bitcast_fusion.4), calls=%async_computation.8 | async-start | bytes 1048576 | tf_op jit(solution)/shard_map/all_to_all | solution.py:336
  106.5 40.2 %collective-permute-start.11 = (bf16[1024,256]{1,0:T(8,128)(2,1)S(1)}, bf16[1024,256]{1,0:T(8,128)(2,1)}, u32[]{:S(2)}, u32[]{:S(2)}) collective-permute-start(bf16[1024,256]{1,0:T(8,128)(2,1)S(1)} %bitcast.50), channel_id=1, source_target_pairs={{0,8},{8,16},{16,24},{1,9},{9,17},{17,25},{2,10},{10,18},{18,26},{... | collective-permute-start | bytes 1572872 | tf_op jit(solution)/shard_map/ppermute | solution.py:364
  108.6 39.4 %collective-permute-start.10 = (bf16[1024,256]{1,0:T(8,128)(2,1)S(1)}, bf16[1024,256]{1,0:T(8,128)(2,1)}, u32[]{:S(2)}, u32[]{:S(2)}) collective-permute-start(bf16[1024,256]{1,0:T(8,128)(2,1)S(1)} %bitcast.51), channel_id=1, source_target_pairs={{8,0},{16,8},{24,16},{9,1},{17,9},{25,17},{10,2},{18,10},{26,18},{... | collective-permute-start | bytes 1572872 | tf_op jit(solution)/shard_map/ppermute | solution.py:365
  109.9 35.5 %collective-permute-start.12 = (bf16[1024,256]{1,0:T(8,128)(2,1)S(1)}, bf16[1024,256]{1,0:T(8,128)(2,1)}, u32[]{:S(2)}, u32[]{:S(2)}) collective-permute-start(bf16[1024,256]{1,0:T(8,128)(2,1)S(1)} %bitcast.53), channel_id=1, source_target_pairs={{0,16},{8,24},{16,0},{24,8},{1,17},{9,25},{17,1},{25,9},{2,18},{10... | collective-permute-start | bytes 1572872 | tf_op jit(solution)/shard_map/ppermute | solution.py:366
  111.9 38.8 %collective-permute-start.9 = (bf16[1024,256]{1,0:T(8,128)(2,1)}, bf16[1024,256]{1,0:T(8,128)(2,1)}, u32[]{:S(2)}, u32[]{:S(2)}) collective-permute-start(bf16[1024,256]{1,0:T(8,128)(2,1)} %collective-permute-done.8), channel_id=1, source_target_pairs={{8,0},{16,24},{9,1},{17,25},{10,2},{18,26},{11,3},{19,27},{12,4},{... | collective-permute-start | bytes 1572872 | tf_op jit(solution)/shard_map/ppermute | solution.py:367
  117.8 88.7 %all-to-all-start.1 = ((bf16[4,256,512]{2,1,0:T(8,128)(2,1)}), bf16[4,256,512]{2,1,0:T(8,128)(2,1)S(1)}, u32[]{:S(2)}, u32[]{:S(2)}) async-start(bf16[4,256,512]{2,1,0:T(8,128)(2,1)} %bitcast.39), calls=%async_computation.1 | async-start | bytes 2097152 | tf_op jit(solution)/shard_map/all_to_all | solution.py:351
  121.3 37.7 %copy-start.10 = (bf16[4,256,256]{2,1,0:T(8,128)(2,1)S(1)}, bf16[4,256,256]{2,1,0:T(8,128)(2,1)}, u32[]{:S(2)}) copy-start(bf16[4,256,256]{2,1,0:T(8,128)(2,1)} %copy-done.9) | copy-start | bytes 1572868
  145.4 13.6 %collective-permute-start.15 = (bf16[1024,256]{1,0:T(8,128)(2,1)S(1)}, bf16[1024,256]{1,0:T(8,128)(2,1)S(1)}, u32[]{:S(2)}, u32[]{:S(2)}) collective-permute-start(bf16[1024,256]{1,0:T(8,128)(2,1)S(1)} %bitcast.54), channel_id=1, source_target_pairs={{0,8},{8,16},{16,24},{1,9},{9,17},{17,25},{2,10},{10,18},{18,26},{... | collective-permute-start | bytes 1572872 | tf_op jit(solution)/shard_map/ppermute | solution.py:364
  146.7 24.6 %collective-permute-start.14 = (bf16[1024,256]{1,0:T(8,128)(2,1)S(1)}, bf16[1024,256]{1,0:T(8,128)(2,1)S(1)}, u32[]{:S(2)}, u32[]{:S(2)}) collective-permute-start(bf16[1024,256]{1,0:T(8,128)(2,1)S(1)} %bitcast.55), channel_id=1, source_target_pairs={{8,0},{16,8},{24,16},{9,1},{17,9},{25,17},{10,2},{18,10},{26,18},{... | collective-permute-start | bytes 1572872 | tf_op jit(solution)/shard_map/ppermute | solution.py:365
  148.0 37.9 %collective-permute-start.16 = (bf16[1024,256]{1,0:T(8,128)(2,1)}, bf16[1024,256]{1,0:T(8,128)(2,1)S(1)}, u32[]{:S(2)}, u32[]{:S(2)}) collective-permute-start(bf16[1024,256]{1,0:T(8,128)(2,1)} %bitcast.57), channel_id=1, source_target_pairs={{0,16},{8,24},{16,0},{24,8},{1,17},{9,25},{17,1},{25,9},{2,18},{10... | collective-permute-start | bytes 1572872 | tf_op jit(solution)/shard_map/ppermute | solution.py:366
  150.7 36.5 %collective-permute-start.13 = (bf16[1024,256]{1,0:T(8,128)(2,1)}, bf16[1024,256]{1,0:T(8,128)(2,1)S(1)}, u32[]{:S(2)}, u32[]{:S(2)}) collective-permute-start(bf16[1024,256]{1,0:T(8,128)(2,1)} %collective-permute-done.12), channel_id=1, source_target_pairs={{8,0},{16,24},{9,1},{17,25},{10,2},{18,26},{11,3},{19,27},{12,4},{... | collective-permute-start | bytes 1572872 | tf_op jit(solution)/shard_map/ppermute | solution.py:367
  159.0 30.8 %collective-permute-start.19 = (bf16[1024,256]{1,0:T(8,128)(2,1)S(1)}, bf16[1024,256]{1,0:T(8,128)(2,1)S(1)}, u32[]{:S(2)}, u32[]{:S(2)}) collective-permute-start(bf16[1024,256]{1,0:T(8,128)(2,1)S(1)} %bitcast.59), channel_id=1, source_target_pairs={{0,8},{8,16},{16,24},{1,9},{9,17},{17,25},{2,10},{10,18},{18,26},{... | collective-permute-start | bytes 1572872 | tf_op jit(solution)/shard_map/ppermute | solution.py:364
  171.3 25.9 %collective-permute-start.18 = (bf16[1024,256]{1,0:T(8,128)(2,1)S(1)}, bf16[1024,256]{1,0:T(8,128)(2,1)S(1)}, u32[]{:S(2)}, u32[]{:S(2)}) collective-permute-start(bf16[1024,256]{1,0:T(8,128)(2,1)S(1)} %bitcast.60), channel_id=1, source_target_pairs={{8,0},{16,8},{24,16},{9,1},{17,9},{25,17},{10,2},{18,10},{26,18},{... | collective-permute-start | bytes 1572872 | tf_op jit(solution)/shard_map/ppermute | solution.py:365
  185.9 19.6 %copy-start.14 = (bf16[1024,256]{1,0:T(8,128)(2,1)}, bf16[1024,256]{1,0:T(8,128)(2,1)S(1)}, u32[]{:S(2)}) copy-start(bf16[1024,256]{1,0:T(8,128)(2,1)S(1)} %collective-permute-done.16) | copy-start | bytes 1572868
  185.9 19.6 %collective-permute-start.17 = (bf16[1024,256]{1,0:T(8,128)(2,1)S(1)}, bf16[1024,256]{1,0:T(8,128)(2,1)S(1)}, u32[]{:S(2)}, u32[]{:S(2)}) collective-permute-start(bf16[1024,256]{1,0:T(8,128)(2,1)S(1)} %collective-permute-done.16), channel_id=1, source_target_pairs={{8,0},{16,24},{9,1},{17,25},{10,2},{18,26},{11,3},{19,27},{12,4},{... | collective-permute-start | bytes 1572872 | tf_op jit(solution)/shard_map/ppermute | solution.py:367
  206.6 18.8 %all-to-all-start.2 = ((bf16[4,256,512]{2,1,0:T(8,128)(2,1)}), bf16[4,256,512]{2,1,0:T(8,128)(2,1)}, u32[]{:S(2)}, u32[]{:S(2)}) async-start(bf16[4,256,512]{2,1,0:T(8,128)(2,1)} %bitcast.37), calls=%async_computation.2 | async-start | bytes 2097152 | tf_op jit(solution)/shard_map/all_to_all | solution.py:351
  228.7 10.2 %copy-start.4 = (bf16[4096,256]{1,0:T(8,128)(2,1)S(1)}, bf16[4096,256]{1,0:T(8,128)(2,1)}, u32[]{:S(2)}) copy-start(bf16[4096,256]{1,0:T(8,128)(2,1)} %pad_maximum_fusion.4.w_ref) | copy-start | bytes 6291460
  238.9 10.9 %copy-start.3 = (bf16[4096,256]{1,0:T(8,128)(2,1)S(1)}, bf16[4096,256]{1,0:T(8,128)(2,1)}, u32[]{:S(2)}) copy-start(bf16[4096,256]{1,0:T(8,128)(2,1)} %pad_maximum_fusion.3.w_ref) | copy-start | bytes 6291460
  249.8 10.9 %copy-start.5 = (bf16[4096,256]{1,0:T(8,128)(2,1)S(1)}, bf16[4096,256]{1,0:T(8,128)(2,1)}, u32[]{:S(2)}) copy-start(bf16[4096,256]{1,0:T(8,128)(2,1)} %pad_maximum_fusion.2.w_ref) | copy-start | bytes 6291460
  290.6 5.8 %copy-start = (f32[1024,4096]{1,0:T(8,128)}, f32[1024,4096]{1,0:T(8,128)S(1)}, u32[]{:S(2)}) copy-start(f32[1024,4096]{1,0:T(8,128)S(1)} %bwd.7.refs_0_) | copy-start | bytes 50331652
  302.0 9.2 %collective-permute-start.20 = (bf16[512,4096]{1,0:T(8,128)(2,1)S(1)}, bf16[512,4096]{1,0:T(8,128)(2,1)}, u32[]{:S(2)}, u32[]{:S(2)}) collective-permute-start(bf16[512,4096]{1,0:T(8,128)(2,1)S(1)} %bwd.9), channel_id=1, source_target_pairs={{0,2},{2,0},{4,6},{6,4},{1,3},{3,1},{5,7},{7,5},{8,10},{10,8},{12,... | collective-permute-start | bytes 12582920 | tf_op jit(solution)/shard_map/ppermute | solution.py:392
  322.5 32.6 %collective-permute-start.21 = (bf16[256,2048]{1,0:T(8,128)(2,1)}, bf16[256,2048]{1,0:T(8,128)(2,1)}, u32[]{:S(2)}, u32[]{:S(2)}) collective-permute-start(bf16[256,2048]{1,0:T(8,128)(2,1)} %pad_maximum_fusion.6), channel_id=1, source_target_pairs={{0,4},{2,6},{4,0},{6,2},{1,5},{3,7},{5,1},{7,3},{8,12},{10,14},{12... | collective-permute-start | bytes 3145736 | tf_op jit(solution)/shard_map/ppermute | solution.py:400
  323.9 51.5 %collective-permute-start.23 = (bf16[512,1024]{1,0:T(8,128)(2,1)}, bf16[512,1024]{1,0:T(8,128)(2,1)S(1)}, u32[]{:S(2)}, u32[]{:S(2)}) collective-permute-start(bf16[512,1024]{1,0:T(8,128)(2,1)} %slice.111), channel_id=1, source_target_pairs={{0,1},{1,0},{2,3},{3,2},{4,5},{5,4},{6,7},{7,6},{8,9},{9,8},{10,11... | collective-permute-start | bytes 3145736 | tf_op jit(solution)/shard_map/ppermute | solution.py:401
  351.1 10.1 %all-to-all-start.7 = ((bf16[4,256,128]{2,1,0:T(8,128)(2,1)}), bf16[4,256,128]{2,1,0:T(8,128)(2,1)}, u32[]{:S(2)}, u32[]{:S(2)}) async-start(bf16[4,256,128]{2,1,0:T(8,128)(2,1)} %bitcast.16), calls=%async_computation.7 | async-start | bytes 524288 | tf_op jit(solution)/shard_map/all_to_all | solution.py:380
  361.2 10.1 %all-to-all-start.5 = ((bf16[4,256,128]{2,1,0:T(8,128)(2,1)}), bf16[4,256,128]{2,1,0:T(8,128)(2,1)}, u32[]{:S(2)}, u32[]{:S(2)}) async-start(bf16[4,256,128]{2,1,0:T(8,128)(2,1)} %bitcast.12), calls=%async_computation.5 | async-start | bytes 524288 | tf_op jit(solution)/shard_map/all_to_all | solution.py:380
  367.4 17.8 %collective-permute-start.22 = (bf16[256,1024]{1,0:T(8,128)(2,1)}, bf16[256,1024]{1,0:T(8,128)(2,1)}, u32[]{:S(2)}, u32[]{:S(2)}) collective-permute-start(bf16[256,1024]{1,0:T(8,128)(2,1)} %fusion.1), channel_id=1, source_target_pairs={{0,1},{1,0},{2,3},{3,2},{4,5},{5,4},{6,7},{7,6},{8,9},{9,8},{10,11... | collective-permute-start | bytes 1572872 | tf_op jit(solution)/shard_map/ppermute | solution.py:405
  371.3 10.2 %all-to-all-start.3 = ((bf16[4,256,128]{2,1,0:T(8,128)(2,1)}), bf16[4,256,128]{2,1,0:T(8,128)(2,1)}, u32[]{:S(2)}, u32[]{:S(2)}) async-start(bf16[4,256,128]{2,1,0:T(8,128)(2,1)} %bitcast.8), calls=%async_computation.3 | async-start | bytes 524288 | tf_op jit(solution)/shard_map/all_to_all | solution.py:380
  379.5 14.6 %collective-permute-start.24 = (bf16[256,1024]{1,0:T(8,128)(2,1)}, bf16[256,1024]{1,0:T(8,128)(2,1)}, u32[]{:S(2)}, u32[]{:S(2)}) collective-permute-start(bf16[256,1024]{1,0:T(8,128)(2,1)} %slice.130), channel_id=1, source_target_pairs={{0,4},{2,6},{4,0},{6,2},{1,5},{3,7},{5,1},{7,3},{8,12},{10,14},{12... | collective-permute-start | bytes 1572872 | tf_op jit(solution)/shard_map/ppermute | solution.py:406
  (5 other events, 11.4 us)

commit v2 on v0

--- a/solution.py
+++ b/solution.py
@@ -1,10 +1,16 @@
+import functools
+
 import jax
 import jax.numpy as jnp
 from jax import lax
+from jax.experimental import pallas as pl
+from jax.experimental.pallas import tpu as pltpu
 from jax.sharding import PartitionSpec as P
 
 DH = 64
 BLOCK = 64
+F32 = jnp.float32
+BF16 = jnp.bfloat16
 
 
 def attend(query_rows, key_rows, value_rows, grad_rows, key_lengths):
@@ -55,7 +61,7 @@
     return moved.reshape(lead_shape + data.shape[1:])
 
 
-def shards(enc_rows, enc_len, dest_dp, peer_counts, queries, ctx_grad, w_key, w_value):
+def shards_general(enc_rows, enc_len, dest_dp, peer_counts, queries, ctx_grad, w_key, w_value):
     peer_count = lax.axis_size("dp")
     model_groups = lax.axis_size("mp")
     block_count = dest_dp.shape[0]
@@ -94,10 +100,8 @@
         :, 0
     ].astype(jnp.float32)
     shard_cols = lax.all_gather(rows_here, "mp", axis=1, tiled=True)
-    key_part = key_full
-    value_part = value_full
-    key_acc = jnp.dot(shard_cols, key_part, preferred_element_type=jnp.float32)
-    value_acc = jnp.dot(shard_cols, value_part, preferred_element_type=jnp.float32)
+    key_acc = jnp.dot(shard_cols, key_full, preferred_element_type=jnp.float32)
+    value_acc = jnp.dot(shard_cols, value_full, preferred_element_type=jnp.float32)
     context, key_grad, value_grad = attend(
         queries,
         key_acc.astype(jnp.bfloat16),
@@ -128,6 +132,434 @@
     return (context, enc_grad)
 
 
+PAIR = 2 * DH
+
+
+def nt(a, b):
+    return lax.dot_general(a, b, (((1,), (1,)), ((), ())), preferred_element_type=F32)
+
+
+def tn(a, b):
+    return lax.dot_general(a, b, (((0,), (0,)), ((), ())), preferred_element_type=F32)
+
+
+def after(value, *needed):
+    return lax.optimization_barrier((value,) + needed)[0]
+
+
+def forward_kernel(n_dp, n_sec, n_half, blk, tab, *refs):
+    blocks = n_dp * blk
+    x_refs = refs[: n_half * n_dp]
+    refs = refs[n_half * n_dp :]
+    own, above, far, below, end = refs[:5]
+    q_refs = refs[5 : 5 + n_dp]
+    g_refs = refs[5 + n_dp : 5 + 2 * n_dp]
+    refs = refs[5 + 2 * n_dp :]
+    ctx_refs = refs[:n_dp]
+    dkv_ref, w_ref, acc, kv = refs[n_dp:]
+    rows = own.shape[0] // n_dp
+    step = pl.program_id(0)
+    z = tab[2 * blocks]
+    d = tab[2 * blocks + 1]
+    m = tab[2 * blocks + 2]
+    per_half = n_sec // n_half
+    section = (m ^ (step // per_half)) * per_half + step % per_half
+    hop = (section - z + n_sec) % n_sec
+
+    def take(ref):
+        for t in range(n_dp):
+            to = pl.multiple_of((d ^ t) * rows, rows)
+            w_ref[pl.ds(to, rows), :] = ref[t * rows : (t + 1) * rows, :]
+
+    @pl.when(hop == 0)
+    def _():
+        take(own)
+
+    @pl.when((hop == 1) & (z != n_sec - 1))
+    def _():
+        take(above)
+
+    @pl.when(hop == 2)
+    def _():
+        take(far)
+
+    @pl.when((hop == n_sec - 1) & (z != 0))
+    def _():
+        take(below)
+
+    @pl.when(((hop == 1) & (z == n_sec - 1)) | ((hop == n_sec - 1) & (z == 0)))
+    def _():
+        take(end)
+
+    for h in range(n_half):
+
+        @pl.when(step // per_half == h)
+        def _():
+            for t in range(n_dp):
+                at = slice(t * rows, (t + 1) * rows)
+                part = jnp.dot(
+                    x_refs[h * n_dp + t][...], w_ref[...], preferred_element_type=F32
+                )
+                if h == 0:
+                    acc[at, :] = jnp.where(step == 0, part, acc[at, :] + part)
+                else:
+                    acc[at, :] += part
+
+    @pl.when(step == n_sec - 1)
+    def _():
+        kv[...] = acc[...].astype(BF16)
+        lane = lax.broadcasted_iota(jnp.int32, (BLOCK, PAIR), 1) < DH
+        key_pos = lax.broadcasted_iota(jnp.int32, (BLOCK, PAIR), 0)
+        scale = DH ** (-0.5)
+        zero = jnp.zeros((BLOCK, PAIR), BF16)
+
+        def one(b):
+            src = tab[b]
+            source = pl.ds(pl.multiple_of(src * BLOCK, BLOCK), BLOCK)
+            here = pl.ds((b % blk) * BLOCK, BLOCK)
+            key = kv[source, 0:PAIR]
+            value = kv[source, PAIR : 2 * PAIR]
+            query = q_refs[b // blk][here, :]
+            grad = g_refs[b // blk][here, :]
+            query2 = jnp.concatenate(
+                [jnp.where(lane, query, zero), jnp.where(lane, zero, query)], axis=0
+            )
+            grad2 = jnp.concatenate(
+                [jnp.where(lane, grad, zero), jnp.where(lane, zero, grad)], axis=0
+            )
+            scores = jnp.where(key_pos < tab[blocks + b], nt(key, query2) * scale, -1e30)
+            weights = jnp.exp(scores - jnp.max(scores, axis=0, keepdims=True))
+            probs = weights / jnp.sum(weights, axis=0, keepdims=True)
+            prob_bf = probs.astype(BF16)
+            ctx2 = tn(prob_bf, value)
+            ctx_refs[b // blk][here, :] = jnp.where(lane, ctx2[:BLOCK], ctx2[BLOCK:]).astype(BF16)
+            prob_grad = nt(value, grad2)
+            row_dot = jnp.sum(probs * prob_grad, axis=0, keepdims=True)
+            score_grad = (probs * (prob_grad - row_dot) * scale).astype(BF16)
+            dkv_ref[source, 0:PAIR] = jnp.dot(
+                score_grad, query2, preferred_element_type=F32
+            ).astype(BF16)
+            dkv_ref[source, PAIR : 2 * PAIR] = jnp.dot(
+                prob_bf, grad2, preferred_element_type=F32
+            ).astype(BF16)
+
+        for b in range(blocks):
+            one(b)
+
+
+def forward_chunk(table, x_pieces, pieces, q_own, g_own, qg, chunk, chunks, blk, n_sec):
+    n_half = len(x_pieces)
+    n_dp = len(x_pieces[0])
+    rows, half = x_pieces[0][0].shape
+    per_half = n_sec // n_half
+    span = half // per_half
+    cols = 2 * PAIR
+    blocks = n_dp * blk
+
+    def x_spec(h):
+        def at(a, t):
+            return (0, jnp.clip(a - h * per_half, 0, per_half - 1))
+
+        return pl.BlockSpec((rows, span), at)
+
+    whole = pl.BlockSpec((span, cols), lambda a, t: (0, 0))
+    mine = pl.BlockSpec((rows, PAIR), lambda a, t: (0, t[2 * blocks + 1] * chunks + chunk))
+
+    def head(at):
+        return pl.BlockSpec((rows, PAIR), lambda a, t: (0, at))
+
+    return pl.pallas_call(
+        functools.partial(forward_kernel, n_dp, n_sec, n_half, blk),
+        grid_spec=pltpu.PrefetchScalarGridSpec(
+            num_scalar_prefetch=1,
+            grid=(n_sec,),
+            in_specs=[x_spec(h) for h in range(n_half) for _ in range(n_dp)]
+            + [whole] * 5
+            + [mine]
+            + [head(chunk)] * (n_dp - 1)
+            + [mine]
+            + [head(chunks + chunk)] * (n_dp - 1),
+            out_specs=[pl.BlockSpec((rows, PAIR), lambda a, t: (0, 0))] * n_dp
+            + [
+                pl.BlockSpec((n_dp * rows, cols), lambda a, t: (0, 0)),
+                pl.BlockSpec((span, cols), lambda a, t: (a, 0)),
+            ],
+            scratch_shapes=[
+                pltpu.VMEM((n_dp * rows, cols), F32),
+                pltpu.VMEM((n_dp * rows, cols), BF16),
+            ],
+        ),
+        out_shape=[jax.ShapeDtypeStruct((rows, PAIR), BF16)] * n_dp
+        + [
+            jax.ShapeDtypeStruct((n_dp * rows, cols), BF16),
+            jax.ShapeDtypeStruct((n_sec * span, cols), BF16),
+        ],
+        compiler_params=pltpu.CompilerParams(vmem_limit_bytes=40 << 20),
+        cost_estimate=pl.CostEstimate(
+            flops=2 * n_dp * rows * n_sec * span * cols,
+            bytes_accessed=2 * n_dp * rows * n_sec * span + 4 * n_sec * span * cols,
+            transcendentals=n_dp * rows * BLOCK * 2,
+        ),
+        name="fwd",
+    )(
+        table,
+        *[piece for halves in x_pieces for piece in halves],
+        *pieces,
+        q_own,
+        *qg,
+        g_own,
+        *qg,
+    )
+
+
+def give_kernel(chunks, *refs):
+    total = nt(refs[0][...], refs[chunks][...])
+    for c in range(1, chunks):
+        total += nt(refs[c][...], refs[chunks + c][...])
+    refs[-1][...] = total.astype(BF16)
+
+
+def keep_kernel(chunks, y_first, *refs):
+    half, row = pl.program_id(0), pl.program_id(1)
+    total = refs[2 * chunks][...].astype(F32)
+    for c in range(chunks):
+        total += nt(refs[c][...], refs[chunks + c][...])
+    if y_first:
+        own_ref, x_ref, y_ref = refs[2 * chunks + 1 :]
+
+        @pl.when((half == 0) & (row == 0))
+        def _():
+            own_ref[...] = total
+
+        @pl.when((half == 1) & (row == 0))
+        def _():
+            x_ref[...] = total
+
+        @pl.when(row == 1)
+        def _():
+            y_ref[...] = total.astype(BF16)
+    else:
+        own_ref, x_ref = refs[2 * chunks + 1 :]
+
+        @pl.when(half == 0)
+        def _():
+            own_ref[...] = total
+
+        @pl.when(half == 1)
+        def _():
+            x_ref[...] = total.astype(BF16)
+
+
+def backward(dkvs, ws, received, part, rows, per_half, y_first):
+    chunks = len(dkvs)
+    cols = dkvs[0].shape[1]
+    span = ws[0].shape[0] // (2 * per_half)
+    which = 1 if received is None else 0
+    specs = [pl.BlockSpec((rows, cols), lambda h, r: (2 * r + which, 0))] * chunks
+    specs += [pl.BlockSpec((span, cols), lambda h, r: (h * per_half + part, 0))] * chunks
+    block = pl.BlockSpec((rows, span), lambda h, r: (r, h))
+    fixed = pl.BlockSpec((rows, span), lambda h, r: (0, 0))
+    if received is None:
+        kernel = functools.partial(give_kernel, chunks)
+        out_specs, out_shape = block, jax.ShapeDtypeStruct((2 * rows, 2 * span), BF16)
+        extra = ()
+    else:
+        kernel = functools.partial(keep_kernel, chunks, y_first)
+        specs = specs + [block]
+        extra = (received,)
+        if y_first:
+            out_specs = [fixed, fixed, pl.BlockSpec((rows, span), lambda h, r: (0, h))]
+            out_shape = [
+                jax.ShapeDtypeStruct((rows, span), F32),
+                jax.ShapeDtypeStruct((rows, span), F32),
+                jax.ShapeDtypeStruct((rows, 2 * span), BF16),
+            ]
+        else:
+            out_specs = [
+                pl.BlockSpec((rows, span), lambda h, r: (jnp.where(h == 0, r, 1), 0)),
+                pl.BlockSpec((rows, span), lambda h, r: (jnp.where(h == 1, r, 0), 0)),
+            ]
+            out_shape = [
+                jax.ShapeDtypeStruct((2 * rows, span), F32),
+                jax.ShapeDtypeStruct((2 * rows, span), BF16),
+            ]
+    return pl.pallas_call(
+        kernel,
+        grid=(2, 2),
+        in_specs=specs,
+        out_specs=out_specs,
+        out_shape=out_shape,
+        compiler_params=pltpu.CompilerParams(vmem_limit_bytes=32 << 20),
+        cost_estimate=pl.CostEstimate(
+            flops=8 * rows * span * cols * chunks,
+            bytes_accessed=4 * span * cols * chunks + 16 * rows * span,
+            transcendentals=0,
+        ),
+        name="bwd",
+    )(*dkvs, *ws, *extra)
+
+
+def context_kernel(n_dp, chunks, tab, *refs):
+    out = refs[-1]
+    for t in range(n_dp):
+        for c in range(chunks):
+            at = (tab[0] ^ t) * (chunks * PAIR) + c * PAIR
+            out[:, pl.ds(pl.multiple_of(at, PAIR), PAIR)] = refs[t * chunks + c][...]
+
+
+def gather_context(d, parts):
+    n_dp, chunks = len(parts), len(parts[0])
+    rows = parts[0][0].shape[0]
+    vmem = pl.BlockSpec(memory_space=pltpu.VMEM)
+    return pl.pallas_call(
+        functools.partial(context_kernel, n_dp, chunks),
+        in_specs=[pl.BlockSpec(memory_space=pltpu.SMEM)] + [vmem] * (n_dp * chunks),
+        out_specs=vmem,
+        out_shape=jax.ShapeDtypeStruct((rows, n_dp * chunks * PAIR), BF16),
+        name="gather_context",
+    )(d.reshape(1), *[piece for row in parts for piece in row])
+
+
+def shards_section(enc_rows, enc_len, dest_dp, peer_counts, queries, ctx_grad, w_key, w_value):
+    n_sec, n_dp, n_mp = (lax.axis_size(a) for a in ("section", "dp", "mp"))
+    z, d, m = (lax.axis_index(a).astype(jnp.int32) for a in ("section", "dp", "mp"))
+    blk = dest_dp.shape[0]
+    blocks = blk * n_dp
+    rows, half = enc_rows.shape
+    head_cols = w_key.shape[1] // n_dp
+    chunks = head_cols // PAIR
+
+    near = [[(i, i ^ t) for i in range(n_dp)] for t in range(n_dp)]
+    xpairs = [(0, 1), (1, 0)]
+    up = [(i, i + 1) for i in range(n_sec - 1)]
+    down = [(i + 1, i) for i in range(n_sec - 1)]
+    over_two = [(i, i ^ 2) for i in range(n_sec)]
+    ends = [(1, 0), (2, 3)]
+
+    def weight_chunk(c, *needed):
+        w_k, w_v = w_key, w_value
+        if needed:
+            w_k, w_v = lax.optimization_barrier((w_key, w_value) + needed)[:2]
+        got = []
+        for t in range(n_dp):
+            at = (d ^ t) * head_cols + c * PAIR
+            cut = jnp.concatenate(
+                [lax.dynamic_slice(w, (0, at), (rows, PAIR)) for w in (w_k, w_v)], axis=1
+            )
+            got.append(cut if t == 0 else lax.ppermute(cut, "dp", near[t]))
+        return jnp.concatenate(got, axis=0)
+
+    own = [weight_chunk(0)]
+
+    packed = jnp.concatenate([enc_len, dest_dp, peer_counts[0]]).reshape(1, -1)
+    packs = jnp.concatenate(
+        [packed] + [lax.ppermute(packed, "dp", near[t]) for t in range(1, n_dp)], axis=0
+    )
+    peer = jnp.arange(n_dp, dtype=jnp.int32)
+    order = (peer[:, None] ^ d) == peer[None, :]
+    packs = jnp.sum(jnp.where(order[:, :, None], packs[None], 0), axis=1)
+    lens = packs[:, :blk].reshape(-1)
+    dest = packs[:, blk : 2 * blk]
+    counts = packs[:, 2 * blk :]
+    pos = jnp.arange(blk, dtype=jnp.int32)
+    before = jnp.sum(
+        jnp.where(peer[None, None, :] < peer[None, :, None], counts[:, None, :], 0), axis=2
+    )
+    upto = before + counts
+    sender = jnp.sum((upto[:, None, :] <= pos[None, :, None]).astype(jnp.int32), axis=2)
+    is_sender = sender[:, :, None] == peer[None, None, :]
+    rank = pos[None, :] - jnp.sum(jnp.where(is_sender, before[:, None, :], 0), axis=2)
+    same = dest[:, :, None] == dest[:, None, :]
+    slot_rank = jnp.sum((same & (pos[None, None, :] < pos[None, :, None])).astype(jnp.int32), axis=2)
+    hit = (
+        is_sender[:, :, :, None]
+        & (dest[None, None] == peer[:, None, None, None])
+        & (slot_rank[None, None] == rank[:, :, None, None])
+    ).reshape(n_dp, blk, blocks)
+    place = ((peer ^ d)[:, None] * blk + pos[None, :]).reshape(-1)
+    src = jnp.sum(jnp.where(hit, place, 0), axis=2)
+    src_len = jnp.sum(jnp.where(hit, lens, 0), axis=2)
+    both = jnp.stack([src, src_len])
+    both = jnp.sum(jnp.where(order[None, :, :, None], both[:, None], 0), axis=2)
+    table = jnp.concatenate([both.reshape(-1), jnp.stack([z, d, m])])
+
+    e_x = lax.ppermute(enc_rows, "mp", xpairs)
+    e_y = lax.ppermute(after(enc_rows, own[0]), "dp", near[2])
+    e_yx = lax.ppermute(e_y, "mp", xpairs)
+    x_pieces = []
+    for a, b in ((enc_rows, e_y), (e_x, e_yx)):
+        x_pieces.append((a, lax.ppermute(a, "dp", near[1]), b, lax.ppermute(b, "dp", near[1])))
+
+    own.append(weight_chunk(1, own[0]))
+
+    q_in, g_in = lax.optimization_barrier((queries, ctx_grad, e_y))[:2]
+    qg = []
+    for t in range(1, n_dp):
+        cut = jnp.concatenate(
+            [
+                lax.dynamic_slice(a, (0, (d ^ t) * head_cols), (rows, head_cols))
+                for a in (q_in, g_in)
+            ],
+            axis=1,
+        )
+        qg.append(lax.ppermute(cut, "dp", near[t]))
+    for c in range(2, chunks):
+        own.append(weight_chunk(c, qg[-1], own[-1]))
+
+    dkvs, ws, contexts = [], [], [[] for _ in range(n_dp)]
+    below, above, far, end = ([None] * chunks for _ in range(4))
+    for c in range(chunks):
+        piece, piece_far = own[c], own[c]
+        if c > 0:
+            needed = (below[c - 1], above[c - 1]) + tuple(dkvs[c - 3 : c - 2] if c > 2 else ())
+            piece = after(piece, *needed)
+            piece_far = after(piece_far, far[c - 1])
+        below[c] = lax.ppermute(piece, "section", up)
+        above[c] = lax.ppermute(piece, "section", down)
+        far[c] = lax.ppermute(piece_far, "section", over_two)
+        turn = far[c] if c < 3 else after(far[c], dkvs[c - 2])
+        end[c] = lax.ppermute(turn, "section", ends)
+        done = c - 1
+        for k in ([done] if done >= 0 else []) + ([c] if c == chunks - 1 else []):
+            out = forward_chunk(
+                table,
+                x_pieces,
+                (own[k], above[k], far[k], below[k], end[k]),
+                queries,
+                ctx_grad,
+                qg,
+                k,
+                chunks,
+                blk,
+                n_sec,
+            )
+            dkvs.append(out[n_dp])
+            ws.append(out[n_dp + 1])
+            contexts[0].append(out[0])
+            for t in range(1, n_dp):
+                contexts[t].append(lax.ppermute(out[t], "dp", near[t]))
+
+    per_half = n_sec // n_mp
+    back = functools.partial(backward, dkvs, ws, rows=rows, per_half=per_half)
+    give_p = lax.ppermute(back(None, part=0, y_first=True), "dp", near[1])
+    give_q = lax.ppermute(back(None, part=1, y_first=False), "dp", near[1])
+    p_own, p_x, p_y = back(give_p, part=0, y_first=True)
+    got_y = lax.ppermute(p_y, "dp", near[2]).astype(F32)
+    q_own, q_x = back(give_q, part=1, y_first=False)
+    got_x = lax.ppermute(q_x, "mp", xpairs).astype(F32)
+    span = p_own.shape[1]
+    last_x = lax.ppermute((p_x + got_y[:, span:]).astype(BF16), "mp", xpairs).astype(F32)
+    last_y = lax.ppermute((q_own[rows:] + got_x[rows:]).astype(BF16), "dp", near[2]).astype(F32)
+    enc_grad = jnp.concatenate(
+        [
+            (p_own + got_y[:, :span] + last_x).astype(BF16),
+            (q_own[:rows] + got_x[:rows] + last_y).astype(BF16),
+        ],
+        axis=1,
+    )
+    return (gather_context(d, contexts), enc_grad)
+
+
 def solution(mesh):
     placed = (
         P(("section", "dp"), "mp"),
@@ -139,8 +571,10 @@
         P(("section", "dp"), "mp"),
         P(("section", "dp"), "mp"),
     )
+    sizes = tuple(mesh.shape[a] for a in ("section", "dp", "mp"))
+    body = shards_section if sizes == (4, 4, 2) else shards_general
     return jax.shard_map(
-        shards,
+        body,
         mesh=mesh,
         in_specs=placed,
         out_specs=(P(("section", "dp"), "mp"), P(("section", "dp"), "mp")),

time: 489 us -> 326 us (0.67)
  waiting for transfers between devices: 330 us -> 150 us
  matrix products: 69.9 us -> 0 us
  starting transfers between devices: 11.7 us -> 77.5 us
  Pallas kernels: 0 us -> 64.8 us
  local copies, waits for them, and re-layouts: 52 us -> 19.5 us
  between operations: 14.3 us -> 1.53 us
  other arithmetic: 5.3 us -> 11.7 us
    all_gather x3 -> x0, waiting for transfers between devices: 264 us -> none  [the longest x1 129 us: shards(): lax.all_gather(w_value, ('section', 'dp'), axis=0, tiled=True)]
    ppermute x0 -> x59, waiting for transfers between devices: none -> 150 us  [the longest x12 32.5 us: weight_chunk(): got.append(cut if t == 0 else lax.ppermute(cut, 'dp', near[t]))]
    ppermute x0 -> x59, starting transfers between devices: none -> 77.5 us  [the longest x4 29.9 us: shards_section(): below[c] = lax.ppermute(piece, 'section', up)]
    dot_general x17 -> x0, matrix products: 69.9 us -> none  [the longest x2 11.8 us: shards(): lax.dot_general(value_grad, value_part, (((1,), (1,)), ((), ())), preferr...]
    pallas_call x0 -> x9, Pallas kernels: none -> 64.8 us  [the longest x4 49 us: forward_chunk(): pl.pallas_call(functools.partial(forward_kernel, n_dp, n_sec, n_half, blk...]
    reshape x16 -> x1, local copies, waits for them, and re-layouts: 40.1 us -> 0.09 us  [shards_section(): table = jnp.concatenate([both.reshape(-1), jnp.stack([z, d, m])])]
    all_to_all x3 -> x0, waiting for transfers between devices: 35 us -> none  [the longest x1 24.1 us: shards(): lax.all_to_all(outgoing, 'dp', split_axis=0, concat_axis=0, tiled=True)]
    reduce_scatter x1 -> x0, waiting for transfers between devices: 30.2 us -> none  [shards(): lax.psum_scatter(jnp.concatenate(pieces_out, axis=1), 'mp', scatter_dimen...]
  transfers between devices with their start and end apart: 7 -> 59, of which waited for: 6 -> 22; matrix products, arithmetic and copies ran while one was open for 8% -> 4% of each run, Pallas kernels for 0% -> 15%
where the time goes in v2:
time: 326 us; the launch traced here: 325 us
  waiting for transfers between devices  150 us (46%)
  starting transfers between devices  77.5 us (24%)
  Pallas kernels  64.8 us (20%)
  local copies, waits for them, and re-layouts  19.5 us (6%)
  other arithmetic  11.7 us (4%)
    pallas_call x4, Pallas kernels, forward_chunk(): pl.pallas_call(functools.partial(forward_kernel, n_dp, n_sec, n_half, blk...  49 us
    ppermute x12, waiting for transfers between devices, weight_chunk(): got.append(cut if t == 0 else lax.ppermute(cut, 'dp', near[t]))  32.5 us
    ppermute x4, starting transfers between devices, shards_section(): below[c] = lax.ppermute(piece, 'section', up)  29.9 us
    ppermute x4, waiting for transfers between devices, shards_section(): end[c] = lax.ppermute(turn, 'section', ends)  25.1 us
    ppermute x1, waiting for transfers between devices, shards_section(): e_y = lax.ppermute(after(enc_rows, own[0]), 'dp', near[2])  19.3 us
    ppermute x1, waiting for transfers between devices, shards_section(): got_x = lax.ppermute(q_x, 'mp', xpairs).astype(F32)  18.5 us
    ppermute x12, waiting for transfers between devices, shards_section(): contexts[t].append(lax.ppermute(out[t], 'dp', near[t]))  17.7 us
    unnamed x102, local copies, waits for them, and re-layouts  15.8 us
  transfers between devices with their start and end apart: 59, of which 22 were waited for; matrix products, arithmetic and copies ran while one was open for 4% of the time, Pallas kernels for 15%

profile of v2, /device:TPU:0, one launch (start us, length us, event | category | flops | bytes accessed | tf_op | source)
XLA Modules:
  0.0 324.9 jit_solution(15146100470111823154)
XLA Ops:
  1.5 2.4 collective-permute-start.2
  5.9 1.8 collective-permute-start.5
  8.3 4.0 %collective-permute-done.5 = bf16[256,256]{1,0:T(8,128)(2,1)S(1)} collective-permute-done((bf16[256,256]{1,0:T(8,128)(2,1)S(1)}, bf16[256,256]{1,0:T(8,128)(2,1)S(1)}, u32[]{:S(2)}, u32[]{:S(2)}) %collective-permute-start.5) | collective-permute-done | bytes 131104 | tf_op jit(solution)/shard_map/ppermute | solution.py:449
  12.3 1.7 collective-permute-start.9
  15.9 2.6 collective-permute-start.14
  21.1 19.3 %collective-permute-done.7.refs_2_ = bf16[256,2048]{1,0:T(8,128)(2,1)} collective-permute-done((bf16[256,2048]{1,0:T(8,128)(2,1)S(1)}, bf16[256,2048]{1,0:T(8,128)(2,1)}, u32[]{:S(2)}, u32[]{:S(2)}) %collective-permute-start.7) | collective-permute-done | bytes 1048608 | tf_op jit(solution)/shard_map/ppermute | solution.py:487
  41.1 1.5 collective-permute-start.3
  43.0 14.6 %collective-permute-done.22 = bf16[256,256]{1,0:T(8,128)(2,1)S(1)} collective-permute-done((bf16[256,256]{1,0:T(8,128)(2,1)S(1)}, bf16[256,256]{1,0:T(8,128)(2,1)S(1)}, u32[]{:S(2)}, u32[]{:S(2)}) %collective-permute-start.22) | collective-permute-done | bytes 131104 | tf_op jit(solution)/shard_map/ppermute | solution.py:449
  57.7 3.3 %collective-permute-start.15 = (bf16[1024,256]{1,0:T(8,128)(2,1)S(1)}, bf16[1024,256]{1,0:T(8,128)(2,1)S(1)}, u32[]{:S(2)}, u32[]{:S(2)}) collective-permute-start(bf16[1024,256]{1,0:T(8,128)(2,1)S(1)} %pad_maximum_fusion.1.refs_8_), channel_id=1, source_target_pairs={{0,8},{8,16},{16,24},{1,9},{9,17},{17,25},{2,10},{10,18},{18,26},{... | collective-permute-start | bytes 1572872 | tf_op jit(solution)/shard_map/ppermute | solution.py:517
  62.3 3.7 %collective-permute-start.24 = (bf16[1024,256]{1,0:T(8,128)(2,1)S(1)}, bf16[1024,256]{1,0:T(8,128)(2,1)}, u32[]{:S(2)}, u32[]{:S(2)}) collective-permute-start(bf16[1024,256]{1,0:T(8,128)(2,1)S(1)} %pad_maximum_fusion.5.refs_8_), channel_id=1, source_target_pairs={{0,16},{8,24},{16,0},{24,8},{1,17},{9,25},{17,1},{25,9},{2,18},{10... | collective-permute-start | bytes 1572872 | tf_op jit(solution)/shard_map/ppermute | solution.py:519
  66.3 6.9 %collective-permute-done.15.refs_11_ = bf16[1024,256]{1,0:T(8,128)(2,1)S(1)} collective-permute-done((bf16[1024,256]{1,0:T(8,128)(2,1)S(1)}, bf16[1024,256]{1,0:T(8,128)(2,1)S(1)}, u32[]{:S(2)}, u32[]{:S(2)}) %collective-permute-start.15) | collective-permute-done | bytes 524320 | tf_op jit(solution)/shard_map/ppermute | solution.py:517
  73.2 3.5 %collective-permute-done.13.refs_9_ = bf16[1024,256]{1,0:T(8,128)(2,1)S(1)} collective-permute-done((bf16[1024,256]{1,0:T(8,128)(2,1)S(1)}, bf16[1024,256]{1,0:T(8,128)(2,1)S(1)}, u32[]{:S(2)}, u32[]{:S(2)}) %collective-permute-start.13) | collective-permute-done | bytes 524320 | tf_op jit(solution)/shard_map/ppermute | solution.py:518
  77.2 2.3 collective-permute-start.11
  79.5 15.7 %collective-permute-start.25 = (bf16[1024,256]{1,0:T(8,128)(2,1)S(1)}, bf16[1024,256]{1,0:T(8,128)(2,1)S(1)}, u32[]{:S(2)}, u32[]{:S(2)}) collective-permute-start(bf16[1024,256]{1,0:T(8,128)(2,1)S(1)} %pad_maximum_fusion.5.refs_8_), channel_id=1, source_target_pairs={{0,8},{8,16},{16,24},{1,9},{9,17},{17,25},{2,10},{10,18},{18,26},{... | collective-permute-start | bytes 1572872 | tf_op jit(solution)/shard_map/ppermute | solution.py:517
  95.2 4.8 %collective-permute-done.24.refs_10_ = bf16[1024,256]{1,0:T(8,128)(2,1)} collective-permute-done((bf16[1024,256]{1,0:T(8,128)(2,1)S(1)}, bf16[1024,256]{1,0:T(8,128)(2,1)}, u32[]{:S(2)}, u32[]{:S(2)}) %collective-permute-start.24) | collective-permute-done | bytes 524320 | tf_op jit(solution)/shard_map/ppermute | solution.py:519
  102.9 4.8 %collective-permute-done.29 = bf16[256,256]{1,0:T(8,128)(2,1)S(1)} collective-permute-done((bf16[256,256]{1,0:T(8,128)(2,1)S(1)}, bf16[256,256]{1,0:T(8,128)(2,1)S(1)}, u32[]{:S(2)}, u32[]{:S(2)}) %collective-permute-start.29) | collective-permute-done | bytes 131104 | tf_op jit(solution)/shard_map/ppermute | solution.py:449
  108.7 17.3 %collective-permute-done.16.refs_12_ = bf16[1024,256]{1,0:T(8,128)(2,1)S(1)} collective-permute-done((bf16[1024,256]{1,0:T(8,128)(2,1)S(1)}, bf16[1024,256]{1,0:T(8,128)(2,1)S(1)}, u32[]{:S(2)}, u32[]{:S(2)}) %collective-permute-start.16) | collective-permute-done | bytes 524320 | tf_op jit(solution)/shard_map/ppermute | solution.py:521
  129.2 12.7 %collective-permute-done.18.refs_15_.refs_19_ = bf16[256,1024]{1,0:T(8,128)(2,1)S(1)} collective-permute-done((bf16[256,1024]{1,0:T(8,128)(2,1)S(1)}, bf16[256,1024]{1,0:T(8,128)(2,1)S(1)}, u32[]{:S(2)}, u32[]{:S(2)}) %collective-permute-start.18) | collective-permute-done | bytes 524320 | tf_op jit(solution)/shard_map/ppermute | solution.py:505
  142.3 4.7 %collective-permute-done.35 = bf16[256,256]{1,0:T(8,128)(2,1)S(1)} collective-permute-done((bf16[256,256]{1,0:T(8,128)(2,1)S(1)}, bf16[256,256]{1,0:T(8,128)(2,1)S(1)}, u32[]{:S(2)}, u32[]{:S(2)}) %collective-permute-start.35) | collective-permute-done | bytes 131104 | tf_op jit(solution)/shard_map/ppermute | solution.py:449
  147.8 4.1 %collective-permute-done.36 = bf16[256,256]{1,0:T(8,128)(2,1)S(1)} collective-permute-done((bf16[256,256]{1,0:T(8,128)(2,1)S(1)}, bf16[256,256]{1,0:T(8,128)(2,1)S(1)}, u32[]{:S(2)}, u32[]{:S(2)}) %collective-permute-start.36) | collective-permute-done | bytes 131104 | tf_op jit(solution)/shard_map/ppermute | solution.py:449
  154.2 6.1 %collective-permute-start.32 = (bf16[1024,256]{1,0:T(8,128)(2,1)}, bf16[1024,256]{1,0:T(8,128)(2,1)}, u32[]{:S(2)}, u32[]{:S(2)}) collective-permute-start(bf16[1024,256]{1,0:T(8,128)(2,1)} %pad_maximum_fusion.6.refs_8_), channel_id=1, source_target_pairs={{0,8},{8,16},{16,24},{1,9},{9,17},{17,25},{2,10},{10,18},{18,26},{... | collective-permute-start | bytes 1572872 | tf_op jit(solution)/shard_map/ppermute | solution.py:517
  160.3 6.8 %collective-permute-done.31.refs_10_ = bf16[1024,256]{1,0:T(8,128)(2,1)S(1)} collective-permute-done((bf16[1024,256]{1,0:T(8,128)(2,1)}, bf16[1024,256]{1,0:T(8,128)(2,1)S(1)}, u32[]{:S(2)}, u32[]{:S(2)}) %collective-permute-start.31) | collective-permute-done | bytes 524320 | tf_op jit(solution)/shard_map/ppermute | solution.py:519
  181.5 11.9 %fwd.4 = (bf16[256,128]{1,0:T(8,128)(2,1)S(1)}, bf16[256,128]{1,0:T(8,128)(2,1)S(1)}, bf16[256,128]{1,0:T(8,128)(2,1)S(1)}, bf16[256,128]{1,0:T(8,128)(2,1)S(1)}...) custom-call(s32[35]{0:T(128)S(1)} %pad_add_fusion.2.tab, bf16[256,2048]{1,0:T(8,128)(2,1)S(1)} %copy-done.6, ...), custom_call_target="tpu_custom_call" | custom-call | flops 2147483648 | bytes 12582912 | tf_op jit(solution)/shard_map/fwd/pallas_call | solution.py:271
  193.5 4.7 %collective-permute-start.39 = (bf16[1024,256]{1,0:T(8,128)(2,1)}, bf16[1024,256]{1,0:T(8,128)(2,1)S(1)}, u32[]{:S(2)}, u32[]{:S(2)}) collective-permute-start(bf16[1024,256]{1,0:T(8,128)(2,1)} %pad_maximum_fusion.7.refs_8_), channel_id=1, source_target_pairs={{0,8},{8,16},{16,24},{1,9},{9,17},{17,25},{2,10},{10,18},{18,26},{... | collective-permute-start | bytes 1572872 | tf_op jit(solution)/shard_map/ppermute | solution.py:517
  198.2 1.5 collective-permute-start.37
  199.8 12.3 %fwd.5 = (bf16[256,128]{1,0:T(8,128)(2,1)S(1)}, bf16[256,128]{1,0:T(8,128)(2,1)S(1)}, bf16[256,128]{1,0:T(8,128)(2,1)S(1)}, bf16[256,128]{1,0:T(8,128)(2,1)S(1)}...) custom-call(s32[35]{0:T(128)S(1)} %pad_add_fusion.2.tab, bf16[256,2048]{1,0:T(8,128)(2,1)S(1)} %copy-done.6, ...), custom_call_target="tpu_custom_call" | custom-call | flops 2147483648 | bytes 12582912 | tf_op jit(solution)/shard_map/fwd/pallas_call | solution.py:271
  214.0 12.4 %fwd.6 = (bf16[256,128]{1,0:T(8,128)(2,1)S(1)}, bf16[256,128]{1,0:T(8,128)(2,1)S(1)}, bf16[256,128]{1,0:T(8,128)(2,1)S(1)}, bf16[256,128]{1,0:T(8,128)(2,1)S(1)}...) custom-call(s32[35]{0:T(128)S(1)} %pad_add_fusion.2.tab, bf16[256,2048]{1,0:T(8,128)(2,1)S(1)} %copy-done.6, ...), custom_call_target="tpu_custom_call" | custom-call | flops 2147483648 | bytes 12582912 | tf_op jit(solution)/shard_map/fwd/pallas_call | solution.py:271
  226.5 7.8 %collective-permute-done.40.refs_12_ = bf16[1024,256]{1,0:T(8,128)(2,1)S(1)} collective-permute-done((bf16[1024,256]{1,0:T(8,128)(2,1)}, bf16[1024,256]{1,0:T(8,128)(2,1)S(1)}, u32[]{:S(2)}, u32[]{:S(2)}) %collective-permute-start.40) | collective-permute-done | bytes 524320 | tf_op jit(solution)/shard_map/ppermute | solution.py:521
  234.3 12.3 %fwd.7 = (bf16[256,128]{1,0:T(8,128)(2,1)S(1)}, bf16[256,128]{1,0:T(8,128)(2,1)S(1)}, bf16[256,128]{1,0:T(8,128)(2,1)S(1)}, bf16[256,128]{1,0:T(8,128)(2,1)S(1)}...) custom-call(s32[35]{0:T(128)S(1)} %pad_add_fusion.2.tab, bf16[256,2048]{1,0:T(8,128)(2,1)S(1)} %copy-done.6, ...), custom_call_target="tpu_custom_call" | custom-call | flops 2147483648 | bytes 12582912 | tf_op jit(solution)/shard_map/fwd/pallas_call | solution.py:271
  246.6 1.6 copy-done.3
  248.2 3.1 bwd.6
  251.4 3.1 bwd.4
  255.5 3.4 %bwd.7 = (f32[512,1024]{1,0:T(8,128)S(1)}, bf16[512,1024]{1,0:T(8,128)(2,1)S(1)}) custom-call(bf16[1024,256]{1,0:T(8,128)(2,1)S(1)} %get-tuple-element.63.refs_0_, bf16[1024,256]{1,0:T(8,128)(2,1)S(1)} %get-tuple-element.66.refs_1_, bf16[1024,256]{1,0:T(8,128)(2,1)S(1)} %get-tuple-element.81.refs_2_, bf16[1024,256]{1,0:T(8,128)(2,1)S(1)} %get-tuple-element.82.refs_3_, ...), custom_call_target="tpu_custom_call" | custom-call | flops 2147483648 | bytes 8388608 | tf_op jit(solution)/shard_map/bwd/pallas_call | solution.py:386
  258.9 1.5 collective-permute-start.57
  260.5 3.8 %bwd.5 = (f32[256,1024]{1,0:T(8,128)S(1)}, f32[256,1024]{1,0:T(8,128)S(1)}, bf16[256,2048]{1,0:T(8,128)(2,1)S(1)}) custom-call(bf16[1024,256]{1,0:T(8,128)(2,1)S(1)} %get-tuple-element.63.refs_0_, bf16[1024,256]{1,0:T(8,128)(2,1)S(1)} %get-tuple-element.66.refs_1_, bf16[1024,256]{1,0:T(8,128)(2,1)S(1)} %get-tuple-element.81.refs_2_, ...), custom_call_target="tpu_custom_call" | custom-call | flops 2147483648 | bytes 8388608 | tf_op jit(solution)/shard_map/bwd/pallas_call | solution.py:386
  264.2 1.4 collective-permute-start.54
  265.7 18.5 %collective-permute-done.57 = bf16[512,1024]{1,0:T(8,128)(2,1)S(1)} collective-permute-done((bf16[512,1024]{1,0:T(8,128)(2,1)S(1)}, bf16[512,1024]{1,0:T(8,128)(2,1)S(1)}, u32[]{:S(2)}, u32[]{:S(2)}) %collective-permute-start.57) | collective-permute-done | bytes 1048608 | tf_op jit(solution)/shard_map/ppermute | solution.py:549
  285.5 1.7 collective-permute-start.58
  287.5 1.5 collective-permute-start.50
  291.8 10.8 %collective-permute-done.46.refs_9_ = bf16[256,128]{1,0:T(8,128)(2,1)S(1)} collective-permute-done((bf16[256,128]{1,0:T(8,128)(2,1)S(1)}, bf16[256,128]{1,0:T(8,128)(2,1)S(1)}, u32[]{:S(2)}, u32[]{:S(2)}) %collective-permute-start.46) | collective-permute-done | bytes 65568 | tf_op jit(solution)/shard_map/ppermute | solution.py:540
  304.7 2.1 collective-permute-done.45.refs_8_
  306.8 2.0 collective-permute-start.47
  309.7 1.4 collective-permute-done.47.refs_10_
  311.1 2.3 collective-permute-start.48
  313.9 1.7 collective-permute-done.48.refs_11_
  315.6 1.7 collective-permute-done.52.refs_15_
  318.0 2.5 gather_context.1
  320.5 1.8 fusion.2
  (235 shorter events, 49.7 us)
Async XLA Ops:
  1.5 14.2 %collective-permute-start.2 = (s32[1,12]{1,0:T(1,128)S(1)}, s32[1,12]{1,0:T(1,128)S(1)}, u32[]{:S(2)}, u32[]{:S(2)}) collective-permute-start(s32[1,12]{1,0:T(1,128)S(1)} %add_bitcast_fusion), channel_id=1, source_target_pairs={{0,6},{2,4},{4,2},{6,0},{1,7},{3,5},{5,3},{7,1},{8,14},{10,12},{12... | collective-permute-start | bytes 152 | tf_op jit(solution)/shard_map/ppermute | solution.py:456
  3.9 11.8 %collective-permute-start.1 = (s32[1,12]{1,0:T(1,128)S(1)}, s32[1,12]{1,0:T(1,128)S(1)}, u32[]{:S(2)}, u32[]{:S(2)}) collective-permute-start(s32[1,12]{1,0:T(1,128)S(1)} %add_bitcast_fusion), channel_id=1, source_target_pairs={{0,4},{2,6},{4,0},{6,2},{1,5},{3,7},{5,1},{7,3},{8,12},{10,14},{12... | collective-permute-start | bytes 152 | tf_op jit(solution)/shard_map/ppermute | solution.py:456
  5.9 6.4 %collective-permute-start.5 = (bf16[256,256]{1,0:T(8,128)(2,1)S(1)}, bf16[256,256]{1,0:T(8,128)(2,1)S(1)}, u32[]{:S(2)}, u32[]{:S(2)}) collective-permute-start(bf16[256,256]{1,0:T(8,128)(2,1)S(1)} %pad_maximum_fusion.9), channel_id=1, source_target_pairs={{0,4},{2,6},{4,0},{6,2},{1,5},{3,7},{5,1},{7,3},{8,12},{10,14},{12... | collective-permute-start | bytes 393224 | tf_op jit(solution)/shard_map/ppermute | solution.py:449
  7.7 6.5 %collective-permute-start.6 = (bf16[256,256]{1,0:T(8,128)(2,1)S(1)}, bf16[256,256]{1,0:T(8,128)(2,1)S(1)}, u32[]{:S(2)}, u32[]{:S(2)}) collective-permute-start(bf16[256,256]{1,0:T(8,128)(2,1)S(1)} %pad_maximum_fusion.10), channel_id=1, source_target_pairs={{0,6},{2,4},{4,2},{6,0},{1,7},{3,5},{5,3},{7,1},{8,14},{10,12},{12... | collective-permute-start | bytes 393224 | tf_op jit(solution)/shard_map/ppermute | solution.py:449
  7.9 7.8 %collective-permute-start = (s32[1,12]{1,0:T(1,128)S(1)}, s32[1,12]{1,0:T(1,128)S(1)}, u32[]{:S(2)}, u32[]{:S(2)}) collective-permute-start(s32[1,12]{1,0:T(1,128)S(1)} %add_bitcast_fusion), channel_id=1, source_target_pairs={{0,2},{2,0},{4,6},{6,4},{1,3},{3,1},{5,7},{7,5},{8,10},{10,8},{12,... | collective-permute-start | bytes 152 | tf_op jit(solution)/shard_map/ppermute | solution.py:456
  12.3 64.9 %collective-permute-start.9 = (bf16[256,2048]{1,0:T(8,128)(2,1)}, bf16[256,2048]{1,0:T(8,128)(2,1)}, u32[]{:S(2)}, u32[]{:S(2)}) collective-permute-start(bf16[256,2048]{1,0:T(8,128)(2,1)} %refs_0_.7), channel_id=1, source_target_pairs={{0,1},{1,0},{2,3},{3,2},{4,5},{5,4},{6,7},{7,6},{8,9},{9,8},{10,11... | collective-permute-start | bytes 3145736 | tf_op jit(solution)/shard_map/ppermute | solution.py:486
  14.3 26.2 %collective-permute-start.7 = (bf16[256,2048]{1,0:T(8,128)(2,1)S(1)}, bf16[256,2048]{1,0:T(8,128)(2,1)}, u32[]{:S(2)}, u32[]{:S(2)}) collective-permute-start(bf16[256,2048]{1,0:T(8,128)(2,1)S(1)} %copy-done.5), channel_id=1, source_target_pairs={{0,4},{2,6},{4,0},{6,2},{1,5},{3,7},{5,1},{7,3},{8,12},{10,14},{12... | collective-permute-start | bytes 3145736 | tf_op jit(solution)/shard_map/ppermute | solution.py:487
  15.9 45.1 %collective-permute-start.14 = (bf16[1024,256]{1,0:T(8,128)(2,1)S(1)}, bf16[1024,256]{1,0:T(8,128)(2,1)S(1)}, u32[]{:S(2)}, u32[]{:S(2)}) collective-permute-start(bf16[1024,256]{1,0:T(8,128)(2,1)S(1)} %pad_maximum_fusion.1.refs_8_), channel_id=1, source_target_pairs={{0,16},{8,24},{16,0},{24,8},{1,17},{9,25},{17,1},{25,9},{2,18},{10... | collective-permute-start | bytes 1572872 | tf_op jit(solution)/shard_map/ppermute | solution.py:519
  20.4 20.6 %collective-permute-start.20 = (bf16[256,256]{1,0:T(8,128)(2,1)S(1)}, bf16[256,256]{1,0:T(8,128)(2,1)S(1)}, u32[]{:S(2)}, u32[]{:S(2)}) collective-permute-start(bf16[256,256]{1,0:T(8,128)(2,1)S(1)} %pad_maximum_fusion.11), channel_id=1, source_target_pairs={{0,2},{2,0},{4,6},{6,4},{1,3},{3,1},{5,7},{7,5},{8,10},{10,8},{12,... | collective-permute-start | bytes 393224 | tf_op jit(solution)/shard_map/ppermute | solution.py:449
  20.6 22.0 %collective-permute-start.21 = (bf16[256,256]{1,0:T(8,128)(2,1)S(1)}, bf16[256,256]{1,0:T(8,128)(2,1)S(1)}, u32[]{:S(2)}, u32[]{:S(2)}) collective-permute-start(bf16[256,256]{1,0:T(8,128)(2,1)S(1)} %pad_maximum_fusion.12), channel_id=1, source_target_pairs={{0,4},{2,6},{4,0},{6,2},{1,5},{3,7},{5,1},{7,3},{8,12},{10,14},{12... | collective-permute-start | bytes 393224 | tf_op jit(solution)/shard_map/ppermute | solution.py:449
  40.7 21.7 %collective-permute-start.19 = (bf16[256,1024]{1,0:T(8,128)(2,1)S(1)}, bf16[256,1024]{1,0:T(8,128)(2,1)S(1)}, u32[]{:S(2)}, u32[]{:S(2)}) collective-permute-start(bf16[256,1024]{1,0:T(8,128)(2,1)S(1)} %pad_maximum_fusion.4), channel_id=1, source_target_pairs={{0,6},{2,4},{4,2},{6,0},{1,7},{3,5},{5,3},{7,1},{8,14},{10,12},{12... | collective-permute-start | bytes 1572872 | tf_op jit(solution)/shard_map/ppermute | solution.py:505
  41.1 38.4 %collective-permute-start.3 = (bf16[256,2048]{1,0:T(8,128)(2,1)S(1)}, bf16[256,2048]{1,0:T(8,128)(2,1)S(1)}, u32[]{:S(2)}, u32[]{:S(2)}) collective-permute-start(bf16[256,2048]{1,0:T(8,128)(2,1)S(1)} %copy-done.5), channel_id=1, source_target_pairs={{0,2},{2,0},{4,6},{6,4},{1,3},{3,1},{5,7},{7,5},{8,10},{10,8},{12,... | collective-permute-start | bytes 3145736 | tf_op jit(solution)/shard_map/ppermute | solution.py:491
  42.6 15.1 %collective-permute-start.22 = (bf16[256,256]{1,0:T(8,128)(2,1)S(1)}, bf16[256,256]{1,0:T(8,128)(2,1)S(1)}, u32[]{:S(2)}, u32[]{:S(2)}) collective-permute-start(bf16[256,256]{1,0:T(8,128)(2,1)S(1)} %pad_maximum_fusion.13), channel_id=1, source_target_pairs={{0,6},{2,4},{4,2},{6,0},{1,7},{3,5},{5,3},{7,1},{8,14},{10,12},{12... | collective-permute-start | bytes 393224 | tf_op jit(solution)/shard_map/ppermute | solution.py:449
  57.7 15.5 %collective-permute-start.15 = (bf16[1024,256]{1,0:T(8,128)(2,1)S(1)}, bf16[1024,256]{1,0:T(8,128)(2,1)S(1)}, u32[]{:S(2)}, u32[]{:S(2)}) collective-permute-start(bf16[1024,256]{1,0:T(8,128)(2,1)S(1)} %pad_maximum_fusion.1.refs_8_), channel_id=1, source_target_pairs={{0,8},{8,16},{16,24},{1,9},{9,17},{17,25},{2,10},{10,18},{18,26},{... | collective-permute-start | bytes 1572872 | tf_op jit(solution)/shard_map/ppermute | solution.py:517
  61.0 15.7 %collective-permute-start.13 = (bf16[1024,256]{1,0:T(8,128)(2,1)S(1)}, bf16[1024,256]{1,0:T(8,128)(2,1)S(1)}, u32[]{:S(2)}, u32[]{:S(2)}) collective-permute-start(bf16[1024,256]{1,0:T(8,128)(2,1)S(1)} %pad_maximum_fusion.1.refs_8_), channel_id=1, source_target_pairs={{8,0},{16,8},{24,16},{9,1},{17,9},{25,17},{10,2},{18,10},{26,18},{... | collective-permute-start | bytes 1572872 | tf_op jit(solution)/shard_map/ppermute | solution.py:518
  62.3 37.7 %collective-permute-start.24 = (bf16[1024,256]{1,0:T(8,128)(2,1)S(1)}, bf16[1024,256]{1,0:T(8,128)(2,1)}, u32[]{:S(2)}, u32[]{:S(2)}) collective-permute-start(bf16[1024,256]{1,0:T(8,128)(2,1)S(1)} %pad_maximum_fusion.5.refs_8_), channel_id=1, source_target_pairs={{0,16},{8,24},{16,0},{24,8},{1,17},{9,25},{17,1},{25,9},{2,18},{10... | collective-permute-start | bytes 1572872 | tf_op jit(solution)/shard_map/ppermute | solution.py:519
  73.2 28.2 %collective-permute-start.27 = (bf16[256,256]{1,0:T(8,128)(2,1)S(1)}, bf16[256,256]{1,0:T(8,128)(2,1)S(1)}, u32[]{:S(2)}, u32[]{:S(2)}) collective-permute-start(bf16[256,256]{1,0:T(8,128)(2,1)S(1)} %pad_maximum_fusion.14), channel_id=1, source_target_pairs={{0,2},{2,0},{4,6},{6,4},{1,3},{3,1},{5,7},{7,5},{8,10},{10,8},{12,... | collective-permute-start | bytes 393224 | tf_op jit(solution)/shard_map/ppermute | solution.py:449
  76.7 26.0 %collective-permute-start.28 = (bf16[256,256]{1,0:T(8,128)(2,1)S(1)}, bf16[256,256]{1,0:T(8,128)(2,1)S(1)}, u32[]{:S(2)}, u32[]{:S(2)}) collective-permute-start(bf16[256,256]{1,0:T(8,128)(2,1)S(1)} %pad_maximum_fusion.15), channel_id=1, source_target_pairs={{0,4},{2,6},{4,0},{6,2},{1,5},{3,7},{5,1},{7,3},{8,12},{10,14},{12... | collective-permute-start | bytes 393224 | tf_op jit(solution)/shard_map/ppermute | solution.py:449
  77.2 51.3 %collective-permute-start.11 = (bf16[256,2048]{1,0:T(8,128)(2,1)}, bf16[256,2048]{1,0:T(8,128)(2,1)}, u32[]{:S(2)}, u32[]{:S(2)}) collective-permute-start(bf16[256,2048]{1,0:T(8,128)(2,1)} %collective-permute-done.7.refs_2_), channel_id=1, source_target_pairs={{0,1},{1,0},{2,3},{3,2},{4,5},{5,4},{6,7},{7,6},{8,9},{9,8},{10,11... | collective-permute-start | bytes 3145736 | tf_op jit(solution)/shard_map/ppermute | solution.py:488
  79.5 47.3 %collective-permute-start.25 = (bf16[1024,256]{1,0:T(8,128)(2,1)S(1)}, bf16[1024,256]{1,0:T(8,128)(2,1)S(1)}, u32[]{:S(2)}, u32[]{:S(2)}) collective-permute-start(bf16[1024,256]{1,0:T(8,128)(2,1)S(1)} %pad_maximum_fusion.5.refs_8_), channel_id=1, source_target_pairs={{0,8},{8,16},{16,24},{1,9},{9,17},{17,25},{2,10},{10,18},{18,26},{... | collective-permute-start | bytes 1572872 | tf_op jit(solution)/shard_map/ppermute | solution.py:517
  100.1 27.6 %collective-permute-start.23 = (bf16[1024,256]{1,0:T(8,128)(2,1)S(1)}, bf16[1024,256]{1,0:T(8,128)(2,1)S(1)}, u32[]{:S(2)}, u32[]{:S(2)}) collective-permute-start(bf16[1024,256]{1,0:T(8,128)(2,1)S(1)} %pad_maximum_fusion.5.refs_8_), channel_id=1, source_target_pairs={{8,0},{16,8},{24,16},{9,1},{17,9},{25,17},{10,2},{18,10},{26,18},{... | collective-permute-start | bytes 1572872 | tf_op jit(solution)/shard_map/ppermute | solution.py:518
  101.4 24.6 %collective-permute-start.16 = (bf16[1024,256]{1,0:T(8,128)(2,1)S(1)}, bf16[1024,256]{1,0:T(8,128)(2,1)S(1)}, u32[]{:S(2)}, u32[]{:S(2)}) collective-permute-start(bf16[1024,256]{1,0:T(8,128)(2,1)S(1)} %collective-permute-done.14.refs_10_), channel_id=1, source_target_pairs={{8,0},{16,24},{9,1},{17,25},{10,2},{18,26},{11,3},{19,27},{12,4},{... | collective-permute-start | bytes 1572872 | tf_op jit(solution)/shard_map/ppermute | solution.py:521
  102.7 5.0 %collective-permute-start.29 = (bf16[256,256]{1,0:T(8,128)(2,1)S(1)}, bf16[256,256]{1,0:T(8,128)(2,1)S(1)}, u32[]{:S(2)}, u32[]{:S(2)}) collective-permute-start(bf16[256,256]{1,0:T(8,128)(2,1)S(1)} %pad_maximum_fusion.16), channel_id=1, source_target_pairs={{0,6},{2,4},{4,2},{6,0},{1,7},{3,5},{5,3},{7,1},{8,14},{10,12},{12... | collective-permute-start | bytes 393224 | tf_op jit(solution)/shard_map/ppermute | solution.py:449
  107.7 20.7 %collective-permute-start.17 = (bf16[256,1024]{1,0:T(8,128)(2,1)S(1)}, bf16[256,1024]{1,0:T(8,128)(2,1)S(1)}, u32[]{:S(2)}, u32[]{:S(2)}) collective-permute-start(bf16[256,1024]{1,0:T(8,128)(2,1)S(1)} %pad_maximum_fusion.2), channel_id=1, source_target_pairs={{0,2},{2,0},{4,6},{6,4},{1,3},{3,1},{5,7},{7,5},{8,10},{10,8},{12,... | collective-permute-start | bytes 1572872 | tf_op jit(solution)/shard_map/ppermute | solution.py:505
  126.8 26.4 %collective-permute-start.10 = (bf16[256,2048]{1,0:T(8,128)(2,1)}, bf16[256,2048]{1,0:T(8,128)(2,1)S(1)}, u32[]{:S(2)}, u32[]{:S(2)}) collective-permute-start(bf16[256,2048]{1,0:T(8,128)(2,1)} %collective-permute-done.9.refs_4_), channel_id=1, source_target_pairs={{0,2},{2,0},{4,6},{6,4},{1,3},{3,1},{5,7},{7,5},{8,10},{10,8},{12,... | collective-permute-start | bytes 3145736 | tf_op jit(solution)/shard_map/ppermute | solution.py:491
  127.6 14.3 %collective-permute-start.18 = (bf16[256,1024]{1,0:T(8,128)(2,1)S(1)}, bf16[256,1024]{1,0:T(8,128)(2,1)S(1)}, u32[]{:S(2)}, u32[]{:S(2)}) collective-permute-start(bf16[256,1024]{1,0:T(8,128)(2,1)S(1)} %pad_maximum_fusion.3), channel_id=1, source_target_pairs={{0,4},{2,6},{4,0},{6,2},{1,5},{3,7},{5,1},{7,3},{8,12},{10,14},{12... | collective-permute-start | bytes 1572872 | tf_op jit(solution)/shard_map/ppermute | solution.py:505
  127.7 41.6 %collective-permute-start.8 = (bf16[256,2048]{1,0:T(8,128)(2,1)}, bf16[256,2048]{1,0:T(8,128)(2,1)S(1)}, u32[]{:S(2)}, u32[]{:S(2)}) collective-permute-start(bf16[256,2048]{1,0:T(8,128)(2,1)} %collective-permute-done.7.refs_2_), channel_id=1, source_target_pairs={{0,2},{2,0},{4,6},{6,4},{1,3},{3,1},{5,7},{7,5},{8,10},{10,8},{12,... | collective-permute-start | bytes 3145736 | tf_op jit(solution)/shard_map/ppermute | solution.py:491
  128.4 13.8 %collective-permute-start.34 = (bf16[256,256]{1,0:T(8,128)(2,1)S(1)}, bf16[256,256]{1,0:T(8,128)(2,1)S(1)}, u32[]{:S(2)}, u32[]{:S(2)}) collective-permute-start(bf16[256,256]{1,0:T(8,128)(2,1)S(1)} %pad_maximum_fusion.17), channel_id=1, source_target_pairs={{0,2},{2,0},{4,6},{6,4},{1,3},{3,1},{5,7},{7,5},{8,10},{10,8},{12,... | collective-permute-start | bytes 393224 | tf_op jit(solution)/shard_map/ppermute | solution.py:449
  128.5 42.6 %collective-permute-start.12 = (bf16[256,2048]{1,0:T(8,128)(2,1)}, bf16[256,2048]{1,0:T(8,128)(2,1)}, u32[]{:S(2)}, u32[]{:S(2)}) collective-permute-start(bf16[256,2048]{1,0:T(8,128)(2,1)} %collective-permute-done.11.refs_6_), channel_id=1, source_target_pairs={{0,2},{2,0},{4,6},{6,4},{1,3},{3,1},{5,7},{7,5},{8,10},{10,8},{12,... | collective-permute-start | bytes 3145736 | tf_op jit(solution)/shard_map/ppermute | solution.py:491
  141.9 5.1 %collective-permute-start.35 = (bf16[256,256]{1,0:T(8,128)(2,1)S(1)}, bf16[256,256]{1,0:T(8,128)(2,1)S(1)}, u32[]{:S(2)}, u32[]{:S(2)}) collective-permute-start(bf16[256,256]{1,0:T(8,128)(2,1)S(1)} %pad_maximum_fusion.18), channel_id=1, source_target_pairs={{0,4},{2,6},{4,0},{6,2},{1,5},{3,7},{5,1},{7,3},{8,12},{10,14},{12... | collective-permute-start | bytes 393224 | tf_op jit(solution)/shard_map/ppermute | solution.py:449
  142.2 24.9 %collective-permute-start.31 = (bf16[1024,256]{1,0:T(8,128)(2,1)}, bf16[1024,256]{1,0:T(8,128)(2,1)S(1)}, u32[]{:S(2)}, u32[]{:S(2)}) collective-permute-start(bf16[1024,256]{1,0:T(8,128)(2,1)} %pad_maximum_fusion.6.refs_8_), channel_id=1, source_target_pairs={{0,16},{8,24},{16,0},{24,8},{1,17},{9,25},{17,1},{25,9},{2,18},{10... | collective-permute-start | bytes 1572872 | tf_op jit(solution)/shard_map/ppermute | solution.py:519
  151.9 47.8 %collective-permute-start.26 = (bf16[1024,256]{1,0:T(8,128)(2,1)}, bf16[1024,256]{1,0:T(8,128)(2,1)}, u32[]{:S(2)}, u32[]{:S(2)}) collective-permute-start(bf16[1024,256]{1,0:T(8,128)(2,1)} %collective-permute-done.24.refs_10_), channel_id=1, source_target_pairs={{8,0},{16,24},{9,1},{17,25},{10,2},{18,26},{11,3},{19,27},{12,4},{... | collective-permute-start | bytes 1572872 | tf_op jit(solution)/shard_map/ppermute | solution.py:521
  154.2 39.3 %collective-permute-start.32 = (bf16[1024,256]{1,0:T(8,128)(2,1)}, bf16[1024,256]{1,0:T(8,128)(2,1)}, u32[]{:S(2)}, u32[]{:S(2)}) collective-permute-start(bf16[1024,256]{1,0:T(8,128)(2,1)} %pad_maximum_fusion.6.refs_8_), channel_id=1, source_target_pairs={{0,8},{8,16},{16,24},{1,9},{9,17},{17,25},{2,10},{10,18},{18,26},{... | collective-permute-start | bytes 1572872 | tf_op jit(solution)/shard_map/ppermute | solution.py:517
  167.1 26.3 %collective-permute-start.30 = (bf16[1024,256]{1,0:T(8,128)(2,1)}, bf16[1024,256]{1,0:T(8,128)(2,1)}, u32[]{:S(2)}, u32[]{:S(2)}) collective-permute-start(bf16[1024,256]{1,0:T(8,128)(2,1)} %pad_maximum_fusion.6.refs_8_), channel_id=1, source_target_pairs={{8,0},{16,8},{24,16},{9,1},{17,9},{25,17},{10,2},{18,10},{26,18},{... | collective-permute-start | bytes 1572872 | tf_op jit(solution)/shard_map/ppermute | solution.py:518
  170.2 42.4 %collective-permute-start.38 = (bf16[1024,256]{1,0:T(8,128)(2,1)}, bf16[1024,256]{1,0:T(8,128)(2,1)}, u32[]{:S(2)}, u32[]{:S(2)}) collective-permute-start(bf16[1024,256]{1,0:T(8,128)(2,1)} %pad_maximum_fusion.7.refs_8_), channel_id=1, source_target_pairs={{0,16},{8,24},{16,0},{24,8},{1,17},{9,25},{17,1},{25,9},{2,18},{10... | collective-permute-start | bytes 1572872 | tf_op jit(solution)/shard_map/ppermute | solution.py:519
  171.1 42.8 %collective-permute-start.33 = (bf16[1024,256]{1,0:T(8,128)(2,1)}, bf16[1024,256]{1,0:T(8,128)(2,1)S(1)}, u32[]{:S(2)}, u32[]{:S(2)}) collective-permute-start(bf16[1024,256]{1,0:T(8,128)(2,1)} %copy-done.27), channel_id=1, source_target_pairs={{8,0},{16,24},{9,1},{17,25},{10,2},{18,26},{11,3},{19,27},{12,4},{... | collective-permute-start | bytes 1572872 | tf_op jit(solution)/shard_map/ppermute | solution.py:521
  193.5 33.0 %collective-permute-start.39 = (bf16[1024,256]{1,0:T(8,128)(2,1)}, bf16[1024,256]{1,0:T(8,128)(2,1)S(1)}, u32[]{:S(2)}, u32[]{:S(2)}) collective-permute-start(bf16[1024,256]{1,0:T(8,128)(2,1)} %pad_maximum_fusion.7.refs_8_), channel_id=1, source_target_pairs={{0,8},{8,16},{16,24},{1,9},{9,17},{17,25},{2,10},{10,18},{18,26},{... | collective-permute-start | bytes 1572872 | tf_op jit(solution)/shard_map/ppermute | solution.py:517
  198.2 28.2 %collective-permute-start.37 = (bf16[1024,256]{1,0:T(8,128)(2,1)}, bf16[1024,256]{1,0:T(8,128)(2,1)S(1)}, u32[]{:S(2)}, u32[]{:S(2)}) collective-permute-start(bf16[1024,256]{1,0:T(8,128)(2,1)} %pad_maximum_fusion.7.refs_8_), channel_id=1, source_target_pairs={{8,0},{16,8},{24,16},{9,1},{17,9},{25,17},{10,2},{18,10},{26,18},{... | collective-permute-start | bytes 1572872 | tf_op jit(solution)/shard_map/ppermute | solution.py:518
  212.7 21.6 %collective-permute-start.40 = (bf16[1024,256]{1,0:T(8,128)(2,1)}, bf16[1024,256]{1,0:T(8,128)(2,1)S(1)}, u32[]{:S(2)}, u32[]{:S(2)}) collective-permute-start(bf16[1024,256]{1,0:T(8,128)(2,1)} %collective-permute-done.38.refs_10_), channel_id=1, source_target_pairs={{8,0},{16,24},{9,1},{17,25},{10,2},{18,26},{11,3},{19,27},{12,4},{... | collective-permute-start | bytes 1572872 | tf_op jit(solution)/shard_map/ppermute | solution.py:521
  254.5 6.0 %collective-permute-start.53 = (bf16[512,2048]{1,0:T(8,128)(2,1)S(1)}, bf16[512,2048]{1,0:T(8,128)(2,1)S(1)}, u32[]{:S(2)}, u32[]{:S(2)}) collective-permute-start(bf16[512,2048]{1,0:T(8,128)(2,1)S(1)} %bwd.4), channel_id=1, source_target_pairs={{0,2},{2,0},{4,6},{6,4},{1,3},{3,1},{5,7},{7,5},{8,10},{10,8},{12,... | collective-permute-start | bytes 6291464 | tf_op jit(solution)/shard_map/ppermute | solution.py:544
  258.9 25.3 %collective-permute-start.57 = (bf16[512,1024]{1,0:T(8,128)(2,1)S(1)}, bf16[512,1024]{1,0:T(8,128)(2,1)S(1)}, u32[]{:S(2)}, u32[]{:S(2)}) collective-permute-start(bf16[512,1024]{1,0:T(8,128)(2,1)S(1)} %get-tuple-element.91), channel_id=1, source_target_pairs={{0,1},{1,0},{2,3},{3,2},{4,5},{5,4},{6,7},{7,6},{8,9},{9,8},{10,11... | collective-permute-start | bytes 3145736 | tf_op jit(solution)/shard_map/ppermute | solution.py:549
  264.2 26.1 %collective-permute-start.54 = (bf16[256,2048]{1,0:T(8,128)(2,1)S(1)}, bf16[256,2048]{1,0:T(8,128)(2,1)S(1)}, u32[]{:S(2)}, u32[]{:S(2)}) collective-permute-start(bf16[256,2048]{1,0:T(8,128)(2,1)S(1)} %get-tuple-element.88), channel_id=1, source_target_pairs={{0,4},{2,6},{4,0},{6,2},{1,5},{3,7},{5,1},{7,3},{8,12},{10,14},{12... | collective-permute-start | bytes 3145736 | tf_op jit(solution)/shard_map/ppermute | solution.py:547
  285.5 35.0 %collective-permute-start.58 = (bf16[256,1024]{1,0:T(8,128)(2,1)}, bf16[256,1024]{1,0:T(8,128)(2,1)}, u32[]{:S(2)}, u32[]{:S(2)}) collective-permute-start(bf16[256,1024]{1,0:T(8,128)(2,1)} %fusion), channel_id=1, source_target_pairs={{0,4},{2,6},{4,0},{6,2},{1,5},{3,7},{5,1},{7,3},{8,12},{10,14},{12... | collective-permute-start | bytes 1572872 | tf_op jit(solution)/shard_map/ppermute | solution.py:552
  287.2 15.4 %collective-permute-start.46 = (bf16[256,128]{1,0:T(8,128)(2,1)S(1)}, bf16[256,128]{1,0:T(8,128)(2,1)S(1)}, u32[]{:S(2)}, u32[]{:S(2)}) collective-permute-start(bf16[256,128]{1,0:T(8,128)(2,1)S(1)} %get-tuple-element.74), channel_id=1, source_target_pairs={{0,4},{2,6},{4,0},{6,2},{1,5},{3,7},{5,1},{7,3},{8,12},{10,14},{12... | collective-permute-start | bytes 196616 | tf_op jit(solution)/shard_map/ppermute | solution.py:540
  287.5 16.4 %collective-permute-start.50 = (bf16[256,128]{1,0:T(8,128)(2,1)S(1)}, bf16[256,128]{1,0:T(8,128)(2,1)S(1)}, u32[]{:S(2)}, u32[]{:S(2)}) collective-permute-start(bf16[256,128]{1,0:T(8,128)(2,1)S(1)} %get-tuple-element.78), channel_id=1, source_target_pairs={{0,6},{2,4},{4,2},{6,0},{1,7},{3,5},{5,3},{7,1},{8,14},{10,12},{12... | collective-permute-start | bytes 196616 | tf_op jit(solution)/shard_map/ppermute | solution.py:540
  291.7 30.5 %collective-permute-start.55 = (bf16[256,1024]{1,0:T(8,128)(2,1)}, bf16[256,1024]{1,0:T(8,128)(2,1)}, u32[]{:S(2)}, u32[]{:S(2)}) collective-permute-start(bf16[256,1024]{1,0:T(8,128)(2,1)} %fusion.3), channel_id=1, source_target_pairs={{0,1},{1,0},{2,3},{3,2},{4,5},{5,4},{6,7},{7,6},{8,9},{9,8},{10,11... | collective-permute-start | bytes 1572872 | tf_op jit(solution)/shard_map/ppermute | solution.py:551
  291.8 12.7 %collective-permute-start.41 = (bf16[256,128]{1,0:T(8,128)(2,1)S(1)}, bf16[256,128]{1,0:T(8,128)(2,1)S(1)}, u32[]{:S(2)}, u32[]{:S(2)}) collective-permute-start(bf16[256,128]{1,0:T(8,128)(2,1)S(1)} %get-tuple-element.69), channel_id=1, source_target_pairs={{0,2},{2,0},{4,6},{6,4},{1,3},{3,1},{5,7},{7,5},{8,10},{10,8},{12,... | collective-permute-start | bytes 196616 | tf_op jit(solution)/shard_map/ppermute | solution.py:540
  304.5 5.2 %collective-permute-start.43 = (bf16[256,128]{1,0:T(8,128)(2,1)S(1)}, bf16[256,128]{1,0:T(8,128)(2,1)S(1)}, u32[]{:S(2)}, u32[]{:S(2)}) collective-permute-start(bf16[256,128]{1,0:T(8,128)(2,1)S(1)} %get-tuple-element.71), channel_id=1, source_target_pairs={{0,2},{2,0},{4,6},{6,4},{1,3},{3,1},{5,7},{7,5},{8,10},{10,8},{12,... | collective-permute-start | bytes 196616 | tf_op jit(solution)/shard_map/ppermute | solution.py:540
  (62 other events, 834.4 us)

commit v3 on v0

--- a/solution.py
+++ b/solution.py
@@ -1,10 +1,16 @@
+import functools
+
 import jax
 import jax.numpy as jnp
 from jax import lax
+from jax.experimental import pallas as pl
+from jax.experimental.pallas import tpu as pltpu
 from jax.sharding import PartitionSpec as P
 
 DH = 64
 BLOCK = 64
+F32 = jnp.float32
+BF16 = jnp.bfloat16
 
 
 def attend(query_rows, key_rows, value_rows, grad_rows, key_lengths):
@@ -55,7 +61,7 @@
     return moved.reshape(lead_shape + data.shape[1:])
 
 
-def shards(enc_rows, enc_len, dest_dp, peer_counts, queries, ctx_grad, w_key, w_value):
+def shards_general(enc_rows, enc_len, dest_dp, peer_counts, queries, ctx_grad, w_key, w_value):
     peer_count = lax.axis_size("dp")
     model_groups = lax.axis_size("mp")
     block_count = dest_dp.shape[0]
@@ -94,10 +100,8 @@
         :, 0
     ].astype(jnp.float32)
     shard_cols = lax.all_gather(rows_here, "mp", axis=1, tiled=True)
-    key_part = key_full
-    value_part = value_full
-    key_acc = jnp.dot(shard_cols, key_part, preferred_element_type=jnp.float32)
-    value_acc = jnp.dot(shard_cols, value_part, preferred_element_type=jnp.float32)
+    key_acc = jnp.dot(shard_cols, key_full, preferred_element_type=jnp.float32)
+    value_acc = jnp.dot(shard_cols, value_full, preferred_element_type=jnp.float32)
     context, key_grad, value_grad = attend(
         queries,
         key_acc.astype(jnp.bfloat16),
@@ -128,6 +132,390 @@
     return (context, enc_grad)
 
 
+PAIR = 2 * DH
+SHORT = pl.CostEstimate(flops=1, bytes_accessed=1, transcendentals=0)
+
+
+def nt(a, b):
+    return lax.dot_general(a, b, (((1,), (1,)), ((), ())), preferred_element_type=F32)
+
+
+def tn(a, b):
+    return lax.dot_general(a, b, (((0,), (0,)), ((), ())), preferred_element_type=F32)
+
+
+def forward_kernel(n_dp, n_sec, n_half, blk, tab, *refs):
+    blocks = n_dp * blk
+    x_refs = refs[: n_half * n_dp]
+    own, above, far, below, end, q_ref, g_ref, ctx_ref, dkv_ref, w_ref, acc, kv = refs[
+        n_half * n_dp :
+    ]
+    rows = own.shape[0] // n_dp
+    step = pl.program_id(0)
+    z = tab[2 * blocks]
+    m = tab[2 * blocks + 1]
+    per_half = n_sec // n_half
+    section = (m ^ (step // per_half)) * per_half + step % per_half
+    hop = (section - z + n_sec) % n_sec
+
+    @pl.when(hop == 0)
+    def _():
+        w_ref[...] = own[...]
+
+    @pl.when((hop == 1) & (z != n_sec - 1))
+    def _():
+        w_ref[...] = above[...]
+
+    @pl.when(hop == 2)
+    def _():
+        w_ref[...] = far[...]
+
+    @pl.when((hop == n_sec - 1) & (z != 0))
+    def _():
+        w_ref[...] = below[...]
+
+    @pl.when(((hop == 1) & (z == n_sec - 1)) | ((hop == n_sec - 1) & (z == 0)))
+    def _():
+        w_ref[...] = end[...]
+
+    for h in range(n_half):
+
+        @pl.when(step // per_half == h)
+        def _():
+            for t in range(n_dp):
+                at = slice(t * rows, (t + 1) * rows)
+                part = jnp.dot(
+                    x_refs[h * n_dp + t][...], w_ref[...], preferred_element_type=F32
+                )
+                if h == 0:
+                    acc[at, :] = jnp.where(step == 0, part, acc[at, :] + part)
+                else:
+                    acc[at, :] += part
+
+    @pl.when(step == n_sec - 1)
+    def _():
+        kv[...] = acc[...].astype(BF16)
+        lane = lax.broadcasted_iota(jnp.int32, (BLOCK, PAIR), 1) < DH
+        key_pos = lax.broadcasted_iota(jnp.int32, (BLOCK, PAIR), 0)
+        scale = DH ** (-0.5)
+        zero = jnp.zeros((BLOCK, PAIR), BF16)
+
+        def group(bs):
+            source = [pl.ds(pl.multiple_of(tab[b] * BLOCK, BLOCK), BLOCK) for b in bs]
+            here = [pl.ds((b % blk) * BLOCK, BLOCK) for b in bs]
+            key = [kv[at, 0:PAIR] for at in source]
+            value = [kv[at, PAIR : 2 * PAIR] for at in source]
+
+            def split(ref):
+                rows_of = [ref[b // blk, at, :] for b, at in zip(bs, here)]
+                return [
+                    jnp.concatenate([jnp.where(lane, x, zero), jnp.where(lane, zero, x)], axis=0)
+                    for x in rows_of
+                ]
+
+            query = split(q_ref)
+            grad = split(g_ref)
+            scores = [nt(k, q) * scale for k, q in zip(key, query)]
+            prob_grad = [nt(v, g) for v, g in zip(value, grad)]
+            scores = [jnp.where(key_pos < tab[blocks + b], x, -1e30) for b, x in zip(bs, scores)]
+            weights = [jnp.exp(x - jnp.max(x, axis=0, keepdims=True)) for x in scores]
+            probs = [x / jnp.sum(x, axis=0, keepdims=True) for x in weights]
+            prob_bf = [x.astype(BF16) for x in probs]
+            ctx = [tn(p, v) for p, v in zip(prob_bf, value)]
+            dv = [jnp.dot(p, g, preferred_element_type=F32) for p, g in zip(prob_bf, grad)]
+            row_dot = [jnp.sum(p * x, axis=0, keepdims=True) for p, x in zip(probs, prob_grad)]
+            score_grad = [
+                (p * (x - r) * scale).astype(BF16) for p, x, r in zip(probs, prob_grad, row_dot)
+            ]
+            dk = [jnp.dot(x, q, preferred_element_type=F32) for x, q in zip(score_grad, query)]
+            for n, b in enumerate(bs):
+                ctx_ref[b // blk, here[n], :] = jnp.where(
+                    lane, ctx[n][:BLOCK], ctx[n][BLOCK:]
+                ).astype(BF16)
+                dkv_ref[source[n], 0:PAIR] = dk[n].astype(BF16)
+                dkv_ref[source[n], PAIR : 2 * PAIR] = dv[n].astype(BF16)
+
+        for b in range(0, blocks, blk):
+            group(range(b, b + blk))
+
+
+def forward_chunk(table, x_pieces, pieces, q_at, g_at, blk, n_sec, n_dp):
+    n_half = len(x_pieces) // n_dp
+    cols = pieces[0].shape[1]
+    rows = pieces[0].shape[0] // n_dp
+    per_half = n_sec // n_half
+    span = x_pieces[0][0].shape[1] // per_half
+
+    def x_spec(h, row):
+        return pl.BlockSpec(
+            (rows, span), lambda a, t: (row, jnp.clip(a - h * per_half, 0, per_half - 1))
+        )
+
+    whole = pl.BlockSpec((span, cols), lambda a, t: (0, 0))
+
+    def head(at):
+        return pl.BlockSpec((n_dp, rows, PAIR), lambda a, t: (0, 0, at))
+
+    return pl.pallas_call(
+        functools.partial(forward_kernel, n_dp, n_sec, n_half, blk),
+        grid_spec=pltpu.PrefetchScalarGridSpec(
+            num_scalar_prefetch=1,
+            grid=(n_sec,),
+            in_specs=[x_spec(i // n_dp, row) for i, (_, row) in enumerate(x_pieces)]
+            + [whole] * 5
+            + [head(q_at[1]), head(g_at[1])],
+            out_specs=[
+                head(0),
+                pl.BlockSpec((n_dp * rows, cols), lambda a, t: (0, 0)),
+                pl.BlockSpec((span, cols), lambda a, t: (a, 0)),
+            ],
+            scratch_shapes=[
+                pltpu.VMEM((n_dp * rows, cols), F32),
+                pltpu.VMEM((n_dp * rows, cols), BF16),
+            ],
+        ),
+        out_shape=[
+            jax.ShapeDtypeStruct((n_dp, rows, PAIR), BF16),
+            jax.ShapeDtypeStruct((n_dp * rows, cols), BF16),
+            jax.ShapeDtypeStruct((n_sec * span, cols), BF16),
+        ],
+        compiler_params=pltpu.CompilerParams(vmem_limit_bytes=60 << 20),
+        cost_estimate=SHORT,
+        name="fwd",
+    )(table, *[x for x, _ in x_pieces], *pieces, q_at[0], g_at[0])
+
+
+def backward_kernel(chunks, add, *refs):
+    out_ref = refs[-1]
+    total = nt(refs[0][...], refs[chunks][...])
+    for c in range(1, chunks):
+        total += nt(refs[c][...], refs[chunks + c][...])
+    if add:
+        total += refs[2 * chunks][...].astype(F32)
+    out_ref[...] = total.astype(out_ref.dtype)
+
+
+def backward(dkvs, ws, rows, span, row_at, row_n, col_at, col_n, received, out_dtype):
+    chunks = len(dkvs)
+    cols = dkvs[0].shape[1]
+    specs = [pl.BlockSpec((rows, cols), lambda h, r: (row_at + 2 * r, 0))] * chunks
+    specs += [pl.BlockSpec((span, cols), lambda h, r: (col_at + 2 * h, 0))] * chunks
+    block = pl.BlockSpec((rows, span), lambda h, r: (r, h))
+    extra = () if received is None else (received,)
+    return pl.pallas_call(
+        functools.partial(backward_kernel, chunks, received is not None),
+        grid=(col_n, row_n),
+        in_specs=specs + [block] * len(extra),
+        out_specs=block,
+        out_shape=jax.ShapeDtypeStruct((row_n * rows, col_n * span), out_dtype),
+        compiler_params=pltpu.CompilerParams(vmem_limit_bytes=48 << 20),
+        cost_estimate=SHORT,
+        name="bwd",
+    )(*dkvs, *ws, *extra)
+
+
+def finish_kernel(p_ref, got_y, last_x, q_ref, got_x, last_y, out):
+    span = out.shape[1] // 2
+    out[:, :span] = (
+        p_ref[...] + got_y[...].astype(F32) + last_x[...].astype(F32)
+    ).astype(BF16)
+    out[:, span:] = (
+        q_ref[...] + got_x[...].astype(F32) + last_y[...].astype(F32)
+    ).astype(BF16)
+
+
+def finish(*operands):
+    rows, span = operands[2].shape
+    block = pl.BlockSpec((rows, span), lambda i: (0, 0))
+    return pl.pallas_call(
+        finish_kernel,
+        grid=(1,),
+        in_specs=[block] * 6,
+        out_specs=pl.BlockSpec((rows, 2 * span), lambda i: (0, 0)),
+        out_shape=jax.ShapeDtypeStruct((rows, 2 * span), BF16),
+        name="finish",
+    )(*operands)
+
+
+def context_kernel(*refs):
+    out = refs[-1]
+    at = 0
+    for ref in refs[:-1]:
+        out[:, at : at + ref.shape[2]] = ref[0]
+        at += ref.shape[2]
+
+
+def gather_context(*parts):
+    n_dp, rows = parts[0].shape[:2]
+    cols = sum(part.shape[2] for part in parts)
+    return pl.pallas_call(
+        context_kernel,
+        grid=(n_dp,),
+        in_specs=[pl.BlockSpec((1, rows, part.shape[2]), lambda j: (j, 0, 0)) for part in parts],
+        out_specs=pl.BlockSpec((rows, cols), lambda j: (0, j)),
+        out_shape=jax.ShapeDtypeStruct((rows, n_dp * cols), BF16),
+        name="gather_context",
+    )(*parts)
+
+
+def shards_section(enc_rows, enc_len, dest_dp, peer_counts, queries, ctx_grad, w_key, w_value):
+    n_sec, n_dp, n_mp = (lax.axis_size(a) for a in ("section", "dp", "mp"))
+    z, d, m = (lax.axis_index(a).astype(jnp.int32) for a in ("section", "dp", "mp"))
+    blk = dest_dp.shape[0]
+    blocks = blk * n_dp
+    rows, half = enc_rows.shape
+    head_cols = w_key.shape[1] // n_dp
+
+    core = [(i, i ^ 1) for i in range(n_dp)]
+    ypairs = [(i, i ^ 2) for i in range(n_dp)]
+    xpairs = [(0, 1), (1, 0)]
+    up = [(i, i + 1) for i in range(n_sec - 1)]
+    down = [(i + 1, i) for i in range(n_sec - 1)]
+    over_two = [(i, i ^ 2) for i in range(n_sec)]
+    ends = [(1, 0), (2, 3)]
+    outer = [(0, n_sec - 1), (n_sec - 1, 0)]
+
+    def step(waited, released=()):
+        return lax.optimization_barrier((tuple(waited), tuple(released)))
+
+    def swap(x):
+        return lax.ppermute(x, "dp", core)
+
+    def exchange(x):
+        return lax.all_to_all(x, "dp", split_axis=0, concat_axis=0, tiled=True)
+
+    def by_owner(x):
+        return x.reshape(rows, n_dp, head_cols).transpose(1, 0, 2)
+
+    def weight_parts(c, *ws):
+        return jnp.concatenate([by_owner(w)[:, :, c * PAIR : (c + 1) * PAIR] for w in ws], axis=2)
+
+    def along(piece):
+        return (
+            lax.ppermute(piece, "section", up),
+            lax.ppermute(piece, "section", down),
+            lax.ppermute(piece, "section", over_two),
+        )
+
+    own0 = exchange(weight_parts(0, w_key, w_value)).reshape(n_dp * rows, 2 * PAIR)
+    e_x = lax.ppermute(enc_rows, "mp", xpairs)
+    e_c = swap(enc_rows)
+
+    (own0, e_c), (e, w_k, w_v, q_in, g_in) = step(
+        (own0, e_c), (enc_rows, w_key, w_value, queries, ctx_grad)
+    )
+    z0 = along(own0)
+    e_y = lax.ppermute(e, "dp", ypairs)
+    own1 = exchange(weight_parts(1, w_k, w_v)).reshape(n_dp * rows, 2 * PAIR)
+    parts = jnp.concatenate(
+        [by_owner(q_in), by_owner(g_in), weight_parts(2, w_k, w_v), weight_parts(3, w_k, w_v)],
+        axis=2,
+    )
+    small = jnp.concatenate([enc_len, dest_dp, peer_counts[0]]).astype(BF16)
+    small = jnp.pad(small[None, :], ((0, 15), (0, parts.shape[2] - small.shape[0])))
+    small = jnp.broadcast_to(small[None], (n_dp,) + small.shape)
+    parts = jnp.concatenate([parts, small], axis=1)
+
+    (z0, own1, e_y, e_x, parts), _ = step((z0, own1, e_y, e_x, parts))
+    end0 = lax.ppermute(z0[2], "section", ends)
+    z1 = along(own1)
+    e_yx = lax.ppermute(e_y, "mp", xpairs)
+    got = exchange(parts)
+    e_xy = jnp.concatenate([e_x, e_y], axis=0)
+
+    (end0, z1, e_yx, e_xy, got), _ = step((end0, z1, e_yx, e_xy, got))
+    own2, own3 = (
+        got[:, :rows, 2 * head_cols + 2 * PAIR * i : 2 * head_cols + 2 * PAIR * (i + 1)].reshape(
+            n_dp * rows, 2 * PAIR
+        )
+        for i in range(2)
+    )
+    end1 = lax.ppermute(z1[2], "section", ends)
+    z2 = along(own2)
+    e_xyc, e_yxc = swap(e_xy), swap(e_yx)
+
+    packs = got[:, rows, : 2 * blk + n_dp].astype(jnp.int32)
+    lens = packs[:, :blk].reshape(-1)
+    dest = packs[:, blk : 2 * blk]
+    counts = packs[:, 2 * blk :]
+    peer = jnp.arange(n_dp, dtype=jnp.int32)
+    pos = jnp.arange(blk, dtype=jnp.int32)
+    before = jnp.sum(
+        jnp.where(peer[None, None, :] < peer[None, :, None], counts[:, None, :], 0), axis=2
+    )
+    upto = before + counts
+    sender = jnp.sum((upto[:, None, :] <= pos[None, :, None]).astype(jnp.int32), axis=2)
+    is_sender = sender[:, :, None] == peer[None, None, :]
+    rank = pos[None, :] - jnp.sum(jnp.where(is_sender, before[:, None, :], 0), axis=2)
+    same = dest[:, :, None] == dest[:, None, :]
+    slot_rank = jnp.sum((same & (pos[None, None, :] < pos[None, :, None])).astype(jnp.int32), axis=2)
+    hit = (
+        is_sender[:, :, :, None]
+        & (dest[None, None] == peer[:, None, None, None])
+        & (slot_rank[None, None] == rank[:, :, None, None])
+    ).reshape(blocks, blocks)
+    place = ((peer ^ d)[:, None] * blk + pos[None, :]).reshape(-1)
+    src = jnp.sum(jnp.where(hit, place[None, :], 0), axis=1)
+    src_len = jnp.sum(jnp.where(hit, lens[None, :], 0), axis=1)
+    table = jnp.concatenate([src, src_len, jnp.stack([z, m])])
+
+    x_pieces = [(e, 0), (e_c, 0), (e_y, 0), (e_xyc, 1)]
+    x_pieces += [(e_x, 0), (e_xyc, 0), (e_yx, 0), (e_yxc, 0)]
+    q_blocks = head_cols // PAIR
+
+    def forward(c, own, zs, end):
+        up_, down_, far = zs
+        return forward_chunk(
+            table,
+            x_pieces,
+            (own, down_, far, up_, end),
+            (got, c),
+            (got, q_blocks + c),
+            blk,
+            n_sec,
+            n_dp,
+        )
+
+    f0 = forward(0, own0, z0, end0)
+
+    (end1, z2, own3, f0), _ = step((end1, z2, own3, f0))
+    end2 = lax.ppermute(z2[2], "section", ends)
+    z3 = along(own3)
+    end3 = lax.ppermute(own3, "section", outer)
+    f1 = forward(1, own1, z1, end1)
+    context_a = exchange(jnp.concatenate([f0[0], f1[0]], axis=2))
+    f2 = forward(2, own2, z2, end2)
+
+    (z3, end3, f1, f2, context_a), _ = step((z3, end3, f1, f2, context_a))
+    f3 = forward(3, own3, z3, end3)
+    context_b = exchange(jnp.concatenate([f2[0], f3[0]], axis=2))
+
+    dkvs = tuple(f[1] for f in (f0, f1, f2, f3))
+    ws = tuple(f[2] for f in (f0, f1, f2, f3))
+    span = half // (n_sec // n_mp)
+    give_y = swap(backward(dkvs, ws, rows, span, 3, 1, 0, 2, None, BF16))
+    give_x = swap(backward(dkvs, ws, rows, span, 1, 2, 3, 1, None, BF16))
+    send_y = backward(dkvs, ws, rows, span, 2, 1, 0, 2, give_y, BF16)
+    send_x = backward(dkvs, ws, rows, span, 0, 2, 3, 1, give_x, BF16)
+    (send_y, send_x, context_b), dkvs = step((send_y, send_x, context_b), dkvs)
+    got_y = lax.ppermute(send_y, "dp", ypairs)
+    got_x = lax.ppermute(send_x, "mp", xpairs)
+    give_p = swap(backward(dkvs, ws, rows, span, 1, 1, 0, 2, None, BF16))
+    give_q = swap(backward(dkvs, ws, rows, span, 1, 2, 1, 1, None, BF16))
+    p_own = backward(dkvs, ws, rows, span, 0, 1, 0, 2, give_p, F32)
+    q_own = backward(dkvs, ws, rows, span, 0, 2, 1, 1, give_q, F32)
+    context = gather_context(context_a, context_b)
+    got_y, got_x, p_own, q_own, context = lax.optimization_barrier(
+        (got_y, got_x, p_own, q_own, context)
+    )
+    to_x = (p_own[:, span:] + got_y[:, span:].astype(F32)).astype(BF16)
+    to_y = (q_own[rows:] + got_x[rows:].astype(F32)).astype(BF16)
+    last_x = lax.ppermute(to_x, "mp", xpairs)
+    last_y = lax.ppermute(to_y, "dp", ypairs)
+    enc_grad = finish(p_own, got_y, last_x, q_own, got_x, last_y)
+    return (context, enc_grad)
+
+
 def solution(mesh):
     placed = (
         P(("section", "dp"), "mp"),
@@ -139,8 +527,10 @@
         P(("section", "dp"), "mp"),
         P(("section", "dp"), "mp"),
     )
+    sizes = tuple(mesh.shape[a] for a in ("section", "dp", "mp"))
+    body = shards_section if sizes == (4, 4, 2) else shards_general
     return jax.shard_map(
-        shards,
+        body,
         mesh=mesh,
         in_specs=placed,
         out_specs=(P(("section", "dp"), "mp"), P(("section", "dp"), "mp")),

time: 489 us -> 304 us (0.62)
  waiting for transfers between devices: 330 us -> 91.2 us
  Pallas kernels: 0 us -> 80.7 us
  matrix products: 69.9 us -> 0 us
  starting transfers between devices: 11.7 us -> 75.1 us
  local copies, waits for them, and re-layouts: 52 us -> 36.9 us
  between operations: 14.3 us -> 1.27 us
  other arithmetic: 5.3 us -> 14.2 us
    all_gather x3 -> x0, waiting for transfers between devices: 264 us -> none  [the longest x1 129 us: shards(): lax.all_gather(w_value, ('section', 'dp'), axis=0, tiled=True)]
    pallas_call x0 -> x14, Pallas kernels: none -> 80.7 us  [the longest x4 43.6 us: forward_chunk(): pl.pallas_call(functools.partial(forward_kernel, n_dp, n_sec, n_half, blk...]
    ppermute x0 -> x30, waiting for transfers between devices: none -> 71.9 us  [the longest x1 26.8 us: shards_section(): end0 = lax.ppermute(z0[2], 'section', ends)]
    dot_general x17 -> x0, matrix products: 69.9 us -> none  [the longest x2 11.8 us: shards(): lax.dot_general(value_grad, value_part, (((1,), (1,)), ((), ())), preferr...]
    ppermute x0 -> x30, starting transfers between devices: none -> 55.3 us  [the longest x4 21.3 us: along(): lax.ppermute(piece, 'section', up)]
    reshape x16 -> x6, local copies, waits for them, and re-layouts: 40.1 us -> 8.61 us  [by_owner(): return x.reshape(rows, n_dp, head_cols).transpose(1, 0, 2)]
    reduce_scatter x1 -> x0, waiting for transfers between devices: 30.2 us -> none  [shards(): lax.psum_scatter(jnp.concatenate(pieces_out, axis=1), 'mp', scatter_dimen...]
    unnamed x24 -> x81, local copies, waits for them, and re-layouts: 1.01 us -> 18.4 us
  transfers between devices with their start and end apart: 7 -> 35, of which waited for: 6 -> 11; matrix products, arithmetic and copies ran while one was open for 8% -> 13% of each run, Pallas kernels for 0% -> 20%
where the time goes in v3:
time: 304 us; the launch traced here: 299 us
  waiting for transfers between devices  91.2 us (30%)
  Pallas kernels  80.7 us (27%)
  starting transfers between devices  75.1 us (25%)
  local copies, waits for them, and re-layouts  36.9 us (12%)
  other arithmetic  14.2 us (5%)
    pallas_call x4, Pallas kernels, forward_chunk(): pl.pallas_call(functools.partial(forward_kernel, n_dp, n_sec, n_half, blk...  43.6 us
    pallas_call x8, Pallas kernels, backward(): pl.pallas_call(functools.partial(backward_kernel, chunks, received is not...  30.2 us
    ppermute x1, waiting for transfers between devices, shards_section(): end0 = lax.ppermute(z0[2], 'section', ends)  26.8 us
    ppermute x4, starting transfers between devices, along(): lax.ppermute(piece, 'section', up)  21.3 us
    all_to_all x5, starting transfers between devices, exchange(): return lax.all_to_all(x, 'dp', split_axis=0, concat_axis=0, tiled=True)  19.8 us
    all_to_all x5, waiting for transfers between devices, exchange(): return lax.all_to_all(x, 'dp', split_axis=0, concat_axis=0, tiled=True)  19.3 us
    unnamed x81, local copies, waits for them, and re-layouts  18.4 us
    ppermute x1, waiting for transfers between devices, shards_section(): end1 = lax.ppermute(z1[2], 'section', ends)  13.2 us
  transfers between devices with their start and end apart: 35, of which 11 were waited for; matrix products, arithmetic and copies ran while one was open for 13% of the time, Pallas kernels for 20%

profile of v3, /device:TPU:0, one launch (start us, length us, event | category | flops | bytes accessed | tf_op | source)
XLA Modules:
  0.0 299.3 jit_solution(15086102281813712621)
XLA Ops:
  3.6 4.1 %all-to-all-start = ((bf16[4,256,256]{2,1,0:T(8,128)(2,1)}), bf16[4,256,256]{2,1,0:T(8,128)(2,1)}, u32[]{:S(2)}, u32[]{:S(2)}) async-start(bf16[4,256,256]{2,1,0:T(8,128)(2,1)} %pad_maximum_fusion.2), calls=%async_computation | async-start | bytes 1048576 | tf_op jit(solution)/shard_map/all_to_all | solution.py:385
  7.7 2.6 collective-permute-start.5
  10.4 7.1 %all-to-all-done = bf16[4,256,256]{2,1,0:T(8,128)(2,1)} async-done(((bf16[4,256,256]{2,1,0:T(8,128)(2,1)}), bf16[4,256,256]{2,1,0:T(8,128)(2,1)}, u32[]{:S(2)}, u32[]{:S(2)}) %all-to-all-start) | async-done | bytes 524320 | tf_op jit(solution)/shard_map/all_to_all | solution.py:385
  17.5 2.8 collective-permute-start.3
  21.6 5.3 %collective-permute-start.1 = (bf16[1024,256]{1,0:T(8,128)(2,1)}, bf16[1024,256]{1,0:T(8,128)(2,1)}, u32[]{:S(2)}, u32[]{:S(2)}) collective-permute-start(bf16[1024,256]{1,0:T(8,128)(2,1)} %bitcast.2.refs_8_), channel_id=1, source_target_pairs={{0,8},{8,16},{16,24},{1,9},{9,17},{17,25},{2,10},{10,18},{18,26},{... | collective-permute-start | bytes 1572872 | tf_op jit(solution)/shard_map/ppermute | solution.py:395
  27.0 2.3 copy.24
  29.2 2.3 copy.25
  31.5 2.3 copy.26
  33.8 2.3 copy.27
  36.0 1.5 copy.28
  38.8 1.5 copy.30
  42.0 2.5 bitcast_dynamic-update-slice_fusion.1
  44.5 2.3 bitcast_dynamic-update-slice_fusion
  50.9 4.1 %all-to-all-start.1 = ((bf16[4,256,256]{2,1,0:T(8,128)(2,1)}), bf16[4,256,256]{2,1,0:T(8,128)(2,1)}, u32[]{:S(2)}, u32[]{:S(2)}) async-start(bf16[4,256,256]{2,1,0:T(8,128)(2,1)} %pad_maximum_fusion.3), calls=%async_computation.1 | async-start | bytes 1048576 | tf_op jit(solution)/shard_map/all_to_all | solution.py:385
  55.2 3.9 %pad_maximum_fusion = bf16[4,272,1536]{2,1,0:T(8,128)(2,1)} fusion(bf16[4,16,1536]{2,1,0:T(8,128)(2,1)S(1)} %broadcast_in_dim.48, bf16[4,256,1536]{2,1,0:T(8,128)(2,1)} %get-tuple-element.134), kind=kLoop, calls=%fused_computation | loop fusion | flops 6684672 | bytes 6684672 | tf_op jit(solution)/shard_map/concatenate | solution.py:417
  59.1 12.2 %all-to-all-done.1 = bf16[4,256,256]{2,1,0:T(8,128)(2,1)} async-done(((bf16[4,256,256]{2,1,0:T(8,128)(2,1)}), bf16[4,256,256]{2,1,0:T(8,128)(2,1)}, u32[]{:S(2)}, u32[]{:S(2)}) %all-to-all-start.1) | async-done | bytes 524320 | tf_op jit(solution)/shard_map/all_to_all | solution.py:385
  72.2 3.7 %all-to-all-start.2 = ((bf16[4,272,1536]{2,1,0:T(8,128)(2,1)}), bf16[4,272,1536]{2,1,0:T(8,128)(2,1)S(1)}, u32[]{:S(2)}, u32[]{:S(2)}) async-start(bf16[4,272,1536]{2,1,0:T(8,128)(2,1)} %pad_maximum_fusion), calls=%async_computation.2 | async-start | bytes 6684672 | tf_op jit(solution)/shard_map/all_to_all | solution.py:385
  76.0 1.6 collective-permute-start.10
  79.3 5.4 %collective-permute-start.7 = (bf16[1024,256]{1,0:T(8,128)(2,1)}, bf16[1024,256]{1,0:T(8,128)(2,1)}, u32[]{:S(2)}, u32[]{:S(2)}) collective-permute-start(bf16[1024,256]{1,0:T(8,128)(2,1)} %bitcast.7.refs_8_), channel_id=1, source_target_pairs={{0,8},{8,16},{16,24},{1,9},{9,17},{17,25},{2,10},{10,18},{18,26},{... | collective-permute-start | bytes 1572872 | tf_op jit(solution)/shard_map/ppermute | solution.py:395
  86.1 3.1 %pad_maximum_fusion.1 = bf16[512,2048]{1,0:T(8,128)(2,1)} fusion(bf16[256,2048]{1,0:T(8,128)(2,1)} %copy-done.16, bf16[256,2048]{1,0:T(8,128)(2,1)} %copy-done.15), kind=kLoop, calls=%fused_computation.1 | loop fusion | flops 4194304 | bytes 4194304 | tf_op jit(solution)/shard_map/concatenate | solution.py:424
  89.2 26.8 %collective-permute-done.6.refs_12_ = bf16[1024,256]{1,0:T(8,128)(2,1)} collective-permute-done((bf16[1024,256]{1,0:T(8,128)(2,1)}, bf16[1024,256]{1,0:T(8,128)(2,1)}, u32[]{:S(2)}, u32[]{:S(2)}) %collective-permute-start.6) | collective-permute-done | bytes 524320 | tf_op jit(solution)/shard_map/ppermute | solution.py:420
  117.5 3.7 %collective-permute-start.14 = (bf16[1024,256]{1,0:T(8,128)(2,1)}, bf16[1024,256]{1,0:T(8,128)(2,1)}, u32[]{:S(2)}, u32[]{:S(2)}) collective-permute-start(bf16[1024,256]{1,0:T(8,128)(2,1)} %bitcast.14.refs_8_), channel_id=1, source_target_pairs={{0,16},{8,24},{16,0},{24,8},{1,17},{9,25},{17,1},{25,9},{2,18},{10... | collective-permute-start | bytes 1572872 | tf_op jit(solution)/shard_map/ppermute | solution.py:397
  122.4 5.8 %collective-permute-start.12 = (bf16[1024,256]{1,0:T(8,128)(2,1)}, bf16[1024,256]{1,0:T(8,128)(2,1)}, u32[]{:S(2)}, u32[]{:S(2)}) collective-permute-start(bf16[1024,256]{1,0:T(8,128)(2,1)} %bitcast.14.refs_8_), channel_id=1, source_target_pairs={{0,8},{8,16},{16,24},{1,9},{9,17},{17,25},{2,10},{10,18},{18,26},{... | collective-permute-start | bytes 1572872 | tf_op jit(solution)/shard_map/ppermute | solution.py:395
  129.0 2.3 collective-permute-done.16.refs_7_
  134.4 10.9 %fwd.4 = (bf16[4,256,128]{2,1,0:T(8,128)(2,1)}, bf16[1024,256]{1,0:T(8,128)(2,1)}, bf16[4096,256]{1,0:T(8,128)(2,1)}) custom-call(s32[34]{0:T(128)} %pad_add_fusion.tab, bf16[256,2048]{1,0:T(8,128)(2,1)} %refs_0_.3, bf16[256,2048]{1,0:T(8,128)(2,1)} %copy-done.18, bf16[256,2048]{1,0:T(8,128)(2,1)} %copy-done.16, ...), custom_call_target="tpu_custom_call" | custom-call | flops 1 | bytes 1 | tf_op jit(solution)/shard_map/fwd/pallas_call | solution.py:259
  145.2 13.2 %collective-permute-done.11.refs_12_ = bf16[1024,256]{1,0:T(8,128)(2,1)} collective-permute-done((bf16[1024,256]{1,0:T(8,128)(2,1)}, bf16[1024,256]{1,0:T(8,128)(2,1)}, u32[]{:S(2)}, u32[]{:S(2)}) %collective-permute-start.11) | collective-permute-done | bytes 524320 | tf_op jit(solution)/shard_map/ppermute | solution.py:433
  159.9 8.4 %collective-permute-start.20 = (bf16[1024,256]{1,0:T(8,128)(2,1)}, bf16[1024,256]{1,0:T(8,128)(2,1)S(1)}, u32[]{:S(2)}, u32[]{:S(2)}) collective-permute-start(bf16[1024,256]{1,0:T(8,128)(2,1)} %bitcast.15.refs_8_), channel_id=1, source_target_pairs={{0,24},{24,0},{1,25},{25,1},{2,26},{26,2},{3,27},{27,3},{4,28},{28... | collective-permute-start | bytes 1572872 | tf_op jit(solution)/shard_map/ppermute | solution.py:484
  169.6 4.8 %collective-permute-start.17 = (bf16[1024,256]{1,0:T(8,128)(2,1)}, bf16[1024,256]{1,0:T(8,128)(2,1)S(1)}, u32[]{:S(2)}, u32[]{:S(2)}) collective-permute-start(bf16[1024,256]{1,0:T(8,128)(2,1)} %bitcast.15.refs_8_), channel_id=1, source_target_pairs={{0,8},{8,16},{16,24},{1,9},{9,17},{17,25},{2,10},{10,18},{18,26},{... | collective-permute-start | bytes 1572872 | tf_op jit(solution)/shard_map/ppermute | solution.py:395
  174.4 10.8 %fwd.5 = (bf16[4,256,128]{2,1,0:T(8,128)(2,1)}, bf16[1024,256]{1,0:T(8,128)(2,1)}, bf16[4096,256]{1,0:T(8,128)(2,1)}) custom-call(s32[34]{0:T(128)} %pad_add_fusion.tab, bf16[256,2048]{1,0:T(8,128)(2,1)} %refs_0_.3, bf16[256,2048]{1,0:T(8,128)(2,1)} %copy-done.18, bf16[256,2048]{1,0:T(8,128)(2,1)} %copy-done.16, ...), custom_call_target="tpu_custom_call" | custom-call | flops 1 | bytes 1 | tf_op jit(solution)/shard_map/fwd/pallas_call | solution.py:259
  185.3 1.8 pad_maximum_fusion.4
  187.1 3.5 %all-to-all-start.3 = ((bf16[4,256,256]{2,1,0:T(8,128)(2,1)}), bf16[4,256,256]{2,1,0:T(8,128)(2,1)S(1)}, u32[]{:S(2)}, u32[]{:S(2)}) async-start(bf16[4,256,256]{2,1,0:T(8,128)(2,1)} %pad_maximum_fusion.4), calls=%async_computation.3 | async-start | bytes 1048576 | tf_op jit(solution)/shard_map/all_to_all | solution.py:385
  191.4 10.8 %fwd.6 = (bf16[4,256,128]{2,1,0:T(8,128)(2,1)}, bf16[1024,256]{1,0:T(8,128)(2,1)}, bf16[4096,256]{1,0:T(8,128)(2,1)}) custom-call(s32[34]{0:T(128)} %pad_add_fusion.tab, bf16[256,2048]{1,0:T(8,128)(2,1)} %refs_0_.3, bf16[256,2048]{1,0:T(8,128)(2,1)} %copy-done.18, bf16[256,2048]{1,0:T(8,128)(2,1)} %copy-done.16, ...), custom_call_target="tpu_custom_call" | custom-call | flops 1 | bytes 1 | tf_op jit(solution)/shard_map/fwd/pallas_call | solution.py:259
  202.4 5.3 %collective-permute-done.18.refs_9_ = bf16[1024,256]{1,0:T(8,128)(2,1)S(1)} collective-permute-done((bf16[1024,256]{1,0:T(8,128)(2,1)}, bf16[1024,256]{1,0:T(8,128)(2,1)S(1)}, u32[]{:S(2)}, u32[]{:S(2)}) %collective-permute-start.18) | collective-permute-done | bytes 524320 | tf_op jit(solution)/shard_map/ppermute | solution.py:396
  208.7 11.1 %fwd.7 = (bf16[4,256,128]{2,1,0:T(8,128)(2,1)}, bf16[1024,256]{1,0:T(8,128)(2,1)}, bf16[4096,256]{1,0:T(8,128)(2,1)}) custom-call(s32[34]{0:T(128)} %pad_add_fusion.tab, bf16[256,2048]{1,0:T(8,128)(2,1)} %refs_0_.3, bf16[256,2048]{1,0:T(8,128)(2,1)} %copy-done.18, bf16[256,2048]{1,0:T(8,128)(2,1)} %copy-done.16, ...), custom_call_target="tpu_custom_call" | custom-call | flops 1 | bytes 1 | tf_op jit(solution)/shard_map/fwd/pallas_call | solution.py:259
  221.0 3.7 %bwd.8 = bf16[256,2048]{1,0:T(8,128)(2,1)} custom-call(bf16[1024,256]{1,0:T(8,128)(2,1)S(1)} %copy-done.2, bf16[1024,256]{1,0:T(8,128)(2,1)S(1)} %copy-done.3, bf16[1024,256]{1,0:T(8,128)(2,1)S(1)} %copy-done.4, bf16[1024,256]{1,0:T(8,128)(2,1)S(1)} %copy-done.8, bf16[4096,256]{1,0:T(8,128)(2,1)S(1)} %copy-done, ...), custom_call_target="tpu_custom_call" | custom-call | flops 1 | bytes 1 | tf_op jit(solution)/shard_map/bwd/pallas_call | solution.py:305
  224.6 3.7 %bwd.10 = bf16[512,1024]{1,0:T(8,128)(2,1)} custom-call(bf16[1024,256]{1,0:T(8,128)(2,1)S(1)} %copy-done.2, bf16[1024,256]{1,0:T(8,128)(2,1)S(1)} %copy-done.3, bf16[1024,256]{1,0:T(8,128)(2,1)S(1)} %copy-done.4, bf16[1024,256]{1,0:T(8,128)(2,1)S(1)} %copy-done.8, bf16[4096,256]{1,0:T(8,128)(2,1)S(1)} %copy-done, ...), custom_call_target="tpu_custom_call" | custom-call | flops 1 | bytes 1 | tf_op jit(solution)/shard_map/bwd/pallas_call | solution.py:305
  229.7 4.4 %all-to-all-start.4 = ((bf16[4,256,256]{2,1,0:T(8,128)(2,1)}), bf16[4,256,256]{2,1,0:T(8,128)(2,1)}, u32[]{:S(2)}, u32[]{:S(2)}) async-start(bf16[4,256,256]{2,1,0:T(8,128)(2,1)} %pad_maximum_fusion.5), calls=%async_computation.4 | async-start | bytes 1048576 | tf_op jit(solution)/shard_map/all_to_all | solution.py:385
  236.2 4.0 %bwd.9 = bf16[256,2048]{1,0:T(8,128)(2,1)} custom-call(bf16[1024,256]{1,0:T(8,128)(2,1)S(1)} %copy-done.2, bf16[1024,256]{1,0:T(8,128)(2,1)S(1)} %copy-done.3, bf16[1024,256]{1,0:T(8,128)(2,1)S(1)} %copy-done.5, bf16[1024,256]{1,0:T(8,128)(2,1)S(1)} %copy-done.9, bf16[4096,256]{1,0:T(8,128)(2,1)} %get-tuple-element.109.refs_4_, ...), custom_call_target="tpu_custom_call" | custom-call | flops 1 | bytes 1 | tf_op jit(solution)/shard_map/bwd/pallas_call | solution.py:305
  240.2 4.2 %bwd.11 = bf16[512,1024]{1,0:T(8,128)(2,1)} custom-call(bf16[1024,256]{1,0:T(8,128)(2,1)S(1)} %copy-done.2, bf16[1024,256]{1,0:T(8,128)(2,1)S(1)} %copy-done.3, bf16[1024,256]{1,0:T(8,128)(2,1)S(1)} %copy-done.5, bf16[1024,256]{1,0:T(8,128)(2,1)S(1)} %copy-done.9, bf16[4096,256]{1,0:T(8,128)(2,1)} %get-tuple-element.109.refs_4_, ...), custom_call_target="tpu_custom_call" | custom-call | flops 1 | bytes 1 | tf_op jit(solution)/shard_map/bwd/pallas_call | solution.py:305
  246.5 3.7 %bwd.12 = bf16[256,2048]{1,0:T(8,128)(2,1)} custom-call(bf16[1024,256]{1,0:T(8,128)(2,1)S(1)} %copy-done.2, bf16[1024,256]{1,0:T(8,128)(2,1)S(1)} %copy-done.3, bf16[1024,256]{1,0:T(8,128)(2,1)S(1)} %copy-done.6, bf16[1024,256]{1,0:T(8,128)(2,1)S(1)} %copy-done.10, bf16[4096,256]{1,0:T(8,128)(2,1)S(1)} %copy-done.1, ...), custom_call_target="tpu_custom_call" | custom-call | flops 1 | bytes 1 | tf_op jit(solution)/shard_map/bwd/pallas_call | solution.py:305
  250.4 3.7 %bwd.14 = bf16[512,1024]{1,0:T(8,128)(2,1)} custom-call(bf16[1024,256]{1,0:T(8,128)(2,1)S(1)} %copy-done.2, bf16[1024,256]{1,0:T(8,128)(2,1)S(1)} %copy-done.3, bf16[1024,256]{1,0:T(8,128)(2,1)S(1)} %copy-done.6, bf16[1024,256]{1,0:T(8,128)(2,1)S(1)} %copy-done.10, bf16[4096,256]{1,0:T(8,128)(2,1)S(1)} %copy-done.1, ...), custom_call_target="tpu_custom_call" | custom-call | flops 1 | bytes 1 | tf_op jit(solution)/shard_map/bwd/pallas_call | solution.py:305
  254.3 1.8 collective-permute-start.24
  256.6 3.4 %gather_context.1 = bf16[256,2048]{1,0:T(8,128)(2,1)} custom-call(bf16[4,256,256]{2,1,0:T(8,128)(2,1)} %copy-done.24, bf16[4,256,256]{2,1,0:T(8,128)(2,1)} %all-to-all-done.4.refs_1_), custom_call_target="tpu_custom_call" | custom-call | tf_op jit(solution)/shard_map/gather_context/pallas_call | solution.py:351
  262.1 3.3 %bwd.13.p_ref = f32[256,2048]{1,0:T(8,128)S(1)} custom-call(bf16[1024,256]{1,0:T(8,128)(2,1)S(1)} %copy-done.2, bf16[1024,256]{1,0:T(8,128)(2,1)S(1)} %copy-done.3, bf16[1024,256]{1,0:T(8,128)(2,1)S(1)} %copy-done.7, bf16[1024,256]{1,0:T(8,128)(2,1)S(1)} %copy-done.11, bf16[4096,256]{1,0:T(8,128)(2,1)} %get-tuple-element.109.refs_4_, ...), custom_call_target="tpu_custom_call" | custom-call | flops 1 | bytes 1 | tf_op jit(solution)/shard_map/bwd/pallas_call | solution.py:305
  265.5 4.0 %bwd.15.q_ref = f32[512,1024]{1,0:T(8,128)S(1)} custom-call(bf16[1024,256]{1,0:T(8,128)(2,1)S(1)} %copy-done.2, bf16[1024,256]{1,0:T(8,128)(2,1)S(1)} %copy-done.3, bf16[1024,256]{1,0:T(8,128)(2,1)S(1)} %copy-done.7, bf16[1024,256]{1,0:T(8,128)(2,1)S(1)} %copy-done.11, bf16[4096,256]{1,0:T(8,128)(2,1)} %get-tuple-element.109.refs_4_, ...), custom_call_target="tpu_custom_call" | custom-call | flops 1 | bytes 1 | tf_op jit(solution)/shard_map/bwd/pallas_call | solution.py:305
  269.4 10.4 %collective-permute-done.24.got_y = bf16[256,2048]{1,0:T(8,128)(2,1)S(1)} collective-permute-done((bf16[256,2048]{1,0:T(8,128)(2,1)}, bf16[256,2048]{1,0:T(8,128)(2,1)S(1)}, u32[]{:S(2)}, u32[]{:S(2)}) %collective-permute-start.24) | collective-permute-done | bytes 1048608 | tf_op jit(solution)/shard_map/ppermute | solution.py:501
  282.5 11.7 %collective-permute-done.29.last_y = bf16[256,1024]{1,0:T(8,128)(2,1)S(1)} collective-permute-done((bf16[256,1024]{1,0:T(8,128)(2,1)S(1)}, bf16[256,1024]{1,0:T(8,128)(2,1)S(1)}, u32[]{:S(2)}, u32[]{:S(2)}) %collective-permute-start.29) | collective-permute-done | bytes 524320 | tf_op jit(solution)/shard_map/ppermute | solution.py:514
  295.8 3.4 %finish.1 = bf16[256,2048]{1,0:T(8,128)(2,1)} custom-call(f32[256,2048]{1,0:T(8,128)} %copy-done.12, bf16[256,2048]{1,0:T(8,128)(2,1)} %copy-done.22, bf16[256,1024]{1,0:T(8,128)(2,1)} %copy-done.31, f32[512,1024]{1,0:T(8,128)} %copy-done.13, bf16[512,1024]{1,0:T(8,128)(2,1)} %copy-done.23, bf16[256,1024]{1,0:T(8,128)(2,1)} %copy-done.30), custom_call_target="tpu_custom_call" | custom-call | tf_op jit(solution)/shard_map/finish/pallas_call | solution.py:330
  (159 shorter events, 40.7 us)
Async XLA Ops:
  0.6 16.9 %collective-permute-start = (bf16[256,2048]{1,0:T(8,128)(2,1)}, bf16[256,2048]{1,0:T(8,128)(2,1)S(1)}, u32[]{:S(2)}, u32[]{:S(2)}) collective-permute-start(bf16[256,2048]{1,0:T(8,128)(2,1)} %refs_0_.3), channel_id=1, source_target_pairs={{0,2},{2,0},{4,6},{6,4},{1,3},{3,1},{5,7},{7,5},{8,10},{10,8},{12,... | collective-permute-start | bytes 3145736 | tf_op jit(solution)/shard_map/ppermute | solution.py:382
  2.5 7.9 %copy-start.37 = (s32[1,4]{1,0:T(1,128)S(1)}, s32[1,4]{1,0:T(1,128)}, u32[]{:S(2)}) copy-start(s32[1,4]{1,0:T(1,128)} %param.11) | copy-start | bytes 52
  3.6 13.9 %all-to-all-start = ((bf16[4,256,256]{2,1,0:T(8,128)(2,1)}), bf16[4,256,256]{2,1,0:T(8,128)(2,1)}, u32[]{:S(2)}, u32[]{:S(2)}) async-start(bf16[4,256,256]{2,1,0:T(8,128)(2,1)} %pad_maximum_fusion.2), calls=%async_computation | async-start | bytes 1048576 | tf_op jit(solution)/shard_map/all_to_all | solution.py:385
  7.7 51.3 %collective-permute-start.5 = (bf16[256,2048]{1,0:T(8,128)(2,1)S(1)}, bf16[256,2048]{1,0:T(8,128)(2,1)S(1)}, u32[]{:S(2)}, u32[]{:S(2)}) collective-permute-start(bf16[256,2048]{1,0:T(8,128)(2,1)S(1)} %copy-done.17), channel_id=1, source_target_pairs={{0,1},{1,0},{2,3},{3,2},{4,5},{5,4},{6,7},{7,6},{8,9},{9,8},{10,11... | collective-permute-start | bytes 3145736 | tf_op jit(solution)/shard_map/ppermute | solution.py:401
  17.5 16.2 %copy-start.18 = (bf16[256,2048]{1,0:T(8,128)(2,1)}, bf16[256,2048]{1,0:T(8,128)(2,1)S(1)}, u32[]{:S(2)}) copy-start(bf16[256,2048]{1,0:T(8,128)(2,1)S(1)} %collective-permute-done.refs_1_) | copy-start | bytes 3145732
  17.5 53.7 %collective-permute-start.3 = (bf16[1024,256]{1,0:T(8,128)(2,1)}, bf16[1024,256]{1,0:T(8,128)(2,1)}, u32[]{:S(2)}, u32[]{:S(2)}) collective-permute-start(bf16[1024,256]{1,0:T(8,128)(2,1)} %bitcast.2.refs_8_), channel_id=1, source_target_pairs={{0,16},{8,24},{16,0},{24,8},{1,17},{9,25},{17,1},{25,9},{2,18},{10... | collective-permute-start | bytes 1572872 | tf_op jit(solution)/shard_map/ppermute | solution.py:397
  20.3 50.9 %collective-permute-start.2 = (bf16[1024,256]{1,0:T(8,128)(2,1)}, bf16[1024,256]{1,0:T(8,128)(2,1)}, u32[]{:S(2)}, u32[]{:S(2)}) collective-permute-start(bf16[1024,256]{1,0:T(8,128)(2,1)} %bitcast.2.refs_8_), channel_id=1, source_target_pairs={{8,0},{16,8},{24,16},{9,1},{17,9},{25,17},{10,2},{18,10},{26,18},{... | collective-permute-start | bytes 1572872 | tf_op jit(solution)/shard_map/ppermute | solution.py:396
  21.6 49.6 %collective-permute-start.1 = (bf16[1024,256]{1,0:T(8,128)(2,1)}, bf16[1024,256]{1,0:T(8,128)(2,1)}, u32[]{:S(2)}, u32[]{:S(2)}) collective-permute-start(bf16[1024,256]{1,0:T(8,128)(2,1)} %bitcast.2.refs_8_), channel_id=1, source_target_pairs={{0,8},{8,16},{16,24},{1,9},{9,17},{17,25},{2,10},{10,18},{18,26},{... | collective-permute-start | bytes 1572872 | tf_op jit(solution)/shard_map/ppermute | solution.py:395
  41.7 29.6 %collective-permute-start.4 = (bf16[256,2048]{1,0:T(8,128)(2,1)S(1)}, bf16[256,2048]{1,0:T(8,128)(2,1)S(1)}, u32[]{:S(2)}, u32[]{:S(2)}) collective-permute-start(bf16[256,2048]{1,0:T(8,128)(2,1)S(1)} %copy-done.17), channel_id=1, source_target_pairs={{0,4},{2,6},{4,0},{6,2},{1,5},{3,7},{5,1},{7,3},{8,12},{10,14},{12... | collective-permute-start | bytes 3145736 | tf_op jit(solution)/shard_map/ppermute | solution.py:408
  50.9 20.3 %all-to-all-start.1 = ((bf16[4,256,256]{2,1,0:T(8,128)(2,1)}), bf16[4,256,256]{2,1,0:T(8,128)(2,1)}, u32[]{:S(2)}, u32[]{:S(2)}) async-start(bf16[4,256,256]{2,1,0:T(8,128)(2,1)} %pad_maximum_fusion.3), calls=%async_computation.1 | async-start | bytes 1048576 | tf_op jit(solution)/shard_map/all_to_all | solution.py:385
  59.1 12.2 %copy-start.15 = (bf16[256,2048]{1,0:T(8,128)(2,1)}, bf16[256,2048]{1,0:T(8,128)(2,1)S(1)}, u32[]{:S(2)}) copy-start(bf16[256,2048]{1,0:T(8,128)(2,1)S(1)} %collective-permute-done.5.refs_4_) | copy-start | bytes 3145732
  72.2 43.9 %all-to-all-start.2 = ((bf16[4,272,1536]{2,1,0:T(8,128)(2,1)}), bf16[4,272,1536]{2,1,0:T(8,128)(2,1)S(1)}, u32[]{:S(2)}, u32[]{:S(2)}) async-start(bf16[4,272,1536]{2,1,0:T(8,128)(2,1)} %pad_maximum_fusion), calls=%async_computation.2 | async-start | bytes 6684672 | tf_op jit(solution)/shard_map/all_to_all | solution.py:385
  76.0 40.1 %collective-permute-start.10 = (bf16[256,2048]{1,0:T(8,128)(2,1)}, bf16[256,2048]{1,0:T(8,128)(2,1)}, u32[]{:S(2)}, u32[]{:S(2)}) collective-permute-start(bf16[256,2048]{1,0:T(8,128)(2,1)} %copy-done.16), channel_id=1, source_target_pairs={{0,1},{1,0},{2,3},{3,2},{4,5},{5,4},{6,7},{7,6},{8,9},{9,8},{10,11... | collective-permute-start | bytes 3145736 | tf_op jit(solution)/shard_map/ppermute | solution.py:422
  77.5 38.6 %collective-permute-start.9 = (bf16[1024,256]{1,0:T(8,128)(2,1)}, bf16[1024,256]{1,0:T(8,128)(2,1)}, u32[]{:S(2)}, u32[]{:S(2)}) collective-permute-start(bf16[1024,256]{1,0:T(8,128)(2,1)} %bitcast.7.refs_8_), channel_id=1, source_target_pairs={{0,16},{8,24},{16,0},{24,8},{1,17},{9,25},{17,1},{25,9},{2,18},{10... | collective-permute-start | bytes 1572872 | tf_op jit(solution)/shard_map/ppermute | solution.py:397
  78.0 38.0 %collective-permute-start.8 = (bf16[1024,256]{1,0:T(8,128)(2,1)}, bf16[1024,256]{1,0:T(8,128)(2,1)}, u32[]{:S(2)}, u32[]{:S(2)}) collective-permute-start(bf16[1024,256]{1,0:T(8,128)(2,1)} %bitcast.7.refs_8_), channel_id=1, source_target_pairs={{8,0},{16,8},{24,16},{9,1},{17,9},{25,17},{10,2},{18,10},{26,18},{... | collective-permute-start | bytes 1572872 | tf_op jit(solution)/shard_map/ppermute | solution.py:396
  79.3 36.8 %collective-permute-start.7 = (bf16[1024,256]{1,0:T(8,128)(2,1)}, bf16[1024,256]{1,0:T(8,128)(2,1)}, u32[]{:S(2)}, u32[]{:S(2)}) collective-permute-start(bf16[1024,256]{1,0:T(8,128)(2,1)} %bitcast.7.refs_8_), channel_id=1, source_target_pairs={{0,8},{8,16},{16,24},{1,9},{9,17},{17,25},{2,10},{10,18},{18,26},{... | collective-permute-start | bytes 1572872 | tf_op jit(solution)/shard_map/ppermute | solution.py:395
  84.7 31.4 %collective-permute-start.6 = (bf16[1024,256]{1,0:T(8,128)(2,1)}, bf16[1024,256]{1,0:T(8,128)(2,1)}, u32[]{:S(2)}, u32[]{:S(2)}) collective-permute-start(bf16[1024,256]{1,0:T(8,128)(2,1)} %collective-permute-done.3.refs_10_), channel_id=1, source_target_pairs={{8,0},{16,24},{9,1},{17,25},{10,2},{18,26},{11,3},{19,27},{12,4},{... | collective-permute-start | bytes 1572872 | tf_op jit(solution)/shard_map/ppermute | solution.py:420
  116.1 18.2 %copy-start.14 = (bf16[4,272,1536]{2,1,0:T(8,128)(2,1)}, bf16[4,272,1536]{2,1,0:T(8,128)(2,1)S(1)}, u32[]{:S(2)}) copy-start(bf16[4,272,1536]{2,1,0:T(8,128)(2,1)S(1)} %all-to-all-done.2.refs_13_.refs_14_) | copy-start | bytes 10027012
  116.1 18.2 %collective-permute-start.15 = (bf16[512,2048]{1,0:T(8,128)(2,1)}, bf16[512,2048]{1,0:T(8,128)(2,1)}, u32[]{:S(2)}, u32[]{:S(2)}) collective-permute-start(bf16[512,2048]{1,0:T(8,128)(2,1)} %pad_maximum_fusion.1), channel_id=1, source_target_pairs={{0,2},{2,0},{4,6},{6,4},{1,3},{3,1},{5,7},{7,5},{8,10},{10,8},{12,... | collective-permute-start | bytes 6291464 | tf_op jit(solution)/shard_map/ppermute | solution.py:382
  117.5 40.9 %collective-permute-start.14 = (bf16[1024,256]{1,0:T(8,128)(2,1)}, bf16[1024,256]{1,0:T(8,128)(2,1)}, u32[]{:S(2)}, u32[]{:S(2)}) collective-permute-start(bf16[1024,256]{1,0:T(8,128)(2,1)} %bitcast.14.refs_8_), channel_id=1, source_target_pairs={{0,16},{8,24},{16,0},{24,8},{1,17},{9,25},{17,1},{25,9},{2,18},{10... | collective-permute-start | bytes 1572872 | tf_op jit(solution)/shard_map/ppermute | solution.py:397
  121.2 37.3 %collective-permute-start.13 = (bf16[1024,256]{1,0:T(8,128)(2,1)}, bf16[1024,256]{1,0:T(8,128)(2,1)}, u32[]{:S(2)}, u32[]{:S(2)}) collective-permute-start(bf16[1024,256]{1,0:T(8,128)(2,1)} %bitcast.14.refs_8_), channel_id=1, source_target_pairs={{8,0},{16,8},{24,16},{9,1},{17,9},{25,17},{10,2},{18,10},{26,18},{... | collective-permute-start | bytes 1572872 | tf_op jit(solution)/shard_map/ppermute | solution.py:396
  122.4 36.0 %collective-permute-start.12 = (bf16[1024,256]{1,0:T(8,128)(2,1)}, bf16[1024,256]{1,0:T(8,128)(2,1)}, u32[]{:S(2)}, u32[]{:S(2)}) collective-permute-start(bf16[1024,256]{1,0:T(8,128)(2,1)} %bitcast.14.refs_8_), channel_id=1, source_target_pairs={{0,8},{8,16},{16,24},{1,9},{9,17},{17,25},{2,10},{10,18},{18,26},{... | collective-permute-start | bytes 1572872 | tf_op jit(solution)/shard_map/ppermute | solution.py:395
  128.3 3.0 %collective-permute-start.16 = (bf16[256,2048]{1,0:T(8,128)(2,1)}, bf16[256,2048]{1,0:T(8,128)(2,1)}, u32[]{:S(2)}, u32[]{:S(2)}) collective-permute-start(bf16[256,2048]{1,0:T(8,128)(2,1)} %collective-permute-done.10.refs_6_), channel_id=1, source_target_pairs={{0,2},{2,0},{4,6},{6,4},{1,3},{3,1},{5,7},{7,5},{8,10},{10,8},{12,... | collective-permute-start | bytes 3145736 | tf_op jit(solution)/shard_map/ppermute | solution.py:382
  131.3 27.1 %collective-permute-start.11 = (bf16[1024,256]{1,0:T(8,128)(2,1)}, bf16[1024,256]{1,0:T(8,128)(2,1)}, u32[]{:S(2)}, u32[]{:S(2)}) collective-permute-start(bf16[1024,256]{1,0:T(8,128)(2,1)} %collective-permute-done.9.refs_10_), channel_id=1, source_target_pairs={{8,0},{16,24},{9,1},{17,25},{10,2},{18,26},{11,3},{19,27},{12,4},{... | collective-permute-start | bytes 1572872 | tf_op jit(solution)/shard_map/ppermute | solution.py:433
  158.4 26.8 %copy-start.33 = (bf16[4,256,128]{2,1,0:T(8,128)(2,1)S(1)}, bf16[4,256,128]{2,1,0:T(8,128)(2,1)}, u32[]{:S(2)}) copy-start(bf16[4,256,128]{2,1,0:T(8,128)(2,1)} %get-tuple-element.101) | copy-start | bytes 786436
  158.4 32.1 %collective-permute-start.21 = (bf16[1024,256]{1,0:T(8,128)(2,1)}, bf16[1024,256]{1,0:T(8,128)(2,1)S(1)}, u32[]{:S(2)}, u32[]{:S(2)}) collective-permute-start(bf16[1024,256]{1,0:T(8,128)(2,1)} %collective-permute-done.14.refs_10_), channel_id=1, source_target_pairs={{8,0},{16,24},{9,1},{17,25},{10,2},{18,26},{11,3},{19,27},{12,4},{... | collective-permute-start | bytes 1572872 | tf_op jit(solution)/shard_map/ppermute | solution.py:482
  159.9 42.3 %collective-permute-start.20 = (bf16[1024,256]{1,0:T(8,128)(2,1)}, bf16[1024,256]{1,0:T(8,128)(2,1)S(1)}, u32[]{:S(2)}, u32[]{:S(2)}) collective-permute-start(bf16[1024,256]{1,0:T(8,128)(2,1)} %bitcast.15.refs_8_), channel_id=1, source_target_pairs={{0,24},{24,0},{1,25},{25,1},{2,26},{26,2},{3,27},{27,3},{4,28},{28... | collective-permute-start | bytes 1572872 | tf_op jit(solution)/shard_map/ppermute | solution.py:484
  168.3 34.1 %collective-permute-start.19 = (bf16[1024,256]{1,0:T(8,128)(2,1)}, bf16[1024,256]{1,0:T(8,128)(2,1)S(1)}, u32[]{:S(2)}, u32[]{:S(2)}) collective-permute-start(bf16[1024,256]{1,0:T(8,128)(2,1)} %bitcast.15.refs_8_), channel_id=1, source_target_pairs={{0,16},{8,24},{16,0},{24,8},{1,17},{9,25},{17,1},{25,9},{2,18},{10... | collective-permute-start | bytes 1572872 | tf_op jit(solution)/shard_map/ppermute | solution.py:397
  168.3 39.4 %collective-permute-start.18 = (bf16[1024,256]{1,0:T(8,128)(2,1)}, bf16[1024,256]{1,0:T(8,128)(2,1)S(1)}, u32[]{:S(2)}, u32[]{:S(2)}) collective-permute-start(bf16[1024,256]{1,0:T(8,128)(2,1)} %bitcast.15.refs_8_), channel_id=1, source_target_pairs={{8,0},{16,8},{24,16},{9,1},{17,9},{25,17},{10,2},{18,10},{26,18},{... | collective-permute-start | bytes 1572872 | tf_op jit(solution)/shard_map/ppermute | solution.py:396
  169.6 38.1 %collective-permute-start.17 = (bf16[1024,256]{1,0:T(8,128)(2,1)}, bf16[1024,256]{1,0:T(8,128)(2,1)S(1)}, u32[]{:S(2)}, u32[]{:S(2)}) collective-permute-start(bf16[1024,256]{1,0:T(8,128)(2,1)} %bitcast.15.refs_8_), channel_id=1, source_target_pairs={{0,8},{8,16},{16,24},{1,9},{9,17},{17,25},{2,10},{10,18},{18,26},{... | collective-permute-start | bytes 1572872 | tf_op jit(solution)/shard_map/ppermute | solution.py:395
  187.1 15.1 %all-to-all-start.3 = ((bf16[4,256,256]{2,1,0:T(8,128)(2,1)}), bf16[4,256,256]{2,1,0:T(8,128)(2,1)S(1)}, u32[]{:S(2)}, u32[]{:S(2)}) async-start(bf16[4,256,256]{2,1,0:T(8,128)(2,1)} %pad_maximum_fusion.4), calls=%async_computation.3 | async-start | bytes 1048576 | tf_op jit(solution)/shard_map/all_to_all | solution.py:385
  208.7 11.2 %copy-start = (bf16[4096,256]{1,0:T(8,128)(2,1)S(1)}, bf16[4096,256]{1,0:T(8,128)(2,1)}, u32[]{:S(2)}) copy-start(bf16[4096,256]{1,0:T(8,128)(2,1)} %get-tuple-element.109.refs_4_) | copy-start | bytes 6291460
  208.7 11.2 %copy-start.2 = (bf16[1024,256]{1,0:T(8,128)(2,1)S(1)}, bf16[1024,256]{1,0:T(8,128)(2,1)}, u32[]{:S(2)}) copy-start(bf16[1024,256]{1,0:T(8,128)(2,1)} %get-tuple-element.117.refs_0_) | copy-start | bytes 1572868
  208.7 11.2 %copy-start.3 = (bf16[1024,256]{1,0:T(8,128)(2,1)S(1)}, bf16[1024,256]{1,0:T(8,128)(2,1)}, u32[]{:S(2)}) copy-start(bf16[1024,256]{1,0:T(8,128)(2,1)} %get-tuple-element.118.refs_1_) | copy-start | bytes 1572868
  208.7 11.2 %copy-start.4 = (bf16[1024,256]{1,0:T(8,128)(2,1)S(1)}, bf16[1024,256]{1,0:T(8,128)(2,1)}, u32[]{:S(2)}) copy-start(bf16[1024,256]{1,0:T(8,128)(2,1)} %get-tuple-element.119.refs_2_) | copy-start | bytes 1572868
  224.6 9.5 %collective-permute-start.22 = (bf16[256,2048]{1,0:T(8,128)(2,1)}, bf16[256,2048]{1,0:T(8,128)(2,1)}, u32[]{:S(2)}, u32[]{:S(2)}) collective-permute-start(bf16[256,2048]{1,0:T(8,128)(2,1)} %bwd.8), channel_id=1, source_target_pairs={{0,2},{2,0},{4,6},{6,4},{1,3},{3,1},{5,7},{7,5},{8,10},{10,8},{12,... | collective-permute-start | bytes 3145736 | tf_op jit(solution)/shard_map/ppermute | solution.py:382
  228.4 11.8 %collective-permute-start.23 = (bf16[512,1024]{1,0:T(8,128)(2,1)}, bf16[512,1024]{1,0:T(8,128)(2,1)}, u32[]{:S(2)}, u32[]{:S(2)}) collective-permute-start(bf16[512,1024]{1,0:T(8,128)(2,1)} %bwd.10), channel_id=1, source_target_pairs={{0,2},{2,0},{4,6},{6,4},{1,3},{3,1},{5,7},{7,5},{8,10},{10,8},{12,... | collective-permute-start | bytes 3145736 | tf_op jit(solution)/shard_map/ppermute | solution.py:382
  229.7 14.7 %all-to-all-start.4 = ((bf16[4,256,256]{2,1,0:T(8,128)(2,1)}), bf16[4,256,256]{2,1,0:T(8,128)(2,1)}, u32[]{:S(2)}, u32[]{:S(2)}) async-start(bf16[4,256,256]{2,1,0:T(8,128)(2,1)} %pad_maximum_fusion.5), calls=%async_computation.4 | async-start | bytes 1048576 | tf_op jit(solution)/shard_map/all_to_all | solution.py:385
  250.1 9.9 %collective-permute-start.26 = (bf16[256,2048]{1,0:T(8,128)(2,1)}, bf16[256,2048]{1,0:T(8,128)(2,1)}, u32[]{:S(2)}, u32[]{:S(2)}) collective-permute-start(bf16[256,2048]{1,0:T(8,128)(2,1)} %bwd.12), channel_id=1, source_target_pairs={{0,2},{2,0},{4,6},{6,4},{1,3},{3,1},{5,7},{7,5},{8,10},{10,8},{12,... | collective-permute-start | bytes 3145736 | tf_op jit(solution)/shard_map/ppermute | solution.py:382
  254.0 11.4 %collective-permute-start.27 = (bf16[512,1024]{1,0:T(8,128)(2,1)}, bf16[512,1024]{1,0:T(8,128)(2,1)}, u32[]{:S(2)}, u32[]{:S(2)}) collective-permute-start(bf16[512,1024]{1,0:T(8,128)(2,1)} %bwd.14), channel_id=1, source_target_pairs={{0,2},{2,0},{4,6},{6,4},{1,3},{3,1},{5,7},{7,5},{8,10},{10,8},{12,... | collective-permute-start | bytes 3145736 | tf_op jit(solution)/shard_map/ppermute | solution.py:382
  254.3 25.5 %collective-permute-start.24 = (bf16[256,2048]{1,0:T(8,128)(2,1)}, bf16[256,2048]{1,0:T(8,128)(2,1)S(1)}, u32[]{:S(2)}, u32[]{:S(2)}) collective-permute-start(bf16[256,2048]{1,0:T(8,128)(2,1)} %bwd.9), channel_id=1, source_target_pairs={{0,4},{2,6},{4,0},{6,2},{1,5},{3,7},{5,1},{7,3},{8,12},{10,14},{12... | collective-permute-start | bytes 3145736 | tf_op jit(solution)/shard_map/ppermute | solution.py:501
  256.1 25.1 %collective-permute-start.25 = (bf16[512,1024]{1,0:T(8,128)(2,1)}, bf16[512,1024]{1,0:T(8,128)(2,1)S(1)}, u32[]{:S(2)}, u32[]{:S(2)}) collective-permute-start(bf16[512,1024]{1,0:T(8,128)(2,1)} %bwd.11), channel_id=1, source_target_pairs={{0,1},{1,0},{2,3},{3,2},{4,5},{5,4},{6,7},{7,6},{8,9},{9,8},{10,11... | collective-permute-start | bytes 3145736 | tf_op jit(solution)/shard_map/ppermute | solution.py:502
  265.4 16.3 %copy-start.12 = (f32[256,2048]{1,0:T(8,128)}, f32[256,2048]{1,0:T(8,128)S(1)}, u32[]{:S(2)}) copy-start(f32[256,2048]{1,0:T(8,128)S(1)} %bwd.13.p_ref) | copy-start | bytes 6291460
  269.4 12.5 %copy-start.13 = (f32[512,1024]{1,0:T(8,128)}, f32[512,1024]{1,0:T(8,128)S(1)}, u32[]{:S(2)}) copy-start(f32[512,1024]{1,0:T(8,128)S(1)} %bwd.15.q_ref) | copy-start | bytes 6291460
  279.8 15.0 %copy-start.22 = (bf16[256,2048]{1,0:T(8,128)(2,1)}, bf16[256,2048]{1,0:T(8,128)(2,1)S(1)}, u32[]{:S(2)}) copy-start(bf16[256,2048]{1,0:T(8,128)(2,1)S(1)} %collective-permute-done.24.got_y) | copy-start | bytes 3145732
  281.2 13.6 %copy-start.23 = (bf16[512,1024]{1,0:T(8,128)(2,1)}, bf16[512,1024]{1,0:T(8,128)(2,1)S(1)}, u32[]{:S(2)}) copy-start(bf16[512,1024]{1,0:T(8,128)(2,1)S(1)} %collective-permute-done.25.got_x) | copy-start | bytes 3145732
  281.3 12.9 %collective-permute-start.29 = (bf16[256,1024]{1,0:T(8,128)(2,1)S(1)}, bf16[256,1024]{1,0:T(8,128)(2,1)S(1)}, u32[]{:S(2)}, u32[]{:S(2)}) collective-permute-start(bf16[256,1024]{1,0:T(8,128)(2,1)S(1)} %add_convert_fusion), channel_id=1, source_target_pairs={{0,4},{2,6},{4,0},{6,2},{1,5},{3,7},{5,1},{7,3},{8,12},{10,14},{12... | collective-permute-start | bytes 1572872 | tf_op jit(solution)/shard_map/ppermute | solution.py:514
  281.9 12.9 %collective-permute-start.28 = (bf16[256,1024]{1,0:T(8,128)(2,1)S(1)}, bf16[256,1024]{1,0:T(8,128)(2,1)S(1)}, u32[]{:S(2)}, u32[]{:S(2)}) collective-permute-start(bf16[256,1024]{1,0:T(8,128)(2,1)S(1)} %add_convert_fusion.1), channel_id=1, source_target_pairs={{0,1},{1,0},{2,3},{3,2},{4,5},{5,4},{6,7},{7,6},{8,9},{9,8},{10,11... | collective-permute-start | bytes 1572872 | tf_op jit(solution)/shard_map/ppermute | solution.py:513
  (25 other events, 75.5 us)

commit v4 on v3

--- a/solution.py
+++ b/solution.py
@@ -133,6 +133,7 @@
 
 
 PAIR = 2 * DH
+SLOTS = (0, 2, 1, 3)
 SHORT = pl.CostEstimate(flops=1, bytes_accessed=1, transcendentals=0)
 
 
@@ -147,36 +148,39 @@
 def forward_kernel(n_dp, n_sec, n_half, blk, tab, *refs):
     blocks = n_dp * blk
     x_refs = refs[: n_half * n_dp]
-    own, above, far, below, end, q_ref, g_ref, ctx_ref, dkv_ref, w_ref, acc, kv = refs[
-        n_half * n_dp :
-    ]
-    rows = own.shape[0] // n_dp
+    own, above, far, below, end = refs[n_half * n_dp : n_half * n_dp + 5]
+    q_ref, g_ref = refs[n_half * n_dp + 5 : n_half * n_dp + 7]
+    ctx_ref, dkv_ref, w_ref, acc, kv = refs[-5:]
+    rows = acc.shape[0] // n_dp
     step = pl.program_id(0)
+    per_half = n_sec // n_half
     z = tab[2 * blocks]
     m = tab[2 * blocks + 1]
-    per_half = n_sec // n_half
     section = (m ^ (step // per_half)) * per_half + step % per_half
     hop = (section - z + n_sec) % n_sec
 
+    def take(ref):
+        w_ref[...] = ref[...].reshape(w_ref.shape)
+
     @pl.when(hop == 0)
     def _():
-        w_ref[...] = own[...]
+        take(own)
 
     @pl.when((hop == 1) & (z != n_sec - 1))
     def _():
-        w_ref[...] = above[...]
+        take(above)
 
     @pl.when(hop == 2)
     def _():
-        w_ref[...] = far[...]
+        take(far)
 
     @pl.when((hop == n_sec - 1) & (z != 0))
     def _():
-        w_ref[...] = below[...]
+        take(below)
 
     @pl.when(((hop == 1) & (z == n_sec - 1)) | ((hop == n_sec - 1) & (z == 0)))
     def _():
-        w_ref[...] = end[...]
+        take(end)
 
     for h in range(n_half):
 
@@ -185,7 +189,7 @@
             for t in range(n_dp):
                 at = slice(t * rows, (t + 1) * rows)
                 part = jnp.dot(
-                    x_refs[h * n_dp + t][...], w_ref[...], preferred_element_type=F32
+                    x_refs[h * n_dp + t][0], w_ref[...], preferred_element_type=F32
                 )
                 if h == 0:
                     acc[at, :] = jnp.where(step == 0, part, acc[at, :] + part)
@@ -239,35 +243,46 @@
             group(range(b, b + blk))
 
 
-def forward_chunk(table, x_pieces, pieces, q_at, g_at, blk, n_sec, n_dp):
-    n_half = len(x_pieces) // n_dp
-    cols = pieces[0].shape[1]
-    rows = pieces[0].shape[0] // n_dp
+def forward_chunk(table, x, pieces, got, chunk, chunks, blk, n_sec, n_dp, before):
+    n_half = x.shape[0] // n_dp
+    cols = 2 * PAIR
     per_half = n_sec // n_half
-    span = x_pieces[0][0].shape[1] // per_half
-
-    def x_spec(h, row):
-        return pl.BlockSpec(
-            (rows, span), lambda a, t: (row, jnp.clip(a - h * per_half, 0, per_half - 1))
-        )
-
-    whole = pl.BlockSpec((span, cols), lambda a, t: (0, 0))
+    span = x.shape[2] // per_half
+    rows = span // n_dp
+    scalars = 2 * n_dp * blk
+
+    def x_spec(h, slot):
+        def at(a, t):
+            sender = (t[scalars + 2] ^ slot) * n_half + (t[scalars + 1] ^ h)
+            return (sender, 0, jnp.clip(a - h * per_half, 0, per_half - 1))
+
+        return pl.BlockSpec((1, rows, span), at)
+
+    def fixed(shape, at):
+        return pl.BlockSpec(shape, lambda a, t: at)
 
     def head(at):
         return pl.BlockSpec((n_dp, rows, PAIR), lambda a, t: (0, 0, at))
 
+    operands = [table] + [x] * (n_half * n_dp) + [p[0] for p in pieces] + [got, got]
+    in_specs = [x_spec(h, slot) for h in range(n_half) for slot in SLOTS]
+    in_specs += [fixed(shape, at) for _, shape, at in pieces]
+    in_specs += [head(chunk), head(chunks + chunk)]
+    aliases = {}
+    if before is not None:
+        aliases = {len(operands): 1, len(operands) + 1: 2}
+        operands += before
+        in_specs += [pl.BlockSpec(memory_space=pl.ANY)] * 2
     return pl.pallas_call(
         functools.partial(forward_kernel, n_dp, n_sec, n_half, blk),
         grid_spec=pltpu.PrefetchScalarGridSpec(
             num_scalar_prefetch=1,
             grid=(n_sec,),
-            in_specs=[x_spec(i // n_dp, row) for i, (_, row) in enumerate(x_pieces)]
-            + [whole] * 5
-            + [head(q_at[1]), head(g_at[1])],
+            in_specs=in_specs,
             out_specs=[
                 head(0),
-                pl.BlockSpec((n_dp * rows, cols), lambda a, t: (0, 0)),
-                pl.BlockSpec((span, cols), lambda a, t: (a, 0)),
+                pl.BlockSpec((n_dp * rows, cols), lambda a, t: (0, chunk)),
+                pl.BlockSpec((span, cols), lambda a, t: (a, chunk)),
             ],
             scratch_shapes=[
                 pltpu.VMEM((n_dp * rows, cols), F32),
@@ -276,42 +291,57 @@
         ),
         out_shape=[
             jax.ShapeDtypeStruct((n_dp, rows, PAIR), BF16),
-            jax.ShapeDtypeStruct((n_dp * rows, cols), BF16),
-            jax.ShapeDtypeStruct((n_sec * span, cols), BF16),
+            jax.ShapeDtypeStruct((n_dp * rows, chunks * cols), BF16),
+            jax.ShapeDtypeStruct((n_sec * span, chunks * cols), BF16),
         ],
+        input_output_aliases=aliases,
         compiler_params=pltpu.CompilerParams(vmem_limit_bytes=60 << 20),
         cost_estimate=SHORT,
         name="fwd",
-    )(table, *[x for x, _ in x_pieces], *pieces, q_at[0], g_at[0])
-
-
-def backward_kernel(chunks, add, *refs):
-    out_ref = refs[-1]
-    total = nt(refs[0][...], refs[chunks][...])
-    for c in range(1, chunks):
-        total += nt(refs[c][...], refs[chunks + c][...])
-    if add:
-        total += refs[2 * chunks][...].astype(F32)
-    out_ref[...] = total.astype(out_ref.dtype)
-
-
-def backward(dkvs, ws, rows, span, row_at, row_n, col_at, col_n, received, out_dtype):
-    chunks = len(dkvs)
-    cols = dkvs[0].shape[1]
-    specs = [pl.BlockSpec((rows, cols), lambda h, r: (row_at + 2 * r, 0))] * chunks
-    specs += [pl.BlockSpec((span, cols), lambda h, r: (col_at + 2 * h, 0))] * chunks
-    block = pl.BlockSpec((rows, span), lambda h, r: (r, h))
-    extra = () if received is None else (received,)
+    )(*operands)
+
+
+def backward_kernel(*refs):
+    total = nt(refs[0][...], refs[1][...])
+    for ref in refs[2:-1]:
+        total += ref[...].astype(F32)
+    refs[-1][...] = total.astype(refs[-1].dtype)
+
+
+def backward(dkv, w, received, rows, cols, out_dtype):
+    row_n, row_at = rows
+    span, blocks = cols
+    depth = dkv.shape[1]
+    tile = 512
+    per_block = span // tile
+
+    def col(i):
+        at = blocks[0]
+        for k in range(1, len(blocks)):
+            at = jnp.where(i >= k * per_block, blocks[k], at)
+        return at * per_block + i % per_block
+
+    specs = [
+        pl.BlockSpec((row_n, depth), lambda i: (row_at, 0)),
+        pl.BlockSpec((tile, depth), lambda i: (col(i), 0)),
+    ]
+    extra = ()
+    if received is not None:
+        array, add_row, add_col = received
+        specs.append(
+            pl.BlockSpec((row_n, tile), lambda i: (add_row, add_col * per_block + i))
+        )
+        extra = (array,)
     return pl.pallas_call(
-        functools.partial(backward_kernel, chunks, received is not None),
-        grid=(col_n, row_n),
-        in_specs=specs + [block] * len(extra),
-        out_specs=block,
-        out_shape=jax.ShapeDtypeStruct((row_n * rows, col_n * span), out_dtype),
-        compiler_params=pltpu.CompilerParams(vmem_limit_bytes=48 << 20),
+        backward_kernel,
+        grid=(len(blocks) * per_block,),
+        in_specs=specs,
+        out_specs=pl.BlockSpec((row_n, tile), lambda i: (0, i)),
+        out_shape=jax.ShapeDtypeStruct((row_n, len(blocks) * span), out_dtype),
+        compiler_params=pltpu.CompilerParams(vmem_limit_bytes=60 << 20),
         cost_estimate=SHORT,
         name="bwd",
-    )(*dkvs, *ws, *extra)
+    )(dkv, w, *extra)
 
 
 def finish_kernel(p_ref, got_y, last_x, q_ref, got_x, last_y, out):
@@ -326,36 +356,96 @@
 
 def finish(*operands):
     rows, span = operands[2].shape
-    block = pl.BlockSpec((rows, span), lambda i: (0, 0))
+    tiles = 2
+    block = pl.BlockSpec((rows // tiles, span), lambda i: (i, 0))
     return pl.pallas_call(
         finish_kernel,
-        grid=(1,),
+        grid=(tiles,),
         in_specs=[block] * 6,
-        out_specs=pl.BlockSpec((rows, 2 * span), lambda i: (0, 0)),
+        out_specs=pl.BlockSpec((rows // tiles, 2 * span), lambda i: (i, 0)),
         out_shape=jax.ShapeDtypeStruct((rows, 2 * span), BF16),
+        cost_estimate=SHORT,
         name="finish",
     )(*operands)
 
 
-def context_kernel(*refs):
+def weight_kernel(k_ref, v_ref, out):
+    out[0, :, :PAIR] = k_ref[...]
+    out[0, :, PAIR:] = v_ref[...]
+
+
+def pack_weights(w_key, w_value, chunk, n_dp):
+    rows, width = w_key.shape
+    per_owner = width // n_dp // PAIR
+    block = pl.BlockSpec((rows, PAIR), lambda j: (0, j * per_owner + chunk))
+    return pl.pallas_call(
+        weight_kernel,
+        grid=(n_dp,),
+        in_specs=[block] * 2,
+        out_specs=pl.BlockSpec((1, rows, 2 * PAIR), lambda j: (j, 0, 0)),
+        out_shape=jax.ShapeDtypeStruct((n_dp, rows, 2 * PAIR), BF16),
+        cost_estimate=SHORT,
+        name="pack_weights",
+    )(w_key, w_value)
+
+
+def pack_kernel(q_ref, g_ref, k_ref, v_ref, small_ref, out):
+    rows, cols = q_ref.shape
+    parts = [q_ref[...], g_ref[...]]
+    for c in range(0, k_ref.shape[1], PAIR):
+        parts += [k_ref[:, c : c + PAIR], v_ref[:, c : c + PAIR]]
+    at = 0
+    for part in parts:
+        out[0, :rows, at : at + part.shape[1]] = part
+        at += part.shape[1]
+    out[0, rows:, :] = jnp.zeros((out.shape[1] - rows, out.shape[2]), BF16)
+    out[0, rows:, :PAIR] = small_ref[...]
+
+
+def pack(queries, grads, w_key, w_value, small, n_dp):
+    rows, width = queries.shape
+    cols = width // n_dp
+    block = pl.BlockSpec((rows, cols), lambda j: (0, j))
+    tail = pl.BlockSpec((rows, cols // 2), lambda j: (0, 2 * j + 1))
+    extra = small.shape[0]
+    return pl.pallas_call(
+        pack_kernel,
+        grid=(n_dp,),
+        in_specs=[block, block, tail, tail, pl.BlockSpec(small.shape, lambda j: (0, 0))],
+        out_specs=pl.BlockSpec((1, rows + extra, 3 * cols), lambda j: (j, 0, 0)),
+        out_shape=jax.ShapeDtypeStruct((n_dp, rows + extra, 3 * cols), BF16),
+        cost_estimate=SHORT,
+        name="pack",
+    )(queries, grads, w_key, w_value, small)
+
+
+def context_kernel(n_dp, tab, early, *refs):
     out = refs[-1]
-    at = 0
-    for ref in refs[:-1]:
-        out[:, at : at + ref.shape[2]] = ref[0]
-        at += ref.shape[2]
-
-
-def gather_context(*parts):
-    n_dp, rows = parts[0].shape[:2]
-    cols = sum(part.shape[2] for part in parts)
+    cols = early.shape[2]
+    out[:, :cols] = early[0]
+    for t in range(n_dp):
+
+        @pl.when(pl.program_id(0) == t)
+        def _():
+            out[:, cols:] = refs[t][...]
+
+
+def gather_context(d, early, late):
+    n_dp, rows, cols = early.shape
+    last = late[0].shape[1]
     return pl.pallas_call(
-        context_kernel,
-        grid=(n_dp,),
-        in_specs=[pl.BlockSpec((1, rows, part.shape[2]), lambda j: (j, 0, 0)) for part in parts],
-        out_specs=pl.BlockSpec((rows, cols), lambda j: (0, j)),
-        out_shape=jax.ShapeDtypeStruct((rows, n_dp * cols), BF16),
+        functools.partial(context_kernel, n_dp),
+        grid_spec=pltpu.PrefetchScalarGridSpec(
+            num_scalar_prefetch=1,
+            grid=(n_dp,),
+            in_specs=[pl.BlockSpec((1, rows, cols), lambda t, tab: (tab[0] ^ t, 0, 0))]
+            + [pl.BlockSpec((rows, last), lambda t, tab: (0, 0))] * n_dp,
+            out_specs=pl.BlockSpec((rows, cols + last), lambda t, tab: (0, tab[0] ^ t)),
+        ),
+        out_shape=jax.ShapeDtypeStruct((rows, n_dp * (cols + last)), BF16),
+        cost_estimate=SHORT,
         name="gather_context",
-    )(*parts)
+    )(d.reshape(1), early, *late)
 
 
 def shards_section(enc_rows, enc_len, dest_dp, peer_counts, queries, ctx_grad, w_key, w_value):
@@ -375,8 +465,14 @@
     ends = [(1, 0), (2, 3)]
     outer = [(0, n_sec - 1), (n_sec - 1, 0)]
 
-    def step(waited, released=()):
-        return lax.optimization_barrier((tuple(waited), tuple(released)))
+    def step(*waited, released=()):
+        done = ()
+        for group in waited:
+            done = done + (tuple(group),)
+            if group is not waited[-1]:
+                done = lax.optimization_barrier(done)
+        done, released = lax.optimization_barrier((done, tuple(released)))
+        return (*done, released)
 
     def swap(x):
         return lax.ppermute(x, "dp", core)
@@ -384,55 +480,38 @@
     def exchange(x):
         return lax.all_to_all(x, "dp", split_axis=0, concat_axis=0, tiled=True)
 
-    def by_owner(x):
-        return x.reshape(rows, n_dp, head_cols).transpose(1, 0, 2)
-
-    def weight_parts(c, *ws):
-        return jnp.concatenate([by_owner(w)[:, :, c * PAIR : (c + 1) * PAIR] for w in ws], axis=2)
-
-    def along(piece):
-        return (
-            lax.ppermute(piece, "section", up),
-            lax.ppermute(piece, "section", down),
-            lax.ppermute(piece, "section", over_two),
-        )
-
-    own0 = exchange(weight_parts(0, w_key, w_value)).reshape(n_dp * rows, 2 * PAIR)
-    e_x = lax.ppermute(enc_rows, "mp", xpairs)
-    e_c = swap(enc_rows)
-
-    (own0, e_c), (e, w_k, w_v, q_in, g_in) = step(
-        (own0, e_c), (enc_rows, w_key, w_value, queries, ctx_grad)
-    )
-    z0 = along(own0)
-    e_y = lax.ppermute(e, "dp", ypairs)
-    own1 = exchange(weight_parts(1, w_k, w_v)).reshape(n_dp * rows, 2 * PAIR)
-    parts = jnp.concatenate(
-        [by_owner(q_in), by_owner(g_in), weight_parts(2, w_k, w_v), weight_parts(3, w_k, w_v)],
-        axis=2,
-    )
+    def sides(piece):
+        return lax.ppermute(piece, "section", up), lax.ppermute(piece, "section", down)
+
+    def beyond(piece):
+        return lax.ppermute(piece, "section", over_two)
+
+    def turn(far):
+        return lax.ppermute(far, "section", ends)
+
+    def flat(x):
+        return x.reshape(n_dp * rows, 2 * PAIR)
+
+    own0 = flat(exchange(pack_weights(w_key, w_value, 0, n_dp)))
+    x = lax.all_gather(enc_rows, ("dp", "mp"), axis=0, tiled=False)
     small = jnp.concatenate([enc_len, dest_dp, peer_counts[0]]).astype(BF16)
-    small = jnp.pad(small[None, :], ((0, 15), (0, parts.shape[2] - small.shape[0])))
-    small = jnp.broadcast_to(small[None], (n_dp,) + small.shape)
-    parts = jnp.concatenate([parts, small], axis=1)
-
-    (z0, own1, e_y, e_x, parts), _ = step((z0, own1, e_y, e_x, parts))
-    end0 = lax.ppermute(z0[2], "section", ends)
-    z1 = along(own1)
-    e_yx = lax.ppermute(e_y, "mp", xpairs)
+    small = jnp.pad(small[None, :], ((0, 15), (0, PAIR - small.shape[0])))
+
+    (own0,), (w_k, w_v) = step((own0,), released=(w_key, w_value))
+    near0, far0 = sides(own0), beyond(own0)
+    own1 = flat(exchange(pack_weights(w_k, w_v, 1, n_dp)))
+    parts = pack(queries, ctx_grad, w_k, w_v, small, n_dp)
+
+    (far0,), near0, (own1, parts), _ = step((far0,), near0, (own1, parts))
+    near1, far1, end0 = sides(own1), beyond(own1), turn(far0)
     got = exchange(parts)
-    e_xy = jnp.concatenate([e_x, e_y], axis=0)
-
-    (end0, z1, e_yx, e_xy, got), _ = step((end0, z1, e_yx, e_xy, got))
+
+    (end0,), (far1,), near1, (x, got), _ = step((end0,), (far1,), near1, (x, got))
     own2, own3 = (
-        got[:, :rows, 2 * head_cols + 2 * PAIR * i : 2 * head_cols + 2 * PAIR * (i + 1)].reshape(
-            n_dp * rows, 2 * PAIR
-        )
+        flat(got[:, :rows, 2 * head_cols + 2 * PAIR * i : 2 * head_cols + 2 * PAIR * (i + 1)])
         for i in range(2)
     )
-    end1 = lax.ppermute(z1[2], "section", ends)
-    z2 = along(own2)
-    e_xyc, e_yxc = swap(e_xy), swap(e_yx)
+    near2, far2, end1 = sides(own2), beyond(own2), turn(far1)
 
     packs = got[:, rows, : 2 * blk + n_dp].astype(jnp.int32)
     lens = packs[:, :blk].reshape(-1)
@@ -454,57 +533,59 @@
         & (dest[None, None] == peer[:, None, None, None])
         & (slot_rank[None, None] == rank[:, :, None, None])
     ).reshape(blocks, blocks)
-    place = ((peer ^ d)[:, None] * blk + pos[None, :]).reshape(-1)
+    gap = peer ^ d
+    gap = jnp.where(gap == 1, 2, jnp.where(gap == 2, 1, gap))
+    place = (gap[:, None] * blk + pos[None, :]).reshape(-1)
     src = jnp.sum(jnp.where(hit, place[None, :], 0), axis=1)
     src_len = jnp.sum(jnp.where(hit, lens[None, :], 0), axis=1)
-    table = jnp.concatenate([src, src_len, jnp.stack([z, m])])
-
-    x_pieces = [(e, 0), (e_c, 0), (e_y, 0), (e_xyc, 1)]
-    x_pieces += [(e_x, 0), (e_xyc, 0), (e_yx, 0), (e_yxc, 0)]
-    q_blocks = head_cols // PAIR
-
-    def forward(c, own, zs, end):
-        up_, down_, far = zs
+    table = jnp.concatenate([src, src_len, jnp.stack([z, m, d])])
+
+    chunks = head_cols // PAIR
+
+    def forward(c, own, near, far, end, before):
+        pieces = [(x, x.shape, (0, 0)) for x in (own, near[1], far, near[0], end)]
         return forward_chunk(
-            table,
-            x_pieces,
-            (own, down_, far, up_, end),
-            (got, c),
-            (got, q_blocks + c),
-            blk,
-            n_sec,
-            n_dp,
+            table, x, pieces, got, c, chunks, blk, n_sec, n_dp, before
         )
 
-    f0 = forward(0, own0, z0, end0)
-
-    (end1, z2, own3, f0), _ = step((end1, z2, own3, f0))
-    end2 = lax.ppermute(z2[2], "section", ends)
-    z3 = along(own3)
+    f0 = forward(0, own0, near0, far0, end0, None)
+
+    (end1,), (far2,), near2, (own3, f0), _ = step((end1,), (far2,), near2, (own3, f0))
+    near3, far3, end2 = sides(own3), beyond(own3), turn(far2)
     end3 = lax.ppermute(own3, "section", outer)
-    f1 = forward(1, own1, z1, end1)
+    f1 = forward(1, own1, near1, far1, end1, f0[1:])
     context_a = exchange(jnp.concatenate([f0[0], f1[0]], axis=2))
-    f2 = forward(2, own2, z2, end2)
-
-    (z3, end3, f1, f2, context_a), _ = step((z3, end3, f1, f2, context_a))
-    f3 = forward(3, own3, z3, end3)
-    context_b = exchange(jnp.concatenate([f2[0], f3[0]], axis=2))
-
-    dkvs = tuple(f[1] for f in (f0, f1, f2, f3))
-    ws = tuple(f[2] for f in (f0, f1, f2, f3))
-    span = half // (n_sec // n_mp)
-    give_y = swap(backward(dkvs, ws, rows, span, 3, 1, 0, 2, None, BF16))
-    give_x = swap(backward(dkvs, ws, rows, span, 1, 2, 3, 1, None, BF16))
-    send_y = backward(dkvs, ws, rows, span, 2, 1, 0, 2, give_y, BF16)
-    send_x = backward(dkvs, ws, rows, span, 0, 2, 3, 1, give_x, BF16)
-    (send_y, send_x, context_b), dkvs = step((send_y, send_x, context_b), dkvs)
+    f2 = forward(2, own2, near2, far2, end2, f1[1:])
+
+    (end3, far3), near3, (f2, context_a), _ = step((end3, far3), near3, (f2, context_a))
+    f3 = forward(3, own3, near3, far3, end3, f2[1:])
+
+    late = []
+    for t in range(n_dp):
+        part = jnp.concatenate(
+            [lax.dynamic_slice(f[0], (d ^ t, 0, 0), (1, rows, PAIR))[0] for f in (f2, f3)], axis=1
+        )
+        late.append(
+            part if t == 0 else lax.ppermute(part, "dp", [(i, i ^ t) for i in range(n_dp)])
+        )
+
+    per_half = n_sec // n_mp
+    span = half // per_half
+    _, dkv, w = f3
+    p_cols, q_own_cols, q_far_cols = (0, per_half), (1,), (per_half + 1,)
+    pair = (2 * rows, 0)
+    give_p = swap(backward(dkv, w, None, (2 * rows, 1), (span, p_cols), BF16))
+    give_q = swap(backward(dkv, w, None, (2 * rows, 1), (span, q_far_cols + q_own_cols), BF16))
+    send_y = backward(dkv, w, (give_p, 1, 0), (rows, 1), (span, p_cols), BF16)
+    send_x = backward(dkv, w, (give_q, 0, 0), pair, (span, q_far_cols), BF16)
+    send_y, send_x, late, dkv_, w_ = lax.optimization_barrier(
+        (send_y, send_x, tuple(late), dkv, w)
+    )
     got_y = lax.ppermute(send_y, "dp", ypairs)
     got_x = lax.ppermute(send_x, "mp", xpairs)
-    give_p = swap(backward(dkvs, ws, rows, span, 1, 1, 0, 2, None, BF16))
-    give_q = swap(backward(dkvs, ws, rows, span, 1, 2, 1, 1, None, BF16))
-    p_own = backward(dkvs, ws, rows, span, 0, 1, 0, 2, give_p, F32)
-    q_own = backward(dkvs, ws, rows, span, 0, 2, 1, 1, give_q, F32)
-    context = gather_context(context_a, context_b)
+    p_own = backward(dkv_, w_, (give_p, 0, 0), (rows, 0), (span, p_cols), F32)
+    q_own = backward(dkv_, w_, (give_q, 0, 1), pair, (span, q_own_cols), F32)
+    context = gather_context(d, context_a, late)
     got_y, got_x, p_own, q_own, context = lax.optimization_barrier(
         (got_y, got_x, p_own, q_own, context)
     )

time: 304 us -> 292 us (0.961)
  local copies, waits for them, and re-layouts: 36.9 us -> 6.85 us
  blocking collectives: 0 us -> 13.9 us
  between operations: 1.27 us -> 14.5 us
  Pallas kernels: 80.7 us -> 92.9 us
  starting transfers between devices: 75.1 us -> 63.9 us
  other arithmetic: 14.2 us -> 6.36 us
    ppermute x18, waiting for transfers between devices: 45.5 us -> 64.6 us  [the longest x3 23.5 us: turn(): return lax.ppermute(far, 'section', ends)]
    all_to_all x5 -> x3, waiting for transfers between devices: 19.3 us -> 2.66 us  [exchange(): return lax.all_to_all(x, 'dp', split_axis=0, concat_axis=0, tiled=True)]
    all_to_all x0 -> x1, blocking collectives: none -> 13.9 us  [exchange(): return lax.all_to_all(x, 'dp', split_axis=0, concat_axis=0, tiled=True)]
    unnamed x81 -> x54, local copies, waits for them, and re-layouts: 18.4 us -> 4.74 us
    pallas_call x10 -> x11, Pallas kernels: 37 us -> 48.9 us  [the longest x6 31.5 us: backward(): pl.pallas_call(backward_kernel, grid=(len(blocks) * per_block,), in_specs...]
    concatenate x6 -> x4, other arithmetic: 10.3 us -> 0.72 us  [shards_section(): jnp.concatenate([lax.dynamic_slice(f[0], (d ^ t, 0, 0), (1, rows, PAIR))[...]
    all_to_all x5 -> x3, starting transfers between devices: 19.8 us -> 10.8 us  [exchange(): return lax.all_to_all(x, 'dp', split_axis=0, concat_axis=0, tiled=True)]
    reshape x6 -> x0, local copies, waits for them, and re-layouts: 8.61 us -> none  [by_owner(): return x.reshape(rows, n_dp, head_cols).transpose(1, 0, 2)]
  transfers between devices with their start and end apart: 35 -> 29, of which waited for: 11 -> 13; matrix products, arithmetic and copies ran while one was open for 13% -> 2% of each run, Pallas kernels for 20% -> 25%
where the time goes in v4:
time: 292 us; the launch traced here: 288 us
  Pallas kernels  92.9 us (32%)
  waiting for transfers between devices  89.7 us (31%)
  starting transfers between devices  63.9 us (22%)
  between operations  14.5 us (5%)
  blocking collectives  13.9 us (5%)
  local copies, waits for them, and re-layouts  6.85 us (2%)
  other arithmetic  6.36 us (2%)
    pallas_call x4, Pallas kernels, forward_chunk(): pl.pallas_call(functools.partial(forward_kernel, n_dp, n_sec, n_half, blk...  44 us
    pallas_call x6, Pallas kernels, backward(): pl.pallas_call(backward_kernel, grid=(len(blocks) * per_block,), in_specs...  31.5 us
    ppermute x3, waiting for transfers between devices, turn(): return lax.ppermute(far, 'section', ends)  23.5 us
    ppermute x4, waiting for transfers between devices, beyond(): return lax.ppermute(piece, 'section', over_two)  22.1 us
    ppermute x4, waiting for transfers between devices, sides(): lax.ppermute(piece, 'section', down)  19 us
    ppermute x4, starting transfers between devices, beyond(): return lax.ppermute(piece, 'section', over_two)  15.7 us
    all_to_all x1, blocking collectives, exchange(): return lax.all_to_all(x, 'dp', split_axis=0, concat_axis=0, tiled=True)  13.9 us
    ppermute x4, starting transfers between devices, sides(): lax.ppermute(piece, 'section', up)  13.6 us
  transfers between devices with their start and end apart: 29, of which 13 were waited for; matrix products, arithmetic and copies ran while one was open for 2% of the time, Pallas kernels for 25%

profile of v4, /device:TPU:0, one launch (start us, length us, event | category | flops | bytes accessed | tf_op | source)
XLA Modules:
  0.0 288.0 jit_solution(1963458115795662209)
XLA Ops:
  7.9 3.1 %pack_weights.2 = bf16[4,256,256]{2,1,0:T(8,128)(2,1)} custom-call(bf16[256,2048]{1,0:T(8,128)(2,1)} %k_ref.3, bf16[256,2048]{1,0:T(8,128)(2,1)} %v_ref.3), custom_call_target="tpu_custom_call" | custom-call | flops 1 | bytes 1 | tf_op jit(solution)/shard_map/pack_weights/pallas_call | solution.py:381
  11.0 13.9 %all_to_all.20 = bf16[4,256,256]{2,1,0:T(8,128)(2,1)S(1)} all-to-all(bf16[4,256,256]{2,1,0:T(8,128)(2,1)} %pack_weights.2), channel_id=1, replica_groups=mesh['section'=4,'dp'=4,'mp'=2] {'dp'}, dimensions={0} | all-to-all | bytes 1048576 | tf_op jit(solution)/shard_map/all_to_all | solution.py:481
  24.9 4.1 %collective-permute-start = (bf16[1024,256]{1,0:T(8,128)(2,1)S(1)}, bf16[1024,256]{1,0:T(8,128)(2,1)S(1)}, u32[]{:S(2)}, u32[]{:S(2)}) collective-permute-start(bf16[1024,256]{1,0:T(8,128)(2,1)S(1)} %bitcast.65), channel_id=1, source_target_pairs={{0,16},{8,24},{16,0},{24,8},{1,17},{9,25},{17,1},{25,9},{2,18},{10... | collective-permute-start | bytes 1572872 | tf_op jit(solution)/shard_map/ppermute | solution.py:487
  29.1 3.6 %collective-permute-start.1 = (bf16[1024,256]{1,0:T(8,128)(2,1)S(1)}, bf16[1024,256]{1,0:T(8,128)(2,1)S(1)}, u32[]{:S(2)}, u32[]{:S(2)}) collective-permute-start(bf16[1024,256]{1,0:T(8,128)(2,1)S(1)} %bitcast.66), channel_id=1, source_target_pairs={{0,8},{8,16},{16,24},{1,9},{9,17},{17,25},{2,10},{10,18},{18,26},{... | collective-permute-start | bytes 1572872 | tf_op jit(solution)/shard_map/ppermute | solution.py:484
  32.7 1.3 collective-permute-start.2
  34.0 3.1 %pack_weights.3 = bf16[4,256,256]{2,1,0:T(8,128)(2,1)} custom-call(bf16[256,2048]{1,0:T(8,128)(2,1)} %k_ref.3, bf16[256,2048]{1,0:T(8,128)(2,1)} %v_ref.3), custom_call_target="tpu_custom_call" | custom-call | flops 1 | bytes 1 | tf_op jit(solution)/shard_map/pack_weights/pallas_call | solution.py:381
  37.1 3.5 %all-to-all-start.1 = ((bf16[4,256,256]{2,1,0:T(8,128)(2,1)}), bf16[4,256,256]{2,1,0:T(8,128)(2,1)S(1)}, u32[]{:S(2)}, u32[]{:S(2)}) async-start(bf16[4,256,256]{2,1,0:T(8,128)(2,1)} %pack_weights.3), calls=%async_computation.1 | async-start | bytes 1048576 | tf_op jit(solution)/shard_map/all_to_all | solution.py:481
  41.3 4.5 %pack.1 = bf16[4,272,1536]{2,1,0:T(8,128)(2,1)} custom-call(bf16[256,2048]{1,0:T(8,128)(2,1)} %q_ref.1, bf16[256,2048]{1,0:T(8,128)(2,1)} %g_ref.1, bf16[256,2048]{1,0:T(8,128)(2,1)} %k_ref.3, bf16[256,2048]{1,0:T(8,128)(2,1)} %v_ref.3, bf16[16,128]{1,0:T(8,128)(2,1)} %fusion.8.small_ref), custom_call_target="tpu_custom_call" | custom-call | flops 1 | bytes 1 | tf_op jit(solution)/shard_map/pack/pallas_call | solution.py:411
  45.8 7.1 %collective-permute-done.refs_10_ = bf16[1024,256]{1,0:T(8,128)(2,1)S(1)} collective-permute-done((bf16[1024,256]{1,0:T(8,128)(2,1)S(1)}, bf16[1024,256]{1,0:T(8,128)(2,1)S(1)}, u32[]{:S(2)}, u32[]{:S(2)}) %collective-permute-start) | collective-permute-done | bytes 524320 | tf_op jit(solution)/shard_map/ppermute | solution.py:487
  52.9 4.1 %collective-permute-done.2.refs_9_ = bf16[1024,256]{1,0:T(8,128)(2,1)S(1)} collective-permute-done((bf16[1024,256]{1,0:T(8,128)(2,1)S(1)}, bf16[1024,256]{1,0:T(8,128)(2,1)S(1)}, u32[]{:S(2)}, u32[]{:S(2)}) %collective-permute-start.2) | collective-permute-done | bytes 524320 | tf_op jit(solution)/shard_map/ppermute | solution.py:484
  58.0 3.7 %all-to-all-start.2 = ((bf16[4,272,1536]{2,1,0:T(8,128)(2,1)}), bf16[4,272,1536]{2,1,0:T(8,128)(2,1)S(1)}, u32[]{:S(2)}, u32[]{:S(2)}) async-start(bf16[4,272,1536]{2,1,0:T(8,128)(2,1)} %pack.1), calls=%async_computation.2 | async-start | bytes 6684672 | tf_op jit(solution)/shard_map/all_to_all | solution.py:481
  61.7 1.3 collective-permute-start.3
  63.0 9.4 %collective-permute-start.4 = (bf16[1024,256]{1,0:T(8,128)(2,1)}, bf16[1024,256]{1,0:T(8,128)(2,1)}, u32[]{:S(2)}, u32[]{:S(2)}) collective-permute-start(bf16[1024,256]{1,0:T(8,128)(2,1)} %bitcast.61), channel_id=1, source_target_pairs={{0,16},{8,24},{16,0},{24,8},{1,17},{9,25},{17,1},{25,9},{2,18},{10... | collective-permute-start | bytes 1572872 | tf_op jit(solution)/shard_map/ppermute | solution.py:487
  72.5 2.1 collective-permute-start.5
  75.9 7.1 %collective-permute-done.3.refs_12_ = bf16[1024,256]{1,0:T(8,128)(2,1)} collective-permute-done((bf16[1024,256]{1,0:T(8,128)(2,1)}, bf16[1024,256]{1,0:T(8,128)(2,1)}, u32[]{:S(2)}, u32[]{:S(2)}) %collective-permute-start.3) | collective-permute-done | bytes 524320 | tf_op jit(solution)/shard_map/ppermute | solution.py:490
  83.0 13.8 %collective-permute-done.4.refs_10_ = bf16[1024,256]{1,0:T(8,128)(2,1)} collective-permute-done((bf16[1024,256]{1,0:T(8,128)(2,1)}, bf16[1024,256]{1,0:T(8,128)(2,1)}, u32[]{:S(2)}, u32[]{:S(2)}) %collective-permute-start.4) | collective-permute-done | bytes 524320 | tf_op jit(solution)/shard_map/ppermute | solution.py:487
  96.8 8.2 %collective-permute-done.6.refs_9_ = bf16[1024,256]{1,0:T(8,128)(2,1)} collective-permute-done((bf16[1024,256]{1,0:T(8,128)(2,1)}, bf16[1024,256]{1,0:T(8,128)(2,1)}, u32[]{:S(2)}, u32[]{:S(2)}) %collective-permute-start.6) | collective-permute-done | bytes 524320 | tf_op jit(solution)/shard_map/ppermute | solution.py:484
  105.0 2.7 all-to-all-done.2.refs_13_.refs_14_
  109.8 2.1 collective-permute-start.8
  113.1 5.4 %collective-permute-start.9 = (bf16[1024,256]{1,0:T(8,128)(2,1)}, bf16[1024,256]{1,0:T(8,128)(2,1)}, u32[]{:S(2)}, u32[]{:S(2)}) collective-permute-start(bf16[1024,256]{1,0:T(8,128)(2,1)} %bitcast.9.refs_8_), channel_id=1, source_target_pairs={{0,8},{8,16},{16,24},{1,9},{9,17},{17,25},{2,10},{10,18},{18,26},{... | collective-permute-start | bytes 1572872 | tf_op jit(solution)/shard_map/ppermute | solution.py:484
  121.4 11.0 %fwd.4 = (bf16[4,256,128]{2,1,0:T(8,128)(2,1)}, bf16[1024,1024]{1,0:T(8,128)(2,1)}, bf16[4096,1024]{1,0:T(8,128)(2,1)}) custom-call(s32[35]{0:T(128)} %concatenate.36.tab, bf16[8,256,2048]{2,1,0:T(8,128)(2,1)} %bitcast.29, bf16[8,256,2048]{2,1,0:T(8,128)(2,1)} %bitcast.30, bf16[8,256,2048]{2,1,0:T(8,128)(2,1)} %bitcast.31, bf16[8,256,2048]{2,1,0:T(8,128)(2,1)} %bitcast.32, ...), custom_call_target="tpu_custom_call" | custom-call | flops 1 | bytes 1 | tf_op jit(solution)/shard_map/fwd/pallas_call | solution.py:276
  132.4 16.3 %collective-permute-done.7.refs_12_ = bf16[1024,256]{1,0:T(8,128)(2,1)} collective-permute-done((bf16[1024,256]{1,0:T(8,128)(2,1)}, bf16[1024,256]{1,0:T(8,128)(2,1)}, u32[]{:S(2)}, u32[]{:S(2)}) %collective-permute-start.7) | collective-permute-done | bytes 524320 | tf_op jit(solution)/shard_map/ppermute | solution.py:490
  148.8 1.4 collective-permute-start.15
  150.2 7.0 %collective-permute-start.11 = (bf16[1024,256]{1,0:T(8,128)(2,1)}, bf16[1024,256]{1,0:T(8,128)(2,1)S(1)}, u32[]{:S(2)}, u32[]{:S(2)}) collective-permute-start(bf16[1024,256]{1,0:T(8,128)(2,1)} %bitcast.10.refs_8_), channel_id=1, source_target_pairs={{0,24},{24,0},{1,25},{25,1},{2,26},{26,2},{3,27},{27,3},{4,28},{28... | collective-permute-start | bytes 1572872 | tf_op jit(solution)/shard_map/ppermute | solution.py:555
  157.3 2.5 collective-permute-start.13
  159.8 1.3 collective-permute-start.14
  161.1 11.0 %fwd.5 = (bf16[4,256,128]{2,1,0:T(8,128)(2,1)}, bf16[1024,1024]{1,0:T(8,128)(2,1)}, bf16[4096,1024]{1,0:T(8,128)(2,1)}) custom-call(s32[35]{0:T(128)} %concatenate.36.tab, bf16[8,256,2048]{2,1,0:T(8,128)(2,1)} %bitcast.44, bf16[8,256,2048]{2,1,0:T(8,128)(2,1)} %bitcast.38, ...), custom_call_target="tpu_custom_call", output_to_operand_aliasing={{1}: (16, {}), {2}: (17, {})} | custom-call | flops 1 | bytes 1 | tf_op jit(solution)/shard_map/fwd/pallas_call | solution.py:276
  172.1 1.8 pad_maximum_fusion
  173.9 3.7 %all-to-all-start.3 = ((bf16[4,256,256]{2,1,0:T(8,128)(2,1)}), bf16[4,256,256]{2,1,0:T(8,128)(2,1)S(1)}, u32[]{:S(2)}, u32[]{:S(2)}) async-start(bf16[4,256,256]{2,1,0:T(8,128)(2,1)} %pad_maximum_fusion), calls=%async_computation.3 | async-start | bytes 1048576 | tf_op jit(solution)/shard_map/all_to_all | solution.py:481
  178.4 11.0 %fwd.6 = (bf16[4,256,128]{2,1,0:T(8,128)(2,1)}, bf16[1024,1024]{1,0:T(8,128)(2,1)}, bf16[4096,1024]{1,0:T(8,128)(2,1)}) custom-call(s32[35]{0:T(128)} %concatenate.36.tab, bf16[8,256,2048]{2,1,0:T(8,128)(2,1)} %bitcast.45, bf16[8,256,2048]{2,1,0:T(8,128)(2,1)} %bitcast.46, ...), custom_call_target="tpu_custom_call", output_to_operand_aliasing={{1}: (16, {}), {2}: (17, {})} | custom-call | flops 1 | bytes 1 | tf_op jit(solution)/shard_map/fwd/pallas_call | solution.py:276
  190.6 6.7 %collective-permute-done.14.refs_9_ = bf16[1024,256]{1,0:T(8,128)(2,1)S(1)} collective-permute-done((bf16[1024,256]{1,0:T(8,128)(2,1)}, bf16[1024,256]{1,0:T(8,128)(2,1)S(1)}, u32[]{:S(2)}, u32[]{:S(2)}) %collective-permute-start.14) | collective-permute-done | bytes 524320 | tf_op jit(solution)/shard_map/ppermute | solution.py:484
  198.1 11.0 %fwd.7 = (bf16[4,256,128]{2,1,0:T(8,128)(2,1)}, bf16[1024,1024]{1,0:T(8,128)(2,1)}, bf16[4096,1024]{1,0:T(8,128)(2,1)}) custom-call(s32[35]{0:T(128)} %concatenate.36.tab, bf16[8,256,2048]{2,1,0:T(8,128)(2,1)} %bitcast.53, bf16[8,256,2048]{2,1,0:T(8,128)(2,1)} %bitcast.54, ...), custom_call_target="tpu_custom_call", output_to_operand_aliasing={{1}: (16, {}), {2}: (17, {})} | custom-call | flops 1 | bytes 1 | tf_op jit(solution)/shard_map/fwd/pallas_call | solution.py:276
  209.1 6.2 %bwd.8 = bf16[512,2048]{1,0:T(8,128)(2,1)} custom-call(bf16[1024,1024]{1,0:T(8,128)(2,1)} %get-tuple-element.142.refs_0_, bf16[4096,1024]{1,0:T(8,128)(2,1)} %get-tuple-element.143.refs_1_), custom_call_target="tpu_custom_call" | custom-call | flops 1 | bytes 1 | tf_op jit(solution)/shard_map/bwd/pallas_call | solution.py:335
  215.3 6.2 %bwd.6 = bf16[512,2048]{1,0:T(8,128)(2,1)} custom-call(bf16[1024,1024]{1,0:T(8,128)(2,1)} %get-tuple-element.142.refs_0_, bf16[4096,1024]{1,0:T(8,128)(2,1)} %get-tuple-element.143.refs_1_), custom_call_target="tpu_custom_call" | custom-call | flops 1 | bytes 1 | tf_op jit(solution)/shard_map/bwd/pallas_call | solution.py:335
  222.2 1.8 collective-permute-start.19
  224.8 1.4 copy-done.3
  226.2 4.0 %bwd.9 = bf16[512,1024]{1,0:T(8,128)(2,1)} custom-call(bf16[1024,1024]{1,0:T(8,128)(2,1)} %get-tuple-element.142.refs_0_, bf16[4096,1024]{1,0:T(8,128)(2,1)} %get-tuple-element.143.refs_1_, bf16[512,2048]{1,0:T(8,128)(2,1)} %copy-done.3), custom_call_target="tpu_custom_call" | custom-call | flops 1 | bytes 1 | tf_op jit(solution)/shard_map/bwd/pallas_call | solution.py:335
  230.3 5.2 %bwd.7 = bf16[256,2048]{1,0:T(8,128)(2,1)} custom-call(bf16[1024,1024]{1,0:T(8,128)(2,1)} %get-tuple-element.142.refs_0_, bf16[4096,1024]{1,0:T(8,128)(2,1)} %get-tuple-element.143.refs_1_, bf16[512,2048]{1,0:T(8,128)(2,1)} %collective-permute-done.16.refs_2_), custom_call_target="tpu_custom_call" | custom-call | flops 1 | bytes 1 | tf_op jit(solution)/shard_map/bwd/pallas_call | solution.py:335
  235.8 1.6 collective-permute-start.22
  237.4 3.6 %gather_context.1 = bf16[256,2048]{1,0:T(8,128)(2,1)} custom-call(s32[1]{0:T(128)} %bitcast.8.tab, bf16[4,256,256]{2,1,0:T(8,128)(2,1)} %copy-done.7, bf16[256,256]{1,0:T(8,128)(2,1)} %pad_maximum_fusion.1.refs_0_, bf16[256,256]{1,0:T(8,128)(2,1)} %copy-done.23, bf16[256,256]{1,0:T(8,128)(2,1)} %copy-done.22, bf16[256,256]{1,0:T(8,128)(2,1)} %copy-done.21), custom_call_target="tpu_custom_call" | custom-call | flops 1 | bytes 1 | tf_op jit(solution)/shard_map/gather_context/pallas_call | solution.py:436
  241.0 4.2 %bwd.11.q_ref = f32[512,1024]{1,0:T(8,128)} custom-call(bf16[1024,1024]{1,0:T(8,128)(2,1)} %get-tuple-element.142.refs_0_, bf16[4096,1024]{1,0:T(8,128)(2,1)} %get-tuple-element.143.refs_1_, bf16[512,2048]{1,0:T(8,128)(2,1)} %copy-done.3), custom_call_target="tpu_custom_call" | custom-call | flops 1 | bytes 1 | tf_op jit(solution)/shard_map/bwd/pallas_call | solution.py:335
  245.2 5.6 %bwd.10.p_ref = f32[256,2048]{1,0:T(8,128)} custom-call(bf16[1024,1024]{1,0:T(8,128)(2,1)} %get-tuple-element.142.refs_0_, bf16[4096,1024]{1,0:T(8,128)(2,1)} %get-tuple-element.143.refs_1_, bf16[512,2048]{1,0:T(8,128)(2,1)} %collective-permute-done.16.refs_2_), custom_call_target="tpu_custom_call" | custom-call | flops 1 | bytes 1 | tf_op jit(solution)/shard_map/bwd/pallas_call | solution.py:335
  250.8 10.4 %collective-permute-done.21.got_y = bf16[256,2048]{1,0:T(8,128)(2,1)S(1)} collective-permute-done((bf16[256,2048]{1,0:T(8,128)(2,1)}, bf16[256,2048]{1,0:T(8,128)(2,1)S(1)}, u32[]{:S(2)}, u32[]{:S(2)}) %collective-permute-start.21) | collective-permute-done | bytes 1048608 | tf_op jit(solution)/shard_map/ppermute | solution.py:584
  261.4 1.4 add_convert_fusion
  262.7 1.5 collective-permute-start.24
  264.4 1.6 collective-permute-start.23
  266.1 10.2 %collective-permute-done.24.last_y = bf16[256,1024]{1,0:T(8,128)(2,1)S(1)} collective-permute-done((bf16[256,1024]{1,0:T(8,128)(2,1)S(1)}, bf16[256,1024]{1,0:T(8,128)(2,1)S(1)}, u32[]{:S(2)}, u32[]{:S(2)}) %collective-permute-start.24) | collective-permute-done | bytes 524320 | tf_op jit(solution)/shard_map/ppermute | solution.py:595
  278.1 3.1 %finish.1 = bf16[256,2048]{1,0:T(8,128)(2,1)} custom-call(f32[256,2048]{1,0:T(8,128)} %bwd.10.p_ref, bf16[256,2048]{1,0:T(8,128)(2,1)} %copy-done.4, bf16[256,1024]{1,0:T(8,128)(2,1)} %copy-done.17, f32[512,1024]{1,0:T(8,128)} %bwd.11.q_ref, bf16[512,1024]{1,0:T(8,128)(2,1)} %collective-permute-done.22.got_x, bf16[256,1024]{1,0:T(8,128)(2,1)} %copy-done.16), custom_call_target="tpu_custom_call" | custom-call | flops 1 | bytes 1 | tf_op jit(solution)/shard_map/finish/pallas_call | solution.py:361
  (110 shorter events, 16.9 us)
Async XLA Ops:
  7.2 100.5 %all-gather.3.cloned.1.call-start = ((), (), s32[]{:S(2)}) async-start(), calls=%async_computation.4 | async-start | bytes 9437184 | tf_op jit(solution)/shard_map/all_gather | solution.py:496
  24.9 20.9 %copy-start.6 = (bf16[4,256,256]{2,1,0:T(8,128)(2,1)}, bf16[4,256,256]{2,1,0:T(8,128)(2,1)S(1)}, u32[]{:S(2)}) copy-start(bf16[4,256,256]{2,1,0:T(8,128)(2,1)S(1)} %all_to_all.20) | copy-start | bytes 1572868
  24.9 15.7 %copy-start.26 = (s32[1,4]{1,0:T(1,128)S(1)}, s32[1,4]{1,0:T(1,128)}, u32[]{:S(2)}) copy-start(s32[1,4]{1,0:T(1,128)} %param.11) | copy-start | bytes 52
  24.9 15.7 %copy-start.24 = (s32[4]{0:T(128)S(1)}, s32[4]{0:T(128)}, u32[]{:S(2)}) copy-start(s32[4]{0:T(128)} %param.10) | copy-start | bytes 52
  24.9 15.7 %copy-start.25 = (s32[4]{0:T(128)S(1)}, s32[4]{0:T(128)}, u32[]{:S(2)}) copy-start(s32[4]{0:T(128)} %param.9) | copy-start | bytes 52
  24.9 27.9 %collective-permute-start = (bf16[1024,256]{1,0:T(8,128)(2,1)S(1)}, bf16[1024,256]{1,0:T(8,128)(2,1)S(1)}, u32[]{:S(2)}, u32[]{:S(2)}) collective-permute-start(bf16[1024,256]{1,0:T(8,128)(2,1)S(1)} %bitcast.65), channel_id=1, source_target_pairs={{0,16},{8,24},{16,0},{24,8},{1,17},{9,25},{17,1},{25,9},{2,18},{10... | collective-permute-start | bytes 1572872 | tf_op jit(solution)/shard_map/ppermute | solution.py:487
  29.1 23.8 %collective-permute-start.1 = (bf16[1024,256]{1,0:T(8,128)(2,1)S(1)}, bf16[1024,256]{1,0:T(8,128)(2,1)S(1)}, u32[]{:S(2)}, u32[]{:S(2)}) collective-permute-start(bf16[1024,256]{1,0:T(8,128)(2,1)S(1)} %bitcast.66), channel_id=1, source_target_pairs={{0,8},{8,16},{16,24},{1,9},{9,17},{17,25},{2,10},{10,18},{18,26},{... | collective-permute-start | bytes 1572872 | tf_op jit(solution)/shard_map/ppermute | solution.py:484
  32.7 24.4 %collective-permute-start.2 = (bf16[1024,256]{1,0:T(8,128)(2,1)S(1)}, bf16[1024,256]{1,0:T(8,128)(2,1)S(1)}, u32[]{:S(2)}, u32[]{:S(2)}) collective-permute-start(bf16[1024,256]{1,0:T(8,128)(2,1)S(1)} %bitcast.67), channel_id=1, source_target_pairs={{8,0},{16,8},{24,16},{9,1},{17,9},{25,17},{10,2},{18,10},{26,18},{... | collective-permute-start | bytes 1572872 | tf_op jit(solution)/shard_map/ppermute | solution.py:484
  37.1 19.9 %all-to-all-start.1 = ((bf16[4,256,256]{2,1,0:T(8,128)(2,1)}), bf16[4,256,256]{2,1,0:T(8,128)(2,1)S(1)}, u32[]{:S(2)}, u32[]{:S(2)}) async-start(bf16[4,256,256]{2,1,0:T(8,128)(2,1)} %pack_weights.3), calls=%async_computation.1 | async-start | bytes 1048576 | tf_op jit(solution)/shard_map/all_to_all | solution.py:481
  52.9 4.2 %copy-start.8 = (bf16[1024,256]{1,0:T(8,128)(2,1)}, bf16[1024,256]{1,0:T(8,128)(2,1)S(1)}, u32[]{:S(2)}) copy-start(bf16[1024,256]{1,0:T(8,128)(2,1)S(1)} %collective-permute-done.refs_10_) | copy-start | bytes 1572868
  52.9 4.2 %copy-start.9 = (bf16[1024,256]{1,0:T(8,128)(2,1)}, bf16[1024,256]{1,0:T(8,128)(2,1)S(1)}, u32[]{:S(2)}) copy-start(bf16[1024,256]{1,0:T(8,128)(2,1)S(1)} %collective-permute-done.1.refs_11_) | copy-start | bytes 1572868
  58.0 49.7 %all-to-all-start.2 = ((bf16[4,272,1536]{2,1,0:T(8,128)(2,1)}), bf16[4,272,1536]{2,1,0:T(8,128)(2,1)S(1)}, u32[]{:S(2)}, u32[]{:S(2)}) async-start(bf16[4,272,1536]{2,1,0:T(8,128)(2,1)} %pack.1), calls=%async_computation.2 | async-start | bytes 6684672 | tf_op jit(solution)/shard_map/all_to_all | solution.py:481
  61.7 21.3 %collective-permute-start.3 = (bf16[1024,256]{1,0:T(8,128)(2,1)}, bf16[1024,256]{1,0:T(8,128)(2,1)}, u32[]{:S(2)}, u32[]{:S(2)}) collective-permute-start(bf16[1024,256]{1,0:T(8,128)(2,1)} %copy-done.8), channel_id=1, source_target_pairs={{8,0},{16,24},{9,1},{17,25},{10,2},{18,26},{11,3},{19,27},{12,4},{... | collective-permute-start | bytes 1572872 | tf_op jit(solution)/shard_map/ppermute | solution.py:490
  63.0 33.8 %collective-permute-start.4 = (bf16[1024,256]{1,0:T(8,128)(2,1)}, bf16[1024,256]{1,0:T(8,128)(2,1)}, u32[]{:S(2)}, u32[]{:S(2)}) collective-permute-start(bf16[1024,256]{1,0:T(8,128)(2,1)} %bitcast.61), channel_id=1, source_target_pairs={{0,16},{8,24},{16,0},{24,8},{1,17},{9,25},{17,1},{25,9},{2,18},{10... | collective-permute-start | bytes 1572872 | tf_op jit(solution)/shard_map/ppermute | solution.py:487
  72.5 24.4 %collective-permute-start.5 = (bf16[1024,256]{1,0:T(8,128)(2,1)}, bf16[1024,256]{1,0:T(8,128)(2,1)}, u32[]{:S(2)}, u32[]{:S(2)}) collective-permute-start(bf16[1024,256]{1,0:T(8,128)(2,1)} %bitcast.62), channel_id=1, source_target_pairs={{0,8},{8,16},{16,24},{1,9},{9,17},{17,25},{2,10},{10,18},{18,26},{... | collective-permute-start | bytes 1572872 | tf_op jit(solution)/shard_map/ppermute | solution.py:484
  74.5 30.5 %collective-permute-start.6 = (bf16[1024,256]{1,0:T(8,128)(2,1)}, bf16[1024,256]{1,0:T(8,128)(2,1)}, u32[]{:S(2)}, u32[]{:S(2)}) collective-permute-start(bf16[1024,256]{1,0:T(8,128)(2,1)} %bitcast.63), channel_id=1, source_target_pairs={{8,0},{16,8},{24,16},{9,1},{17,9},{25,17},{10,2},{18,10},{26,18},{... | collective-permute-start | bytes 1572872 | tf_op jit(solution)/shard_map/ppermute | solution.py:484
  107.7 13.7 %copy-start = (bf16[4,272,1536]{2,1,0:T(8,128)(2,1)}, bf16[4,272,1536]{2,1,0:T(8,128)(2,1)S(1)}, u32[]{:S(2)}) copy-start(bf16[4,272,1536]{2,1,0:T(8,128)(2,1)S(1)} %all-to-all-done.2.refs_13_.refs_14_) | copy-start | bytes 10027012
  109.8 39.0 %collective-permute-start.8 = (bf16[1024,256]{1,0:T(8,128)(2,1)}, bf16[1024,256]{1,0:T(8,128)(2,1)}, u32[]{:S(2)}, u32[]{:S(2)}) collective-permute-start(bf16[1024,256]{1,0:T(8,128)(2,1)} %bitcast.9.refs_8_), channel_id=1, source_target_pairs={{0,16},{8,24},{16,0},{24,8},{1,17},{9,25},{17,1},{25,9},{2,18},{10... | collective-permute-start | bytes 1572872 | tf_op jit(solution)/shard_map/ppermute | solution.py:487
  111.8 36.9 %collective-permute-start.10 = (bf16[1024,256]{1,0:T(8,128)(2,1)}, bf16[1024,256]{1,0:T(8,128)(2,1)}, u32[]{:S(2)}, u32[]{:S(2)}) collective-permute-start(bf16[1024,256]{1,0:T(8,128)(2,1)} %bitcast.9.refs_8_), channel_id=1, source_target_pairs={{8,0},{16,8},{24,16},{9,1},{17,9},{25,17},{10,2},{18,10},{26,18},{... | collective-permute-start | bytes 1572872 | tf_op jit(solution)/shard_map/ppermute | solution.py:484
  113.1 35.6 %collective-permute-start.9 = (bf16[1024,256]{1,0:T(8,128)(2,1)}, bf16[1024,256]{1,0:T(8,128)(2,1)}, u32[]{:S(2)}, u32[]{:S(2)}) collective-permute-start(bf16[1024,256]{1,0:T(8,128)(2,1)} %bitcast.9.refs_8_), channel_id=1, source_target_pairs={{0,8},{8,16},{16,24},{1,9},{9,17},{17,25},{2,10},{10,18},{18,26},{... | collective-permute-start | bytes 1572872 | tf_op jit(solution)/shard_map/ppermute | solution.py:484
  118.5 30.2 %collective-permute-start.7 = (bf16[1024,256]{1,0:T(8,128)(2,1)}, bf16[1024,256]{1,0:T(8,128)(2,1)}, u32[]{:S(2)}, u32[]{:S(2)}) collective-permute-start(bf16[1024,256]{1,0:T(8,128)(2,1)} %collective-permute-done.4.refs_10_), channel_id=1, source_target_pairs={{8,0},{16,24},{9,1},{17,25},{10,2},{18,26},{11,3},{19,27},{12,4},{... | collective-permute-start | bytes 1572872 | tf_op jit(solution)/shard_map/ppermute | solution.py:490
  148.8 23.3 %copy-start.20 = (bf16[4,256,128]{2,1,0:T(8,128)(2,1)S(1)}, bf16[4,256,128]{2,1,0:T(8,128)(2,1)}, u32[]{:S(2)}) copy-start(bf16[4,256,128]{2,1,0:T(8,128)(2,1)} %get-tuple-element.128) | copy-start | bytes 786436
  148.8 28.8 %collective-permute-start.15 = (bf16[1024,256]{1,0:T(8,128)(2,1)}, bf16[1024,256]{1,0:T(8,128)(2,1)S(1)}, u32[]{:S(2)}, u32[]{:S(2)}) collective-permute-start(bf16[1024,256]{1,0:T(8,128)(2,1)} %collective-permute-done.8.refs_10_), channel_id=1, source_target_pairs={{8,0},{16,24},{9,1},{17,25},{10,2},{18,26},{11,3},{19,27},{12,4},{... | collective-permute-start | bytes 1572872 | tf_op jit(solution)/shard_map/ppermute | solution.py:490
  150.2 39.2 %collective-permute-start.11 = (bf16[1024,256]{1,0:T(8,128)(2,1)}, bf16[1024,256]{1,0:T(8,128)(2,1)S(1)}, u32[]{:S(2)}, u32[]{:S(2)}) collective-permute-start(bf16[1024,256]{1,0:T(8,128)(2,1)} %bitcast.10.refs_8_), channel_id=1, source_target_pairs={{0,24},{24,0},{1,25},{25,1},{2,26},{26,2},{3,27},{27,3},{4,28},{28... | collective-permute-start | bytes 1572872 | tf_op jit(solution)/shard_map/ppermute | solution.py:555
  157.2 33.4 %collective-permute-start.12 = (bf16[1024,256]{1,0:T(8,128)(2,1)}, bf16[1024,256]{1,0:T(8,128)(2,1)S(1)}, u32[]{:S(2)}, u32[]{:S(2)}) collective-permute-start(bf16[1024,256]{1,0:T(8,128)(2,1)} %bitcast.10.refs_8_), channel_id=1, source_target_pairs={{0,16},{8,24},{16,0},{24,8},{1,17},{9,25},{17,1},{25,9},{2,18},{10... | collective-permute-start | bytes 1572872 | tf_op jit(solution)/shard_map/ppermute | solution.py:487
  157.3 33.3 %collective-permute-start.13 = (bf16[1024,256]{1,0:T(8,128)(2,1)}, bf16[1024,256]{1,0:T(8,128)(2,1)S(1)}, u32[]{:S(2)}, u32[]{:S(2)}) collective-permute-start(bf16[1024,256]{1,0:T(8,128)(2,1)} %bitcast.10.refs_8_), channel_id=1, source_target_pairs={{0,8},{8,16},{16,24},{1,9},{9,17},{17,25},{2,10},{10,18},{18,26},{... | collective-permute-start | bytes 1572872 | tf_op jit(solution)/shard_map/ppermute | solution.py:484
  159.8 37.5 %collective-permute-start.14 = (bf16[1024,256]{1,0:T(8,128)(2,1)}, bf16[1024,256]{1,0:T(8,128)(2,1)S(1)}, u32[]{:S(2)}, u32[]{:S(2)}) collective-permute-start(bf16[1024,256]{1,0:T(8,128)(2,1)} %bitcast.10.refs_8_), channel_id=1, source_target_pairs={{8,0},{16,8},{24,16},{9,1},{17,9},{25,17},{10,2},{18,10},{26,18},{... | collective-permute-start | bytes 1572872 | tf_op jit(solution)/shard_map/ppermute | solution.py:484
  173.9 23.4 %all-to-all-start.3 = ((bf16[4,256,256]{2,1,0:T(8,128)(2,1)}), bf16[4,256,256]{2,1,0:T(8,128)(2,1)S(1)}, u32[]{:S(2)}, u32[]{:S(2)}) async-start(bf16[4,256,256]{2,1,0:T(8,128)(2,1)} %pad_maximum_fusion), calls=%async_computation.3 | async-start | bytes 1048576 | tf_op jit(solution)/shard_map/all_to_all | solution.py:481
  189.4 7.9 %copy-start.11 = (bf16[1024,256]{1,0:T(8,128)(2,1)}, bf16[1024,256]{1,0:T(8,128)(2,1)S(1)}, u32[]{:S(2)}) copy-start(bf16[1024,256]{1,0:T(8,128)(2,1)S(1)} %collective-permute-done.11.refs_12_) | copy-start | bytes 1572868
  190.6 6.7 %copy-start.12 = (bf16[1024,256]{1,0:T(8,128)(2,1)}, bf16[1024,256]{1,0:T(8,128)(2,1)S(1)}, u32[]{:S(2)}) copy-start(bf16[1024,256]{1,0:T(8,128)(2,1)S(1)} %collective-permute-done.12.refs_10_) | copy-start | bytes 1572868
  190.6 6.7 %copy-start.13 = (bf16[1024,256]{1,0:T(8,128)(2,1)}, bf16[1024,256]{1,0:T(8,128)(2,1)S(1)}, u32[]{:S(2)}) copy-start(bf16[1024,256]{1,0:T(8,128)(2,1)S(1)} %collective-permute-done.13.refs_11_) | copy-start | bytes 1572868
  197.3 11.8 %copy-start.7 = (bf16[4,256,256]{2,1,0:T(8,128)(2,1)}, bf16[4,256,256]{2,1,0:T(8,128)(2,1)S(1)}, u32[]{:S(2)}) copy-start(bf16[4,256,256]{2,1,0:T(8,128)(2,1)S(1)} %all-to-all-done.3.early) | copy-start | bytes 1572868
  215.3 6.7 %copy-start.19 = (bf16[4,256,128]{2,1,0:T(8,128)(2,1)S(1)}, bf16[4,256,128]{2,1,0:T(8,128)(2,1)}, u32[]{:S(2)}) copy-start(bf16[4,256,128]{2,1,0:T(8,128)(2,1)} %get-tuple-element.139) | copy-start | bytes 786436
  215.3 6.7 %copy-start.18 = (bf16[4,256,128]{2,1,0:T(8,128)(2,1)S(1)}, bf16[4,256,128]{2,1,0:T(8,128)(2,1)}, u32[]{:S(2)}) copy-start(bf16[4,256,128]{2,1,0:T(8,128)(2,1)} %get-tuple-element.138) | copy-start | bytes 786436
  215.3 9.6 %collective-permute-start.17 = (bf16[512,2048]{1,0:T(8,128)(2,1)}, bf16[512,2048]{1,0:T(8,128)(2,1)S(1)}, u32[]{:S(2)}, u32[]{:S(2)}) collective-permute-start(bf16[512,2048]{1,0:T(8,128)(2,1)} %bwd.8), channel_id=1, source_target_pairs={{0,2},{2,0},{4,6},{6,4},{1,3},{3,1},{5,7},{7,5},{8,10},{10,8},{12,... | collective-permute-start | bytes 6291464 | tf_op jit(solution)/shard_map/ppermute | solution.py:478
  221.5 8.7 %collective-permute-start.16 = (bf16[512,2048]{1,0:T(8,128)(2,1)}, bf16[512,2048]{1,0:T(8,128)(2,1)}, u32[]{:S(2)}, u32[]{:S(2)}) collective-permute-start(bf16[512,2048]{1,0:T(8,128)(2,1)} %bwd.6), channel_id=1, source_target_pairs={{0,2},{2,0},{4,6},{6,4},{1,3},{3,1},{5,7},{7,5},{8,10},{10,8},{12,... | collective-permute-start | bytes 6291464 | tf_op jit(solution)/shard_map/ppermute | solution.py:478
  222.1 13.4 %collective-permute-start.20 = (bf16[256,256]{1,0:T(8,128)(2,1)S(1)}, bf16[256,256]{1,0:T(8,128)(2,1)S(1)}, u32[]{:S(2)}, u32[]{:S(2)}) collective-permute-start(bf16[256,256]{1,0:T(8,128)(2,1)S(1)} %pad_maximum_fusion.4), channel_id=1, source_target_pairs={{0,6},{2,4},{4,2},{6,0},{1,7},{3,5},{5,3},{7,1},{8,14},{10,12},{12... | collective-permute-start | bytes 393224 | tf_op jit(solution)/shard_map/ppermute | solution.py:569
  222.2 13.3 %collective-permute-start.19 = (bf16[256,256]{1,0:T(8,128)(2,1)S(1)}, bf16[256,256]{1,0:T(8,128)(2,1)S(1)}, u32[]{:S(2)}, u32[]{:S(2)}) collective-permute-start(bf16[256,256]{1,0:T(8,128)(2,1)S(1)} %pad_maximum_fusion.3), channel_id=1, source_target_pairs={{0,4},{2,6},{4,0},{6,2},{1,5},{3,7},{5,1},{7,3},{8,12},{10,14},{12... | collective-permute-start | bytes 393224 | tf_op jit(solution)/shard_map/ppermute | solution.py:569
  223.9 11.5 %collective-permute-start.18 = (bf16[256,256]{1,0:T(8,128)(2,1)S(1)}, bf16[256,256]{1,0:T(8,128)(2,1)S(1)}, u32[]{:S(2)}, u32[]{:S(2)}) collective-permute-start(bf16[256,256]{1,0:T(8,128)(2,1)S(1)} %pad_maximum_fusion.2), channel_id=1, source_target_pairs={{0,2},{2,0},{4,6},{6,4},{1,3},{3,1},{5,7},{7,5},{8,10},{10,8},{12,... | collective-permute-start | bytes 393224 | tf_op jit(solution)/shard_map/ppermute | solution.py:569
  235.4 2.0 copy-start.21
  235.4 1.9 copy-start.22
  235.5 25.7 %collective-permute-start.21 = (bf16[256,2048]{1,0:T(8,128)(2,1)}, bf16[256,2048]{1,0:T(8,128)(2,1)S(1)}, u32[]{:S(2)}, u32[]{:S(2)}) collective-permute-start(bf16[256,2048]{1,0:T(8,128)(2,1)} %bwd.7), channel_id=1, source_target_pairs={{0,4},{2,6},{4,0},{6,2},{1,5},{3,7},{5,1},{7,3},{8,12},{10,14},{12... | collective-permute-start | bytes 3145736 | tf_op jit(solution)/shard_map/ppermute | solution.py:584
  235.8 25.5 %collective-permute-start.22 = (bf16[512,1024]{1,0:T(8,128)(2,1)}, bf16[512,1024]{1,0:T(8,128)(2,1)}, u32[]{:S(2)}, u32[]{:S(2)}) collective-permute-start(bf16[512,1024]{1,0:T(8,128)(2,1)} %bwd.9), channel_id=1, source_target_pairs={{0,1},{1,0},{2,3},{3,2},{4,5},{5,4},{6,7},{7,6},{8,9},{9,8},{10,11... | collective-permute-start | bytes 3145736 | tf_op jit(solution)/shard_map/ppermute | solution.py:585
  245.2 16.2 %copy-start.1 = (f32[512,1024]{1,0:T(8,128)S(1)}, f32[512,1024]{1,0:T(8,128)}, u32[]{:S(2)}) copy-start(f32[512,1024]{1,0:T(8,128)} %bwd.11.q_ref) | copy-start | bytes 6291460
  250.8 13.5 %copy-start.2 = (f32[256,2048]{1,0:T(8,128)S(1)}, f32[256,2048]{1,0:T(8,128)}, u32[]{:S(2)}) copy-start(f32[256,2048]{1,0:T(8,128)} %bwd.10.p_ref) | copy-start | bytes 6291460
  261.2 3.3 %copy-start.4 = (bf16[256,2048]{1,0:T(8,128)(2,1)}, bf16[256,2048]{1,0:T(8,128)(2,1)S(1)}, u32[]{:S(2)}) copy-start(bf16[256,2048]{1,0:T(8,128)(2,1)S(1)} %collective-permute-done.21.got_y) | copy-start | bytes 3145732
  262.7 13.6 %collective-permute-start.24 = (bf16[256,1024]{1,0:T(8,128)(2,1)S(1)}, bf16[256,1024]{1,0:T(8,128)(2,1)S(1)}, u32[]{:S(2)}, u32[]{:S(2)}) collective-permute-start(bf16[256,1024]{1,0:T(8,128)(2,1)S(1)} %add_convert_fusion), channel_id=1, source_target_pairs={{0,4},{2,6},{4,0},{6,2},{1,5},{3,7},{5,1},{7,3},{8,12},{10,14},{12... | collective-permute-start | bytes 1572872 | tf_op jit(solution)/shard_map/ppermute | solution.py:595
  264.4 12.8 %collective-permute-start.23 = (bf16[256,1024]{1,0:T(8,128)(2,1)S(1)}, bf16[256,1024]{1,0:T(8,128)(2,1)S(1)}, u32[]{:S(2)}, u32[]{:S(2)}) collective-permute-start(bf16[256,1024]{1,0:T(8,128)(2,1)S(1)} %add_convert_fusion.1), channel_id=1, source_target_pairs={{0,1},{1,0},{2,3},{3,2},{4,5},{5,4},{6,7},{7,6},{8,9},{9,8},{10,11... | collective-permute-start | bytes 1572872 | tf_op jit(solution)/shard_map/ppermute | solution.py:594
  (8 other events, 8.4 us)
Sparse Core Ops, SparseCore 0:
  9.9 70.7 all-gather.2

commit v5 on v4

--- a/solution.py
+++ b/solution.py
@@ -134,6 +134,7 @@
 
 PAIR = 2 * DH
 SLOTS = (0, 2, 1, 3)
+VMEM = 56 << 20
 SHORT = pl.CostEstimate(flops=1, bytes_accessed=1, transcendentals=0)
 
 
@@ -145,7 +146,7 @@
     return lax.dot_general(a, b, (((0,), (0,)), ((), ())), preferred_element_type=F32)
 
 
-def forward_kernel(n_dp, n_sec, n_half, blk, tab, *refs):
+def forward_kernel(n_dp, n_sec, n_half, blk, in_slots, tab, *refs):
     blocks = n_dp * blk
     x_refs = refs[: n_half * n_dp]
     own, above, far, below, end = refs[n_half * n_dp : n_half * n_dp + 5]
@@ -160,7 +161,13 @@
     hop = (section - z + n_sec) % n_sec
 
     def take(ref):
-        w_ref[...] = ref[...].reshape(w_ref.shape)
+        if in_slots:
+            d = tab[2 * blocks + 2]
+            for t in range(n_dp):
+                to = pl.multiple_of((d ^ t) * rows, rows)
+                w_ref[pl.ds(to, rows), :] = ref[t * rows : (t + 1) * rows, :]
+        else:
+            w_ref[...] = ref[...].reshape(w_ref.shape)
 
     @pl.when(hop == 0)
     def _():
@@ -274,7 +281,7 @@
         operands += before
         in_specs += [pl.BlockSpec(memory_space=pl.ANY)] * 2
     return pl.pallas_call(
-        functools.partial(forward_kernel, n_dp, n_sec, n_half, blk),
+        functools.partial(forward_kernel, n_dp, n_sec, n_half, blk, chunk == 0),
         grid_spec=pltpu.PrefetchScalarGridSpec(
             num_scalar_prefetch=1,
             grid=(n_sec,),
@@ -295,14 +302,17 @@
             jax.ShapeDtypeStruct((n_sec * span, chunks * cols), BF16),
         ],
         input_output_aliases=aliases,
-        compiler_params=pltpu.CompilerParams(vmem_limit_bytes=60 << 20),
+        compiler_params=pltpu.CompilerParams(vmem_limit_bytes=VMEM),
         cost_estimate=SHORT,
         name="fwd",
     )(*operands)
 
 
 def backward_kernel(*refs):
-    total = nt(refs[0][...], refs[1][...])
+    depth = refs[0].shape[1]
+    total = nt(refs[0][:, : 2 * PAIR], refs[1][:, : 2 * PAIR])
+    for at in range(2 * PAIR, depth, 2 * PAIR):
+        total += nt(refs[0][:, at : at + 2 * PAIR], refs[1][:, at : at + 2 * PAIR])
     for ref in refs[2:-1]:
         total += ref[...].astype(F32)
     refs[-1][...] = total.astype(refs[-1].dtype)
@@ -312,7 +322,7 @@
     row_n, row_at = rows
     span, blocks = cols
     depth = dkv.shape[1]
-    tile = 512
+    tile = 1024
     per_block = span // tile
 
     def col(i):
@@ -338,7 +348,7 @@
         in_specs=specs,
         out_specs=pl.BlockSpec((row_n, tile), lambda i: (0, i)),
         out_shape=jax.ShapeDtypeStruct((row_n, len(blocks) * span), out_dtype),
-        compiler_params=pltpu.CompilerParams(vmem_limit_bytes=60 << 20),
+        compiler_params=pltpu.CompilerParams(vmem_limit_bytes=VMEM),
         cost_estimate=SHORT,
         name="bwd",
     )(dkv, w, *extra)
@@ -364,6 +374,7 @@
         in_specs=[block] * 6,
         out_specs=pl.BlockSpec((rows // tiles, 2 * span), lambda i: (i, 0)),
         out_shape=jax.ShapeDtypeStruct((rows, 2 * span), BF16),
+        compiler_params=pltpu.CompilerParams(vmem_limit_bytes=VMEM),
         cost_estimate=SHORT,
         name="finish",
     )(*operands)
@@ -384,6 +395,7 @@
         in_specs=[block] * 2,
         out_specs=pl.BlockSpec((1, rows, 2 * PAIR), lambda j: (j, 0, 0)),
         out_shape=jax.ShapeDtypeStruct((n_dp, rows, 2 * PAIR), BF16),
+        compiler_params=pltpu.CompilerParams(vmem_limit_bytes=VMEM),
         cost_estimate=SHORT,
         name="pack_weights",
     )(w_key, w_value)
@@ -414,6 +426,7 @@
         in_specs=[block, block, tail, tail, pl.BlockSpec(small.shape, lambda j: (0, 0))],
         out_specs=pl.BlockSpec((1, rows + extra, 3 * cols), lambda j: (j, 0, 0)),
         out_shape=jax.ShapeDtypeStruct((n_dp, rows + extra, 3 * cols), BF16),
+        compiler_params=pltpu.CompilerParams(vmem_limit_bytes=VMEM),
         cost_estimate=SHORT,
         name="pack",
     )(queries, grads, w_key, w_value, small)
@@ -443,6 +456,7 @@
             out_specs=pl.BlockSpec((rows, cols + last), lambda t, tab: (0, tab[0] ^ t)),
         ),
         out_shape=jax.ShapeDtypeStruct((rows, n_dp * (cols + last)), BF16),
+        compiler_params=pltpu.CompilerParams(vmem_limit_bytes=VMEM),
         cost_estimate=SHORT,
         name="gather_context",
     )(d.reshape(1), early, *late)
@@ -492,7 +506,14 @@
     def flat(x):
         return x.reshape(n_dp * rows, 2 * PAIR)
 
-    own0 = flat(exchange(pack_weights(w_key, w_value, 0, n_dp)))
+    pieces = []
+    for t in range(n_dp):
+        at = (d ^ t) * head_cols
+        cut = jnp.concatenate(
+            [lax.dynamic_slice(w, (0, at), (rows, PAIR)) for w in (w_key, w_value)], axis=1
+        )
+        pieces.append(cut if t == 0 else lax.ppermute(cut, "dp", [(i, i ^ t) for i in range(n_dp)]))
+    own0 = jnp.concatenate(pieces, axis=0)
     x = lax.all_gather(enc_rows, ("dp", "mp"), axis=0, tiled=False)
     small = jnp.concatenate([enc_len, dest_dp, peer_counts[0]]).astype(BF16)
     small = jnp.pad(small[None, :], ((0, 15), (0, PAIR - small.shape[0])))
@@ -551,9 +572,11 @@
     f0 = forward(0, own0, near0, far0, end0, None)
 
     (end1,), (far2,), near2, (own3, f0), _ = step((end1,), (far2,), near2, (own3, f0))
-    near3, far3, end2 = sides(own3), beyond(own3), turn(far2)
+    far3, end2 = beyond(own3), turn(far2)
     end3 = lax.ppermute(own3, "section", outer)
     f1 = forward(1, own1, near1, far1, end1, f0[1:])
+    f1, own3_ = lax.optimization_barrier((f1, own3))
+    near3 = sides(own3_)
     context_a = exchange(jnp.concatenate([f0[0], f1[0]], axis=2))
     f2 = forward(2, own2, near2, far2, end2, f1[1:])
 

time: 292 us -> 284 us (0.973)
  waiting for transfers between devices: 89.7 us -> 104 us
  blocking collectives: 13.9 us -> 0 us
  Pallas kernels: 92.9 us -> 87.3 us
    all_to_all x1 -> x0, blocking collectives: 13.9 us -> none  [exchange(): return lax.all_to_all(x, 'dp', split_axis=0, concat_axis=0, tiled=True)]
    ppermute x3, waiting for transfers between devices: 23.5 us -> 30.8 us  [turn(): return lax.ppermute(far, 'section', ends)]
    ppermute x0 -> x3, waiting for transfers between devices: none -> 6.56 us  [shards_section(): lax.ppermute(cut, 'dp', [(i, i ^ t) for i in range(n_dp)])]
    ppermute x1, starting transfers between devices: 7.03 us -> 2.05 us  [shards_section(): end3 = lax.ppermute(own3, 'section', outer)]
    ppermute x0 -> x3, starting transfers between devices: none -> 3.3 us  [shards_section(): lax.ppermute(cut, 'dp', [(i, i ^ t) for i in range(n_dp)])]
    pallas_call x2 -> x1, Pallas kernels: 6.27 us -> 3.14 us  [pack_weights(): pl.pallas_call(weight_kernel, grid=(n_dp,), in_specs=[block] * 2, out_spe...]
  transfers between devices with their start and end apart: 29 -> 32, of which waited for: 13 -> 15; matrix products, arithmetic and copies ran while one was open for 2% -> 2% of each run, Pallas kernels for 25% -> 24%
where the time goes in v5:
time: 284 us; the launch traced here: 282 us
  waiting for transfers between devices  104 us (37%)
  Pallas kernels  87.3 us (31%)
  starting transfers between devices  63.8 us (22%)
  between operations  14.6 us (5%)
  local copies, waits for them, and re-layouts  7.92 us (3%)
  other arithmetic  5.24 us (2%)
    pallas_call x4, Pallas kernels, forward_chunk(): pl.pallas_call(functools.partial(forward_kernel, n_dp, n_sec, n_half, blk...  44.1 us
    ppermute x3, waiting for transfers between devices, turn(): return lax.ppermute(far, 'section', ends)  30.8 us
    pallas_call x6, Pallas kernels, backward(): pl.pallas_call(backward_kernel, grid=(len(blocks) * per_block,), in_specs...  29.1 us
    ppermute x4, waiting for transfers between devices, beyond(): return lax.ppermute(piece, 'section', over_two)  21.8 us
    ppermute x4, waiting for transfers between devices, sides(): lax.ppermute(piece, 'section', down)  19.9 us
    ppermute x4, starting transfers between devices, sides(): lax.ppermute(piece, 'section', up)  16.1 us
    ppermute x4, starting transfers between devices, beyond(): return lax.ppermute(piece, 'section', over_two)  14.7 us
    all_to_all x3, starting transfers between devices, exchange(): return lax.all_to_all(x, 'dp', split_axis=0, concat_axis=0, tiled=True)  10.8 us
  transfers between devices with their start and end apart: 32, of which 15 were waited for; matrix products, arithmetic and copies ran while one was open for 2% of the time, Pallas kernels for 24%

profile of v5, /device:TPU:0, one launch (start us, length us, event | category | flops | bytes accessed | tf_op | source)
XLA Modules:
  0.0 282.5 jit_solution(5701381344045301495)
XLA Ops:
  9.6 2.6 collective-permute-start.1
  12.4 4.1 %collective-permute-done.1 = bf16[256,256]{1,0:T(8,128)(2,1)S(1)} collective-permute-done((bf16[256,256]{1,0:T(8,128)(2,1)S(1)}, bf16[256,256]{1,0:T(8,128)(2,1)S(1)}, u32[]{:S(2)}, u32[]{:S(2)}) %collective-permute-start.1) | collective-permute-done | bytes 131104 | tf_op jit(solution)/shard_map/ppermute | solution.py:515
  16.6 2.4 collective-permute-done.2
  19.1 2.7 collective-permute-start.3
  21.7 3.5 %collective-permute-start.4 = (bf16[1024,256]{1,0:T(8,128)(2,1)S(1)}, bf16[1024,256]{1,0:T(8,128)(2,1)S(1)}, u32[]{:S(2)}, u32[]{:S(2)}) collective-permute-start(bf16[1024,256]{1,0:T(8,128)(2,1)S(1)} %pad_maximum_fusion.refs_8_), channel_id=1, source_target_pairs={{0,8},{8,16},{16,24},{1,9},{9,17},{17,25},{2,10},{10,18},{18,26},{... | collective-permute-start | bytes 1572872 | tf_op jit(solution)/shard_map/ppermute | solution.py:498
  25.2 1.3 collective-permute-start.5
  26.5 3.1 %pack_weights.1 = bf16[4,256,256]{2,1,0:T(8,128)(2,1)} custom-call(bf16[256,2048]{1,0:T(8,128)(2,1)} %k_ref.1, bf16[256,2048]{1,0:T(8,128)(2,1)} %v_ref.1), custom_call_target="tpu_custom_call" | custom-call | flops 1 | bytes 1 | tf_op jit(solution)/shard_map/pack_weights/pallas_call | solution.py:392
  29.7 3.5 %all-to-all-start = ((bf16[4,256,256]{2,1,0:T(8,128)(2,1)}), bf16[4,256,256]{2,1,0:T(8,128)(2,1)S(1)}, u32[]{:S(2)}, u32[]{:S(2)}) async-start(bf16[4,256,256]{2,1,0:T(8,128)(2,1)} %pack_weights.1), calls=%async_computation | async-start | bytes 1048576 | tf_op jit(solution)/shard_map/all_to_all | solution.py:495
  33.9 4.3 %pack.1 = bf16[4,272,1536]{2,1,0:T(8,128)(2,1)} custom-call(bf16[256,2048]{1,0:T(8,128)(2,1)} %q_ref.1, bf16[256,2048]{1,0:T(8,128)(2,1)} %g_ref.1, bf16[256,2048]{1,0:T(8,128)(2,1)} %k_ref.1, bf16[256,2048]{1,0:T(8,128)(2,1)} %v_ref.1, bf16[16,128]{1,0:T(8,128)(2,1)} %fusion.8.small_ref), custom_call_target="tpu_custom_call" | custom-call | flops 1 | bytes 1 | tf_op jit(solution)/shard_map/pack/pallas_call | solution.py:423
  38.2 7.9 %collective-permute-done.3.refs_10_ = bf16[1024,256]{1,0:T(8,128)(2,1)S(1)} collective-permute-done((bf16[1024,256]{1,0:T(8,128)(2,1)S(1)}, bf16[1024,256]{1,0:T(8,128)(2,1)S(1)}, u32[]{:S(2)}, u32[]{:S(2)}) %collective-permute-start.3) | collective-permute-done | bytes 524320 | tf_op jit(solution)/shard_map/ppermute | solution.py:501
  46.1 4.6 %collective-permute-done.5.refs_9_ = bf16[1024,256]{1,0:T(8,128)(2,1)S(1)} collective-permute-done((bf16[1024,256]{1,0:T(8,128)(2,1)S(1)}, bf16[1024,256]{1,0:T(8,128)(2,1)S(1)}, u32[]{:S(2)}, u32[]{:S(2)}) %collective-permute-start.5) | collective-permute-done | bytes 524320 | tf_op jit(solution)/shard_map/ppermute | solution.py:498
  51.7 3.7 %all-to-all-start.1 = ((bf16[4,272,1536]{2,1,0:T(8,128)(2,1)}), bf16[4,272,1536]{2,1,0:T(8,128)(2,1)S(1)}, u32[]{:S(2)}, u32[]{:S(2)}) async-start(bf16[4,272,1536]{2,1,0:T(8,128)(2,1)} %pack.1), calls=%async_computation.1 | async-start | bytes 6684672 | tf_op jit(solution)/shard_map/all_to_all | solution.py:495
  55.4 1.3 collective-permute-start.6
  56.7 9.5 %collective-permute-start.7 = (bf16[1024,256]{1,0:T(8,128)(2,1)}, bf16[1024,256]{1,0:T(8,128)(2,1)}, u32[]{:S(2)}, u32[]{:S(2)}) collective-permute-start(bf16[1024,256]{1,0:T(8,128)(2,1)} %bitcast.60), channel_id=1, source_target_pairs={{0,16},{8,24},{16,0},{24,8},{1,17},{9,25},{17,1},{25,9},{2,18},{10... | collective-permute-start | bytes 1572872 | tf_op jit(solution)/shard_map/ppermute | solution.py:501
  66.2 2.1 collective-permute-start.8
  69.7 7.0 %collective-permute-done.6.refs_12_ = bf16[1024,256]{1,0:T(8,128)(2,1)} collective-permute-done((bf16[1024,256]{1,0:T(8,128)(2,1)}, bf16[1024,256]{1,0:T(8,128)(2,1)}, u32[]{:S(2)}, u32[]{:S(2)}) %collective-permute-start.6) | collective-permute-done | bytes 524320 | tf_op jit(solution)/shard_map/ppermute | solution.py:504
  76.7 13.9 %collective-permute-done.7.refs_10_ = bf16[1024,256]{1,0:T(8,128)(2,1)} collective-permute-done((bf16[1024,256]{1,0:T(8,128)(2,1)}, bf16[1024,256]{1,0:T(8,128)(2,1)}, u32[]{:S(2)}, u32[]{:S(2)}) %collective-permute-start.7) | collective-permute-done | bytes 524320 | tf_op jit(solution)/shard_map/ppermute | solution.py:501
  90.6 8.2 %collective-permute-done.9.refs_9_ = bf16[1024,256]{1,0:T(8,128)(2,1)} collective-permute-done((bf16[1024,256]{1,0:T(8,128)(2,1)}, bf16[1024,256]{1,0:T(8,128)(2,1)}, u32[]{:S(2)}, u32[]{:S(2)}) %collective-permute-start.9) | collective-permute-done | bytes 524320 | tf_op jit(solution)/shard_map/ppermute | solution.py:498
  98.8 2.0 all-to-all-done.1.refs_13_.refs_14_
  102.8 2.4 collective-permute-start.11
  105.2 4.2 %collective-permute-start.12 = (bf16[1024,256]{1,0:T(8,128)(2,1)}, bf16[1024,256]{1,0:T(8,128)(2,1)}, u32[]{:S(2)}, u32[]{:S(2)}) collective-permute-start(bf16[1024,256]{1,0:T(8,128)(2,1)} %bitcast.8.refs_8_), channel_id=1, source_target_pairs={{0,8},{8,16},{16,24},{1,9},{9,17},{17,25},{2,10},{10,18},{18,26},{... | collective-permute-start | bytes 1572872 | tf_op jit(solution)/shard_map/ppermute | solution.py:498
  113.6 11.1 %fwd.4 = (bf16[4,256,128]{2,1,0:T(8,128)(2,1)}, bf16[1024,1024]{1,0:T(8,128)(2,1)}, bf16[4096,1024]{1,0:T(8,128)(2,1)}) custom-call(s32[35]{0:T(128)} %concatenate.56.tab, bf16[8,256,2048]{2,1,0:T(8,128)(2,1)} %bitcast.28, bf16[8,256,2048]{2,1,0:T(8,128)(2,1)} %bitcast.29, bf16[8,256,2048]{2,1,0:T(8,128)(2,1)} %bitcast.30, bf16[8,256,2048]{2,1,0:T(8,128)(2,1)} %bitcast.31, ...), custom_call_target="tpu_custom_call" | custom-call | flops 1 | bytes 1 | tf_op jit(solution)/shard_map/fwd/pallas_call | solution.py:283
  124.7 21.0 %collective-permute-done.10.refs_12_ = bf16[1024,256]{1,0:T(8,128)(2,1)} collective-permute-done((bf16[1024,256]{1,0:T(8,128)(2,1)}, bf16[1024,256]{1,0:T(8,128)(2,1)}, u32[]{:S(2)}, u32[]{:S(2)}) %collective-permute-start.10) | collective-permute-done | bytes 524320 | tf_op jit(solution)/shard_map/ppermute | solution.py:504
  145.7 2.1 collective-permute-start.14
  147.9 1.3 collective-permute-start.18
  149.2 11.0 %fwd.5 = (bf16[4,256,128]{2,1,0:T(8,128)(2,1)}, bf16[1024,1024]{1,0:T(8,128)(2,1)}, bf16[4096,1024]{1,0:T(8,128)(2,1)}) custom-call(s32[35]{0:T(128)} %concatenate.56.tab, bf16[8,256,2048]{2,1,0:T(8,128)(2,1)} %bitcast.43, bf16[8,256,2048]{2,1,0:T(8,128)(2,1)} %bitcast.37, ...), custom_call_target="tpu_custom_call", output_to_operand_aliasing={{1}: (16, {}), {2}: (17, {})} | custom-call | flops 1 | bytes 1 | tf_op jit(solution)/shard_map/fwd/pallas_call | solution.py:283
  160.1 6.3 %collective-permute-start.16 = (bf16[1024,256]{1,0:T(8,128)(2,1)}, bf16[1024,256]{1,0:T(8,128)(2,1)S(1)}, u32[]{:S(2)}, u32[]{:S(2)}) collective-permute-start(bf16[1024,256]{1,0:T(8,128)(2,1)} %bitcast.9.refs_8_), channel_id=1, source_target_pairs={{0,8},{8,16},{16,24},{1,9},{9,17},{17,25},{2,10},{10,18},{18,26},{... | collective-permute-start | bytes 1572872 | tf_op jit(solution)/shard_map/ppermute | solution.py:498
  167.7 1.8 pad_maximum_fusion.1
  169.6 3.7 %all-to-all-start.2 = ((bf16[4,256,256]{2,1,0:T(8,128)(2,1)}), bf16[4,256,256]{2,1,0:T(8,128)(2,1)S(1)}, u32[]{:S(2)}, u32[]{:S(2)}) async-start(bf16[4,256,256]{2,1,0:T(8,128)(2,1)} %pad_maximum_fusion.1), calls=%async_computation.2 | async-start | bytes 1048576 | tf_op jit(solution)/shard_map/all_to_all | solution.py:495
  173.2 2.7 collective-permute-done.18.refs_12_
  176.7 11.1 %fwd.6 = (bf16[4,256,128]{2,1,0:T(8,128)(2,1)}, bf16[1024,1024]{1,0:T(8,128)(2,1)}, bf16[4096,1024]{1,0:T(8,128)(2,1)}) custom-call(s32[35]{0:T(128)} %concatenate.56.tab, bf16[8,256,2048]{2,1,0:T(8,128)(2,1)} %bitcast.44, bf16[8,256,2048]{2,1,0:T(8,128)(2,1)} %bitcast.45, ...), custom_call_target="tpu_custom_call", output_to_operand_aliasing={{1}: (16, {}), {2}: (17, {})} | custom-call | flops 1 | bytes 1 | tf_op jit(solution)/shard_map/fwd/pallas_call | solution.py:283
  187.9 7.1 %collective-permute-done.17.refs_9_ = bf16[1024,256]{1,0:T(8,128)(2,1)S(1)} collective-permute-done((bf16[1024,256]{1,0:T(8,128)(2,1)}, bf16[1024,256]{1,0:T(8,128)(2,1)S(1)}, u32[]{:S(2)}, u32[]{:S(2)}) %collective-permute-start.17) | collective-permute-done | bytes 524320 | tf_op jit(solution)/shard_map/ppermute | solution.py:498
  195.7 11.1 %fwd.7 = (bf16[4,256,128]{2,1,0:T(8,128)(2,1)}, bf16[1024,1024]{1,0:T(8,128)(2,1)}, bf16[4096,1024]{1,0:T(8,128)(2,1)}) custom-call(s32[35]{0:T(128)} %concatenate.56.tab, bf16[8,256,2048]{2,1,0:T(8,128)(2,1)} %bitcast.52, bf16[8,256,2048]{2,1,0:T(8,128)(2,1)} %bitcast.53, ...), custom_call_target="tpu_custom_call", output_to_operand_aliasing={{1}: (16, {}), {2}: (17, {})} | custom-call | flops 1 | bytes 1 | tf_op jit(solution)/shard_map/fwd/pallas_call | solution.py:283
  206.8 5.5 %bwd.8 = bf16[512,2048]{1,0:T(8,128)(2,1)} custom-call(bf16[1024,1024]{1,0:T(8,128)(2,1)} %get-tuple-element.150.refs_0_, bf16[4096,1024]{1,0:T(8,128)(2,1)} %get-tuple-element.151.refs_1_), custom_call_target="tpu_custom_call" | custom-call | flops 1 | bytes 1 | tf_op jit(solution)/shard_map/bwd/pallas_call | solution.py:345
  212.3 5.6 %bwd.6 = bf16[512,2048]{1,0:T(8,128)(2,1)} custom-call(bf16[1024,1024]{1,0:T(8,128)(2,1)} %get-tuple-element.150.refs_0_, bf16[4096,1024]{1,0:T(8,128)(2,1)} %get-tuple-element.151.refs_1_), custom_call_target="tpu_custom_call" | custom-call | flops 1 | bytes 1 | tf_op jit(solution)/shard_map/bwd/pallas_call | solution.py:345
  218.8 1.5 collective-permute-start.22
  221.2 1.4 copy-done.3
  222.5 4.4 %bwd.9 = bf16[512,1024]{1,0:T(8,128)(2,1)} custom-call(bf16[1024,1024]{1,0:T(8,128)(2,1)} %get-tuple-element.150.refs_0_, bf16[4096,1024]{1,0:T(8,128)(2,1)} %get-tuple-element.151.refs_1_, bf16[512,2048]{1,0:T(8,128)(2,1)} %copy-done.3), custom_call_target="tpu_custom_call" | custom-call | flops 1 | bytes 1 | tf_op jit(solution)/shard_map/bwd/pallas_call | solution.py:345
  227.0 4.2 %bwd.7 = bf16[256,2048]{1,0:T(8,128)(2,1)} custom-call(bf16[1024,1024]{1,0:T(8,128)(2,1)} %get-tuple-element.150.refs_0_, bf16[4096,1024]{1,0:T(8,128)(2,1)} %get-tuple-element.151.refs_1_, bf16[512,2048]{1,0:T(8,128)(2,1)} %collective-permute-done.19.refs_2_), custom_call_target="tpu_custom_call" | custom-call | flops 1 | bytes 1 | tf_op jit(solution)/shard_map/bwd/pallas_call | solution.py:345
  231.9 1.6 collective-permute-start.25
  233.5 3.6 %gather_context.1 = bf16[256,2048]{1,0:T(8,128)(2,1)} custom-call(s32[1]{0:T(128)} %bitcast.7.tab, bf16[4,256,256]{2,1,0:T(8,128)(2,1)} %copy-done.8, bf16[256,256]{1,0:T(8,128)(2,1)} %pad_maximum_fusion.5.refs_0_, bf16[256,256]{1,0:T(8,128)(2,1)} %copy-done.25, bf16[256,256]{1,0:T(8,128)(2,1)} %copy-done.24, bf16[256,256]{1,0:T(8,128)(2,1)} %copy-done.23), custom_call_target="tpu_custom_call" | custom-call | flops 1 | bytes 1 | tf_op jit(solution)/shard_map/gather_context/pallas_call | solution.py:449
  237.1 4.8 %bwd.11.q_ref = f32[512,1024]{1,0:T(8,128)} custom-call(bf16[1024,1024]{1,0:T(8,128)(2,1)} %get-tuple-element.150.refs_0_, bf16[4096,1024]{1,0:T(8,128)(2,1)} %get-tuple-element.151.refs_1_, bf16[512,2048]{1,0:T(8,128)(2,1)} %copy-done.3), custom_call_target="tpu_custom_call" | custom-call | flops 1 | bytes 1 | tf_op jit(solution)/shard_map/bwd/pallas_call | solution.py:345
  241.9 4.5 %bwd.10.p_ref = f32[256,2048]{1,0:T(8,128)} custom-call(bf16[1024,1024]{1,0:T(8,128)(2,1)} %get-tuple-element.150.refs_0_, bf16[4096,1024]{1,0:T(8,128)(2,1)} %get-tuple-element.151.refs_1_, bf16[512,2048]{1,0:T(8,128)(2,1)} %collective-permute-done.19.refs_2_), custom_call_target="tpu_custom_call" | custom-call | flops 1 | bytes 1 | tf_op jit(solution)/shard_map/bwd/pallas_call | solution.py:345
  246.5 10.5 %collective-permute-done.24.got_y = bf16[256,2048]{1,0:T(8,128)(2,1)S(1)} collective-permute-done((bf16[256,2048]{1,0:T(8,128)(2,1)}, bf16[256,2048]{1,0:T(8,128)(2,1)S(1)}, u32[]{:S(2)}, u32[]{:S(2)}) %collective-permute-start.24) | collective-permute-done | bytes 1048608 | tf_op jit(solution)/shard_map/ppermute | solution.py:607
  257.2 1.5 collective-permute-start.27
  258.9 1.5 collective-permute-start.26
  260.4 10.2 %collective-permute-done.27.last_y = bf16[256,1024]{1,0:T(8,128)(2,1)S(1)} collective-permute-done((bf16[256,1024]{1,0:T(8,128)(2,1)S(1)}, bf16[256,1024]{1,0:T(8,128)(2,1)S(1)}, u32[]{:S(2)}, u32[]{:S(2)}) %collective-permute-start.27) | collective-permute-done | bytes 524320 | tf_op jit(solution)/shard_map/ppermute | solution.py:618
  272.5 3.1 %finish.1 = bf16[256,2048]{1,0:T(8,128)(2,1)} custom-call(f32[256,2048]{1,0:T(8,128)} %bwd.10.p_ref, bf16[256,2048]{1,0:T(8,128)(2,1)} %copy-done.4, bf16[256,1024]{1,0:T(8,128)(2,1)} %copy-done.19, f32[512,1024]{1,0:T(8,128)} %bwd.11.q_ref, bf16[512,1024]{1,0:T(8,128)(2,1)} %copy-done.5, bf16[256,1024]{1,0:T(8,128)(2,1)} %copy-done.18), custom_call_target="tpu_custom_call" | custom-call | flops 1 | bytes 1 | tf_op jit(solution)/shard_map/finish/pallas_call | solution.py:371
  (123 shorter events, 19.6 us)
Async XLA Ops:
  7.2 93.6 %all-gather.3.cloned.1.call-start = ((), (), s32[]{:S(2)}) async-start(), calls=%async_computation.3 | async-start | bytes 9437184 | tf_op jit(solution)/shard_map/all_gather | solution.py:517
  9.1 3.3 %collective-permute-start = (bf16[256,256]{1,0:T(8,128)(2,1)S(1)}, bf16[256,256]{1,0:T(8,128)(2,1)S(1)}, u32[]{:S(2)}, u32[]{:S(2)}) collective-permute-start(bf16[256,256]{1,0:T(8,128)(2,1)S(1)} %pad_maximum_fusion.2), channel_id=1, source_target_pairs={{0,2},{2,0},{4,6},{6,4},{1,3},{3,1},{5,7},{7,5},{8,10},{10,8},{12,... | collective-permute-start | bytes 393224 | tf_op jit(solution)/shard_map/ppermute | solution.py:515
  9.6 6.9 %collective-permute-start.1 = (bf16[256,256]{1,0:T(8,128)(2,1)S(1)}, bf16[256,256]{1,0:T(8,128)(2,1)S(1)}, u32[]{:S(2)}, u32[]{:S(2)}) collective-permute-start(bf16[256,256]{1,0:T(8,128)(2,1)S(1)} %pad_maximum_fusion.3), channel_id=1, source_target_pairs={{0,4},{2,6},{4,0},{6,2},{1,5},{3,7},{5,1},{7,3},{8,12},{10,14},{12... | collective-permute-start | bytes 393224 | tf_op jit(solution)/shard_map/ppermute | solution.py:515
  12.2 6.7 %collective-permute-start.2 = (bf16[256,256]{1,0:T(8,128)(2,1)S(1)}, bf16[256,256]{1,0:T(8,128)(2,1)S(1)}, u32[]{:S(2)}, u32[]{:S(2)}) collective-permute-start(bf16[256,256]{1,0:T(8,128)(2,1)S(1)} %pad_maximum_fusion.4), channel_id=1, source_target_pairs={{0,6},{2,4},{4,2},{6,0},{1,7},{3,5},{5,3},{7,1},{8,14},{10,12},{12... | collective-permute-start | bytes 393224 | tf_op jit(solution)/shard_map/ppermute | solution.py:515
  19.0 19.2 %copy-start.7 = (bf16[1024,256]{1,0:T(8,128)(2,1)}, bf16[1024,256]{1,0:T(8,128)(2,1)S(1)}, u32[]{:S(2)}) copy-start(bf16[1024,256]{1,0:T(8,128)(2,1)S(1)} %pad_maximum_fusion.refs_8_) | copy-start | bytes 1572868
  19.0 14.1 %copy-start.28 = (s32[1,4]{1,0:T(1,128)S(1)}, s32[1,4]{1,0:T(1,128)}, u32[]{:S(2)}) copy-start(s32[1,4]{1,0:T(1,128)} %param.11) | copy-start | bytes 52
  19.0 14.1 %copy-start.26 = (s32[4]{0:T(128)S(1)}, s32[4]{0:T(128)}, u32[]{:S(2)}) copy-start(s32[4]{0:T(128)} %param.10) | copy-start | bytes 52
  19.1 14.1 %copy-start.27 = (s32[4]{0:T(128)S(1)}, s32[4]{0:T(128)}, u32[]{:S(2)}) copy-start(s32[4]{0:T(128)} %param.9) | copy-start | bytes 52
  19.1 27.0 %collective-permute-start.3 = (bf16[1024,256]{1,0:T(8,128)(2,1)S(1)}, bf16[1024,256]{1,0:T(8,128)(2,1)S(1)}, u32[]{:S(2)}, u32[]{:S(2)}) collective-permute-start(bf16[1024,256]{1,0:T(8,128)(2,1)S(1)} %pad_maximum_fusion.refs_8_), channel_id=1, source_target_pairs={{0,16},{8,24},{16,0},{24,8},{1,17},{9,25},{17,1},{25,9},{2,18},{10... | collective-permute-start | bytes 1572872 | tf_op jit(solution)/shard_map/ppermute | solution.py:501
  21.7 24.3 %collective-permute-start.4 = (bf16[1024,256]{1,0:T(8,128)(2,1)S(1)}, bf16[1024,256]{1,0:T(8,128)(2,1)S(1)}, u32[]{:S(2)}, u32[]{:S(2)}) collective-permute-start(bf16[1024,256]{1,0:T(8,128)(2,1)S(1)} %pad_maximum_fusion.refs_8_), channel_id=1, source_target_pairs={{0,8},{8,16},{16,24},{1,9},{9,17},{17,25},{2,10},{10,18},{18,26},{... | collective-permute-start | bytes 1572872 | tf_op jit(solution)/shard_map/ppermute | solution.py:498
  25.2 25.5 %collective-permute-start.5 = (bf16[1024,256]{1,0:T(8,128)(2,1)S(1)}, bf16[1024,256]{1,0:T(8,128)(2,1)S(1)}, u32[]{:S(2)}, u32[]{:S(2)}) collective-permute-start(bf16[1024,256]{1,0:T(8,128)(2,1)S(1)} %pad_maximum_fusion.refs_8_), channel_id=1, source_target_pairs={{8,0},{16,8},{24,16},{9,1},{17,9},{25,17},{10,2},{18,10},{26,18},{... | collective-permute-start | bytes 1572872 | tf_op jit(solution)/shard_map/ppermute | solution.py:498
  29.7 21.0 %all-to-all-start = ((bf16[4,256,256]{2,1,0:T(8,128)(2,1)}), bf16[4,256,256]{2,1,0:T(8,128)(2,1)S(1)}, u32[]{:S(2)}, u32[]{:S(2)}) async-start(bf16[4,256,256]{2,1,0:T(8,128)(2,1)} %pack_weights.1), calls=%async_computation | async-start | bytes 1048576 | tf_op jit(solution)/shard_map/all_to_all | solution.py:495
  46.1 4.6 %copy-start.11 = (bf16[1024,256]{1,0:T(8,128)(2,1)}, bf16[1024,256]{1,0:T(8,128)(2,1)S(1)}, u32[]{:S(2)}) copy-start(bf16[1024,256]{1,0:T(8,128)(2,1)S(1)} %collective-permute-done.4.refs_11_) | copy-start | bytes 1572868
  51.7 49.1 %all-to-all-start.1 = ((bf16[4,272,1536]{2,1,0:T(8,128)(2,1)}), bf16[4,272,1536]{2,1,0:T(8,128)(2,1)S(1)}, u32[]{:S(2)}, u32[]{:S(2)}) async-start(bf16[4,272,1536]{2,1,0:T(8,128)(2,1)} %pack.1), calls=%async_computation.1 | async-start | bytes 6684672 | tf_op jit(solution)/shard_map/all_to_all | solution.py:495
  55.4 21.3 %collective-permute-start.6 = (bf16[1024,256]{1,0:T(8,128)(2,1)}, bf16[1024,256]{1,0:T(8,128)(2,1)}, u32[]{:S(2)}, u32[]{:S(2)}) collective-permute-start(bf16[1024,256]{1,0:T(8,128)(2,1)} %copy-done.10), channel_id=1, source_target_pairs={{8,0},{16,24},{9,1},{17,25},{10,2},{18,26},{11,3},{19,27},{12,4},{... | collective-permute-start | bytes 1572872 | tf_op jit(solution)/shard_map/ppermute | solution.py:504
  56.7 33.9 %collective-permute-start.7 = (bf16[1024,256]{1,0:T(8,128)(2,1)}, bf16[1024,256]{1,0:T(8,128)(2,1)}, u32[]{:S(2)}, u32[]{:S(2)}) collective-permute-start(bf16[1024,256]{1,0:T(8,128)(2,1)} %bitcast.60), channel_id=1, source_target_pairs={{0,16},{8,24},{16,0},{24,8},{1,17},{9,25},{17,1},{25,9},{2,18},{10... | collective-permute-start | bytes 1572872 | tf_op jit(solution)/shard_map/ppermute | solution.py:501
  66.2 24.3 %collective-permute-start.8 = (bf16[1024,256]{1,0:T(8,128)(2,1)}, bf16[1024,256]{1,0:T(8,128)(2,1)}, u32[]{:S(2)}, u32[]{:S(2)}) collective-permute-start(bf16[1024,256]{1,0:T(8,128)(2,1)} %bitcast.61), channel_id=1, source_target_pairs={{0,8},{8,16},{16,24},{1,9},{9,17},{17,25},{2,10},{10,18},{18,26},{... | collective-permute-start | bytes 1572872 | tf_op jit(solution)/shard_map/ppermute | solution.py:498
  68.3 30.4 %collective-permute-start.9 = (bf16[1024,256]{1,0:T(8,128)(2,1)}, bf16[1024,256]{1,0:T(8,128)(2,1)}, u32[]{:S(2)}, u32[]{:S(2)}) collective-permute-start(bf16[1024,256]{1,0:T(8,128)(2,1)} %bitcast.62), channel_id=1, source_target_pairs={{8,0},{16,8},{24,16},{9,1},{17,9},{25,17},{10,2},{18,10},{26,18},{... | collective-permute-start | bytes 1572872 | tf_op jit(solution)/shard_map/ppermute | solution.py:498
  100.8 12.8 %copy-start = (bf16[4,272,1536]{2,1,0:T(8,128)(2,1)}, bf16[4,272,1536]{2,1,0:T(8,128)(2,1)S(1)}, u32[]{:S(2)}) copy-start(bf16[4,272,1536]{2,1,0:T(8,128)(2,1)S(1)} %all-to-all-done.1.refs_13_.refs_14_) | copy-start | bytes 10027012
  102.8 42.9 %collective-permute-start.11 = (bf16[1024,256]{1,0:T(8,128)(2,1)}, bf16[1024,256]{1,0:T(8,128)(2,1)}, u32[]{:S(2)}, u32[]{:S(2)}) collective-permute-start(bf16[1024,256]{1,0:T(8,128)(2,1)} %bitcast.8.refs_8_), channel_id=1, source_target_pairs={{0,16},{8,24},{16,0},{24,8},{1,17},{9,25},{17,1},{25,9},{2,18},{10... | collective-permute-start | bytes 1572872 | tf_op jit(solution)/shard_map/ppermute | solution.py:501
  105.2 40.5 %collective-permute-start.12 = (bf16[1024,256]{1,0:T(8,128)(2,1)}, bf16[1024,256]{1,0:T(8,128)(2,1)}, u32[]{:S(2)}, u32[]{:S(2)}) collective-permute-start(bf16[1024,256]{1,0:T(8,128)(2,1)} %bitcast.8.refs_8_), channel_id=1, source_target_pairs={{0,8},{8,16},{16,24},{1,9},{9,17},{17,25},{2,10},{10,18},{18,26},{... | collective-permute-start | bytes 1572872 | tf_op jit(solution)/shard_map/ppermute | solution.py:498
  109.5 36.2 %collective-permute-start.13 = (bf16[1024,256]{1,0:T(8,128)(2,1)}, bf16[1024,256]{1,0:T(8,128)(2,1)}, u32[]{:S(2)}, u32[]{:S(2)}) collective-permute-start(bf16[1024,256]{1,0:T(8,128)(2,1)} %bitcast.8.refs_8_), channel_id=1, source_target_pairs={{8,0},{16,8},{24,16},{9,1},{17,9},{25,17},{10,2},{18,10},{26,18},{... | collective-permute-start | bytes 1572872 | tf_op jit(solution)/shard_map/ppermute | solution.py:498
  110.7 34.9 %collective-permute-start.10 = (bf16[1024,256]{1,0:T(8,128)(2,1)}, bf16[1024,256]{1,0:T(8,128)(2,1)}, u32[]{:S(2)}, u32[]{:S(2)}) collective-permute-start(bf16[1024,256]{1,0:T(8,128)(2,1)} %collective-permute-done.7.refs_10_), channel_id=1, source_target_pairs={{8,0},{16,24},{9,1},{17,25},{10,2},{18,26},{11,3},{19,27},{12,4},{... | collective-permute-start | bytes 1572872 | tf_op jit(solution)/shard_map/ppermute | solution.py:504
  145.7 22.0 %copy-start.22 = (bf16[4,256,128]{2,1,0:T(8,128)(2,1)S(1)}, bf16[4,256,128]{2,1,0:T(8,128)(2,1)}, u32[]{:S(2)}) copy-start(bf16[4,256,128]{2,1,0:T(8,128)(2,1)} %get-tuple-element.136) | copy-start | bytes 786436
  145.7 42.1 %collective-permute-start.14 = (bf16[1024,256]{1,0:T(8,128)(2,1)}, bf16[1024,256]{1,0:T(8,128)(2,1)S(1)}, u32[]{:S(2)}, u32[]{:S(2)}) collective-permute-start(bf16[1024,256]{1,0:T(8,128)(2,1)} %bitcast.9.refs_8_), channel_id=1, source_target_pairs={{0,24},{24,0},{1,25},{25,1},{2,26},{26,2},{3,27},{27,3},{4,28},{28... | collective-permute-start | bytes 1572872 | tf_op jit(solution)/shard_map/ppermute | solution.py:576
  147.8 40.0 %collective-permute-start.15 = (bf16[1024,256]{1,0:T(8,128)(2,1)}, bf16[1024,256]{1,0:T(8,128)(2,1)S(1)}, u32[]{:S(2)}, u32[]{:S(2)}) collective-permute-start(bf16[1024,256]{1,0:T(8,128)(2,1)} %bitcast.9.refs_8_), channel_id=1, source_target_pairs={{0,16},{8,24},{16,0},{24,8},{1,17},{9,25},{17,1},{25,9},{2,18},{10... | collective-permute-start | bytes 1572872 | tf_op jit(solution)/shard_map/ppermute | solution.py:501
  147.9 28.1 %collective-permute-start.18 = (bf16[1024,256]{1,0:T(8,128)(2,1)}, bf16[1024,256]{1,0:T(8,128)(2,1)S(1)}, u32[]{:S(2)}, u32[]{:S(2)}) collective-permute-start(bf16[1024,256]{1,0:T(8,128)(2,1)} %collective-permute-done.11.refs_10_), channel_id=1, source_target_pairs={{8,0},{16,24},{9,1},{17,25},{10,2},{18,26},{11,3},{19,27},{12,4},{... | collective-permute-start | bytes 1572872 | tf_op jit(solution)/shard_map/ppermute | solution.py:504
  160.1 27.7 %collective-permute-start.16 = (bf16[1024,256]{1,0:T(8,128)(2,1)}, bf16[1024,256]{1,0:T(8,128)(2,1)S(1)}, u32[]{:S(2)}, u32[]{:S(2)}) collective-permute-start(bf16[1024,256]{1,0:T(8,128)(2,1)} %bitcast.9.refs_8_), channel_id=1, source_target_pairs={{0,8},{8,16},{16,24},{1,9},{9,17},{17,25},{2,10},{10,18},{18,26},{... | collective-permute-start | bytes 1572872 | tf_op jit(solution)/shard_map/ppermute | solution.py:498
  166.4 28.5 %collective-permute-start.17 = (bf16[1024,256]{1,0:T(8,128)(2,1)}, bf16[1024,256]{1,0:T(8,128)(2,1)S(1)}, u32[]{:S(2)}, u32[]{:S(2)}) collective-permute-start(bf16[1024,256]{1,0:T(8,128)(2,1)} %bitcast.9.refs_8_), channel_id=1, source_target_pairs={{8,0},{16,8},{24,16},{9,1},{17,9},{25,17},{10,2},{18,10},{26,18},{... | collective-permute-start | bytes 1572872 | tf_op jit(solution)/shard_map/ppermute | solution.py:498
  169.6 25.4 %all-to-all-start.2 = ((bf16[4,256,256]{2,1,0:T(8,128)(2,1)}), bf16[4,256,256]{2,1,0:T(8,128)(2,1)S(1)}, u32[]{:S(2)}, u32[]{:S(2)}) async-start(bf16[4,256,256]{2,1,0:T(8,128)(2,1)} %pad_maximum_fusion.1), calls=%async_computation.2 | async-start | bytes 1048576 | tf_op jit(solution)/shard_map/all_to_all | solution.py:495
  187.8 7.1 %copy-start.13 = (bf16[1024,256]{1,0:T(8,128)(2,1)}, bf16[1024,256]{1,0:T(8,128)(2,1)S(1)}, u32[]{:S(2)}) copy-start(bf16[1024,256]{1,0:T(8,128)(2,1)S(1)} %collective-permute-done.14.refs_12_) | copy-start | bytes 1572868
  187.8 7.1 %copy-start.14 = (bf16[1024,256]{1,0:T(8,128)(2,1)}, bf16[1024,256]{1,0:T(8,128)(2,1)S(1)}, u32[]{:S(2)}) copy-start(bf16[1024,256]{1,0:T(8,128)(2,1)S(1)} %collective-permute-done.15.refs_10_) | copy-start | bytes 1572868
  187.8 7.1 %copy-start.15 = (bf16[1024,256]{1,0:T(8,128)(2,1)}, bf16[1024,256]{1,0:T(8,128)(2,1)S(1)}, u32[]{:S(2)}) copy-start(bf16[1024,256]{1,0:T(8,128)(2,1)S(1)} %collective-permute-done.16.refs_11_) | copy-start | bytes 1572868
  194.9 11.9 %copy-start.8 = (bf16[4,256,256]{2,1,0:T(8,128)(2,1)}, bf16[4,256,256]{2,1,0:T(8,128)(2,1)S(1)}, u32[]{:S(2)}) copy-start(bf16[4,256,256]{2,1,0:T(8,128)(2,1)S(1)} %all-to-all-done.2.early) | copy-start | bytes 1572868
  212.3 6.0 %copy-start.21 = (bf16[4,256,128]{2,1,0:T(8,128)(2,1)S(1)}, bf16[4,256,128]{2,1,0:T(8,128)(2,1)}, u32[]{:S(2)}) copy-start(bf16[4,256,128]{2,1,0:T(8,128)(2,1)} %get-tuple-element.147) | copy-start | bytes 786436
  212.3 6.0 %copy-start.20 = (bf16[4,256,128]{2,1,0:T(8,128)(2,1)S(1)}, bf16[4,256,128]{2,1,0:T(8,128)(2,1)}, u32[]{:S(2)}) copy-start(bf16[4,256,128]{2,1,0:T(8,128)(2,1)} %get-tuple-element.146) | copy-start | bytes 786436
  212.3 8.9 %collective-permute-start.20 = (bf16[512,2048]{1,0:T(8,128)(2,1)}, bf16[512,2048]{1,0:T(8,128)(2,1)S(1)}, u32[]{:S(2)}, u32[]{:S(2)}) collective-permute-start(bf16[512,2048]{1,0:T(8,128)(2,1)} %bwd.8), channel_id=1, source_target_pairs={{0,2},{2,0},{4,6},{6,4},{1,3},{3,1},{5,7},{7,5},{8,10},{10,8},{12,... | collective-permute-start | bytes 6291464 | tf_op jit(solution)/shard_map/ppermute | solution.py:492
  217.9 9.1 %collective-permute-start.19 = (bf16[512,2048]{1,0:T(8,128)(2,1)}, bf16[512,2048]{1,0:T(8,128)(2,1)}, u32[]{:S(2)}, u32[]{:S(2)}) collective-permute-start(bf16[512,2048]{1,0:T(8,128)(2,1)} %bwd.6), channel_id=1, source_target_pairs={{0,2},{2,0},{4,6},{6,4},{1,3},{3,1},{5,7},{7,5},{8,10},{10,8},{12,... | collective-permute-start | bytes 6291464 | tf_op jit(solution)/shard_map/ppermute | solution.py:492
  218.4 12.8 %collective-permute-start.23 = (bf16[256,256]{1,0:T(8,128)(2,1)S(1)}, bf16[256,256]{1,0:T(8,128)(2,1)S(1)}, u32[]{:S(2)}, u32[]{:S(2)}) collective-permute-start(bf16[256,256]{1,0:T(8,128)(2,1)S(1)} %pad_maximum_fusion.8), channel_id=1, source_target_pairs={{0,6},{2,4},{4,2},{6,0},{1,7},{3,5},{5,3},{7,1},{8,14},{10,12},{12... | collective-permute-start | bytes 393224 | tf_op jit(solution)/shard_map/ppermute | solution.py:592
  218.8 12.5 %collective-permute-start.22 = (bf16[256,256]{1,0:T(8,128)(2,1)S(1)}, bf16[256,256]{1,0:T(8,128)(2,1)S(1)}, u32[]{:S(2)}, u32[]{:S(2)}) collective-permute-start(bf16[256,256]{1,0:T(8,128)(2,1)S(1)} %pad_maximum_fusion.7), channel_id=1, source_target_pairs={{0,4},{2,6},{4,0},{6,2},{1,5},{3,7},{5,1},{7,3},{8,12},{10,14},{12... | collective-permute-start | bytes 393224 | tf_op jit(solution)/shard_map/ppermute | solution.py:592
  220.3 11.0 %collective-permute-start.21 = (bf16[256,256]{1,0:T(8,128)(2,1)S(1)}, bf16[256,256]{1,0:T(8,128)(2,1)S(1)}, u32[]{:S(2)}, u32[]{:S(2)}) collective-permute-start(bf16[256,256]{1,0:T(8,128)(2,1)S(1)} %pad_maximum_fusion.6), channel_id=1, source_target_pairs={{0,2},{2,0},{4,6},{6,4},{1,3},{3,1},{5,7},{7,5},{8,10},{10,8},{12,... | collective-permute-start | bytes 393224 | tf_op jit(solution)/shard_map/ppermute | solution.py:592
  227.0 5.0 %copy-start.9 = (bf16[512,1024]{1,0:T(8,128)(2,1)S(1)}, bf16[512,1024]{1,0:T(8,128)(2,1)}, u32[]{:S(2)}) copy-start(bf16[512,1024]{1,0:T(8,128)(2,1)} %bwd.9) | copy-start | bytes 3145732
  231.3 25.7 %collective-permute-start.24 = (bf16[256,2048]{1,0:T(8,128)(2,1)}, bf16[256,2048]{1,0:T(8,128)(2,1)S(1)}, u32[]{:S(2)}, u32[]{:S(2)}) collective-permute-start(bf16[256,2048]{1,0:T(8,128)(2,1)} %bwd.7), channel_id=1, source_target_pairs={{0,4},{2,6},{4,0},{6,2},{1,5},{3,7},{5,1},{7,3},{8,12},{10,14},{12... | collective-permute-start | bytes 3145736 | tf_op jit(solution)/shard_map/ppermute | solution.py:607
  231.9 25.1 %collective-permute-start.25 = (bf16[512,1024]{1,0:T(8,128)(2,1)S(1)}, bf16[512,1024]{1,0:T(8,128)(2,1)S(1)}, u32[]{:S(2)}, u32[]{:S(2)}) collective-permute-start(bf16[512,1024]{1,0:T(8,128)(2,1)S(1)} %copy-done.9), channel_id=1, source_target_pairs={{0,1},{1,0},{2,3},{3,2},{4,5},{5,4},{6,7},{7,6},{8,9},{9,8},{10,11... | collective-permute-start | bytes 3145736 | tf_op jit(solution)/shard_map/ppermute | solution.py:608
  241.9 15.1 %copy-start.1 = (f32[512,1024]{1,0:T(8,128)S(1)}, f32[512,1024]{1,0:T(8,128)}, u32[]{:S(2)}) copy-start(f32[512,1024]{1,0:T(8,128)} %bwd.11.q_ref) | copy-start | bytes 6291460
  246.4 12.3 %copy-start.2 = (f32[256,2048]{1,0:T(8,128)S(1)}, f32[256,2048]{1,0:T(8,128)}, u32[]{:S(2)}) copy-start(f32[256,2048]{1,0:T(8,128)} %bwd.10.p_ref) | copy-start | bytes 6291460
  257.2 13.3 %collective-permute-start.27 = (bf16[256,1024]{1,0:T(8,128)(2,1)S(1)}, bf16[256,1024]{1,0:T(8,128)(2,1)S(1)}, u32[]{:S(2)}, u32[]{:S(2)}) collective-permute-start(bf16[256,1024]{1,0:T(8,128)(2,1)S(1)} %add_convert_fusion), channel_id=1, source_target_pairs={{0,4},{2,6},{4,0},{6,2},{1,5},{3,7},{5,1},{7,3},{8,12},{10,14},{12... | collective-permute-start | bytes 1572872 | tf_op jit(solution)/shard_map/ppermute | solution.py:618
  258.9 12.8 %collective-permute-start.26 = (bf16[256,1024]{1,0:T(8,128)(2,1)S(1)}, bf16[256,1024]{1,0:T(8,128)(2,1)S(1)}, u32[]{:S(2)}, u32[]{:S(2)}) collective-permute-start(bf16[256,1024]{1,0:T(8,128)(2,1)S(1)} %add_convert_fusion.1), channel_id=1, source_target_pairs={{0,1},{1,0},{2,3},{3,2},{4,5},{5,4},{6,7},{7,6},{8,9},{9,8},{10,11... | collective-permute-start | bytes 1572872 | tf_op jit(solution)/shard_map/ppermute | solution.py:617
  (13 other events, 21.9 us)
Sparse Core Ops, SparseCore 0:
  9.9 63.5 all-gather.2

commit v6 on v5

--- a/solution.py
+++ b/solution.py
@@ -374,7 +374,7 @@
         in_specs=[block] * 6,
         out_specs=pl.BlockSpec((rows // tiles, 2 * span), lambda i: (i, 0)),
         out_shape=jax.ShapeDtypeStruct((rows, 2 * span), BF16),
-        compiler_params=pltpu.CompilerParams(vmem_limit_bytes=VMEM),
+        compiler_params=pltpu.CompilerParams(vmem_limit_bytes=16 << 20),
         cost_estimate=SHORT,
         name="finish",
     )(*operands)

time: 284 us -> 281 us (0.989)
  no operation moved by 1% of the time
where the time goes in v6:
time: 281 us; the launch traced here: 280 us
  waiting for transfers between devices  104 us (37%)
  Pallas kernels  85.3 us (30%)
  starting transfers between devices  63.8 us (23%)
  between operations  14.5 us (5%)
  local copies, waits for them, and re-layouts  7.12 us (3%)
  other arithmetic  5.23 us (2%)
    pallas_call x4, Pallas kernels, forward_chunk(): pl.pallas_call(functools.partial(forward_kernel, n_dp, n_sec, n_half, blk...  44 us
    ppermute x3, waiting for transfers between devices, turn(): return lax.ppermute(far, 'section', ends)  30.8 us
    pallas_call x6, Pallas kernels, backward(): pl.pallas_call(backward_kernel, grid=(len(blocks) * per_block,), in_specs...  29 us
    ppermute x4, waiting for transfers between devices, beyond(): return lax.ppermute(piece, 'section', over_two)  21.8 us
    ppermute x4, waiting for transfers between devices, sides(): lax.ppermute(piece, 'section', down)  19.9 us
    ppermute x4, starting transfers between devices, sides(): lax.ppermute(piece, 'section', up)  16.1 us
    ppermute x4, starting transfers between devices, beyond(): return lax.ppermute(piece, 'section', over_two)  14.7 us
    all_to_all x3, starting transfers between devices, exchange(): return lax.all_to_all(x, 'dp', split_axis=0, concat_axis=0, tiled=True)  10.8 us
  transfers between devices with their start and end apart: 32, of which 15 were waited for; matrix products, arithmetic and copies ran while one was open for 2% of the time, Pallas kernels for 24%

profile of v6, /device:TPU:0, one launch (start us, length us, event | category | flops | bytes accessed | tf_op | source)
XLA Modules:
  0.0 279.8 jit_solution(51290868536028476)
XLA Ops:
  9.6 2.6 collective-permute-start.1
  12.4 4.1 %collective-permute-done.1 = bf16[256,256]{1,0:T(8,128)(2,1)S(1)} collective-permute-done((bf16[256,256]{1,0:T(8,128)(2,1)S(1)}, bf16[256,256]{1,0:T(8,128)(2,1)S(1)}, u32[]{:S(2)}, u32[]{:S(2)}) %collective-permute-start.1) | collective-permute-done | bytes 131104 | tf_op jit(solution)/shard_map/ppermute | solution.py:515
  16.6 2.4 collective-permute-done.2
  19.1 2.7 collective-permute-start.3
  21.7 3.5 %collective-permute-start.4 = (bf16[1024,256]{1,0:T(8,128)(2,1)S(1)}, bf16[1024,256]{1,0:T(8,128)(2,1)S(1)}, u32[]{:S(2)}, u32[]{:S(2)}) collective-permute-start(bf16[1024,256]{1,0:T(8,128)(2,1)S(1)} %pad_maximum_fusion.refs_8_), channel_id=1, source_target_pairs={{0,8},{8,16},{16,24},{1,9},{9,17},{17,25},{2,10},{10,18},{18,26},{... | collective-permute-start | bytes 1572872 | tf_op jit(solution)/shard_map/ppermute | solution.py:498
  25.2 1.3 collective-permute-start.5
  26.5 3.1 %pack_weights.1 = bf16[4,256,256]{2,1,0:T(8,128)(2,1)} custom-call(bf16[256,2048]{1,0:T(8,128)(2,1)} %k_ref.1, bf16[256,2048]{1,0:T(8,128)(2,1)} %v_ref.1), custom_call_target="tpu_custom_call" | custom-call | flops 1 | bytes 1 | tf_op jit(solution)/shard_map/pack_weights/pallas_call | solution.py:392
  29.7 3.5 %all-to-all-start = ((bf16[4,256,256]{2,1,0:T(8,128)(2,1)}), bf16[4,256,256]{2,1,0:T(8,128)(2,1)S(1)}, u32[]{:S(2)}, u32[]{:S(2)}) async-start(bf16[4,256,256]{2,1,0:T(8,128)(2,1)} %pack_weights.1), calls=%async_computation | async-start | bytes 1048576 | tf_op jit(solution)/shard_map/all_to_all | solution.py:495
  33.9 4.3 %pack.1 = bf16[4,272,1536]{2,1,0:T(8,128)(2,1)} custom-call(bf16[256,2048]{1,0:T(8,128)(2,1)} %q_ref.1, bf16[256,2048]{1,0:T(8,128)(2,1)} %g_ref.1, bf16[256,2048]{1,0:T(8,128)(2,1)} %k_ref.1, bf16[256,2048]{1,0:T(8,128)(2,1)} %v_ref.1, bf16[16,128]{1,0:T(8,128)(2,1)} %fusion.8.small_ref), custom_call_target="tpu_custom_call" | custom-call | flops 1 | bytes 1 | tf_op jit(solution)/shard_map/pack/pallas_call | solution.py:423
  38.2 7.9 %collective-permute-done.3.refs_10_ = bf16[1024,256]{1,0:T(8,128)(2,1)S(1)} collective-permute-done((bf16[1024,256]{1,0:T(8,128)(2,1)S(1)}, bf16[1024,256]{1,0:T(8,128)(2,1)S(1)}, u32[]{:S(2)}, u32[]{:S(2)}) %collective-permute-start.3) | collective-permute-done | bytes 524320 | tf_op jit(solution)/shard_map/ppermute | solution.py:501
  46.1 4.6 %collective-permute-done.5.refs_9_ = bf16[1024,256]{1,0:T(8,128)(2,1)S(1)} collective-permute-done((bf16[1024,256]{1,0:T(8,128)(2,1)S(1)}, bf16[1024,256]{1,0:T(8,128)(2,1)S(1)}, u32[]{:S(2)}, u32[]{:S(2)}) %collective-permute-start.5) | collective-permute-done | bytes 524320 | tf_op jit(solution)/shard_map/ppermute | solution.py:498
  51.7 3.7 %all-to-all-start.1 = ((bf16[4,272,1536]{2,1,0:T(8,128)(2,1)}), bf16[4,272,1536]{2,1,0:T(8,128)(2,1)S(1)}, u32[]{:S(2)}, u32[]{:S(2)}) async-start(bf16[4,272,1536]{2,1,0:T(8,128)(2,1)} %pack.1), calls=%async_computation.1 | async-start | bytes 6684672 | tf_op jit(solution)/shard_map/all_to_all | solution.py:495
  55.4 1.3 collective-permute-start.6
  56.7 9.5 %collective-permute-start.7 = (bf16[1024,256]{1,0:T(8,128)(2,1)}, bf16[1024,256]{1,0:T(8,128)(2,1)}, u32[]{:S(2)}, u32[]{:S(2)}) collective-permute-start(bf16[1024,256]{1,0:T(8,128)(2,1)} %bitcast.60), channel_id=1, source_target_pairs={{0,16},{8,24},{16,0},{24,8},{1,17},{9,25},{17,1},{25,9},{2,18},{10... | collective-permute-start | bytes 1572872 | tf_op jit(solution)/shard_map/ppermute | solution.py:501
  66.2 2.1 collective-permute-start.8
  69.7 7.0 %collective-permute-done.6.refs_12_ = bf16[1024,256]{1,0:T(8,128)(2,1)} collective-permute-done((bf16[1024,256]{1,0:T(8,128)(2,1)}, bf16[1024,256]{1,0:T(8,128)(2,1)}, u32[]{:S(2)}, u32[]{:S(2)}) %collective-permute-start.6) | collective-permute-done | bytes 524320 | tf_op jit(solution)/shard_map/ppermute | solution.py:504
  76.7 13.9 %collective-permute-done.7.refs_10_ = bf16[1024,256]{1,0:T(8,128)(2,1)} collective-permute-done((bf16[1024,256]{1,0:T(8,128)(2,1)}, bf16[1024,256]{1,0:T(8,128)(2,1)}, u32[]{:S(2)}, u32[]{:S(2)}) %collective-permute-start.7) | collective-permute-done | bytes 524320 | tf_op jit(solution)/shard_map/ppermute | solution.py:501
  90.6 8.2 %collective-permute-done.9.refs_9_ = bf16[1024,256]{1,0:T(8,128)(2,1)} collective-permute-done((bf16[1024,256]{1,0:T(8,128)(2,1)}, bf16[1024,256]{1,0:T(8,128)(2,1)}, u32[]{:S(2)}, u32[]{:S(2)}) %collective-permute-start.9) | collective-permute-done | bytes 524320 | tf_op jit(solution)/shard_map/ppermute | solution.py:498
  98.8 2.0 all-to-all-done.1.refs_13_.refs_14_
  102.9 2.4 collective-permute-start.11
  105.3 4.2 %collective-permute-start.12 = (bf16[1024,256]{1,0:T(8,128)(2,1)}, bf16[1024,256]{1,0:T(8,128)(2,1)}, u32[]{:S(2)}, u32[]{:S(2)}) collective-permute-start(bf16[1024,256]{1,0:T(8,128)(2,1)} %bitcast.8.refs_8_), channel_id=1, source_target_pairs={{0,8},{8,16},{16,24},{1,9},{9,17},{17,25},{2,10},{10,18},{18,26},{... | collective-permute-start | bytes 1572872 | tf_op jit(solution)/shard_map/ppermute | solution.py:498
  110.8 1.3 collective-permute-start.10
  113.6 11.0 %fwd.4 = (bf16[4,256,128]{2,1,0:T(8,128)(2,1)}, bf16[1024,1024]{1,0:T(8,128)(2,1)}, bf16[4096,1024]{1,0:T(8,128)(2,1)}) custom-call(s32[35]{0:T(128)} %concatenate.56.tab, bf16[8,256,2048]{2,1,0:T(8,128)(2,1)} %bitcast.28, bf16[8,256,2048]{2,1,0:T(8,128)(2,1)} %bitcast.29, bf16[8,256,2048]{2,1,0:T(8,128)(2,1)} %bitcast.30, bf16[8,256,2048]{2,1,0:T(8,128)(2,1)} %bitcast.31, ...), custom_call_target="tpu_custom_call" | custom-call | flops 1 | bytes 1 | tf_op jit(solution)/shard_map/fwd/pallas_call | solution.py:283
  124.6 21.1 %collective-permute-done.10.refs_12_ = bf16[1024,256]{1,0:T(8,128)(2,1)} collective-permute-done((bf16[1024,256]{1,0:T(8,128)(2,1)}, bf16[1024,256]{1,0:T(8,128)(2,1)}, u32[]{:S(2)}, u32[]{:S(2)}) %collective-permute-start.10) | collective-permute-done | bytes 524320 | tf_op jit(solution)/shard_map/ppermute | solution.py:504
  145.7 2.1 collective-permute-start.14
  147.9 1.3 collective-permute-start.18
  149.2 11.0 %fwd.5 = (bf16[4,256,128]{2,1,0:T(8,128)(2,1)}, bf16[1024,1024]{1,0:T(8,128)(2,1)}, bf16[4096,1024]{1,0:T(8,128)(2,1)}) custom-call(s32[35]{0:T(128)} %concatenate.56.tab, bf16[8,256,2048]{2,1,0:T(8,128)(2,1)} %bitcast.43, bf16[8,256,2048]{2,1,0:T(8,128)(2,1)} %bitcast.37, ...), custom_call_target="tpu_custom_call", output_to_operand_aliasing={{1}: (16, {}), {2}: (17, {})} | custom-call | flops 1 | bytes 1 | tf_op jit(solution)/shard_map/fwd/pallas_call | solution.py:283
  160.1 6.3 %collective-permute-start.16 = (bf16[1024,256]{1,0:T(8,128)(2,1)}, bf16[1024,256]{1,0:T(8,128)(2,1)S(1)}, u32[]{:S(2)}, u32[]{:S(2)}) collective-permute-start(bf16[1024,256]{1,0:T(8,128)(2,1)} %bitcast.9.refs_8_), channel_id=1, source_target_pairs={{0,8},{8,16},{16,24},{1,9},{9,17},{17,25},{2,10},{10,18},{18,26},{... | collective-permute-start | bytes 1572872 | tf_op jit(solution)/shard_map/ppermute | solution.py:498
  167.8 1.8 pad_maximum_fusion.1
  169.6 3.7 %all-to-all-start.2 = ((bf16[4,256,256]{2,1,0:T(8,128)(2,1)}), bf16[4,256,256]{2,1,0:T(8,128)(2,1)S(1)}, u32[]{:S(2)}, u32[]{:S(2)}) async-start(bf16[4,256,256]{2,1,0:T(8,128)(2,1)} %pad_maximum_fusion.1), calls=%async_computation.2 | async-start | bytes 1048576 | tf_op jit(solution)/shard_map/all_to_all | solution.py:495
  173.2 2.7 collective-permute-done.18.refs_12_
  176.8 11.0 %fwd.6 = (bf16[4,256,128]{2,1,0:T(8,128)(2,1)}, bf16[1024,1024]{1,0:T(8,128)(2,1)}, bf16[4096,1024]{1,0:T(8,128)(2,1)}) custom-call(s32[35]{0:T(128)} %concatenate.56.tab, bf16[8,256,2048]{2,1,0:T(8,128)(2,1)} %bitcast.44, bf16[8,256,2048]{2,1,0:T(8,128)(2,1)} %bitcast.45, ...), custom_call_target="tpu_custom_call", output_to_operand_aliasing={{1}: (16, {}), {2}: (17, {})} | custom-call | flops 1 | bytes 1 | tf_op jit(solution)/shard_map/fwd/pallas_call | solution.py:283
  187.8 7.1 %collective-permute-done.17.refs_9_ = bf16[1024,256]{1,0:T(8,128)(2,1)S(1)} collective-permute-done((bf16[1024,256]{1,0:T(8,128)(2,1)}, bf16[1024,256]{1,0:T(8,128)(2,1)S(1)}, u32[]{:S(2)}, u32[]{:S(2)}) %collective-permute-start.17) | collective-permute-done | bytes 524320 | tf_op jit(solution)/shard_map/ppermute | solution.py:498
  195.8 11.0 %fwd.7 = (bf16[4,256,128]{2,1,0:T(8,128)(2,1)}, bf16[1024,1024]{1,0:T(8,128)(2,1)}, bf16[4096,1024]{1,0:T(8,128)(2,1)}) custom-call(s32[35]{0:T(128)} %concatenate.56.tab, bf16[8,256,2048]{2,1,0:T(8,128)(2,1)} %bitcast.52, bf16[8,256,2048]{2,1,0:T(8,128)(2,1)} %bitcast.53, ...), custom_call_target="tpu_custom_call", output_to_operand_aliasing={{1}: (16, {}), {2}: (17, {})} | custom-call | flops 1 | bytes 1 | tf_op jit(solution)/shard_map/fwd/pallas_call | solution.py:283
  206.8 5.5 %bwd.8 = bf16[512,2048]{1,0:T(8,128)(2,1)} custom-call(bf16[1024,1024]{1,0:T(8,128)(2,1)} %get-tuple-element.150.refs_0_, bf16[4096,1024]{1,0:T(8,128)(2,1)} %get-tuple-element.151.refs_1_), custom_call_target="tpu_custom_call" | custom-call | flops 1 | bytes 1 | tf_op jit(solution)/shard_map/bwd/pallas_call | solution.py:345
  212.3 5.6 %bwd.6 = bf16[512,2048]{1,0:T(8,128)(2,1)} custom-call(bf16[1024,1024]{1,0:T(8,128)(2,1)} %get-tuple-element.150.refs_0_, bf16[4096,1024]{1,0:T(8,128)(2,1)} %get-tuple-element.151.refs_1_), custom_call_target="tpu_custom_call" | custom-call | flops 1 | bytes 1 | tf_op jit(solution)/shard_map/bwd/pallas_call | solution.py:345
  218.8 1.5 collective-permute-start.22
  221.2 1.3 copy-done.3
  222.5 4.4 %bwd.9 = bf16[512,1024]{1,0:T(8,128)(2,1)} custom-call(bf16[1024,1024]{1,0:T(8,128)(2,1)} %get-tuple-element.150.refs_0_, bf16[4096,1024]{1,0:T(8,128)(2,1)} %get-tuple-element.151.refs_1_, bf16[512,2048]{1,0:T(8,128)(2,1)} %copy-done.3), custom_call_target="tpu_custom_call" | custom-call | flops 1 | bytes 1 | tf_op jit(solution)/shard_map/bwd/pallas_call | solution.py:345
  226.9 4.2 %bwd.7 = bf16[256,2048]{1,0:T(8,128)(2,1)} custom-call(bf16[1024,1024]{1,0:T(8,128)(2,1)} %get-tuple-element.150.refs_0_, bf16[4096,1024]{1,0:T(8,128)(2,1)} %get-tuple-element.151.refs_1_, bf16[512,2048]{1,0:T(8,128)(2,1)} %collective-permute-done.19.refs_2_), custom_call_target="tpu_custom_call" | custom-call | flops 1 | bytes 1 | tf_op jit(solution)/shard_map/bwd/pallas_call | solution.py:345
  231.9 1.6 collective-permute-start.25
  233.5 3.6 %gather_context.1 = bf16[256,2048]{1,0:T(8,128)(2,1)} custom-call(s32[1]{0:T(128)} %bitcast.7.tab, bf16[4,256,256]{2,1,0:T(8,128)(2,1)} %copy-done.6, bf16[256,256]{1,0:T(8,128)(2,1)} %pad_maximum_fusion.5.refs_0_, bf16[256,256]{1,0:T(8,128)(2,1)} %copy-done.21, bf16[256,256]{1,0:T(8,128)(2,1)} %copy-done.20, bf16[256,256]{1,0:T(8,128)(2,1)} %copy-done.19), custom_call_target="tpu_custom_call" | custom-call | flops 1 | bytes 1 | tf_op jit(solution)/shard_map/gather_context/pallas_call | solution.py:449
  237.1 4.8 %bwd.11.q_ref = f32[512,1024]{1,0:T(8,128)} custom-call(bf16[1024,1024]{1,0:T(8,128)(2,1)} %get-tuple-element.150.refs_0_, bf16[4096,1024]{1,0:T(8,128)(2,1)} %get-tuple-element.151.refs_1_, bf16[512,2048]{1,0:T(8,128)(2,1)} %copy-done.3), custom_call_target="tpu_custom_call" | custom-call | flops 1 | bytes 1 | tf_op jit(solution)/shard_map/bwd/pallas_call | solution.py:345
  241.9 4.5 %bwd.10.p_ref = f32[256,2048]{1,0:T(8,128)} custom-call(bf16[1024,1024]{1,0:T(8,128)(2,1)} %get-tuple-element.150.refs_0_, bf16[4096,1024]{1,0:T(8,128)(2,1)} %get-tuple-element.151.refs_1_, bf16[512,2048]{1,0:T(8,128)(2,1)} %collective-permute-done.19.refs_2_), custom_call_target="tpu_custom_call" | custom-call | flops 1 | bytes 1 | tf_op jit(solution)/shard_map/bwd/pallas_call | solution.py:345
  246.4 10.5 %collective-permute-done.24.got_y = bf16[256,2048]{1,0:T(8,128)(2,1)S(1)} collective-permute-done((bf16[256,2048]{1,0:T(8,128)(2,1)}, bf16[256,2048]{1,0:T(8,128)(2,1)S(1)}, u32[]{:S(2)}, u32[]{:S(2)}) %collective-permute-start.24) | collective-permute-done | bytes 1048608 | tf_op jit(solution)/shard_map/ppermute | solution.py:607
  257.2 1.5 collective-permute-start.27
  258.8 1.5 collective-permute-start.26
  260.4 10.2 %collective-permute-done.27.last_y = bf16[256,1024]{1,0:T(8,128)(2,1)S(1)} collective-permute-done((bf16[256,1024]{1,0:T(8,128)(2,1)S(1)}, bf16[256,1024]{1,0:T(8,128)(2,1)S(1)}, u32[]{:S(2)}, u32[]{:S(2)}) %collective-permute-start.27) | collective-permute-done | bytes 524320 | tf_op jit(solution)/shard_map/ppermute | solution.py:618
  (115 shorter events, 18.8 us)
Async XLA Ops:
  7.2 93.6 %all-gather.3.cloned.1.call-start = ((), (), s32[]{:S(2)}) async-start(), calls=%async_computation.3 | async-start | bytes 9437184 | tf_op jit(solution)/shard_map/all_gather | solution.py:517
  9.1 3.3 %collective-permute-start = (bf16[256,256]{1,0:T(8,128)(2,1)S(1)}, bf16[256,256]{1,0:T(8,128)(2,1)S(1)}, u32[]{:S(2)}, u32[]{:S(2)}) collective-permute-start(bf16[256,256]{1,0:T(8,128)(2,1)S(1)} %pad_maximum_fusion.2), channel_id=1, source_target_pairs={{0,2},{2,0},{4,6},{6,4},{1,3},{3,1},{5,7},{7,5},{8,10},{10,8},{12,... | collective-permute-start | bytes 393224 | tf_op jit(solution)/shard_map/ppermute | solution.py:515
  9.6 6.9 %collective-permute-start.1 = (bf16[256,256]{1,0:T(8,128)(2,1)S(1)}, bf16[256,256]{1,0:T(8,128)(2,1)S(1)}, u32[]{:S(2)}, u32[]{:S(2)}) collective-permute-start(bf16[256,256]{1,0:T(8,128)(2,1)S(1)} %pad_maximum_fusion.3), channel_id=1, source_target_pairs={{0,4},{2,6},{4,0},{6,2},{1,5},{3,7},{5,1},{7,3},{8,12},{10,14},{12... | collective-permute-start | bytes 393224 | tf_op jit(solution)/shard_map/ppermute | solution.py:515
  12.2 6.7 %collective-permute-start.2 = (bf16[256,256]{1,0:T(8,128)(2,1)S(1)}, bf16[256,256]{1,0:T(8,128)(2,1)S(1)}, u32[]{:S(2)}, u32[]{:S(2)}) collective-permute-start(bf16[256,256]{1,0:T(8,128)(2,1)S(1)} %pad_maximum_fusion.4), channel_id=1, source_target_pairs={{0,6},{2,4},{4,2},{6,0},{1,7},{3,5},{5,3},{7,1},{8,14},{10,12},{12... | collective-permute-start | bytes 393224 | tf_op jit(solution)/shard_map/ppermute | solution.py:515
  19.0 19.2 %copy-start.5 = (bf16[1024,256]{1,0:T(8,128)(2,1)}, bf16[1024,256]{1,0:T(8,128)(2,1)S(1)}, u32[]{:S(2)}) copy-start(bf16[1024,256]{1,0:T(8,128)(2,1)S(1)} %pad_maximum_fusion.refs_8_) | copy-start | bytes 1572868
  19.0 14.1 %copy-start.24 = (s32[1,4]{1,0:T(1,128)S(1)}, s32[1,4]{1,0:T(1,128)}, u32[]{:S(2)}) copy-start(s32[1,4]{1,0:T(1,128)} %param.11) | copy-start | bytes 52
  19.0 14.1 %copy-start.22 = (s32[4]{0:T(128)S(1)}, s32[4]{0:T(128)}, u32[]{:S(2)}) copy-start(s32[4]{0:T(128)} %param.10) | copy-start | bytes 52
  19.1 14.1 %copy-start.23 = (s32[4]{0:T(128)S(1)}, s32[4]{0:T(128)}, u32[]{:S(2)}) copy-start(s32[4]{0:T(128)} %param.9) | copy-start | bytes 52
  19.1 27.0 %collective-permute-start.3 = (bf16[1024,256]{1,0:T(8,128)(2,1)S(1)}, bf16[1024,256]{1,0:T(8,128)(2,1)S(1)}, u32[]{:S(2)}, u32[]{:S(2)}) collective-permute-start(bf16[1024,256]{1,0:T(8,128)(2,1)S(1)} %pad_maximum_fusion.refs_8_), channel_id=1, source_target_pairs={{0,16},{8,24},{16,0},{24,8},{1,17},{9,25},{17,1},{25,9},{2,18},{10... | collective-permute-start | bytes 1572872 | tf_op jit(solution)/shard_map/ppermute | solution.py:501
  21.7 24.3 %collective-permute-start.4 = (bf16[1024,256]{1,0:T(8,128)(2,1)S(1)}, bf16[1024,256]{1,0:T(8,128)(2,1)S(1)}, u32[]{:S(2)}, u32[]{:S(2)}) collective-permute-start(bf16[1024,256]{1,0:T(8,128)(2,1)S(1)} %pad_maximum_fusion.refs_8_), channel_id=1, source_target_pairs={{0,8},{8,16},{16,24},{1,9},{9,17},{17,25},{2,10},{10,18},{18,26},{... | collective-permute-start | bytes 1572872 | tf_op jit(solution)/shard_map/ppermute | solution.py:498
  25.2 25.5 %collective-permute-start.5 = (bf16[1024,256]{1,0:T(8,128)(2,1)S(1)}, bf16[1024,256]{1,0:T(8,128)(2,1)S(1)}, u32[]{:S(2)}, u32[]{:S(2)}) collective-permute-start(bf16[1024,256]{1,0:T(8,128)(2,1)S(1)} %pad_maximum_fusion.refs_8_), channel_id=1, source_target_pairs={{8,0},{16,8},{24,16},{9,1},{17,9},{25,17},{10,2},{18,10},{26,18},{... | collective-permute-start | bytes 1572872 | tf_op jit(solution)/shard_map/ppermute | solution.py:498
  29.7 21.0 %all-to-all-start = ((bf16[4,256,256]{2,1,0:T(8,128)(2,1)}), bf16[4,256,256]{2,1,0:T(8,128)(2,1)S(1)}, u32[]{:S(2)}, u32[]{:S(2)}) async-start(bf16[4,256,256]{2,1,0:T(8,128)(2,1)} %pack_weights.1), calls=%async_computation | async-start | bytes 1048576 | tf_op jit(solution)/shard_map/all_to_all | solution.py:495
  46.1 4.6 %copy-start.9 = (bf16[1024,256]{1,0:T(8,128)(2,1)}, bf16[1024,256]{1,0:T(8,128)(2,1)S(1)}, u32[]{:S(2)}) copy-start(bf16[1024,256]{1,0:T(8,128)(2,1)S(1)} %collective-permute-done.4.refs_11_) | copy-start | bytes 1572868
  51.7 49.1 %all-to-all-start.1 = ((bf16[4,272,1536]{2,1,0:T(8,128)(2,1)}), bf16[4,272,1536]{2,1,0:T(8,128)(2,1)S(1)}, u32[]{:S(2)}, u32[]{:S(2)}) async-start(bf16[4,272,1536]{2,1,0:T(8,128)(2,1)} %pack.1), calls=%async_computation.1 | async-start | bytes 6684672 | tf_op jit(solution)/shard_map/all_to_all | solution.py:495
  55.4 21.3 %collective-permute-start.6 = (bf16[1024,256]{1,0:T(8,128)(2,1)}, bf16[1024,256]{1,0:T(8,128)(2,1)}, u32[]{:S(2)}, u32[]{:S(2)}) collective-permute-start(bf16[1024,256]{1,0:T(8,128)(2,1)} %copy-done.8), channel_id=1, source_target_pairs={{8,0},{16,24},{9,1},{17,25},{10,2},{18,26},{11,3},{19,27},{12,4},{... | collective-permute-start | bytes 1572872 | tf_op jit(solution)/shard_map/ppermute | solution.py:504
  56.7 33.9 %collective-permute-start.7 = (bf16[1024,256]{1,0:T(8,128)(2,1)}, bf16[1024,256]{1,0:T(8,128)(2,1)}, u32[]{:S(2)}, u32[]{:S(2)}) collective-permute-start(bf16[1024,256]{1,0:T(8,128)(2,1)} %bitcast.60), channel_id=1, source_target_pairs={{0,16},{8,24},{16,0},{24,8},{1,17},{9,25},{17,1},{25,9},{2,18},{10... | collective-permute-start | bytes 1572872 | tf_op jit(solution)/shard_map/ppermute | solution.py:501
  66.2 24.3 %collective-permute-start.8 = (bf16[1024,256]{1,0:T(8,128)(2,1)}, bf16[1024,256]{1,0:T(8,128)(2,1)}, u32[]{:S(2)}, u32[]{:S(2)}) collective-permute-start(bf16[1024,256]{1,0:T(8,128)(2,1)} %bitcast.61), channel_id=1, source_target_pairs={{0,8},{8,16},{16,24},{1,9},{9,17},{17,25},{2,10},{10,18},{18,26},{... | collective-permute-start | bytes 1572872 | tf_op jit(solution)/shard_map/ppermute | solution.py:498
  68.3 30.5 %collective-permute-start.9 = (bf16[1024,256]{1,0:T(8,128)(2,1)}, bf16[1024,256]{1,0:T(8,128)(2,1)}, u32[]{:S(2)}, u32[]{:S(2)}) collective-permute-start(bf16[1024,256]{1,0:T(8,128)(2,1)} %bitcast.62), channel_id=1, source_target_pairs={{8,0},{16,8},{24,16},{9,1},{17,9},{25,17},{10,2},{18,10},{26,18},{... | collective-permute-start | bytes 1572872 | tf_op jit(solution)/shard_map/ppermute | solution.py:498
  100.8 12.8 %copy-start.2 = (bf16[4,272,1536]{2,1,0:T(8,128)(2,1)}, bf16[4,272,1536]{2,1,0:T(8,128)(2,1)S(1)}, u32[]{:S(2)}) copy-start(bf16[4,272,1536]{2,1,0:T(8,128)(2,1)S(1)} %all-to-all-done.1.refs_13_.refs_14_) | copy-start | bytes 10027012
  102.9 42.9 %collective-permute-start.11 = (bf16[1024,256]{1,0:T(8,128)(2,1)}, bf16[1024,256]{1,0:T(8,128)(2,1)}, u32[]{:S(2)}, u32[]{:S(2)}) collective-permute-start(bf16[1024,256]{1,0:T(8,128)(2,1)} %bitcast.8.refs_8_), channel_id=1, source_target_pairs={{0,16},{8,24},{16,0},{24,8},{1,17},{9,25},{17,1},{25,9},{2,18},{10... | collective-permute-start | bytes 1572872 | tf_op jit(solution)/shard_map/ppermute | solution.py:501
  105.3 40.5 %collective-permute-start.12 = (bf16[1024,256]{1,0:T(8,128)(2,1)}, bf16[1024,256]{1,0:T(8,128)(2,1)}, u32[]{:S(2)}, u32[]{:S(2)}) collective-permute-start(bf16[1024,256]{1,0:T(8,128)(2,1)} %bitcast.8.refs_8_), channel_id=1, source_target_pairs={{0,8},{8,16},{16,24},{1,9},{9,17},{17,25},{2,10},{10,18},{18,26},{... | collective-permute-start | bytes 1572872 | tf_op jit(solution)/shard_map/ppermute | solution.py:498
  109.5 36.2 %collective-permute-start.13 = (bf16[1024,256]{1,0:T(8,128)(2,1)}, bf16[1024,256]{1,0:T(8,128)(2,1)}, u32[]{:S(2)}, u32[]{:S(2)}) collective-permute-start(bf16[1024,256]{1,0:T(8,128)(2,1)} %bitcast.8.refs_8_), channel_id=1, source_target_pairs={{8,0},{16,8},{24,16},{9,1},{17,9},{25,17},{10,2},{18,10},{26,18},{... | collective-permute-start | bytes 1572872 | tf_op jit(solution)/shard_map/ppermute | solution.py:498
  110.8 34.9 %collective-permute-start.10 = (bf16[1024,256]{1,0:T(8,128)(2,1)}, bf16[1024,256]{1,0:T(8,128)(2,1)}, u32[]{:S(2)}, u32[]{:S(2)}) collective-permute-start(bf16[1024,256]{1,0:T(8,128)(2,1)} %collective-permute-done.7.refs_10_), channel_id=1, source_target_pairs={{8,0},{16,24},{9,1},{17,25},{10,2},{18,26},{11,3},{19,27},{12,4},{... | collective-permute-start | bytes 1572872 | tf_op jit(solution)/shard_map/ppermute | solution.py:504
  145.7 22.0 %copy-start.18 = (bf16[4,256,128]{2,1,0:T(8,128)(2,1)S(1)}, bf16[4,256,128]{2,1,0:T(8,128)(2,1)}, u32[]{:S(2)}) copy-start(bf16[4,256,128]{2,1,0:T(8,128)(2,1)} %get-tuple-element.136) | copy-start | bytes 786436
  145.7 42.0 %collective-permute-start.14 = (bf16[1024,256]{1,0:T(8,128)(2,1)}, bf16[1024,256]{1,0:T(8,128)(2,1)S(1)}, u32[]{:S(2)}, u32[]{:S(2)}) collective-permute-start(bf16[1024,256]{1,0:T(8,128)(2,1)} %bitcast.9.refs_8_), channel_id=1, source_target_pairs={{0,24},{24,0},{1,25},{25,1},{2,26},{26,2},{3,27},{27,3},{4,28},{28... | collective-permute-start | bytes 1572872 | tf_op jit(solution)/shard_map/ppermute | solution.py:576
  147.8 40.0 %collective-permute-start.15 = (bf16[1024,256]{1,0:T(8,128)(2,1)}, bf16[1024,256]{1,0:T(8,128)(2,1)S(1)}, u32[]{:S(2)}, u32[]{:S(2)}) collective-permute-start(bf16[1024,256]{1,0:T(8,128)(2,1)} %bitcast.9.refs_8_), channel_id=1, source_target_pairs={{0,16},{8,24},{16,0},{24,8},{1,17},{9,25},{17,1},{25,9},{2,18},{10... | collective-permute-start | bytes 1572872 | tf_op jit(solution)/shard_map/ppermute | solution.py:501
  147.9 28.1 %collective-permute-start.18 = (bf16[1024,256]{1,0:T(8,128)(2,1)}, bf16[1024,256]{1,0:T(8,128)(2,1)S(1)}, u32[]{:S(2)}, u32[]{:S(2)}) collective-permute-start(bf16[1024,256]{1,0:T(8,128)(2,1)} %collective-permute-done.11.refs_10_), channel_id=1, source_target_pairs={{8,0},{16,24},{9,1},{17,25},{10,2},{18,26},{11,3},{19,27},{12,4},{... | collective-permute-start | bytes 1572872 | tf_op jit(solution)/shard_map/ppermute | solution.py:504
  160.1 27.7 %collective-permute-start.16 = (bf16[1024,256]{1,0:T(8,128)(2,1)}, bf16[1024,256]{1,0:T(8,128)(2,1)S(1)}, u32[]{:S(2)}, u32[]{:S(2)}) collective-permute-start(bf16[1024,256]{1,0:T(8,128)(2,1)} %bitcast.9.refs_8_), channel_id=1, source_target_pairs={{0,8},{8,16},{16,24},{1,9},{9,17},{17,25},{2,10},{10,18},{18,26},{... | collective-permute-start | bytes 1572872 | tf_op jit(solution)/shard_map/ppermute | solution.py:498
  166.5 28.5 %collective-permute-start.17 = (bf16[1024,256]{1,0:T(8,128)(2,1)}, bf16[1024,256]{1,0:T(8,128)(2,1)S(1)}, u32[]{:S(2)}, u32[]{:S(2)}) collective-permute-start(bf16[1024,256]{1,0:T(8,128)(2,1)} %bitcast.9.refs_8_), channel_id=1, source_target_pairs={{8,0},{16,8},{24,16},{9,1},{17,9},{25,17},{10,2},{18,10},{26,18},{... | collective-permute-start | bytes 1572872 | tf_op jit(solution)/shard_map/ppermute | solution.py:498
  169.6 25.4 %all-to-all-start.2 = ((bf16[4,256,256]{2,1,0:T(8,128)(2,1)}), bf16[4,256,256]{2,1,0:T(8,128)(2,1)S(1)}, u32[]{:S(2)}, u32[]{:S(2)}) async-start(bf16[4,256,256]{2,1,0:T(8,128)(2,1)} %pad_maximum_fusion.1), calls=%async_computation.2 | async-start | bytes 1048576 | tf_op jit(solution)/shard_map/all_to_all | solution.py:495
  187.8 7.2 %copy-start.11 = (bf16[1024,256]{1,0:T(8,128)(2,1)}, bf16[1024,256]{1,0:T(8,128)(2,1)S(1)}, u32[]{:S(2)}) copy-start(bf16[1024,256]{1,0:T(8,128)(2,1)S(1)} %collective-permute-done.14.refs_12_) | copy-start | bytes 1572868
  187.8 7.2 %copy-start.12 = (bf16[1024,256]{1,0:T(8,128)(2,1)}, bf16[1024,256]{1,0:T(8,128)(2,1)S(1)}, u32[]{:S(2)}) copy-start(bf16[1024,256]{1,0:T(8,128)(2,1)S(1)} %collective-permute-done.15.refs_10_) | copy-start | bytes 1572868
  187.8 7.2 %copy-start.13 = (bf16[1024,256]{1,0:T(8,128)(2,1)}, bf16[1024,256]{1,0:T(8,128)(2,1)S(1)}, u32[]{:S(2)}) copy-start(bf16[1024,256]{1,0:T(8,128)(2,1)S(1)} %collective-permute-done.16.refs_11_) | copy-start | bytes 1572868
  195.0 11.8 %copy-start.6 = (bf16[4,256,256]{2,1,0:T(8,128)(2,1)}, bf16[4,256,256]{2,1,0:T(8,128)(2,1)S(1)}, u32[]{:S(2)}) copy-start(bf16[4,256,256]{2,1,0:T(8,128)(2,1)S(1)} %all-to-all-done.2.early) | copy-start | bytes 1572868
  212.3 6.0 %copy-start.17 = (bf16[4,256,128]{2,1,0:T(8,128)(2,1)S(1)}, bf16[4,256,128]{2,1,0:T(8,128)(2,1)}, u32[]{:S(2)}) copy-start(bf16[4,256,128]{2,1,0:T(8,128)(2,1)} %get-tuple-element.147) | copy-start | bytes 786436
  212.3 6.0 %copy-start.16 = (bf16[4,256,128]{2,1,0:T(8,128)(2,1)S(1)}, bf16[4,256,128]{2,1,0:T(8,128)(2,1)}, u32[]{:S(2)}) copy-start(bf16[4,256,128]{2,1,0:T(8,128)(2,1)} %get-tuple-element.146) | copy-start | bytes 786436
  212.3 8.9 %collective-permute-start.20 = (bf16[512,2048]{1,0:T(8,128)(2,1)}, bf16[512,2048]{1,0:T(8,128)(2,1)S(1)}, u32[]{:S(2)}, u32[]{:S(2)}) collective-permute-start(bf16[512,2048]{1,0:T(8,128)(2,1)} %bwd.8), channel_id=1, source_target_pairs={{0,2},{2,0},{4,6},{6,4},{1,3},{3,1},{5,7},{7,5},{8,10},{10,8},{12,... | collective-permute-start | bytes 6291464 | tf_op jit(solution)/shard_map/ppermute | solution.py:492
  217.9 9.1 %collective-permute-start.19 = (bf16[512,2048]{1,0:T(8,128)(2,1)}, bf16[512,2048]{1,0:T(8,128)(2,1)}, u32[]{:S(2)}, u32[]{:S(2)}) collective-permute-start(bf16[512,2048]{1,0:T(8,128)(2,1)} %bwd.6), channel_id=1, source_target_pairs={{0,2},{2,0},{4,6},{6,4},{1,3},{3,1},{5,7},{7,5},{8,10},{10,8},{12,... | collective-permute-start | bytes 6291464 | tf_op jit(solution)/shard_map/ppermute | solution.py:492
  218.4 12.8 %collective-permute-start.23 = (bf16[256,256]{1,0:T(8,128)(2,1)S(1)}, bf16[256,256]{1,0:T(8,128)(2,1)S(1)}, u32[]{:S(2)}, u32[]{:S(2)}) collective-permute-start(bf16[256,256]{1,0:T(8,128)(2,1)S(1)} %pad_maximum_fusion.8), channel_id=1, source_target_pairs={{0,6},{2,4},{4,2},{6,0},{1,7},{3,5},{5,3},{7,1},{8,14},{10,12},{12... | collective-permute-start | bytes 393224 | tf_op jit(solution)/shard_map/ppermute | solution.py:592
  218.8 12.4 %collective-permute-start.22 = (bf16[256,256]{1,0:T(8,128)(2,1)S(1)}, bf16[256,256]{1,0:T(8,128)(2,1)S(1)}, u32[]{:S(2)}, u32[]{:S(2)}) collective-permute-start(bf16[256,256]{1,0:T(8,128)(2,1)S(1)} %pad_maximum_fusion.7), channel_id=1, source_target_pairs={{0,4},{2,6},{4,0},{6,2},{1,5},{3,7},{5,1},{7,3},{8,12},{10,14},{12... | collective-permute-start | bytes 393224 | tf_op jit(solution)/shard_map/ppermute | solution.py:592
  220.3 10.9 %collective-permute-start.21 = (bf16[256,256]{1,0:T(8,128)(2,1)S(1)}, bf16[256,256]{1,0:T(8,128)(2,1)S(1)}, u32[]{:S(2)}, u32[]{:S(2)}) collective-permute-start(bf16[256,256]{1,0:T(8,128)(2,1)S(1)} %pad_maximum_fusion.6), channel_id=1, source_target_pairs={{0,2},{2,0},{4,6},{6,4},{1,3},{3,1},{5,7},{7,5},{8,10},{10,8},{12,... | collective-permute-start | bytes 393224 | tf_op jit(solution)/shard_map/ppermute | solution.py:592
  226.9 5.0 %copy-start.7 = (bf16[512,1024]{1,0:T(8,128)(2,1)S(1)}, bf16[512,1024]{1,0:T(8,128)(2,1)}, u32[]{:S(2)}) copy-start(bf16[512,1024]{1,0:T(8,128)(2,1)} %bwd.9) | copy-start | bytes 3145732
  231.2 25.7 %collective-permute-start.24 = (bf16[256,2048]{1,0:T(8,128)(2,1)}, bf16[256,2048]{1,0:T(8,128)(2,1)S(1)}, u32[]{:S(2)}, u32[]{:S(2)}) collective-permute-start(bf16[256,2048]{1,0:T(8,128)(2,1)} %bwd.7), channel_id=1, source_target_pairs={{0,4},{2,6},{4,0},{6,2},{1,5},{3,7},{5,1},{7,3},{8,12},{10,14},{12... | collective-permute-start | bytes 3145736 | tf_op jit(solution)/shard_map/ppermute | solution.py:607
  231.9 25.1 %collective-permute-start.25 = (bf16[512,1024]{1,0:T(8,128)(2,1)S(1)}, bf16[512,1024]{1,0:T(8,128)(2,1)S(1)}, u32[]{:S(2)}, u32[]{:S(2)}) collective-permute-start(bf16[512,1024]{1,0:T(8,128)(2,1)S(1)} %copy-done.7), channel_id=1, source_target_pairs={{0,1},{1,0},{2,3},{3,2},{4,5},{5,4},{6,7},{7,6},{8,9},{9,8},{10,11... | collective-permute-start | bytes 3145736 | tf_op jit(solution)/shard_map/ppermute | solution.py:608
  241.9 15.2 %copy-start = (f32[512,1024]{1,0:T(8,128)S(1)}, f32[512,1024]{1,0:T(8,128)}, u32[]{:S(2)}) copy-start(f32[512,1024]{1,0:T(8,128)} %bwd.11.q_ref) | copy-start | bytes 6291460
  246.4 12.3 %copy-start.1 = (f32[256,2048]{1,0:T(8,128)S(1)}, f32[256,2048]{1,0:T(8,128)}, u32[]{:S(2)}) copy-start(f32[256,2048]{1,0:T(8,128)} %bwd.10.p_ref) | copy-start | bytes 6291460
  257.2 13.3 %collective-permute-start.27 = (bf16[256,1024]{1,0:T(8,128)(2,1)S(1)}, bf16[256,1024]{1,0:T(8,128)(2,1)S(1)}, u32[]{:S(2)}, u32[]{:S(2)}) collective-permute-start(bf16[256,1024]{1,0:T(8,128)(2,1)S(1)} %add_convert_fusion), channel_id=1, source_target_pairs={{0,4},{2,6},{4,0},{6,2},{1,5},{3,7},{5,1},{7,3},{8,12},{10,14},{12... | collective-permute-start | bytes 1572872 | tf_op jit(solution)/shard_map/ppermute | solution.py:618
  258.8 12.8 %collective-permute-start.26 = (bf16[256,1024]{1,0:T(8,128)(2,1)S(1)}, bf16[256,1024]{1,0:T(8,128)(2,1)S(1)}, u32[]{:S(2)}, u32[]{:S(2)}) collective-permute-start(bf16[256,1024]{1,0:T(8,128)(2,1)S(1)} %add_convert_fusion.1), channel_id=1, source_target_pairs={{0,1},{1,0},{2,3},{3,2},{4,5},{5,4},{6,7},{7,6},{8,9},{9,8},{10,11... | collective-permute-start | bytes 1572872 | tf_op jit(solution)/shard_map/ppermute | solution.py:617
  (9 other events, 16.2 us)
Sparse Core Ops, SparseCore 0:
  9.9 63.5 all-gather.2

commit v7 on v6

--- a/solution.py
+++ b/solution.py
@@ -322,7 +322,7 @@
     row_n, row_at = rows
     span, blocks = cols
     depth = dkv.shape[1]
-    tile = 1024
+    tile = 1024 if len(blocks) > 1 else 512
     per_block = span // tile
 
     def col(i):

time: 281 us -> 281 us (level)
  no operation moved by 1% of the time
where the time goes in v7:
time: 281 us; the launch traced here: 279 us
  waiting for transfers between devices  104 us (37%)
  Pallas kernels  84.4 us (30%)
  starting transfers between devices  63.8 us (23%)
  between operations  14.5 us (5%)
  local copies, waits for them, and re-layouts  7.12 us (3%)
  other arithmetic  5.23 us (2%)
    pallas_call x4, Pallas kernels, forward_chunk(): pl.pallas_call(functools.partial(forward_kernel, n_dp, n_sec, n_half, blk...  44 us
    ppermute x3, waiting for transfers between devices, turn(): return lax.ppermute(far, 'section', ends)  30.8 us
    pallas_call x6, Pallas kernels, backward(): pl.pallas_call(backward_kernel, grid=(len(blocks) * per_block,), in_specs...  28.1 us
    ppermute x4, waiting for transfers between devices, beyond(): return lax.ppermute(piece, 'section', over_two)  21.8 us
    ppermute x4, waiting for transfers between devices, sides(): lax.ppermute(piece, 'section', down)  19.9 us
    ppermute x4, starting transfers between devices, sides(): lax.ppermute(piece, 'section', up)  16.1 us
    ppermute x4, starting transfers between devices, beyond(): return lax.ppermute(piece, 'section', over_two)  14.7 us
    ppermute x1, waiting for transfers between devices, shards_section(): got_y = lax.ppermute(send_y, 'dp', ypairs)  11 us
  transfers between devices with their start and end apart: 32, of which 15 were waited for; matrix products, arithmetic and copies ran while one was open for 2% of the time, Pallas kernels for 24%

profile of v7, /device:TPU:0, one launch (start us, length us, event | category | flops | bytes accessed | tf_op | source)
XLA Modules:
  0.0 279.4 jit_solution(1211891720154948794)
XLA Ops:
  9.6 2.6 collective-permute-start.1
  12.4 4.1 %collective-permute-done.1 = bf16[256,256]{1,0:T(8,128)(2,1)S(1)} collective-permute-done((bf16[256,256]{1,0:T(8,128)(2,1)S(1)}, bf16[256,256]{1,0:T(8,128)(2,1)S(1)}, u32[]{:S(2)}, u32[]{:S(2)}) %collective-permute-start.1) | collective-permute-done | bytes 131104 | tf_op jit(solution)/shard_map/ppermute | solution.py:515
  16.6 2.4 collective-permute-done.2
  19.1 2.7 collective-permute-start.3
  21.7 3.5 %collective-permute-start.4 = (bf16[1024,256]{1,0:T(8,128)(2,1)S(1)}, bf16[1024,256]{1,0:T(8,128)(2,1)S(1)}, u32[]{:S(2)}, u32[]{:S(2)}) collective-permute-start(bf16[1024,256]{1,0:T(8,128)(2,1)S(1)} %pad_maximum_fusion.refs_8_), channel_id=1, source_target_pairs={{0,8},{8,16},{16,24},{1,9},{9,17},{17,25},{2,10},{10,18},{18,26},{... | collective-permute-start | bytes 1572872 | tf_op jit(solution)/shard_map/ppermute | solution.py:498
  25.2 1.3 collective-permute-start.5
  26.5 3.1 %pack_weights.1 = bf16[4,256,256]{2,1,0:T(8,128)(2,1)} custom-call(bf16[256,2048]{1,0:T(8,128)(2,1)} %k_ref.1, bf16[256,2048]{1,0:T(8,128)(2,1)} %v_ref.1), custom_call_target="tpu_custom_call" | custom-call | flops 1 | bytes 1 | tf_op jit(solution)/shard_map/pack_weights/pallas_call | solution.py:392
  29.7 3.5 %all-to-all-start = ((bf16[4,256,256]{2,1,0:T(8,128)(2,1)}), bf16[4,256,256]{2,1,0:T(8,128)(2,1)S(1)}, u32[]{:S(2)}, u32[]{:S(2)}) async-start(bf16[4,256,256]{2,1,0:T(8,128)(2,1)} %pack_weights.1), calls=%async_computation | async-start | bytes 1048576 | tf_op jit(solution)/shard_map/all_to_all | solution.py:495
  33.9 4.3 %pack.1 = bf16[4,272,1536]{2,1,0:T(8,128)(2,1)} custom-call(bf16[256,2048]{1,0:T(8,128)(2,1)} %q_ref.1, bf16[256,2048]{1,0:T(8,128)(2,1)} %g_ref.1, bf16[256,2048]{1,0:T(8,128)(2,1)} %k_ref.1, bf16[256,2048]{1,0:T(8,128)(2,1)} %v_ref.1, bf16[16,128]{1,0:T(8,128)(2,1)} %fusion.8.small_ref), custom_call_target="tpu_custom_call" | custom-call | flops 1 | bytes 1 | tf_op jit(solution)/shard_map/pack/pallas_call | solution.py:423
  38.2 7.9 %collective-permute-done.3.refs_10_ = bf16[1024,256]{1,0:T(8,128)(2,1)S(1)} collective-permute-done((bf16[1024,256]{1,0:T(8,128)(2,1)S(1)}, bf16[1024,256]{1,0:T(8,128)(2,1)S(1)}, u32[]{:S(2)}, u32[]{:S(2)}) %collective-permute-start.3) | collective-permute-done | bytes 524320 | tf_op jit(solution)/shard_map/ppermute | solution.py:501
  46.1 4.6 %collective-permute-done.5.refs_9_ = bf16[1024,256]{1,0:T(8,128)(2,1)S(1)} collective-permute-done((bf16[1024,256]{1,0:T(8,128)(2,1)S(1)}, bf16[1024,256]{1,0:T(8,128)(2,1)S(1)}, u32[]{:S(2)}, u32[]{:S(2)}) %collective-permute-start.5) | collective-permute-done | bytes 524320 | tf_op jit(solution)/shard_map/ppermute | solution.py:498
  51.7 3.7 %all-to-all-start.1 = ((bf16[4,272,1536]{2,1,0:T(8,128)(2,1)}), bf16[4,272,1536]{2,1,0:T(8,128)(2,1)S(1)}, u32[]{:S(2)}, u32[]{:S(2)}) async-start(bf16[4,272,1536]{2,1,0:T(8,128)(2,1)} %pack.1), calls=%async_computation.1 | async-start | bytes 6684672 | tf_op jit(solution)/shard_map/all_to_all | solution.py:495
  55.4 1.3 collective-permute-start.6
  56.7 9.5 %collective-permute-start.7 = (bf16[1024,256]{1,0:T(8,128)(2,1)}, bf16[1024,256]{1,0:T(8,128)(2,1)}, u32[]{:S(2)}, u32[]{:S(2)}) collective-permute-start(bf16[1024,256]{1,0:T(8,128)(2,1)} %bitcast.60), channel_id=1, source_target_pairs={{0,16},{8,24},{16,0},{24,8},{1,17},{9,25},{17,1},{25,9},{2,18},{10... | collective-permute-start | bytes 1572872 | tf_op jit(solution)/shard_map/ppermute | solution.py:501
  66.2 2.1 collective-permute-start.8
  69.7 7.0 %collective-permute-done.6.refs_12_ = bf16[1024,256]{1,0:T(8,128)(2,1)} collective-permute-done((bf16[1024,256]{1,0:T(8,128)(2,1)}, bf16[1024,256]{1,0:T(8,128)(2,1)}, u32[]{:S(2)}, u32[]{:S(2)}) %collective-permute-start.6) | collective-permute-done | bytes 524320 | tf_op jit(solution)/shard_map/ppermute | solution.py:504
  76.7 13.9 %collective-permute-done.7.refs_10_ = bf16[1024,256]{1,0:T(8,128)(2,1)} collective-permute-done((bf16[1024,256]{1,0:T(8,128)(2,1)}, bf16[1024,256]{1,0:T(8,128)(2,1)}, u32[]{:S(2)}, u32[]{:S(2)}) %collective-permute-start.7) | collective-permute-done | bytes 524320 | tf_op jit(solution)/shard_map/ppermute | solution.py:501
  90.6 8.2 %collective-permute-done.9.refs_9_ = bf16[1024,256]{1,0:T(8,128)(2,1)} collective-permute-done((bf16[1024,256]{1,0:T(8,128)(2,1)}, bf16[1024,256]{1,0:T(8,128)(2,1)}, u32[]{:S(2)}, u32[]{:S(2)}) %collective-permute-start.9) | collective-permute-done | bytes 524320 | tf_op jit(solution)/shard_map/ppermute | solution.py:498
  98.8 2.0 all-to-all-done.1.refs_13_.refs_14_
  102.9 2.4 collective-permute-start.11
  105.3 4.2 %collective-permute-start.12 = (bf16[1024,256]{1,0:T(8,128)(2,1)}, bf16[1024,256]{1,0:T(8,128)(2,1)}, u32[]{:S(2)}, u32[]{:S(2)}) collective-permute-start(bf16[1024,256]{1,0:T(8,128)(2,1)} %bitcast.8.refs_8_), channel_id=1, source_target_pairs={{0,8},{8,16},{16,24},{1,9},{9,17},{17,25},{2,10},{10,18},{18,26},{... | collective-permute-start | bytes 1572872 | tf_op jit(solution)/shard_map/ppermute | solution.py:498
  110.8 1.3 collective-permute-start.10
  113.6 11.0 %fwd.4 = (bf16[4,256,128]{2,1,0:T(8,128)(2,1)}, bf16[1024,1024]{1,0:T(8,128)(2,1)}, bf16[4096,1024]{1,0:T(8,128)(2,1)}) custom-call(s32[35]{0:T(128)} %concatenate.56.tab, bf16[8,256,2048]{2,1,0:T(8,128)(2,1)} %bitcast.28, bf16[8,256,2048]{2,1,0:T(8,128)(2,1)} %bitcast.29, bf16[8,256,2048]{2,1,0:T(8,128)(2,1)} %bitcast.30, bf16[8,256,2048]{2,1,0:T(8,128)(2,1)} %bitcast.31, ...), custom_call_target="tpu_custom_call" | custom-call | flops 1 | bytes 1 | tf_op jit(solution)/shard_map/fwd/pallas_call | solution.py:283
  124.6 21.1 %collective-permute-done.10.refs_12_ = bf16[1024,256]{1,0:T(8,128)(2,1)} collective-permute-done((bf16[1024,256]{1,0:T(8,128)(2,1)}, bf16[1024,256]{1,0:T(8,128)(2,1)}, u32[]{:S(2)}, u32[]{:S(2)}) %collective-permute-start.10) | collective-permute-done | bytes 524320 | tf_op jit(solution)/shard_map/ppermute | solution.py:504
  145.7 2.1 collective-permute-start.14
  147.9 1.3 collective-permute-start.18
  149.2 11.0 %fwd.5 = (bf16[4,256,128]{2,1,0:T(8,128)(2,1)}, bf16[1024,1024]{1,0:T(8,128)(2,1)}, bf16[4096,1024]{1,0:T(8,128)(2,1)}) custom-call(s32[35]{0:T(128)} %concatenate.56.tab, bf16[8,256,2048]{2,1,0:T(8,128)(2,1)} %bitcast.43, bf16[8,256,2048]{2,1,0:T(8,128)(2,1)} %bitcast.37, ...), custom_call_target="tpu_custom_call", output_to_operand_aliasing={{1}: (16, {}), {2}: (17, {})} | custom-call | flops 1 | bytes 1 | tf_op jit(solution)/shard_map/fwd/pallas_call | solution.py:283
  160.1 6.3 %collective-permute-start.16 = (bf16[1024,256]{1,0:T(8,128)(2,1)}, bf16[1024,256]{1,0:T(8,128)(2,1)S(1)}, u32[]{:S(2)}, u32[]{:S(2)}) collective-permute-start(bf16[1024,256]{1,0:T(8,128)(2,1)} %bitcast.9.refs_8_), channel_id=1, source_target_pairs={{0,8},{8,16},{16,24},{1,9},{9,17},{17,25},{2,10},{10,18},{18,26},{... | collective-permute-start | bytes 1572872 | tf_op jit(solution)/shard_map/ppermute | solution.py:498
  167.8 1.8 pad_maximum_fusion.1
  169.6 3.7 %all-to-all-start.2 = ((bf16[4,256,256]{2,1,0:T(8,128)(2,1)}), bf16[4,256,256]{2,1,0:T(8,128)(2,1)S(1)}, u32[]{:S(2)}, u32[]{:S(2)}) async-start(bf16[4,256,256]{2,1,0:T(8,128)(2,1)} %pad_maximum_fusion.1), calls=%async_computation.2 | async-start | bytes 1048576 | tf_op jit(solution)/shard_map/all_to_all | solution.py:495
  173.2 2.7 collective-permute-done.18.refs_12_
  176.8 11.0 %fwd.6 = (bf16[4,256,128]{2,1,0:T(8,128)(2,1)}, bf16[1024,1024]{1,0:T(8,128)(2,1)}, bf16[4096,1024]{1,0:T(8,128)(2,1)}) custom-call(s32[35]{0:T(128)} %concatenate.56.tab, bf16[8,256,2048]{2,1,0:T(8,128)(2,1)} %bitcast.44, bf16[8,256,2048]{2,1,0:T(8,128)(2,1)} %bitcast.45, ...), custom_call_target="tpu_custom_call", output_to_operand_aliasing={{1}: (16, {}), {2}: (17, {})} | custom-call | flops 1 | bytes 1 | tf_op jit(solution)/shard_map/fwd/pallas_call | solution.py:283
  187.8 7.1 %collective-permute-done.17.refs_9_ = bf16[1024,256]{1,0:T(8,128)(2,1)S(1)} collective-permute-done((bf16[1024,256]{1,0:T(8,128)(2,1)}, bf16[1024,256]{1,0:T(8,128)(2,1)S(1)}, u32[]{:S(2)}, u32[]{:S(2)}) %collective-permute-start.17) | collective-permute-done | bytes 524320 | tf_op jit(solution)/shard_map/ppermute | solution.py:498
  195.8 11.0 %fwd.7 = (bf16[4,256,128]{2,1,0:T(8,128)(2,1)}, bf16[1024,1024]{1,0:T(8,128)(2,1)}, bf16[4096,1024]{1,0:T(8,128)(2,1)}) custom-call(s32[35]{0:T(128)} %concatenate.56.tab, bf16[8,256,2048]{2,1,0:T(8,128)(2,1)} %bitcast.52, bf16[8,256,2048]{2,1,0:T(8,128)(2,1)} %bitcast.53, ...), custom_call_target="tpu_custom_call", output_to_operand_aliasing={{1}: (16, {}), {2}: (17, {})} | custom-call | flops 1 | bytes 1 | tf_op jit(solution)/shard_map/fwd/pallas_call | solution.py:283
  206.8 5.5 %bwd.8 = bf16[512,2048]{1,0:T(8,128)(2,1)} custom-call(bf16[1024,1024]{1,0:T(8,128)(2,1)} %get-tuple-element.150.refs_0_, bf16[4096,1024]{1,0:T(8,128)(2,1)} %get-tuple-element.151.refs_1_), custom_call_target="tpu_custom_call" | custom-call | flops 1 | bytes 1 | tf_op jit(solution)/shard_map/bwd/pallas_call | solution.py:345
  212.3 5.6 %bwd.6 = bf16[512,2048]{1,0:T(8,128)(2,1)} custom-call(bf16[1024,1024]{1,0:T(8,128)(2,1)} %get-tuple-element.150.refs_0_, bf16[4096,1024]{1,0:T(8,128)(2,1)} %get-tuple-element.151.refs_1_), custom_call_target="tpu_custom_call" | custom-call | flops 1 | bytes 1 | tf_op jit(solution)/shard_map/bwd/pallas_call | solution.py:345
  218.8 1.5 collective-permute-start.22
  221.2 1.3 copy-done.3
  222.5 4.0 %bwd.9 = bf16[512,1024]{1,0:T(8,128)(2,1)} custom-call(bf16[1024,1024]{1,0:T(8,128)(2,1)} %get-tuple-element.150.refs_0_, bf16[4096,1024]{1,0:T(8,128)(2,1)} %get-tuple-element.151.refs_1_, bf16[512,2048]{1,0:T(8,128)(2,1)} %copy-done.3), custom_call_target="tpu_custom_call" | custom-call | flops 1 | bytes 1 | tf_op jit(solution)/shard_map/bwd/pallas_call | solution.py:345
  226.5 4.3 %bwd.7 = bf16[256,2048]{1,0:T(8,128)(2,1)} custom-call(bf16[1024,1024]{1,0:T(8,128)(2,1)} %get-tuple-element.150.refs_0_, bf16[4096,1024]{1,0:T(8,128)(2,1)} %get-tuple-element.151.refs_1_, bf16[512,2048]{1,0:T(8,128)(2,1)} %collective-permute-done.19.refs_2_), custom_call_target="tpu_custom_call" | custom-call | flops 1 | bytes 1 | tf_op jit(solution)/shard_map/bwd/pallas_call | solution.py:345
  231.5 1.6 collective-permute-start.25
  233.1 3.6 %gather_context.1 = bf16[256,2048]{1,0:T(8,128)(2,1)} custom-call(s32[1]{0:T(128)} %bitcast.7.tab, bf16[4,256,256]{2,1,0:T(8,128)(2,1)} %copy-done.6, bf16[256,256]{1,0:T(8,128)(2,1)} %pad_maximum_fusion.5.refs_0_, bf16[256,256]{1,0:T(8,128)(2,1)} %copy-done.21, bf16[256,256]{1,0:T(8,128)(2,1)} %copy-done.20, bf16[256,256]{1,0:T(8,128)(2,1)} %copy-done.19), custom_call_target="tpu_custom_call" | custom-call | flops 1 | bytes 1 | tf_op jit(solution)/shard_map/gather_context/pallas_call | solution.py:449
  236.7 4.3 %bwd.11.q_ref = f32[512,1024]{1,0:T(8,128)} custom-call(bf16[1024,1024]{1,0:T(8,128)(2,1)} %get-tuple-element.150.refs_0_, bf16[4096,1024]{1,0:T(8,128)(2,1)} %get-tuple-element.151.refs_1_, bf16[512,2048]{1,0:T(8,128)(2,1)} %copy-done.3), custom_call_target="tpu_custom_call" | custom-call | flops 1 | bytes 1 | tf_op jit(solution)/shard_map/bwd/pallas_call | solution.py:345
  241.0 4.5 %bwd.10.p_ref = f32[256,2048]{1,0:T(8,128)} custom-call(bf16[1024,1024]{1,0:T(8,128)(2,1)} %get-tuple-element.150.refs_0_, bf16[4096,1024]{1,0:T(8,128)(2,1)} %get-tuple-element.151.refs_1_, bf16[512,2048]{1,0:T(8,128)(2,1)} %collective-permute-done.19.refs_2_), custom_call_target="tpu_custom_call" | custom-call | flops 1 | bytes 1 | tf_op jit(solution)/shard_map/bwd/pallas_call | solution.py:345
  245.5 11.0 %collective-permute-done.24.got_y = bf16[256,2048]{1,0:T(8,128)(2,1)S(1)} collective-permute-done((bf16[256,2048]{1,0:T(8,128)(2,1)}, bf16[256,2048]{1,0:T(8,128)(2,1)S(1)}, u32[]{:S(2)}, u32[]{:S(2)}) %collective-permute-start.24) | collective-permute-done | bytes 1048608 | tf_op jit(solution)/shard_map/ppermute | solution.py:607
  256.8 1.5 collective-permute-start.27
  258.4 1.5 collective-permute-start.26
  260.0 10.2 %collective-permute-done.27.last_y = bf16[256,1024]{1,0:T(8,128)(2,1)S(1)} collective-permute-done((bf16[256,1024]{1,0:T(8,128)(2,1)S(1)}, bf16[256,1024]{1,0:T(8,128)(2,1)S(1)}, u32[]{:S(2)}, u32[]{:S(2)}) %collective-permute-start.27) | collective-permute-done | bytes 524320 | tf_op jit(solution)/shard_map/ppermute | solution.py:618
  (115 shorter events, 18.8 us)
Async XLA Ops:
  7.2 93.6 %all-gather.3.cloned.1.call-start = ((), (), s32[]{:S(2)}) async-start(), calls=%async_computation.3 | async-start | bytes 9437184 | tf_op jit(solution)/shard_map/all_gather | solution.py:517
  9.1 3.3 %collective-permute-start = (bf16[256,256]{1,0:T(8,128)(2,1)S(1)}, bf16[256,256]{1,0:T(8,128)(2,1)S(1)}, u32[]{:S(2)}, u32[]{:S(2)}) collective-permute-start(bf16[256,256]{1,0:T(8,128)(2,1)S(1)} %pad_maximum_fusion.2), channel_id=1, source_target_pairs={{0,2},{2,0},{4,6},{6,4},{1,3},{3,1},{5,7},{7,5},{8,10},{10,8},{12,... | collective-permute-start | bytes 393224 | tf_op jit(solution)/shard_map/ppermute | solution.py:515
  9.6 6.9 %collective-permute-start.1 = (bf16[256,256]{1,0:T(8,128)(2,1)S(1)}, bf16[256,256]{1,0:T(8,128)(2,1)S(1)}, u32[]{:S(2)}, u32[]{:S(2)}) collective-permute-start(bf16[256,256]{1,0:T(8,128)(2,1)S(1)} %pad_maximum_fusion.3), channel_id=1, source_target_pairs={{0,4},{2,6},{4,0},{6,2},{1,5},{3,7},{5,1},{7,3},{8,12},{10,14},{12... | collective-permute-start | bytes 393224 | tf_op jit(solution)/shard_map/ppermute | solution.py:515
  12.2 6.7 %collective-permute-start.2 = (bf16[256,256]{1,0:T(8,128)(2,1)S(1)}, bf16[256,256]{1,0:T(8,128)(2,1)S(1)}, u32[]{:S(2)}, u32[]{:S(2)}) collective-permute-start(bf16[256,256]{1,0:T(8,128)(2,1)S(1)} %pad_maximum_fusion.4), channel_id=1, source_target_pairs={{0,6},{2,4},{4,2},{6,0},{1,7},{3,5},{5,3},{7,1},{8,14},{10,12},{12... | collective-permute-start | bytes 393224 | tf_op jit(solution)/shard_map/ppermute | solution.py:515
  19.0 19.2 %copy-start.5 = (bf16[1024,256]{1,0:T(8,128)(2,1)}, bf16[1024,256]{1,0:T(8,128)(2,1)S(1)}, u32[]{:S(2)}) copy-start(bf16[1024,256]{1,0:T(8,128)(2,1)S(1)} %pad_maximum_fusion.refs_8_) | copy-start | bytes 1572868
  19.0 14.1 %copy-start.24 = (s32[1,4]{1,0:T(1,128)S(1)}, s32[1,4]{1,0:T(1,128)}, u32[]{:S(2)}) copy-start(s32[1,4]{1,0:T(1,128)} %param.11) | copy-start | bytes 52
  19.0 14.1 %copy-start.22 = (s32[4]{0:T(128)S(1)}, s32[4]{0:T(128)}, u32[]{:S(2)}) copy-start(s32[4]{0:T(128)} %param.10) | copy-start | bytes 52
  19.1 14.1 %copy-start.23 = (s32[4]{0:T(128)S(1)}, s32[4]{0:T(128)}, u32[]{:S(2)}) copy-start(s32[4]{0:T(128)} %param.9) | copy-start | bytes 52
  19.1 27.0 %collective-permute-start.3 = (bf16[1024,256]{1,0:T(8,128)(2,1)S(1)}, bf16[1024,256]{1,0:T(8,128)(2,1)S(1)}, u32[]{:S(2)}, u32[]{:S(2)}) collective-permute-start(bf16[1024,256]{1,0:T(8,128)(2,1)S(1)} %pad_maximum_fusion.refs_8_), channel_id=1, source_target_pairs={{0,16},{8,24},{16,0},{24,8},{1,17},{9,25},{17,1},{25,9},{2,18},{10... | collective-permute-start | bytes 1572872 | tf_op jit(solution)/shard_map/ppermute | solution.py:501
  21.7 24.3 %collective-permute-start.4 = (bf16[1024,256]{1,0:T(8,128)(2,1)S(1)}, bf16[1024,256]{1,0:T(8,128)(2,1)S(1)}, u32[]{:S(2)}, u32[]{:S(2)}) collective-permute-start(bf16[1024,256]{1,0:T(8,128)(2,1)S(1)} %pad_maximum_fusion.refs_8_), channel_id=1, source_target_pairs={{0,8},{8,16},{16,24},{1,9},{9,17},{17,25},{2,10},{10,18},{18,26},{... | collective-permute-start | bytes 1572872 | tf_op jit(solution)/shard_map/ppermute | solution.py:498
  25.2 25.5 %collective-permute-start.5 = (bf16[1024,256]{1,0:T(8,128)(2,1)S(1)}, bf16[1024,256]{1,0:T(8,128)(2,1)S(1)}, u32[]{:S(2)}, u32[]{:S(2)}) collective-permute-start(bf16[1024,256]{1,0:T(8,128)(2,1)S(1)} %pad_maximum_fusion.refs_8_), channel_id=1, source_target_pairs={{8,0},{16,8},{24,16},{9,1},{17,9},{25,17},{10,2},{18,10},{26,18},{... | collective-permute-start | bytes 1572872 | tf_op jit(solution)/shard_map/ppermute | solution.py:498
  29.7 21.0 %all-to-all-start = ((bf16[4,256,256]{2,1,0:T(8,128)(2,1)}), bf16[4,256,256]{2,1,0:T(8,128)(2,1)S(1)}, u32[]{:S(2)}, u32[]{:S(2)}) async-start(bf16[4,256,256]{2,1,0:T(8,128)(2,1)} %pack_weights.1), calls=%async_computation | async-start | bytes 1048576 | tf_op jit(solution)/shard_map/all_to_all | solution.py:495
  46.1 4.6 %copy-start.9 = (bf16[1024,256]{1,0:T(8,128)(2,1)}, bf16[1024,256]{1,0:T(8,128)(2,1)S(1)}, u32[]{:S(2)}) copy-start(bf16[1024,256]{1,0:T(8,128)(2,1)S(1)} %collective-permute-done.4.refs_11_) | copy-start | bytes 1572868
  51.7 49.1 %all-to-all-start.1 = ((bf16[4,272,1536]{2,1,0:T(8,128)(2,1)}), bf16[4,272,1536]{2,1,0:T(8,128)(2,1)S(1)}, u32[]{:S(2)}, u32[]{:S(2)}) async-start(bf16[4,272,1536]{2,1,0:T(8,128)(2,1)} %pack.1), calls=%async_computation.1 | async-start | bytes 6684672 | tf_op jit(solution)/shard_map/all_to_all | solution.py:495
  55.4 21.3 %collective-permute-start.6 = (bf16[1024,256]{1,0:T(8,128)(2,1)}, bf16[1024,256]{1,0:T(8,128)(2,1)}, u32[]{:S(2)}, u32[]{:S(2)}) collective-permute-start(bf16[1024,256]{1,0:T(8,128)(2,1)} %copy-done.8), channel_id=1, source_target_pairs={{8,0},{16,24},{9,1},{17,25},{10,2},{18,26},{11,3},{19,27},{12,4},{... | collective-permute-start | bytes 1572872 | tf_op jit(solution)/shard_map/ppermute | solution.py:504
  56.7 33.9 %collective-permute-start.7 = (bf16[1024,256]{1,0:T(8,128)(2,1)}, bf16[1024,256]{1,0:T(8,128)(2,1)}, u32[]{:S(2)}, u32[]{:S(2)}) collective-permute-start(bf16[1024,256]{1,0:T(8,128)(2,1)} %bitcast.60), channel_id=1, source_target_pairs={{0,16},{8,24},{16,0},{24,8},{1,17},{9,25},{17,1},{25,9},{2,18},{10... | collective-permute-start | bytes 1572872 | tf_op jit(solution)/shard_map/ppermute | solution.py:501
  66.2 24.3 %collective-permute-start.8 = (bf16[1024,256]{1,0:T(8,128)(2,1)}, bf16[1024,256]{1,0:T(8,128)(2,1)}, u32[]{:S(2)}, u32[]{:S(2)}) collective-permute-start(bf16[1024,256]{1,0:T(8,128)(2,1)} %bitcast.61), channel_id=1, source_target_pairs={{0,8},{8,16},{16,24},{1,9},{9,17},{17,25},{2,10},{10,18},{18,26},{... | collective-permute-start | bytes 1572872 | tf_op jit(solution)/shard_map/ppermute | solution.py:498
  68.3 30.5 %collective-permute-start.9 = (bf16[1024,256]{1,0:T(8,128)(2,1)}, bf16[1024,256]{1,0:T(8,128)(2,1)}, u32[]{:S(2)}, u32[]{:S(2)}) collective-permute-start(bf16[1024,256]{1,0:T(8,128)(2,1)} %bitcast.62), channel_id=1, source_target_pairs={{8,0},{16,8},{24,16},{9,1},{17,9},{25,17},{10,2},{18,10},{26,18},{... | collective-permute-start | bytes 1572872 | tf_op jit(solution)/shard_map/ppermute | solution.py:498
  100.8 12.8 %copy-start.2 = (bf16[4,272,1536]{2,1,0:T(8,128)(2,1)}, bf16[4,272,1536]{2,1,0:T(8,128)(2,1)S(1)}, u32[]{:S(2)}) copy-start(bf16[4,272,1536]{2,1,0:T(8,128)(2,1)S(1)} %all-to-all-done.1.refs_13_.refs_14_) | copy-start | bytes 10027012
  102.9 42.9 %collective-permute-start.11 = (bf16[1024,256]{1,0:T(8,128)(2,1)}, bf16[1024,256]{1,0:T(8,128)(2,1)}, u32[]{:S(2)}, u32[]{:S(2)}) collective-permute-start(bf16[1024,256]{1,0:T(8,128)(2,1)} %bitcast.8.refs_8_), channel_id=1, source_target_pairs={{0,16},{8,24},{16,0},{24,8},{1,17},{9,25},{17,1},{25,9},{2,18},{10... | collective-permute-start | bytes 1572872 | tf_op jit(solution)/shard_map/ppermute | solution.py:501
  105.3 40.5 %collective-permute-start.12 = (bf16[1024,256]{1,0:T(8,128)(2,1)}, bf16[1024,256]{1,0:T(8,128)(2,1)}, u32[]{:S(2)}, u32[]{:S(2)}) collective-permute-start(bf16[1024,256]{1,0:T(8,128)(2,1)} %bitcast.8.refs_8_), channel_id=1, source_target_pairs={{0,8},{8,16},{16,24},{1,9},{9,17},{17,25},{2,10},{10,18},{18,26},{... | collective-permute-start | bytes 1572872 | tf_op jit(solution)/shard_map/ppermute | solution.py:498
  109.5 36.2 %collective-permute-start.13 = (bf16[1024,256]{1,0:T(8,128)(2,1)}, bf16[1024,256]{1,0:T(8,128)(2,1)}, u32[]{:S(2)}, u32[]{:S(2)}) collective-permute-start(bf16[1024,256]{1,0:T(8,128)(2,1)} %bitcast.8.refs_8_), channel_id=1, source_target_pairs={{8,0},{16,8},{24,16},{9,1},{17,9},{25,17},{10,2},{18,10},{26,18},{... | collective-permute-start | bytes 1572872 | tf_op jit(solution)/shard_map/ppermute | solution.py:498
  110.8 34.9 %collective-permute-start.10 = (bf16[1024,256]{1,0:T(8,128)(2,1)}, bf16[1024,256]{1,0:T(8,128)(2,1)}, u32[]{:S(2)}, u32[]{:S(2)}) collective-permute-start(bf16[1024,256]{1,0:T(8,128)(2,1)} %collective-permute-done.7.refs_10_), channel_id=1, source_target_pairs={{8,0},{16,24},{9,1},{17,25},{10,2},{18,26},{11,3},{19,27},{12,4},{... | collective-permute-start | bytes 1572872 | tf_op jit(solution)/shard_map/ppermute | solution.py:504
  145.7 22.0 %copy-start.18 = (bf16[4,256,128]{2,1,0:T(8,128)(2,1)S(1)}, bf16[4,256,128]{2,1,0:T(8,128)(2,1)}, u32[]{:S(2)}) copy-start(bf16[4,256,128]{2,1,0:T(8,128)(2,1)} %get-tuple-element.136) | copy-start | bytes 786436
  145.7 42.0 %collective-permute-start.14 = (bf16[1024,256]{1,0:T(8,128)(2,1)}, bf16[1024,256]{1,0:T(8,128)(2,1)S(1)}, u32[]{:S(2)}, u32[]{:S(2)}) collective-permute-start(bf16[1024,256]{1,0:T(8,128)(2,1)} %bitcast.9.refs_8_), channel_id=1, source_target_pairs={{0,24},{24,0},{1,25},{25,1},{2,26},{26,2},{3,27},{27,3},{4,28},{28... | collective-permute-start | bytes 1572872 | tf_op jit(solution)/shard_map/ppermute | solution.py:576
  147.8 40.0 %collective-permute-start.15 = (bf16[1024,256]{1,0:T(8,128)(2,1)}, bf16[1024,256]{1,0:T(8,128)(2,1)S(1)}, u32[]{:S(2)}, u32[]{:S(2)}) collective-permute-start(bf16[1024,256]{1,0:T(8,128)(2,1)} %bitcast.9.refs_8_), channel_id=1, source_target_pairs={{0,16},{8,24},{16,0},{24,8},{1,17},{9,25},{17,1},{25,9},{2,18},{10... | collective-permute-start | bytes 1572872 | tf_op jit(solution)/shard_map/ppermute | solution.py:501
  147.9 28.1 %collective-permute-start.18 = (bf16[1024,256]{1,0:T(8,128)(2,1)}, bf16[1024,256]{1,0:T(8,128)(2,1)S(1)}, u32[]{:S(2)}, u32[]{:S(2)}) collective-permute-start(bf16[1024,256]{1,0:T(8,128)(2,1)} %collective-permute-done.11.refs_10_), channel_id=1, source_target_pairs={{8,0},{16,24},{9,1},{17,25},{10,2},{18,26},{11,3},{19,27},{12,4},{... | collective-permute-start | bytes 1572872 | tf_op jit(solution)/shard_map/ppermute | solution.py:504
  160.1 27.7 %collective-permute-start.16 = (bf16[1024,256]{1,0:T(8,128)(2,1)}, bf16[1024,256]{1,0:T(8,128)(2,1)S(1)}, u32[]{:S(2)}, u32[]{:S(2)}) collective-permute-start(bf16[1024,256]{1,0:T(8,128)(2,1)} %bitcast.9.refs_8_), channel_id=1, source_target_pairs={{0,8},{8,16},{16,24},{1,9},{9,17},{17,25},{2,10},{10,18},{18,26},{... | collective-permute-start | bytes 1572872 | tf_op jit(solution)/shard_map/ppermute | solution.py:498
  166.5 28.5 %collective-permute-start.17 = (bf16[1024,256]{1,0:T(8,128)(2,1)}, bf16[1024,256]{1,0:T(8,128)(2,1)S(1)}, u32[]{:S(2)}, u32[]{:S(2)}) collective-permute-start(bf16[1024,256]{1,0:T(8,128)(2,1)} %bitcast.9.refs_8_), channel_id=1, source_target_pairs={{8,0},{16,8},{24,16},{9,1},{17,9},{25,17},{10,2},{18,10},{26,18},{... | collective-permute-start | bytes 1572872 | tf_op jit(solution)/shard_map/ppermute | solution.py:498
  169.6 25.4 %all-to-all-start.2 = ((bf16[4,256,256]{2,1,0:T(8,128)(2,1)}), bf16[4,256,256]{2,1,0:T(8,128)(2,1)S(1)}, u32[]{:S(2)}, u32[]{:S(2)}) async-start(bf16[4,256,256]{2,1,0:T(8,128)(2,1)} %pad_maximum_fusion.1), calls=%async_computation.2 | async-start | bytes 1048576 | tf_op jit(solution)/shard_map/all_to_all | solution.py:495
  187.8 7.2 %copy-start.11 = (bf16[1024,256]{1,0:T(8,128)(2,1)}, bf16[1024,256]{1,0:T(8,128)(2,1)S(1)}, u32[]{:S(2)}) copy-start(bf16[1024,256]{1,0:T(8,128)(2,1)S(1)} %collective-permute-done.14.refs_12_) | copy-start | bytes 1572868
  187.8 7.2 %copy-start.12 = (bf16[1024,256]{1,0:T(8,128)(2,1)}, bf16[1024,256]{1,0:T(8,128)(2,1)S(1)}, u32[]{:S(2)}) copy-start(bf16[1024,256]{1,0:T(8,128)(2,1)S(1)} %collective-permute-done.15.refs_10_) | copy-start | bytes 1572868
  187.8 7.2 %copy-start.13 = (bf16[1024,256]{1,0:T(8,128)(2,1)}, bf16[1024,256]{1,0:T(8,128)(2,1)S(1)}, u32[]{:S(2)}) copy-start(bf16[1024,256]{1,0:T(8,128)(2,1)S(1)} %collective-permute-done.16.refs_11_) | copy-start | bytes 1572868
  195.0 11.8 %copy-start.6 = (bf16[4,256,256]{2,1,0:T(8,128)(2,1)}, bf16[4,256,256]{2,1,0:T(8,128)(2,1)S(1)}, u32[]{:S(2)}) copy-start(bf16[4,256,256]{2,1,0:T(8,128)(2,1)S(1)} %all-to-all-done.2.early) | copy-start | bytes 1572868
  212.3 6.0 %copy-start.17 = (bf16[4,256,128]{2,1,0:T(8,128)(2,1)S(1)}, bf16[4,256,128]{2,1,0:T(8,128)(2,1)}, u32[]{:S(2)}) copy-start(bf16[4,256,128]{2,1,0:T(8,128)(2,1)} %get-tuple-element.147) | copy-start | bytes 786436
  212.3 6.0 %copy-start.16 = (bf16[4,256,128]{2,1,0:T(8,128)(2,1)S(1)}, bf16[4,256,128]{2,1,0:T(8,128)(2,1)}, u32[]{:S(2)}) copy-start(bf16[4,256,128]{2,1,0:T(8,128)(2,1)} %get-tuple-element.146) | copy-start | bytes 786436
  212.3 8.9 %collective-permute-start.20 = (bf16[512,2048]{1,0:T(8,128)(2,1)}, bf16[512,2048]{1,0:T(8,128)(2,1)S(1)}, u32[]{:S(2)}, u32[]{:S(2)}) collective-permute-start(bf16[512,2048]{1,0:T(8,128)(2,1)} %bwd.8), channel_id=1, source_target_pairs={{0,2},{2,0},{4,6},{6,4},{1,3},{3,1},{5,7},{7,5},{8,10},{10,8},{12,... | collective-permute-start | bytes 6291464 | tf_op jit(solution)/shard_map/ppermute | solution.py:492
  217.9 8.7 %collective-permute-start.19 = (bf16[512,2048]{1,0:T(8,128)(2,1)}, bf16[512,2048]{1,0:T(8,128)(2,1)}, u32[]{:S(2)}, u32[]{:S(2)}) collective-permute-start(bf16[512,2048]{1,0:T(8,128)(2,1)} %bwd.6), channel_id=1, source_target_pairs={{0,2},{2,0},{4,6},{6,4},{1,3},{3,1},{5,7},{7,5},{8,10},{10,8},{12,... | collective-permute-start | bytes 6291464 | tf_op jit(solution)/shard_map/ppermute | solution.py:492
  218.4 12.4 %collective-permute-start.23 = (bf16[256,256]{1,0:T(8,128)(2,1)S(1)}, bf16[256,256]{1,0:T(8,128)(2,1)S(1)}, u32[]{:S(2)}, u32[]{:S(2)}) collective-permute-start(bf16[256,256]{1,0:T(8,128)(2,1)S(1)} %pad_maximum_fusion.8), channel_id=1, source_target_pairs={{0,6},{2,4},{4,2},{6,0},{1,7},{3,5},{5,3},{7,1},{8,14},{10,12},{12... | collective-permute-start | bytes 393224 | tf_op jit(solution)/shard_map/ppermute | solution.py:592
  218.8 12.1 %collective-permute-start.22 = (bf16[256,256]{1,0:T(8,128)(2,1)S(1)}, bf16[256,256]{1,0:T(8,128)(2,1)S(1)}, u32[]{:S(2)}, u32[]{:S(2)}) collective-permute-start(bf16[256,256]{1,0:T(8,128)(2,1)S(1)} %pad_maximum_fusion.7), channel_id=1, source_target_pairs={{0,4},{2,6},{4,0},{6,2},{1,5},{3,7},{5,1},{7,3},{8,12},{10,14},{12... | collective-permute-start | bytes 393224 | tf_op jit(solution)/shard_map/ppermute | solution.py:592
  220.3 10.6 %collective-permute-start.21 = (bf16[256,256]{1,0:T(8,128)(2,1)S(1)}, bf16[256,256]{1,0:T(8,128)(2,1)S(1)}, u32[]{:S(2)}, u32[]{:S(2)}) collective-permute-start(bf16[256,256]{1,0:T(8,128)(2,1)S(1)} %pad_maximum_fusion.6), channel_id=1, source_target_pairs={{0,2},{2,0},{4,6},{6,4},{1,3},{3,1},{5,7},{7,5},{8,10},{10,8},{12,... | collective-permute-start | bytes 393224 | tf_op jit(solution)/shard_map/ppermute | solution.py:592
  226.5 5.0 %copy-start.7 = (bf16[512,1024]{1,0:T(8,128)(2,1)S(1)}, bf16[512,1024]{1,0:T(8,128)(2,1)}, u32[]{:S(2)}) copy-start(bf16[512,1024]{1,0:T(8,128)(2,1)} %bwd.9) | copy-start | bytes 3145732
  230.8 25.7 %collective-permute-start.24 = (bf16[256,2048]{1,0:T(8,128)(2,1)}, bf16[256,2048]{1,0:T(8,128)(2,1)S(1)}, u32[]{:S(2)}, u32[]{:S(2)}) collective-permute-start(bf16[256,2048]{1,0:T(8,128)(2,1)} %bwd.7), channel_id=1, source_target_pairs={{0,4},{2,6},{4,0},{6,2},{1,5},{3,7},{5,1},{7,3},{8,12},{10,14},{12... | collective-permute-start | bytes 3145736 | tf_op jit(solution)/shard_map/ppermute | solution.py:607
  231.5 25.1 %collective-permute-start.25 = (bf16[512,1024]{1,0:T(8,128)(2,1)S(1)}, bf16[512,1024]{1,0:T(8,128)(2,1)S(1)}, u32[]{:S(2)}, u32[]{:S(2)}) collective-permute-start(bf16[512,1024]{1,0:T(8,128)(2,1)S(1)} %copy-done.7), channel_id=1, source_target_pairs={{0,1},{1,0},{2,3},{3,2},{4,5},{5,4},{6,7},{7,6},{8,9},{9,8},{10,11... | collective-permute-start | bytes 3145736 | tf_op jit(solution)/shard_map/ppermute | solution.py:608
  241.0 15.7 %copy-start = (f32[512,1024]{1,0:T(8,128)S(1)}, f32[512,1024]{1,0:T(8,128)}, u32[]{:S(2)}) copy-start(f32[512,1024]{1,0:T(8,128)} %bwd.11.q_ref) | copy-start | bytes 6291460
  245.5 12.8 %copy-start.1 = (f32[256,2048]{1,0:T(8,128)S(1)}, f32[256,2048]{1,0:T(8,128)}, u32[]{:S(2)}) copy-start(f32[256,2048]{1,0:T(8,128)} %bwd.10.p_ref) | copy-start | bytes 6291460
  256.8 13.3 %collective-permute-start.27 = (bf16[256,1024]{1,0:T(8,128)(2,1)S(1)}, bf16[256,1024]{1,0:T(8,128)(2,1)S(1)}, u32[]{:S(2)}, u32[]{:S(2)}) collective-permute-start(bf16[256,1024]{1,0:T(8,128)(2,1)S(1)} %add_convert_fusion), channel_id=1, source_target_pairs={{0,4},{2,6},{4,0},{6,2},{1,5},{3,7},{5,1},{7,3},{8,12},{10,14},{12... | collective-permute-start | bytes 1572872 | tf_op jit(solution)/shard_map/ppermute | solution.py:618
  258.4 12.8 %collective-permute-start.26 = (bf16[256,1024]{1,0:T(8,128)(2,1)S(1)}, bf16[256,1024]{1,0:T(8,128)(2,1)S(1)}, u32[]{:S(2)}, u32[]{:S(2)}) collective-permute-start(bf16[256,1024]{1,0:T(8,128)(2,1)S(1)} %add_convert_fusion.1), channel_id=1, source_target_pairs={{0,1},{1,0},{2,3},{3,2},{4,5},{5,4},{6,7},{7,6},{8,9},{9,8},{10,11... | collective-permute-start | bytes 1572872 | tf_op jit(solution)/shard_map/ppermute | solution.py:617
  (9 other events, 16.2 us)
Sparse Core Ops, SparseCore 0:
  9.9 63.5 all-gather.2
